TPU v7x, 32 devices: a whole 2x2x4 slice. The times are simulated.
32 devices in a mesh: groups: 2 (over x), ctx: 16 (over z, y, core).
Axes of the slice: x: 2, y: 2, z: 4, core: 2. Of those that a mesh axis runs over, the one named last changes fastest.
Arguments:
- queries: bfloat16 [16384, 1024], P(('groups', 'ctx')), parts along dimension 0, may hold values from -24 to 24
- key_rows: bfloat16 [16384, 1024], P(('groups', 'ctx')), parts along dimension 0, may hold values from -12 to 12
- value_rows: bfloat16 [16384, 1024], P(('groups', 'ctx')), parts along dimension 0, may hold values from -6 to 6
- step_rates: float32 [2, 16384], P(None, ('groups', 'ctx')), parts along dimension 1, may hold values from 0.002 to 0.02
- w_gate: bfloat16 [2048, 512], P('groups'), parts along dimension 0, may hold values from -2 to 2
- w_up: bfloat16 [2048, 512], P('groups'), parts along dimension 0, may hold values from -2 to 2
- w_down: bfloat16 [2048, 512], P('groups'), parts along dimension 0, may hold values from -2 to 2
Outputs:
- layer_out: bfloat16 [16384, 1024], P(('groups', 'ctx')), parts along dimension 0
- new_weights: bfloat16 [6144, 512], P(('groups', 'ctx')), parts along dimension 0
There are 2 independent parts, one for each index of `groups`. A program takes and returns all parts, laid end to end along the dimension named above; each array names one. Nothing has to cross between parts.
All inputs are finite; a program needn't handle non-finite values.
Results may differ from a plain program's by a relative error of at most 0.012.
The roundings to bfloat16 on the way count: a program that leaves them out, or rounds other values in their place, can miss the bound.
Values may be sent and summed in bfloat16 or wider, within the bound.
No kernel may reach another device: no remote copies, remote signals or barrier semaphores. Data moves between devices by JAX's collectives and lax.ppermute only.
A program may use at most 64 MiB of HBM per device.

v0:
```python
import math

import jax
import jax.numpy as jnp
from jax import lax
from jax.sharding import PartitionSpec as P

H = 2
HD = 512
WINDOW = 1024


def passed_along(value, axis, steps):
    count = lax.axis_size(axis)
    leading, last = (max(0, -steps), min(count, count - steps))
    return lax.ppermute(value, axis, [(source, source + steps) for source in range(leading, last)])


def rms_rows(row_values):
    values = row_values.astype(jnp.float32).reshape(row_values.shape[0], H, HD)
    return (values * lax.rsqrt(jnp.mean(values * values, -1, keepdims=True) + 1e-06)).astype(
        jnp.bfloat16
    )


def normalize_rows(old_rows, grad_rows):
    old_values = old_rows.astype(jnp.float32)
    raised = old_values - grad_rows
    factor = jnp.sqrt(jnp.mean(old_values * old_values, -1, keepdims=True) + 1e-06) * lax.rsqrt(
        jnp.mean(raised * raised, -1, keepdims=True) + 1e-06
    )
    return (raised * factor).astype(jnp.bfloat16)


def local(queries, key_rows, value_rows, step_rates, w_gate, w_up, w_down):
    tok_rows = queries.shape[0]
    reach = WINDOW // tok_rows
    earlier_keys = []
    earlier_values = []
    for step in range(reach, 0, -1):
        moved = passed_along((key_rows, value_rows), "ctx", step)
        earlier_keys.append(moved[0])
        earlier_values.append(moved[1])
    all_keys = jnp.concatenate(earlier_keys + [key_rows], 0)
    all_values = jnp.concatenate(earlier_values + [value_rows], 0)
    own_start = lax.axis_index("ctx") * tok_rows
    block_rows = min(512, tok_rows)
    q_block = queries.reshape(block_rows, H, HD)
    k_block = all_keys.reshape(WINDOW + block_rows, H, HD)
    v_block = all_values.reshape(WINDOW + block_rows, H, HD)
    scores = jnp.einsum("qhd,khd->hqk", q_block, k_block, preferred_element_type=jnp.float32) * (
        1.0 / math.sqrt(HD)
    )
    q_pos = 0 + jnp.arange(block_rows, dtype=jnp.int32)
    k_pos = 0 - WINDOW + jnp.arange(WINDOW + block_rows, dtype=jnp.int32)
    allowed = (
        (k_pos[None, :] <= q_pos[:, None])
        & (k_pos[None, :] > q_pos[:, None] - WINDOW)
        & (k_pos[None, :] + own_start >= 0)
    )
    scores = jnp.where(allowed[None], scores, -jnp.inf)
    highest = jnp.max(scores, -1, keepdims=True)
    expo = jnp.exp(scores - highest)
    weights = (expo / jnp.sum(expo, -1, keepdims=True)).astype(jnp.bfloat16)
    result = jnp.einsum("hqk,khd->qhd", weights, v_block, preferred_element_type=jnp.float32)
    pieces = result.astype(jnp.bfloat16)
    q_norm = rms_rows(queries)
    k_norm = rms_rows(key_rows)
    gate_m = w_gate.reshape(H, HD, HD)
    up_m = w_up.reshape(H, HD, HD)
    down_m = w_down.reshape(H, HD, HD)
    pre_gate = jnp.einsum("thd,hjd->thj", k_norm, gate_m, preferred_element_type=jnp.float32)
    pre_up = jnp.einsum("thd,hjd->thj", k_norm, up_m, preferred_element_type=jnp.float32)
    sig = jax.nn.sigmoid(pre_gate)
    active = pre_gate * sig
    gated = (active * pre_up).astype(jnp.bfloat16)
    errors = (-step_rates.T[:, :, None] * pieces.astype(jnp.float32)).astype(jnp.bfloat16)
    grad_down = jnp.einsum("tho,thj->hoj", errors, gated, preferred_element_type=jnp.float32)
    back = jnp.einsum("tho,hoj->thj", errors, down_m, preferred_element_type=jnp.float32)
    d_gate = (back * pre_up * sig * (1.0 + pre_gate * (1.0 - sig))).astype(jnp.bfloat16)
    d_up = (back * active).astype(jnp.bfloat16)
    grad_gate = jnp.einsum("thj,thd->hjd", d_gate, k_norm, preferred_element_type=jnp.float32)
    grad_up = jnp.einsum("thj,thd->hjd", d_up, k_norm, preferred_element_type=jnp.float32)
    grads = jnp.concatenate(
        [grad_gate.reshape(H * HD, HD), grad_up.reshape(H * HD, HD), grad_down.reshape(H * HD, HD)],
        0,
    )
    old_rows = jnp.concatenate([w_gate, w_up, w_down], 0)
    own_count = grads.shape[0] // lax.axis_size("ctx")
    own_first = lax.axis_index("ctx") * own_count
    summed = lax.psum(grads, "ctx")
    fresh = normalize_rows(old_rows, summed)
    own_weights = lax.dynamic_slice_in_dim(fresh, own_first, own_count, 0)
    new_gate = fresh[: H * HD].reshape(H, HD, HD)
    new_up = fresh[H * HD : 2 * H * HD].reshape(H, HD, HD)
    new_down = fresh[2 * H * HD :].reshape(H, HD, HD)
    q_gate = jnp.einsum("thd,hjd->thj", q_norm, new_gate, preferred_element_type=jnp.float32)
    q_up = jnp.einsum("thd,hjd->thj", q_norm, new_up, preferred_element_type=jnp.float32)
    q_gated = (q_gate * jax.nn.sigmoid(q_gate) * q_up).astype(jnp.bfloat16)
    fast_out = jnp.einsum("thj,hoj->tho", q_gated, new_down, preferred_element_type=jnp.float32)
    layer_out = (
        (pieces.astype(jnp.float32) + fast_out).astype(jnp.bfloat16).reshape(tok_rows, H * HD)
    )
    return (layer_out, own_weights)


def solution(mesh):
    return jax.shard_map(
        local,
        mesh=mesh,
        in_specs=(
            P(("groups", "ctx"), None),
            P(("groups", "ctx"), None),
            P(("groups", "ctx"), None),
            P(None, ("groups", "ctx")),
            P("groups", None),
            P("groups", None),
            P("groups", None),
        ),
        out_specs=(P(("groups", "ctx"), None), P(("groups", "ctx"), None)),
        check_vma=False,
    )
```

profile of v0, /device:TPU:0, one launch (start us, length us, event | category | flops | bytes accessed | tf_op | source)
XLA Modules:
  0.0 283.9 jit_solution(13785161849252597991)
XLA Ops:
  7.2 0.0 all-reduce.2.cloned.1.call-start
  7.2 1.5 copy.89
  8.7 5.9 %collective-permute-start.2 = (bf16[512,1024]{0,1:T(8,128)(2,1)S(1)}, bf16[512,1024]{0,1:T(8,128)(2,1)}, u32[]{:S(2)}, u32[]{:S(2)}) collective-permute-start(bf16[512,1024]{0,1:T(8,128)(2,1)S(1)} %copy.89), channel_id=1, source_target_pairs={{0,2},{1,3},{2,4},{3,5},{4,6},{5,7},{6,8},{7,9},{8,10},{9,11},{10,... | collective-permute-start | bytes 3145736 | tf_op jit(solution)/shard_map/ppermute | solution.py:16
  14.6 2.4 collective-permute-start.3
  17.0 3.0 %collective-permute-start = (bf16[512,1024]{1,0:T(8,128)(2,1)}, bf16[512,1024]{1,0:T(8,128)(2,1)}, u32[]{:S(2)}, u32[]{:S(2)}) collective-permute-start(bf16[512,1024]{1,0:T(8,128)(2,1)} %param.9), channel_id=1, source_target_pairs={{0,2},{1,3},{2,4},{3,5},{4,6},{5,7},{6,8},{7,9},{8,10},{9,11},{10,... | collective-permute-start | bytes 3145736 | tf_op jit(solution)/shard_map/ppermute | solution.py:16
  20.0 4.2 %collective-permute-start.1 = (bf16[512,1024]{1,0:T(8,128)(2,1)}, bf16[512,1024]{1,0:T(8,128)(2,1)}, u32[]{:S(2)}, u32[]{:S(2)}) collective-permute-start(bf16[512,1024]{1,0:T(8,128)(2,1)} %param.9), channel_id=1, source_target_pairs={{0,1},{1,2},{2,3},{3,4},{4,5},{5,6},{6,7},{7,8},{8,9},{9,10},{10,1... | collective-permute-start | bytes 3145736 | tf_op jit(solution)/shard_map/ppermute | solution.py:16
  24.2 0.2 multiply_reduce_fusion.1
  24.5 1.6 copy.99
  26.1 0.0 copy-start.5
  26.1 1.9 multiply_convert_fusion.1
  28.0 2.2 fusion.59
  30.2 0.0 copy-done.5
  30.2 2.1 fusion.58
  32.3 2.0 fusion.7
  34.3 25.5 %collective-permute-done = bf16[512,1024]{1,0:T(8,128)(2,1)} collective-permute-done((bf16[512,1024]{1,0:T(8,128)(2,1)}, bf16[512,1024]{1,0:T(8,128)(2,1)}, u32[]{:S(2)}, u32[]{:S(2)}) %collective-permute-start) | collective-permute-done | bytes 1048608 | tf_op jit(solution)/shard_map/ppermute | solution.py:16
  59.7 0.0 collective-permute-done.1
  59.7 3.0 %pad_maximum_fusion.1 = bf16[1536,1024]{1,0:T(8,128)(2,1)} fusion(bf16[512,1024]{1,0:T(8,128)(2,1)S(1)} %copy-done.14, bf16[512,1024]{1,0:T(8,128)(2,1)} %collective-permute-done.1, bf16[512,1024]{1,0:T(8,128)(2,1)} %collective-permute-done), kind=kLoop, calls=%fused_computation.11 | loop fusion | flops 9437184 | bytes 6291456 | tf_op jit(solution)/shard_map/concatenate | solution.py:45
  62.8 4.7 %copy.88 = bf16[1536,1024]{0,1:T(8,128)(2,1)} copy(bf16[1536,1024]{1,0:T(8,128)(2,1)} %pad_maximum_fusion.1) | data formatting | bytes 6291456 | tf_op jit(solution)/shard_map/concatenate | solution.py:45
  67.5 0.0 collective-permute-done.2
  67.5 0.0 collective-permute-done.3
  67.5 1.9 pad_maximum_fusion.2
  69.4 2.4 fusion.31
  71.9 2.2 fusion.57
  74.1 0.4 copy-done.10
  74.5 7.7 %fusion.26 = bf16[2,512,512]{2,1,0:T(8,128)(2,1)} fusion(bf16[1536,2,512]{0,2,1:T(8,128)(2,1)} %bitcast.136, f32[2,512]{1,0:T(2,128)S(1)} %fusion.57, f32[2,1536,512]{2,1,0:T(8,128)} %copy-done.10, pred[512,1536]{0,1:T(8,128)(4,1)} %fusion.7), kind=kOutput, calls=%fused_computation.53 | convolution fusion | flops 1619003904 | bytes 11276288 | tf_op jit(solution)/shard_map/hqk,khd->qhd/dot_general | solution.py:65
  82.3 2.1 fusion.36
  84.4 0.9 fusion.27
  85.3 0.7 copy-done.12
  86.0 1.1 fusion.33
  87.1 0.1 copy-done.13
  87.2 1.0 fusion.29
  88.2 3.4 %pad_maximum_fusion = f32[3072,512]{1,0:T(8,128)} fusion(f32[1024,512]{1,0:T(8,128)S(1)} %bitcast.139, f32[1024,512]{1,0:T(8,128)S(1)} %bitcast.137, f32[1024,512]{1,0:T(8,128)S(1)} %bitcast.138), kind=kLoop, calls=%fused_computation.4 | loop fusion | flops 3145728 | bytes 12582912 | tf_op jit(solution)/shard_map/concatenate | solution.py:84
  91.6 0.0 all-reduce.2.cloned.1.call-update
  91.6 0.3 fusion.9
  91.9 162.4 %all-reduce.2.cloned.1.call-done = f32[3072,512]{1,0:T(8,128)} async-done(((f32[3072,512]{1,0:T(8,128)}), f32[3072,512]{1,0:T(8,128)}) %all-reduce.2.cloned.1.call-update) | async-done | bytes 6291472 | tf_op jit(solution)/shard_map/psum | solution.py:91
  254.3 0.0 copy-start.9
  254.3 4.4 %fusion.1 = (f32[3072]{0:T(1024)S(1)}, f32[3072]{0:T(1024)S(1)}) fusion(bf16[1024,512]{1,0:T(8,128)(2,1)S(1)} %copy-done.3, bf16[1024,512]{1,0:T(8,128)(2,1)S(1)} %copy-done.6, bf16[1024,512]{1,0:T(8,128)(2,1)} %param.11, f32[3072,512]{1,0:T(8,128)} %all-reduce.2.cloned.1.call-done), kind=kLoop, calls=%fused_computation.3 | loop fusion | flops 17295360 | bytes 9461760 | tf_op jit(solution)/shard_map/reduce_sum | solution.py:29
  258.8 0.5 copy-done
  259.2 0.3 copy-done.4
  259.5 0.3 copy-done.7
  259.8 0.3 copy-done.9
  260.1 5.1 %multiply_convert_fusion = bf16[3072,512]{1,0:T(8,128)(2,1)S(1)} fusion(f32[3072,512]{1,0:T(8,128)S(1)} %copy-done, f32[3072]{0:T(1024)S(1)} %rsqrt_multiply_fusion, bf16[1024,512]{1,0:T(8,128)(2,1)S(1)} %copy-done.4, bf16[1024,512]{1,0:T(8,128)(2,1)S(1)} %copy-done.7, bf16[1024,512]{1,0:T(8,128)(2,1)S(1)} %copy-done.9), kind=kLoop, calls=%fused_computation.6 | loop fusion | flops 14155776 | bytes 12595200 | tf_op jit(solution)/shard_map/convert_element_type | solution.py:32
  265.1 0.0 copy-start.2
  265.2 1.5 fusion.56
  266.7 2.1 fusion.40
  268.8 5.3 %fusion.11 = bf16[512,2,512]{0,2,1:T(8,128)(2,1)} fusion(bf16[2,512,512]{2,1,0:T(8,128)(2,1)} %fusion.26, bf16[2,512,512]{2,1,0:T(8,128)(2,1)} %bitcast.142, f32[2,512,512]{1,2,0:T(8,128)} %fusion.40, bf16[2,512,512]{2,1,0:T(8,128)(2,1)} %bitcast.141, f32[512,2]{0,1:T(2,128)S(1)} %add_rsqrt_fusion, bf16[64,2,8,512]{3,2,1,0:T(8,128)(2,1)} %bitcast.128), kind=kOutput, calls=%fused_computation.26 | convolution fusion | flops 1080033280 | bytes 7344128 | tf_op jit(solution)/shard_map/thj,hoj->tho/dot_general | solution.py:100
  274.1 2.3 copy.105
  276.4 0.7 constant_dynamic-slice_fusion
  (30 shorter events, 0.1 us)
Async XLA Ops:
  7.2 247.1 %all-reduce.2.cloned.1.call-start = ((), (), s32[]{:S(2)}) async-start(), calls=%async_computation | async-start | bytes 12582912 | tf_op jit(solution)/shard_map/psum | solution.py:91
  8.7 58.8 %collective-permute-start.2 = (bf16[512,1024]{0,1:T(8,128)(2,1)S(1)}, bf16[512,1024]{0,1:T(8,128)(2,1)}, u32[]{:S(2)}, u32[]{:S(2)}) collective-permute-start(bf16[512,1024]{0,1:T(8,128)(2,1)S(1)} %copy.89), channel_id=1, source_target_pairs={{0,2},{1,3},{2,4},{3,5},{4,6},{5,7},{6,8},{7,9},{8,10},{9,11},{10,... | collective-permute-start | bytes 3145736 | tf_op jit(solution)/shard_map/ppermute | solution.py:16
  14.6 52.9 %collective-permute-start.3 = (bf16[512,1024]{0,1:T(8,128)(2,1)S(1)}, bf16[512,1024]{0,1:T(8,128)(2,1)}, u32[]{:S(2)}, u32[]{:S(2)}) collective-permute-start(bf16[512,1024]{0,1:T(8,128)(2,1)S(1)} %copy.89), channel_id=1, source_target_pairs={{0,1},{1,2},{2,3},{3,4},{4,5},{5,6},{6,7},{7,8},{8,9},{9,10},{10,1... | collective-permute-start | bytes 3145736 | tf_op jit(solution)/shard_map/ppermute | solution.py:16
  17.0 42.7 %collective-permute-start = (bf16[512,1024]{1,0:T(8,128)(2,1)}, bf16[512,1024]{1,0:T(8,128)(2,1)}, u32[]{:S(2)}, u32[]{:S(2)}) collective-permute-start(bf16[512,1024]{1,0:T(8,128)(2,1)} %param.9), channel_id=1, source_target_pairs={{0,2},{1,3},{2,4},{3,5},{4,6},{5,7},{6,8},{7,9},{8,10},{9,11},{10,... | collective-permute-start | bytes 3145736 | tf_op jit(solution)/shard_map/ppermute | solution.py:16
  20.0 39.8 %collective-permute-start.1 = (bf16[512,1024]{1,0:T(8,128)(2,1)}, bf16[512,1024]{1,0:T(8,128)(2,1)}, u32[]{:S(2)}, u32[]{:S(2)}) collective-permute-start(bf16[512,1024]{1,0:T(8,128)(2,1)} %param.9), channel_id=1, source_target_pairs={{0,1},{1,2},{2,3},{3,4},{4,5},{5,6},{6,7},{7,8},{8,9},{9,10},{10,1... | collective-permute-start | bytes 3145736 | tf_op jit(solution)/shard_map/ppermute | solution.py:16
  24.5 3.6 %copy-start.8 = (bf16[1024,512]{1,0:T(8,128)(2,1)S(1)}, bf16[1024,512]{1,0:T(8,128)(2,1)}, u32[]{:S(2)}) copy-start(bf16[1024,512]{1,0:T(8,128)(2,1)} %param.11) | copy-start | bytes 3145732
  26.1 4.1 %copy-start.5 = (bf16[1024,512]{1,0:T(8,128)(2,1)S(1)}, bf16[1024,512]{1,0:T(8,128)(2,1)}, u32[]{:S(2)}) copy-start(bf16[1024,512]{1,0:T(8,128)(2,1)} %param.12) | copy-start | bytes 3145732
  30.2 2.1 copy-start.16
  30.2 29.5 %copy-start.14 = (bf16[512,1024]{1,0:T(8,128)(2,1)S(1)}, bf16[512,1024]{1,0:T(8,128)(2,1)}, u32[]{:S(2)}) copy-start(bf16[512,1024]{1,0:T(8,128)(2,1)} %param.9) | copy-start | bytes 3145732
  67.5 1.9 copy-start.1
  69.4 2.4 copy-start.15
  71.9 2.6 copy-start.10
  74.5 7.8 %copy-start.3 = (bf16[1024,512]{1,0:T(8,128)(2,1)S(1)}, bf16[1024,512]{1,0:T(8,128)(2,1)}, u32[]{:S(2)}) copy-start(bf16[1024,512]{1,0:T(8,128)(2,1)} %param.13) | copy-start | bytes 3145732
  82.3 2.1 copy-start.11
  84.4 1.6 copy-start.12
  86.0 1.2 copy-start.13
  91.6 162.7 %copy-start.6 = (bf16[1024,512]{1,0:T(8,128)(2,1)S(1)}, bf16[1024,512]{1,0:T(8,128)(2,1)}, u32[]{:S(2)}) copy-start(bf16[1024,512]{1,0:T(8,128)(2,1)} %param.12) | copy-start | bytes 3145732
  254.3 4.9 %copy-start = (f32[3072,512]{1,0:T(8,128)S(1)}, f32[3072,512]{1,0:T(8,128)}, u32[]{:S(2)}) copy-start(f32[3072,512]{1,0:T(8,128)} %all-reduce.2.cloned.1.call-done) | copy-start | bytes 18874372
  254.3 5.2 %copy-start.4 = (bf16[1024,512]{1,0:T(8,128)(2,1)S(1)}, bf16[1024,512]{1,0:T(8,128)(2,1)}, u32[]{:S(2)}) copy-start(bf16[1024,512]{1,0:T(8,128)(2,1)} %param.13) | copy-start | bytes 3145732
  254.3 5.5 %copy-start.7 = (bf16[1024,512]{1,0:T(8,128)(2,1)S(1)}, bf16[1024,512]{1,0:T(8,128)(2,1)}, u32[]{:S(2)}) copy-start(bf16[1024,512]{1,0:T(8,128)(2,1)} %param.12) | copy-start | bytes 3145732
  254.3 5.8 %copy-start.9 = (bf16[1024,512]{1,0:T(8,128)(2,1)S(1)}, bf16[1024,512]{1,0:T(8,128)(2,1)}, u32[]{:S(2)}) copy-start(bf16[1024,512]{1,0:T(8,128)(2,1)} %param.11) | copy-start | bytes 3145732
  265.1 1.5 copy-start.2
Sparse Core Ops, SparseCore 0:
  91.7 162.5 all-reduce.1
where the time goes:
time: 284 us
  waiting for transfers between devices  188 us (66%)
  matrix products  26.9 us (9%)
  other arithmetic  24.4 us (9%)
  starting transfers between devices  15.5 us (5%)
  local copies, waits for them, and re-layouts  14.9 us (5%)
  between operations  14.2 us (5%)
    psum x1, waiting for transfers between devices, local(): summed = lax.psum(grads, 'ctx')  162 us
    ppermute x4, waiting for transfers between devices, passed_along(): lax.ppermute(value, axis, [(source, source + steps) for source in range(l...  25.5 us
    ppermute x4, starting transfers between devices, passed_along(): lax.ppermute(value, axis, [(source, source + steps) for source in range(l...  15.5 us
    dot_general x1, matrix products, local(): jnp.einsum('hqk,khd->qhd', weights, v_block, preferred_element_type=jnp.f...  7.75 us
    unnamed x36, local copies, waits for them, and re-layouts  6.35 us
  transfers between devices with their start and end apart: 5, of which 2 were waited for; matrix products, arithmetic and copies ran while one was open for 6% of the time, Pallas kernels for 0%

commit v1 on v0

v1 whole, which is shorter than its diff:
```python
import functools
import math

import jax
import jax.numpy as jnp
from jax import lax
from jax.experimental import pallas as pl
from jax.experimental.pallas import tpu as pltpu
from jax.sharding import Mesh, PartitionSpec as P

H = 2
HD = 512
BLK = 512
BF = jnp.bfloat16
F32 = jnp.float32
SWAP = [(0, 1), (1, 0)]
PARAMS = pltpu.CompilerParams(vmem_limit_bytes=56 << 20)


def mm(a, b, dims):
    return lax.dot_general(a, b, (dims, ((), ())), preferred_element_type=F32)


def mm_t(a, b):
    return mm(a, b, ((1,), (1,)))


def mm_n(a, b):
    return mm(a, b, ((1,), (0,)))


def mm_rows(a, b):
    return mm(a, b, ((0,), (0,)))


def rms(x):
    v = x.astype(F32)
    return (v * lax.rsqrt(jnp.mean(v * v, -1, keepdims=True) + 1e-06)).astype(BF)


def attend_block(q, kbuf, vbuf, ia, ib, ic, a_ok, b_ok, out):
    half = BLK // 2
    scale = 1.0 / math.sqrt(HD)
    p = lax.broadcasted_iota(jnp.int32, (half, half), 0)
    j = lax.broadcasted_iota(jnp.int32, (half, half), 1)
    causal = j <= p
    neg = jnp.float32(-jnp.inf)
    for c in range(2):
        rows = pl.ds(c * half, half)
        qc = q[rows, :]
        tiles = []
        for t in range(2):
            cols = pl.ds(t * half, half)
            if t <= c:
                sc = mm_t(qc, kbuf[ic, cols, :]) * scale
            if t >= c:
                sa = mm_t(qc, kbuf[ia, cols, :]) * scale
                sa = jnp.where(a_ok, sa, neg)
            tiles.append(sc if t < c else sa if t > c else jnp.where(causal, sc, sa))
        sb = mm_t(qc, kbuf[ib]) * scale
        tiles.append(jnp.where(b_ok, sb, neg))
        top = functools.reduce(jnp.maximum, [jnp.max(s, -1, keepdims=True) for s in tiles])
        expo = [jnp.exp(s - top) for s in tiles]
        total = functools.reduce(jnp.add, [jnp.sum(e, -1, keepdims=True) for e in expo])
        inv = 1.0 / total
        w = [(e * inv).astype(BF) for e in expo]
        acc = mm_n(w[2], vbuf[ib])
        zero = jnp.zeros((half, half), BF)
        for t in range(2):
            cols = pl.ds(t * half, half)
            if t <= c:
                acc += mm_n(jnp.where(causal, w[t], zero) if t == c else w[t], vbuf[ic, cols, :])
            if t >= c:
                acc += mm_n(jnp.where(causal, zero, w[t]) if t == c else w[t], vbuf[ia, cols, :])
        out[rows, :] = acc.astype(BF)


def main_kernel(
    where, q_own, q_for, *rest
):
    ks, vs = rest[:5], rest[5:10]
    r_own, r_for, wg, wu, wd = rest[10:15]
    att_own, att_for, keep, send = rest[15:19]
    qbuf, kbuf, vbuf, kn, err, gated, dgate, dup, sems = rest[19:]
    y, k, z = where[0], where[1], where[2]
    copies = []
    for n, (src, dst) in enumerate(
        [(q_own, qbuf.at[0]), (q_for, qbuf.at[1])]
        + [(ks[i], kbuf.at[i]) for i in range(5)]
        + [(vs[i], vbuf.at[i]) for i in range(5)]
    ):
        copy = pltpu.make_async_copy(src, dst, sems.at[n])
        copy.start()
        copies.append(copy)
    for copy in copies:
        copy.wait()
    inner = z > 0
    lower_own = y == 0
    ia_own = jnp.where(lower_own, 2, 1)
    ib_own = jnp.where(y == k, 4, 3)
    ia_for = jnp.where(lower_own, 0, 2)
    ib_for = jnp.where(y == k, 3, 4)
    a_own = inner | (y == 1)
    a_for = inner | (y == 0)
    b_own = inner | (y == 1) | (k == 1)
    b_for = inner | (y == 0) | (k == 1)
    attend_block(qbuf.at[0], kbuf, vbuf, ia_own, ib_own, 0, a_own, b_own, att_own)
    attend_block(qbuf.at[1], kbuf, vbuf, ia_for, ib_for, 1, a_for, b_for, att_for)
    for n, (att, rate) in enumerate([(att_own, r_own), (att_for, r_for)]):
        for c in range(2):
            half = BLK // 2
            rows = pl.ds(c * half, half)
            trows = pl.ds(n * BLK + c * half, half)
            knc = rms(kbuf[n, rows, :])
            e = (-rate[rows, :] * att[rows, :].astype(F32)).astype(BF)
            hg = mm_t(knc, wg[...])
            hu = mm_t(knc, wu[...])
            back = mm_n(e, wd[...])
            sig = jax.nn.sigmoid(hg)
            act = hg * sig
            kn[trows, :] = knc
            err[trows, :] = e
            gated[trows, :] = (act * hu).astype(BF)
            dgate[trows, :] = (back * hu * sig * (1.0 + hg * (1.0 - sig))).astype(BF)
            dup[trows, :] = (back * act).astype(BF)
    part = HD // 2
    for kind, (a, b) in enumerate([(dgate, kn), (dup, kn), (err, gated)]):
        for side in range(2):
            g = mm_rows(a[:, side * part : (side + 1) * part], b[...])

            @pl.when(k == side)
            def _():
                keep[kind] = g

            @pl.when(k != side)
            def _():
                send[kind] = g.astype(BF)


def main_call(where, q_own, q_for, ks, vs, r_own, r_for, w_gate, w_up, w_down):
    anyspec = pl.BlockSpec(memory_space=pl.ANY)
    whole = lambda shape: pl.BlockSpec(shape, lambda i, s: (0,) * len(shape))
    head = pl.BlockSpec((HD, HD), lambda i, s: (s[0], 0))
    part = HD // 2
    return pl.pallas_call(
        main_kernel,
        grid_spec=pltpu.PrefetchScalarGridSpec(
            num_scalar_prefetch=1,
            grid=(1,),
            in_specs=[anyspec] * 12 + [whole((BLK, 1))] * 2 + [head] * 3,
            out_specs=[
                whole((BLK, HD)),
                whole((BLK, HD)),
                whole((3, part, HD)),
                whole((3, part, HD)),
            ],
            scratch_shapes=[
                pltpu.VMEM((2, BLK, HD), BF),
                pltpu.VMEM((5, BLK, HD), BF),
                pltpu.VMEM((5, BLK, HD), BF),
            ]
            + [pltpu.VMEM((2 * BLK, HD), BF)] * 5
            + [pltpu.SemaphoreType.DMA((12,))],
        ),
        out_shape=[
            jax.ShapeDtypeStruct((BLK, HD), BF),
            jax.ShapeDtypeStruct((BLK, HD), BF),
            jax.ShapeDtypeStruct((3, part, HD), F32),
            jax.ShapeDtypeStruct((3, part, HD), BF),
        ],
        compiler_params=PARAMS,
        name="attend_grads",
    )(where, q_own, q_for, *ks, *vs, r_own, r_for, w_gate, w_up, w_down)


def chip_sum_kernel(zs, rows, where, keep, got, own, *sends):
    z = where[2]
    for d in range(zs):
        at = lax.rem(z + d, zs) * rows
        src = pl.ds(pl.multiple_of(at, rows), rows)
        for kind in range(3):
            total = keep[kind, src, :] + got[kind, src, :].astype(F32)
            if d == 0:
                own[kind] = total
            else:
                sends[d - 1][kind] = total.astype(BF)


def chip_sum_call(zs, where, keep, got):
    rows = HD // 2 // zs
    vm = pl.BlockSpec(memory_space=pltpu.VMEM)
    shape = (3, rows, HD)
    return pl.pallas_call(
        functools.partial(chip_sum_kernel, zs, rows),
        in_specs=[pl.BlockSpec(memory_space=pltpu.SMEM), vm, vm],
        out_specs=[vm] * zs,
        out_shape=[jax.ShapeDtypeStruct(shape, F32)]
        + [jax.ShapeDtypeStruct(shape, BF)] * (zs - 1),
        compiler_params=PARAMS,
        name="chip_sum",
    )(where, keep, got)


def update_kernel(where, own, *rest):
    got, olds, out = rest[:-4], rest[-4:-1], rest[-1]
    for kind in range(3):
        grad = own[kind]
        for g in got:
            grad = grad + g[kind].astype(F32)
        old = olds[kind][...].astype(F32)
        raised = old - grad
        factor = jnp.sqrt(jnp.mean(old * old, -1, keepdims=True) + 1e-06) * lax.rsqrt(
            jnp.mean(raised * raised, -1, keepdims=True) + 1e-06
        )
        out[kind] = (raised * factor).astype(BF)


def update_call(zs, where, own, got, w_gate, w_up, w_down):
    rows = HD // 2 // zs
    shape = (3, rows, HD)
    whole = pl.BlockSpec(shape, lambda i, s: (0, 0, 0))
    old = pl.BlockSpec((rows, HD), lambda i, s: ((s[0] * 2 + s[1]) * zs + s[2], 0))
    return pl.pallas_call(
        update_kernel,
        grid_spec=pltpu.PrefetchScalarGridSpec(
            num_scalar_prefetch=1,
            grid=(1,),
            in_specs=[whole] * zs + [old] * 3,
            out_specs=whole,
        ),
        out_shape=jax.ShapeDtypeStruct(shape, BF),
        compiler_params=PARAMS,
        name="update",
    )(where, own, *got, w_gate, w_up, w_down)


def read_block(q, att, w, out):
    half = BLK // 2
    for c in range(2):
        rows = pl.ds(c * half, half)
        qn = rms(q[rows, :])
        hg = mm_t(qn, w[0:HD, :])
        hu = mm_t(qn, w[HD : 2 * HD, :])
        g = (hg * jax.nn.sigmoid(hg) * hu).astype(BF)
        fast = mm_t(g, w[2 * HD : 3 * HD, :])
        out[rows, :] = (att[rows, :].astype(F32) + fast).astype(BF)


def window(w, out, first, count):
    step = math.gcd(count, HD)
    for c in range(count // step):
        r = first + c * step
        block = lax.div(r, HD)
        at = lax.div(block, 2) * HD + lax.rem(r, HD)
        out[c * step : (c + 1) * step, :] = w[pl.ds(pl.multiple_of(at, step), step), :]


def read_foreign_kernel(zs, count, where, *rest):
    mine, theirs = rest[:zs], rest[zs : 2 * zs]
    q, att, out, full, given, kept = rest[2 * zs :]
    y, k, z = where[0], where[1], where[2]
    rows = HD // 2 // zs
    for side, pieces in ((k, mine), (1 - k, theirs)):
        for d in range(zs):
            at = side * (HD // 2) + lax.rem(z - d + zs, zs) * rows
            for kind in range(3):
                full[pl.ds(pl.multiple_of(kind * HD + at, rows), rows), :] = pieces[d][kind]
    me = (z * 2 + y) * 2 + k
    partner = (z * 2 + 1 - y) * 2 + k
    window(full, given, partner * count, count)
    window(full, kept, me * count, count)
    read_block(q, att, full, out)


def read_foreign_call(zs, count, where, mine, theirs, q, att):
    vm = pl.BlockSpec(memory_space=pltpu.VMEM)
    return pl.pallas_call(
        functools.partial(read_foreign_kernel, zs, count),
        in_specs=[pl.BlockSpec(memory_space=pltpu.SMEM)] + [vm] * (2 * zs + 2),
        out_specs=[vm] * 4,
        out_shape=[
            jax.ShapeDtypeStruct((BLK, HD), BF),
            jax.ShapeDtypeStruct((3 * HD, HD), BF),
            jax.ShapeDtypeStruct((count, HD), BF),
            jax.ShapeDtypeStruct((count, HD), BF),
        ],
        compiler_params=PARAMS,
        name="read_foreign",
    )(where, *mine, *theirs, q, att)


def read_own_kernel(q, att, w, out):
    read_block(q, att, w, out)


def read_own_call(q, att, w):
    vm = pl.BlockSpec(memory_space=pltpu.VMEM)
    return pl.pallas_call(
        read_own_kernel,
        in_specs=[vm] * 3,
        out_specs=vm,
        out_shape=jax.ShapeDtypeStruct((BLK, HD), BF),
        compiler_params=PARAMS,
        name="read_own",
    )(q, att, w)


def local(queries, key_rows, value_rows, step_rates, w_gate, w_up, w_down):
    zs = lax.axis_size("z")
    z, y, k = lax.axis_index("z"), lax.axis_index("y"), lax.axis_index("core")
    where = jnp.stack([y, k, z]).astype(jnp.int32)

    def head_of(rows, head):
        return lax.dynamic_slice(rows, (0, head * HD), (BLK, HD))

    def rate_of(head):
        return lax.dynamic_slice(step_rates, (head, 0), (1, BLK))

    def swap(value, axis):
        return lax.ppermute(value, axis, SWAP)

    def shift(value, d, ring=True):
        pairs = [(i, (i + d) % zs) for i in range(zs) if ring or i + d < zs]
        return lax.ppermute(value, "z", pairs)

    k_for = swap(head_of(key_rows, 1 - y), "y")
    v_for = swap(head_of(value_rows, 1 - y), "y")
    q_for = swap(head_of(queries, 1 - y), "y")
    r_for = swap(rate_of(1 - y), "y")
    k_own, v_own, q_own = (head_of(a, y) for a in (key_rows, value_rows, queries))
    r_own = rate_of(y)

    sides = []
    for own, foreign in ((k_own, k_for), (v_own, v_for)):
        low = jnp.where(y == 0, own, foreign)
        high = jnp.where(y == 0, foreign, own)
        halo = shift(high, 1, ring=False)
        low_other = swap(low, "core")
        cross_other = swap(jnp.where(k == 0, high, halo), "core")
        sides.append((own, foreign, halo, low_other, cross_other))

    att_own, att_for, keep, send = main_call(
        where,
        q_own,
        q_for,
        sides[0],
        sides[1],
        r_own.reshape(BLK, 1),
        r_for.reshape(BLK, 1),
        w_gate,
        w_up,
        w_down,
    )
    got = swap(send, "core")
    own_sum, *sends = chip_sum_call(zs, where, keep, got)
    arrived = [shift(s, d) for d, s in enumerate(sends, 1)]
    piece = update_call(zs, where, own_sum, arrived, w_gate, w_up, w_down)
    mine = [piece] + [shift(piece, d) for d in range(1, zs)]
    theirs = [swap(p, "core") for p in mine]
    count = 3 * H * HD // (4 * zs)
    out_for, full, given, kept = read_foreign_call(zs, count, where, mine, theirs, q_for, att_for)
    out_got = swap(out_for, "y")
    rows_got = swap(given, "y")
    out_own = read_own_call(q_own, att_own, full)
    layer_out = jnp.where(
        y == 0,
        jnp.concatenate([out_own, out_got], 1),
        jnp.concatenate([out_got, out_own], 1),
    )
    rows = ((z * 2 + y) * 2 + k) * count + jnp.arange(count, dtype=jnp.int32)
    head = lax.rem(lax.div(rows, HD), 2)
    own_weights = jnp.where((head == y)[:, None], kept, rows_got)
    return (layer_out, own_weights)


def solution(mesh):
    groups, ctx = mesh.devices.shape
    split = Mesh(mesh.devices.reshape(groups, ctx // 4, 2, 2), ("groups", "z", "y", "core"))
    tokens = ("groups", "z", "y", "core")
    return jax.shard_map(
        local,
        mesh=split,
        in_specs=(
            P(tokens, None),
            P(tokens, None),
            P(tokens, None),
            P(None, tokens),
            P("groups", None),
            P("groups", None),
            P("groups", None),
        ),
        out_specs=(P(tokens, None), P(tokens, None)),
        check_vma=False,
    )
```

time: 284 us -> 145 us (0.51)
  waiting for transfers between devices: 188 us -> 68.6 us
  Pallas kernels: 0 us -> 28.2 us
  matrix products: 26.9 us -> 0 us
  other arithmetic: 24.4 us -> 7.85 us
  between operations: 14.2 us -> 0.87 us
  starting transfers between devices: 15.5 us -> 28.4 us
  local copies, waits for them, and re-layouts: 14.9 us -> 10.7 us
    psum x1 -> x0, waiting for transfers between devices: 162 us -> none  [local(): summed = lax.psum(grads, 'ctx')]
    ppermute x4 -> x23, waiting for transfers between devices: 25.5 us -> 68.6 us  [the longest x15 34.5 us: swap(): return lax.ppermute(value, axis, SWAP)]
    pallas_call x0 -> x5, Pallas kernels: none -> 28.2 us  [the longest x1 15 us: main_call(): pl.pallas_call(main_kernel, grid_spec=pltpu.PrefetchScalarGridSpec(num_sc...]
    dot_general x10 -> x0, matrix products: 26.9 us -> none  [the longest x1 7.75 us: local(): jnp.einsum('hqk,khd->qhd', weights, v_block, preferred_element_type=jnp.f...]
    ppermute x4 -> x23, starting transfers between devices: 15.5 us -> 28.4 us  [the longest x8 19.7 us: shift(): return lax.ppermute(value, 'z', pairs)]
    concatenate x3 -> x0, other arithmetic: 8.33 us -> none  [the longest x1 3.37 us: local(): jnp.concatenate([grad_gate.reshape(H * HD, HD), grad_up.reshape(H * HD, H...]
    select_n x0 -> x8, other arithmetic: none -> 7.22 us  [the longest x1 2.5 us: local(): jnp.where(y == 0, jnp.concatenate([out_own, out_got], 1), jnp.concatenate...]
    convert_element_type x2 -> x0, other arithmetic: 6.93 us -> none  [the longest x1 5.05 us: normalize_rows(): return (raised * factor).astype(jnp.bfloat16)]
  transfers between devices with their start and end apart: 5 -> 23, of which waited for: 2 -> 12; matrix products, arithmetic and copies ran while one was open for 6% -> 8% of each run, Pallas kernels for 0% -> 3%
where the time goes in v1:
time: 145 us
  waiting for transfers between devices  68.6 us (47%)
  starting transfers between devices  28.4 us (20%)
  Pallas kernels  28.2 us (19%)
  local copies, waits for them, and re-layouts  10.7 us (7%)
  other arithmetic  7.85 us (5%)
    ppermute x15, waiting for transfers between devices, swap(): return lax.ppermute(value, axis, SWAP)  34.5 us
    ppermute x8, waiting for transfers between devices, shift(): return lax.ppermute(value, 'z', pairs)  34.1 us
    ppermute x8, starting transfers between devices, shift(): return lax.ppermute(value, 'z', pairs)  19.7 us
    pallas_call x1, Pallas kernels, main_call(): pl.pallas_call(main_kernel, grid_spec=pltpu.PrefetchScalarGridSpec(num_sc...  15 us
    ppermute x15, starting transfers between devices, swap(): return lax.ppermute(value, axis, SWAP)  8.66 us
    dynamic_slice x3, local copies, waits for them, and re-layouts, head_of(): return lax.dynamic_slice(rows, (0, head * HD), (BLK, HD))  5.26 us
    pallas_call x1, Pallas kernels, read_foreign_call(): pl.pallas_call(functools.partial(read_foreign_kernel, zs, count), in_spec...  3.97 us
    pallas_call x1, Pallas kernels, read_own_call(): pl.pallas_call(read_own_kernel, in_specs=[vm] * 3, out_specs=vm, out_shap...  3.78 us
  transfers between devices with their start and end apart: 23, of which 12 were waited for; matrix products, arithmetic and copies ran while one was open for 8% of the time, Pallas kernels for 3%

profile of v1, /device:TPU:0, one launch (start us, length us, event | category | flops | bytes accessed | tf_op | source)
XLA Modules:
  0.0 144.7 jit_solution(1209000402712413409)
XLA Ops:
  0.6 1.2 constant_dynamic-slice_fusion.3
  1.8 3.0 %collective-permute-start.1 = (bf16[512,512]{1,0:T(8,128)(2,1)S(1)}, bf16[512,512]{1,0:T(8,128)(2,1)S(1)}, u32[]{:S(2)}, u32[]{:S(2)}) collective-permute-start(bf16[512,512]{1,0:T(8,128)(2,1)S(1)} %constant_dynamic-slice_fusion.3), channel_id=1, source_target_pairs={{0,2},{2,0},{1,3},{3,1},{4,6},{6,4},{5,7},{7,5},{8,10},{10,8},{9,1... | collective-permute-start | bytes 1572872 | tf_op jit(solution)/shard_map/ppermute | solution.py:320
  4.8 1.9 %constant_dynamic-slice_fusion.1 = bf16[512,512]{1,0:T(8,128)(2,1)} fusion(bf16[512,1024]{1,0:T(8,128)(2,1)} %param.9, s32[]{:T(128)S(6)} %select_n.60), kind=kLoop, calls=%fused_computation.14 | loop fusion | bytes 1048580 | tf_op jit(solution)/shard_map/dynamic_slice | solution.py:314
  6.7 10.9 %collective-permute-done.1.rest_1_ = bf16[512,512]{1,0:T(8,128)(2,1)S(1)} collective-permute-done((bf16[512,512]{1,0:T(8,128)(2,1)S(1)}, bf16[512,512]{1,0:T(8,128)(2,1)S(1)}, u32[]{:S(2)}, u32[]{:S(2)}) %collective-permute-start.1) | collective-permute-done | bytes 524320 | tf_op jit(solution)/shard_map/ppermute | solution.py:320
  17.6 1.0 broadcast_select_fusion.4
  18.7 4.2 %collective-permute-start.2 = (bf16[512,512]{1,0:T(8,128)(2,1)S(1)}, bf16[512,512]{1,0:T(8,128)(2,1)S(1)}, u32[]{:S(2)}, u32[]{:S(2)}) collective-permute-start(bf16[512,512]{1,0:T(8,128)(2,1)S(1)} %broadcast_select_fusion.5), channel_id=1, source_target_pairs={{0,4},{4,8},{8,12},{1,5},{5,9},{9,13},{2,6},{6,10},{10,14},{3,7},{... | collective-permute-start | bytes 1572872 | tf_op jit(solution)/shard_map/ppermute | solution.py:324
  22.9 5.1 %collective-permute-done.5.rest_6_ = bf16[512,512]{1,0:T(8,128)(2,1)S(1)} collective-permute-done((bf16[512,512]{1,0:T(8,128)(2,1)}, bf16[512,512]{1,0:T(8,128)(2,1)S(1)}, u32[]{:S(2)}, u32[]{:S(2)}) %collective-permute-start.5) | collective-permute-done | bytes 524320 | tf_op jit(solution)/shard_map/ppermute | solution.py:320
  28.0 1.0 broadcast_select_fusion.2
  29.1 3.7 %collective-permute-start.6 = (bf16[512,512]{1,0:T(8,128)(2,1)S(1)}, bf16[512,512]{1,0:T(8,128)(2,1)S(1)}, u32[]{:S(2)}, u32[]{:S(2)}) collective-permute-start(bf16[512,512]{1,0:T(8,128)(2,1)S(1)} %broadcast_select_fusion.3), channel_id=1, source_target_pairs={{0,4},{4,8},{8,12},{1,5},{5,9},{9,13},{2,6},{6,10},{10,14},{3,7},{... | collective-permute-start | bytes 1572872 | tf_op jit(solution)/shard_map/ppermute | solution.py:324
  32.9 1.6 %collective-permute-start.9 = (f32[1,512]{1,0:T(1,128)S(1)}, f32[1,512]{1,0:T(1,128)S(1)}, u32[]{:S(2)}, u32[]{:S(2)}) collective-permute-start(f32[1,512]{1,0:T(1,128)S(1)} %get-tuple-element.32), channel_id=1, source_target_pairs={{0,2},{2,0},{1,3},{3,1},{4,6},{6,4},{5,7},{7,5},{8,10},{10,8},{9,1... | collective-permute-start | bytes 6152 | tf_op jit(solution)/shard_map/ppermute | solution.py:320
  34.5 2.2 %constant_dynamic-slice_fusion.5 = (bf16[512,512]{1,0:T(8,128)(2,1)}, bf16[512,512]{1,0:T(8,128)(2,1)}) fusion(bf16[512,1024]{1,0:T(8,128)(2,1)} %param.7, s32[]{:T(128)S(6)} %select_n.60, s32[]{:T(128)S(6)} %select_n.59), kind=kLoop, calls=%fused_computation.18 | loop fusion | bytes 2097160 | tf_op jit(solution)/shard_map/dynamic_slice | solution.py:314
  36.7 0.5 collective-permute-start
  37.2 0.5 collective-permute-start.7
  37.7 0.9 broadcast_select_fusion.1
  38.6 4.7 %collective-permute-done.6.rest_7_ = bf16[512,512]{1,0:T(8,128)(2,1)S(1)} collective-permute-done((bf16[512,512]{1,0:T(8,128)(2,1)S(1)}, bf16[512,512]{1,0:T(8,128)(2,1)S(1)}, u32[]{:S(2)}, u32[]{:S(2)}) %collective-permute-start.6) | collective-permute-done | bytes 524320 | tf_op jit(solution)/shard_map/ppermute | solution.py:324
  43.3 0.9 broadcast_select_fusion
  44.2 0.4 collective-permute-start.8
  44.6 0.9 copy.9.rest_10_
  45.5 0.6 pad_add_fusion.where
  46.1 0.8 copy.10.rest_11_
  46.9 2.2 %collective-permute-done.q_for.rest_8_ = bf16[512,512]{1,0:T(8,128)(2,1)S(1)} collective-permute-done((bf16[512,512]{1,0:T(8,128)(2,1)}, bf16[512,512]{1,0:T(8,128)(2,1)S(1)}, u32[]{:S(2)}, u32[]{:S(2)}) %collective-permute-start) | collective-permute-done | bytes 524320 | tf_op jit(solution)/shard_map/ppermute | solution.py:320
  49.2 0.7 copy-done.6
  50.6 15.0 %attend_grads.1 = (bf16[512,512]{1,0:T(8,128)(2,1)}, bf16[512,512]{1,0:T(8,128)(2,1)}, f32[3,256,512]{2,1,0:T(8,128)}, bf16[3,256,512]{2,1,0:T(8,128)(2,1)}) custom-call(s32[3]{0:T(128)} %pad_add_fusion.where, bf16[512,512]{1,0:T(8,128)(2,1)} %get-tuple-element.31.q_own.q, bf16[512,512]{1,0:T(8,128)(2,1)} %copy-done.6, bf16[512,512]{1,0:T(8,128)(2,1)} %copy-done.2, ...), custom_call_target="tpu_custom_call" | custom-call | tf_op jit(solution)/shard_map/attend_grads/pallas_call | solution.py:145
  65.6 2.5 %collective-permute-done.10.got = bf16[3,256,512]{2,1,0:T(8,128)(2,1)S(1)} collective-permute-done((bf16[3,256,512]{2,1,0:T(8,128)(2,1)}, bf16[3,256,512]{2,1,0:T(8,128)(2,1)S(1)}, u32[]{:S(2)}, u32[]{:S(2)}) %collective-permute-start.10) | collective-permute-done | bytes 786464 | tf_op jit(solution)/shard_map/ppermute | solution.py:320
  68.1 0.9 copy-done.9
  69.0 2.7 %chip_sum.1 = (f32[3,64,512]{2,1,0:T(8,128)}, bf16[3,64,512]{2,1,0:T(8,128)(2,1)}, bf16[3,64,512]{2,1,0:T(8,128)(2,1)}, bf16[3,64,512]{2,1,0:T(8,128)(2,1)}) custom-call(s32[3]{0:T(128)} %pad_add_fusion.where, f32[3,256,512]{2,1,0:T(8,128)} %get-tuple-element.15.keep, bf16[3,256,512]{2,1,0:T(8,128)(2,1)} %copy-done.9), custom_call_target="tpu_custom_call" | custom-call | tf_op jit(solution)/shard_map/chip_sum/pallas_call | solution.py:193
  71.7 1.6 %collective-permute-start.11 = (bf16[3,64,512]{2,1,0:T(8,128)(2,1)}, bf16[3,64,512]{2,1,0:T(8,128)(2,1)S(1)}, u32[]{:S(2)}, u32[]{:S(2)}) collective-permute-start(bf16[3,64,512]{2,1,0:T(8,128)(2,1)} %get-tuple-element.18), channel_id=1, source_target_pairs={{0,4},{4,8},{8,12},{12,0},{1,5},{5,9},{9,13},{13,1},{2,6},{6,10},{... | collective-permute-start | bytes 589832 | tf_op jit(solution)/shard_map/ppermute | solution.py:324
  73.2 1.3 collective-permute-start.12
  74.5 2.6 %collective-permute-start.13 = (bf16[3,64,512]{2,1,0:T(8,128)(2,1)}, bf16[3,64,512]{2,1,0:T(8,128)(2,1)S(1)}, u32[]{:S(2)}, u32[]{:S(2)}) collective-permute-start(bf16[3,64,512]{2,1,0:T(8,128)(2,1)} %get-tuple-element.20), channel_id=1, source_target_pairs={{0,12},{4,0},{8,4},{12,8},{1,13},{5,1},{9,5},{13,9},{2,14},{6,2},{... | collective-permute-start | bytes 589832 | tf_op jit(solution)/shard_map/ppermute | solution.py:324
  77.2 4.4 %collective-permute-done.11.rest_0_ = bf16[3,64,512]{2,1,0:T(8,128)(2,1)S(1)} collective-permute-done((bf16[3,64,512]{2,1,0:T(8,128)(2,1)}, bf16[3,64,512]{2,1,0:T(8,128)(2,1)S(1)}, u32[]{:S(2)}, u32[]{:S(2)}) %collective-permute-start.11) | collective-permute-done | bytes 196640 | tf_op jit(solution)/shard_map/ppermute | solution.py:324
  81.6 7.6 %collective-permute-done.12.rest_1_ = bf16[3,64,512]{2,1,0:T(8,128)(2,1)S(1)} collective-permute-done((bf16[3,64,512]{2,1,0:T(8,128)(2,1)}, bf16[3,64,512]{2,1,0:T(8,128)(2,1)S(1)}, u32[]{:S(2)}, u32[]{:S(2)}) %collective-permute-start.12) | collective-permute-done | bytes 196640 | tf_op jit(solution)/shard_map/ppermute | solution.py:324
  89.2 0.7 copy-done.14
  89.9 2.9 %update.1.rest_0_ = bf16[3,64,512]{2,1,0:T(8,128)(2,1)} custom-call(s32[3]{0:T(128)} %pad_add_fusion.where, f32[3,64,512]{2,1,0:T(8,128)} %get-tuple-element.17.own, bf16[3,64,512]{2,1,0:T(8,128)(2,1)} %copy-done.13, bf16[3,64,512]{2,1,0:T(8,128)(2,1)} %copy-done.14, bf16[3,64,512]{2,1,0:T(8,128)(2,1)} %copy-done.15, bf16[1024,512]{1,0:T(8,128)(2,1)} %rest_3_.1, ...), custom_call_target="tpu_custom_call" | custom-call | tf_op jit(solution)/shard_map/update/pallas_call | solution.py:223
  92.8 5.7 %collective-permute-start.16 = (bf16[3,64,512]{2,1,0:T(8,128)(2,1)}, bf16[3,64,512]{2,1,0:T(8,128)(2,1)S(1)}, u32[]{:S(2)}, u32[]{:S(2)}) collective-permute-start(bf16[3,64,512]{2,1,0:T(8,128)(2,1)} %update.1.rest_0_), channel_id=1, source_target_pairs={{0,12},{4,0},{8,4},{12,8},{1,13},{5,1},{9,5},{13,9},{2,14},{6,2},{... | collective-permute-start | bytes 589832 | tf_op jit(solution)/shard_map/ppermute | solution.py:324
  98.5 0.3 collective-permute-start.15
  99.1 5.1 %collective-permute-done.16.rest_3_ = bf16[3,64,512]{2,1,0:T(8,128)(2,1)S(1)} collective-permute-done((bf16[3,64,512]{2,1,0:T(8,128)(2,1)}, bf16[3,64,512]{2,1,0:T(8,128)(2,1)S(1)}, u32[]{:S(2)}, u32[]{:S(2)}) %collective-permute-start.16) | collective-permute-done | bytes 196640 | tf_op jit(solution)/shard_map/ppermute | solution.py:324
  104.3 12.3 %collective-permute-done.15.rest_2_ = bf16[3,64,512]{2,1,0:T(8,128)(2,1)S(1)} collective-permute-done((bf16[3,64,512]{2,1,0:T(8,128)(2,1)}, bf16[3,64,512]{2,1,0:T(8,128)(2,1)S(1)}, u32[]{:S(2)}, u32[]{:S(2)}) %collective-permute-start.15) | collective-permute-done | bytes 196640 | tf_op jit(solution)/shard_map/ppermute | solution.py:324
  116.5 0.5 collective-permute-start.18
  117.1 0.9 collective-permute-done.19.rest_6_
  118.3 0.4 copy-done.21
  118.6 0.3 copy-done.22
  118.9 4.0 %read_foreign.1 = (bf16[512,512]{1,0:T(8,128)(2,1)}, bf16[1536,512]{1,0:T(8,128)(2,1)}, bf16[192,512]{1,0:T(8,128)(2,1)}, bf16[192,512]{1,0:T(8,128)(2,1)}) custom-call(s32[3]{0:T(128)} %pad_add_fusion.where, bf16[3,64,512]{2,1,0:T(8,128)(2,1)} %update.1.rest_0_, bf16[3,64,512]{2,1,0:T(8,128)(2,1)} %copy-done.18, bf16[3,64,512]{2,1,0:T(8,128)(2,1)} %copy-done.17, ...), custom_call_target="tpu_custom_call" | custom-call | tf_op jit(solution)/shard_map/read_foreign/pallas_call | solution.py:277
  122.9 0.5 collective-permute-start.21
  123.4 1.5 %collective-permute-start.22 = (bf16[192,512]{1,0:T(8,128)(2,1)}, bf16[192,512]{1,0:T(8,128)(2,1)S(1)}, u32[]{:S(2)}, u32[]{:S(2)}) collective-permute-start(bf16[192,512]{1,0:T(8,128)(2,1)} %get-tuple-element.25), channel_id=1, source_target_pairs={{0,2},{2,0},{1,3},{3,1},{4,6},{6,4},{5,7},{7,5},{8,10},{10,8},{9,1... | collective-permute-start | bytes 589832 | tf_op jit(solution)/shard_map/ppermute | solution.py:320
  124.9 3.8 %read_own.1 = bf16[512,512]{1,0:T(8,128)(2,1)} custom-call(bf16[512,512]{1,0:T(8,128)(2,1)} %get-tuple-element.31.q_own.q, bf16[512,512]{1,0:T(8,128)(2,1)} %get-tuple-element.14.att, bf16[1536,512]{1,0:T(8,128)(2,1)} %get-tuple-element.22.w), custom_call_target="tpu_custom_call" | custom-call | tf_op jit(solution)/shard_map/read_own/pallas_call | solution.py:298
  128.7 12.7 %collective-permute-done.22 = bf16[192,512]{1,0:T(8,128)(2,1)S(1)} collective-permute-done((bf16[192,512]{1,0:T(8,128)(2,1)}, bf16[192,512]{1,0:T(8,128)(2,1)S(1)}, u32[]{:S(2)}, u32[]{:S(2)}) %collective-permute-start.22) | collective-permute-done | bytes 196640 | tf_op jit(solution)/shard_map/ppermute | solution.py:320
  141.4 0.8 broadcast_select_fusion.6
  142.2 2.5 %maximum_select_fusion = bf16[512,1024]{1,0:T(8,128)(2,1)} fusion(bf16[512,512]{1,0:T(8,128)(2,1)S(1)} %collective-permute-done.21, bf16[512,512]{1,0:T(8,128)(2,1)} %read_own.1, pred[]{:T(512)S(6)} %eq.21), kind=kLoop, calls=%fused_computation | loop fusion | flops 4718592 | bytes 2097153 | tf_op jit(solution)/shard_map/jit(_where)/select_n | solution.py:365
  (69 shorter events, 1.6 us)
Async XLA Ops:
  0.6 17.0 %copy-start.7 = (bf16[512,1024]{1,0:T(8,128)(2,1)S(1)}, bf16[512,1024]{1,0:T(8,128)(2,1)}, u32[]{:S(2)}) copy-start(bf16[512,1024]{1,0:T(8,128)(2,1)} %param.8) | copy-start | bytes 3145732
  1.8 15.8 %collective-permute-start.1 = (bf16[512,512]{1,0:T(8,128)(2,1)S(1)}, bf16[512,512]{1,0:T(8,128)(2,1)S(1)}, u32[]{:S(2)}, u32[]{:S(2)}) collective-permute-start(bf16[512,512]{1,0:T(8,128)(2,1)S(1)} %constant_dynamic-slice_fusion.3), channel_id=1, source_target_pairs={{0,2},{2,0},{1,3},{3,1},{4,6},{6,4},{5,7},{7,5},{8,10},{10,8},{9,1... | collective-permute-start | bytes 1572872 | tf_op jit(solution)/shard_map/ppermute | solution.py:320
  6.7 21.3 %collective-permute-start.5 = (bf16[512,512]{1,0:T(8,128)(2,1)}, bf16[512,512]{1,0:T(8,128)(2,1)S(1)}, u32[]{:S(2)}, u32[]{:S(2)}) collective-permute-start(bf16[512,512]{1,0:T(8,128)(2,1)} %constant_dynamic-slice_fusion.1), channel_id=1, source_target_pairs={{0,2},{2,0},{1,3},{3,1},{4,6},{6,4},{5,7},{7,5},{8,10},{10,8},{9,1... | collective-permute-start | bytes 1572872 | tf_op jit(solution)/shard_map/ppermute | solution.py:320
  6.7 21.3 %copy-start.8 = (bf16[512,1024]{1,0:T(8,128)(2,1)S(1)}, bf16[512,1024]{1,0:T(8,128)(2,1)}, u32[]{:S(2)}) copy-start(bf16[512,1024]{1,0:T(8,128)(2,1)} %param.9) | copy-start | bytes 3145732
  17.6 1.1 copy-start
  18.6 10.4 %copy-start.2 = (bf16[512,512]{1,0:T(8,128)(2,1)}, bf16[512,512]{1,0:T(8,128)(2,1)S(1)}, u32[]{:S(2)}) copy-start(bf16[512,512]{1,0:T(8,128)(2,1)S(1)} %get-tuple-element.29.rest_0_) | copy-start | bytes 1572868
  18.7 14.1 %copy-start.24 = (f32[2,512]{1,0:T(2,128)S(1)}, f32[2,512]{1,0:T(2,128)}, u32[]{:S(2)}) copy-start(f32[2,512]{1,0:T(2,128)} %param.10) | copy-start | bytes 12292
  18.7 18.5 %collective-permute-start.2 = (bf16[512,512]{1,0:T(8,128)(2,1)S(1)}, bf16[512,512]{1,0:T(8,128)(2,1)S(1)}, u32[]{:S(2)}, u32[]{:S(2)}) collective-permute-start(bf16[512,512]{1,0:T(8,128)(2,1)S(1)} %broadcast_select_fusion.5), channel_id=1, source_target_pairs={{0,4},{4,8},{8,12},{1,5},{5,9},{9,13},{2,6},{6,10},{10,14},{3,7},{... | collective-permute-start | bytes 1572872 | tf_op jit(solution)/shard_map/ppermute | solution.py:324
  28.0 1.1 copy-start.1
  29.0 7.7 %copy-start.3 = (bf16[512,512]{1,0:T(8,128)(2,1)}, bf16[512,512]{1,0:T(8,128)(2,1)S(1)}, u32[]{:S(2)}) copy-start(bf16[512,512]{1,0:T(8,128)(2,1)S(1)} %get-tuple-element.27.rest_5_) | copy-start | bytes 1572868
  29.1 14.2 %collective-permute-start.6 = (bf16[512,512]{1,0:T(8,128)(2,1)S(1)}, bf16[512,512]{1,0:T(8,128)(2,1)S(1)}, u32[]{:S(2)}, u32[]{:S(2)}) collective-permute-start(bf16[512,512]{1,0:T(8,128)(2,1)S(1)} %broadcast_select_fusion.3), channel_id=1, source_target_pairs={{0,4},{4,8},{8,12},{1,5},{5,9},{9,13},{2,6},{6,10},{10,14},{3,7},{... | collective-permute-start | bytes 1572872 | tf_op jit(solution)/shard_map/ppermute | solution.py:324
  32.9 11.3 %collective-permute-start.9 = (f32[1,512]{1,0:T(1,128)S(1)}, f32[1,512]{1,0:T(1,128)S(1)}, u32[]{:S(2)}, u32[]{:S(2)}) collective-permute-start(f32[1,512]{1,0:T(1,128)S(1)} %get-tuple-element.32), channel_id=1, source_target_pairs={{0,2},{2,0},{1,3},{3,1},{4,6},{6,4},{5,7},{7,5},{8,10},{10,8},{9,1... | collective-permute-start | bytes 6152 | tf_op jit(solution)/shard_map/ppermute | solution.py:320
  36.7 12.4 %collective-permute-start = (bf16[512,512]{1,0:T(8,128)(2,1)}, bf16[512,512]{1,0:T(8,128)(2,1)S(1)}, u32[]{:S(2)}, u32[]{:S(2)}) collective-permute-start(bf16[512,512]{1,0:T(8,128)(2,1)} %get-tuple-element.30), channel_id=1, source_target_pairs={{0,2},{2,0},{1,3},{3,1},{4,6},{6,4},{5,7},{7,5},{8,10},{10,8},{9,1... | collective-permute-start | bytes 1572872 | tf_op jit(solution)/shard_map/ppermute | solution.py:320
  37.2 12.0 %collective-permute-start.3 = (bf16[512,512]{1,0:T(8,128)(2,1)}, bf16[512,512]{1,0:T(8,128)(2,1)S(1)}, u32[]{:S(2)}, u32[]{:S(2)}) collective-permute-start(bf16[512,512]{1,0:T(8,128)(2,1)} %get-tuple-element.28), channel_id=1, source_target_pairs={{0,1},{1,0},{2,3},{3,2},{4,5},{5,4},{6,7},{7,6},{8,9},{9,8},{10,11... | collective-permute-start | bytes 1572872 | tf_op jit(solution)/shard_map/ppermute | solution.py:320
  37.2 7.0 %copy-start.4 = (bf16[512,512]{1,0:T(8,128)(2,1)}, bf16[512,512]{1,0:T(8,128)(2,1)S(1)}, u32[]{:S(2)}) copy-start(bf16[512,512]{1,0:T(8,128)(2,1)S(1)} %collective-permute-done.2.rest_2_) | copy-start | bytes 1572868
  37.2 11.9 %collective-permute-start.7 = (bf16[512,512]{1,0:T(8,128)(2,1)}, bf16[512,512]{1,0:T(8,128)(2,1)}, u32[]{:S(2)}, u32[]{:S(2)}) collective-permute-start(bf16[512,512]{1,0:T(8,128)(2,1)} %get-tuple-element.26), channel_id=1, source_target_pairs={{0,1},{1,0},{2,3},{3,2},{4,5},{5,4},{6,7},{7,6},{8,9},{9,8},{10,11... | collective-permute-start | bytes 1572872 | tf_op jit(solution)/shard_map/ppermute | solution.py:320
  43.3 5.9 %copy-start.5 = (bf16[512,512]{1,0:T(8,128)(2,1)}, bf16[512,512]{1,0:T(8,128)(2,1)S(1)}, u32[]{:S(2)}) copy-start(bf16[512,512]{1,0:T(8,128)(2,1)S(1)} %collective-permute-done.6.rest_7_) | copy-start | bytes 1572868
  43.3 5.9 %collective-permute-start.4 = (bf16[512,512]{1,0:T(8,128)(2,1)}, bf16[512,512]{1,0:T(8,128)(2,1)S(1)}, u32[]{:S(2)}, u32[]{:S(2)}) collective-permute-start(bf16[512,512]{1,0:T(8,128)(2,1)} %broadcast_select_fusion.1), channel_id=1, source_target_pairs={{0,1},{1,0},{2,3},{3,2},{4,5},{5,4},{6,7},{7,6},{8,9},{9,8},{10,11... | collective-permute-start | bytes 1572872 | tf_op jit(solution)/shard_map/ppermute | solution.py:320
  44.2 5.0 %collective-permute-start.8 = (bf16[512,512]{1,0:T(8,128)(2,1)}, bf16[512,512]{1,0:T(8,128)(2,1)S(1)}, u32[]{:S(2)}, u32[]{:S(2)}) collective-permute-start(bf16[512,512]{1,0:T(8,128)(2,1)} %broadcast_select_fusion), channel_id=1, source_target_pairs={{0,1},{1,0},{2,3},{3,2},{4,5},{5,4},{6,7},{7,6},{8,9},{9,8},{10,11... | collective-permute-start | bytes 1572872 | tf_op jit(solution)/shard_map/ppermute | solution.py:320
  49.1 0.8 copy-start.6
  49.1 1.0 copy-start.10
  49.2 1.2 copy-start.11
  49.2 1.4 copy-start.12
  65.5 2.6 %collective-permute-start.10 = (bf16[3,256,512]{2,1,0:T(8,128)(2,1)}, bf16[3,256,512]{2,1,0:T(8,128)(2,1)S(1)}, u32[]{:S(2)}, u32[]{:S(2)}) collective-permute-start(bf16[3,256,512]{2,1,0:T(8,128)(2,1)} %get-tuple-element.16), channel_id=1, source_target_pairs={{0,1},{1,0},{2,3},{3,2},{4,5},{5,4},{6,7},{7,6},{8,9},{9,8},{10,11... | collective-permute-start | bytes 2359304 | tf_op jit(solution)/shard_map/ppermute | solution.py:320
  68.1 0.9 copy-start.9
  71.7 9.9 %collective-permute-start.11 = (bf16[3,64,512]{2,1,0:T(8,128)(2,1)}, bf16[3,64,512]{2,1,0:T(8,128)(2,1)S(1)}, u32[]{:S(2)}, u32[]{:S(2)}) collective-permute-start(bf16[3,64,512]{2,1,0:T(8,128)(2,1)} %get-tuple-element.18), channel_id=1, source_target_pairs={{0,4},{4,8},{8,12},{12,0},{1,5},{5,9},{9,13},{13,1},{2,6},{6,10},{... | collective-permute-start | bytes 589832 | tf_op jit(solution)/shard_map/ppermute | solution.py:324
  73.2 16.0 %collective-permute-start.12 = (bf16[3,64,512]{2,1,0:T(8,128)(2,1)}, bf16[3,64,512]{2,1,0:T(8,128)(2,1)S(1)}, u32[]{:S(2)}, u32[]{:S(2)}) collective-permute-start(bf16[3,64,512]{2,1,0:T(8,128)(2,1)} %get-tuple-element.19), channel_id=1, source_target_pairs={{0,8},{4,12},{8,0},{12,4},{1,9},{5,13},{9,1},{13,5},{2,10},{6,14},... | collective-permute-start | bytes 589832 | tf_op jit(solution)/shard_map/ppermute | solution.py:324
  74.5 14.6 %collective-permute-start.13 = (bf16[3,64,512]{2,1,0:T(8,128)(2,1)}, bf16[3,64,512]{2,1,0:T(8,128)(2,1)S(1)}, u32[]{:S(2)}, u32[]{:S(2)}) collective-permute-start(bf16[3,64,512]{2,1,0:T(8,128)(2,1)} %get-tuple-element.20), channel_id=1, source_target_pairs={{0,12},{4,0},{8,4},{12,8},{1,13},{5,1},{9,5},{13,9},{2,14},{6,2},{... | collective-permute-start | bytes 589832 | tf_op jit(solution)/shard_map/ppermute | solution.py:324
  81.6 7.6 %copy-start.13 = (bf16[3,64,512]{2,1,0:T(8,128)(2,1)}, bf16[3,64,512]{2,1,0:T(8,128)(2,1)S(1)}, u32[]{:S(2)}) copy-start(bf16[3,64,512]{2,1,0:T(8,128)(2,1)S(1)} %collective-permute-done.11.rest_0_) | copy-start | bytes 589828
  89.2 0.7 copy-start.14
  89.2 0.7 copy-start.15
  92.8 11.5 %collective-permute-start.16 = (bf16[3,64,512]{2,1,0:T(8,128)(2,1)}, bf16[3,64,512]{2,1,0:T(8,128)(2,1)S(1)}, u32[]{:S(2)}, u32[]{:S(2)}) collective-permute-start(bf16[3,64,512]{2,1,0:T(8,128)(2,1)} %update.1.rest_0_), channel_id=1, source_target_pairs={{0,12},{4,0},{8,4},{12,8},{1,13},{5,1},{9,5},{13,9},{2,14},{6,2},{... | collective-permute-start | bytes 589832 | tf_op jit(solution)/shard_map/ppermute | solution.py:324
  98.5 18.0 %collective-permute-start.15 = (bf16[3,64,512]{2,1,0:T(8,128)(2,1)}, bf16[3,64,512]{2,1,0:T(8,128)(2,1)S(1)}, u32[]{:S(2)}, u32[]{:S(2)}) collective-permute-start(bf16[3,64,512]{2,1,0:T(8,128)(2,1)} %update.1.rest_0_), channel_id=1, source_target_pairs={{0,8},{4,12},{8,0},{12,4},{1,9},{5,13},{9,1},{13,5},{2,10},{6,14},... | collective-permute-start | bytes 589832 | tf_op jit(solution)/shard_map/ppermute | solution.py:324
  98.9 17.7 %collective-permute-start.14 = (bf16[3,64,512]{2,1,0:T(8,128)(2,1)}, bf16[3,64,512]{2,1,0:T(8,128)(2,1)S(1)}, u32[]{:S(2)}, u32[]{:S(2)}) collective-permute-start(bf16[3,64,512]{2,1,0:T(8,128)(2,1)} %update.1.rest_0_), channel_id=1, source_target_pairs={{0,4},{4,8},{8,12},{12,0},{1,5},{5,9},{9,13},{13,1},{2,6},{6,10},{... | collective-permute-start | bytes 589832 | tf_op jit(solution)/shard_map/ppermute | solution.py:324
  99.1 17.9 %collective-permute-start.17 = (bf16[3,64,512]{2,1,0:T(8,128)(2,1)}, bf16[3,64,512]{2,1,0:T(8,128)(2,1)S(1)}, u32[]{:S(2)}, u32[]{:S(2)}) collective-permute-start(bf16[3,64,512]{2,1,0:T(8,128)(2,1)} %update.1.rest_0_), channel_id=1, source_target_pairs={{0,1},{1,0},{2,3},{3,2},{4,5},{5,4},{6,7},{7,6},{8,9},{9,8},{10,11... | collective-permute-start | bytes 589832 | tf_op jit(solution)/shard_map/ppermute | solution.py:320
  104.2 14.0 %copy-start.16 = (bf16[3,64,512]{2,1,0:T(8,128)(2,1)}, bf16[3,64,512]{2,1,0:T(8,128)(2,1)S(1)}, u32[]{:S(2)}) copy-start(bf16[3,64,512]{2,1,0:T(8,128)(2,1)S(1)} %collective-permute-done.16.rest_3_) | copy-start | bytes 589828
  104.2 12.8 %collective-permute-start.20 = (bf16[3,64,512]{2,1,0:T(8,128)(2,1)S(1)}, bf16[3,64,512]{2,1,0:T(8,128)(2,1)S(1)}, u32[]{:S(2)}, u32[]{:S(2)}) collective-permute-start(bf16[3,64,512]{2,1,0:T(8,128)(2,1)S(1)} %collective-permute-done.16.rest_3_), channel_id=1, source_target_pairs={{0,1},{1,0},{2,3},{3,2},{4,5},{5,4},{6,7},{7,6},{8,9},{9,8},{10,11... | collective-permute-start | bytes 589832 | tf_op jit(solution)/shard_map/ppermute | solution.py:320
  116.5 1.7 %copy-start.17 = (bf16[3,64,512]{2,1,0:T(8,128)(2,1)}, bf16[3,64,512]{2,1,0:T(8,128)(2,1)S(1)}, u32[]{:S(2)}) copy-start(bf16[3,64,512]{2,1,0:T(8,128)(2,1)S(1)} %collective-permute-done.15.rest_2_) | copy-start | bytes 589828
  116.5 1.4 collective-permute-start.19
  116.5 1.7 %copy-start.18 = (bf16[3,64,512]{2,1,0:T(8,128)(2,1)}, bf16[3,64,512]{2,1,0:T(8,128)(2,1)S(1)}, u32[]{:S(2)}) copy-start(bf16[3,64,512]{2,1,0:T(8,128)(2,1)S(1)} %collective-permute-done.14.rest_1_) | copy-start | bytes 589828
  116.5 1.7 %collective-permute-start.18 = (bf16[3,64,512]{2,1,0:T(8,128)(2,1)S(1)}, bf16[3,64,512]{2,1,0:T(8,128)(2,1)S(1)}, u32[]{:S(2)}, u32[]{:S(2)}) collective-permute-start(bf16[3,64,512]{2,1,0:T(8,128)(2,1)S(1)} %collective-permute-done.14.rest_1_), channel_id=1, source_target_pairs={{0,1},{1,0},{2,3},{3,2},{4,5},{5,4},{6,7},{7,6},{8,9},{9,8},{10,11... | collective-permute-start | bytes 589832 | tf_op jit(solution)/shard_map/ppermute | solution.py:320
  117.0 1.2 copy-start.19
  117.0 1.2 copy-start.20
  118.0 0.7 copy-start.21
  118.2 0.7 copy-start.22
  122.9 19.3 %collective-permute-start.21 = (bf16[512,512]{1,0:T(8,128)(2,1)}, bf16[512,512]{1,0:T(8,128)(2,1)S(1)}, u32[]{:S(2)}, u32[]{:S(2)}) collective-permute-start(bf16[512,512]{1,0:T(8,128)(2,1)} %get-tuple-element.23), channel_id=1, source_target_pairs={{0,2},{2,0},{1,3},{3,1},{4,6},{6,4},{5,7},{7,5},{8,10},{10,8},{9,1... | collective-permute-start | bytes 1572872 | tf_op jit(solution)/shard_map/ppermute | solution.py:320
  123.4 18.0 %collective-permute-start.22 = (bf16[192,512]{1,0:T(8,128)(2,1)}, bf16[192,512]{1,0:T(8,128)(2,1)S(1)}, u32[]{:S(2)}, u32[]{:S(2)}) collective-permute-start(bf16[192,512]{1,0:T(8,128)(2,1)} %get-tuple-element.25), channel_id=1, source_target_pairs={{0,2},{2,0},{1,3},{3,1},{4,6},{6,4},{5,7},{7,5},{8,10},{10,8},{9,1... | collective-permute-start | bytes 589832 | tf_op jit(solution)/shard_map/ppermute | solution.py:320
  124.9 16.4 %copy-start.23 = (bf16[192,512]{1,0:T(8,128)(2,1)S(1)}, bf16[192,512]{1,0:T(8,128)(2,1)}, u32[]{:S(2)}) copy-start(bf16[192,512]{1,0:T(8,128)(2,1)} %get-tuple-element.24) | copy-start | bytes 589828

commit v2 on v0

v2 whole, which is shorter than its diff:
```python
import functools
import math

import jax
import jax.numpy as jnp
from jax import lax
from jax.experimental import pallas as pl
from jax.experimental.pallas import tpu as pltpu
from jax.sharding import Mesh, PartitionSpec as P

H = 2
HD = 512
BLK = 512
HALF = 256
RATE_ROWS = 16
BF = jnp.bfloat16
F32 = jnp.float32
SWAP = [(0, 1), (1, 0)]
PARAMS = pltpu.CompilerParams(vmem_limit_bytes=20 << 20)
VM = pl.BlockSpec(memory_space=pltpu.VMEM)
SM = pl.BlockSpec(memory_space=pltpu.SMEM)


def mm(a, b, dims):
    return lax.dot_general(a, b, (dims, ((), ())), preferred_element_type=F32)


def mm_t(a, b):
    return mm(a, b, ((1,), (1,)))


def mm_n(a, b):
    return mm(a, b, ((1,), (0,)))


def mm_rows(a, b):
    return mm(a, b, ((0,), (0,)))


def rms(x):
    v = x.astype(F32)
    return (v * lax.rsqrt(jnp.mean(v * v, -1, keepdims=True) + 1e-06)).astype(BF)


def shape(dims, dtype=BF):
    return jax.ShapeDtypeStruct(dims, dtype)


def call(kernel, name, outs, scratch=()):
    def run(where, *args):
        return pl.pallas_call(
            kernel,
            in_specs=[SM] + [VM] * len(args),
            out_specs=[VM] * len(outs),
            out_shape=outs,
            scratch_shapes=scratch,
            compiler_params=PARAMS,
            name=name,
        )(where, *args)

    return run


def call_blocks(kernel, name, specs, outs, scratch=()):
    def run(where, *args):
        def whole(dims):
            return pl.BlockSpec(dims, lambda i, s: (0,) * len(dims))

        in_specs = [whole(a.shape) if p is None else p for a, p in zip(args, specs, strict=True)]
        return pl.pallas_call(
            kernel,
            grid_spec=pltpu.PrefetchScalarGridSpec(
                num_scalar_prefetch=1,
                grid=(1,),
                in_specs=in_specs,
                out_specs=[whole(o.shape) for o in outs],
                scratch_shapes=scratch,
            ),
            out_shape=outs,
            compiler_params=PARAMS,
            name=name,
        )(where, *args)

    return run


def pack_kernel(where, key, value, out):
    out[:, 0:HD] = key[...]
    out[:, HD : 2 * HD] = value[...]


def pack(where, key_rows, value_rows, first, count, own):
    def block(i, s):
        return (first // count, s[0] if own else 1 - s[0])

    return pl.pallas_call(
        pack_kernel,
        grid_spec=pltpu.PrefetchScalarGridSpec(
            num_scalar_prefetch=1,
            grid=(1,),
            in_specs=[pl.BlockSpec((count, HD), block)] * 2,
            out_specs=pl.BlockSpec((count, 2 * HD), lambda i, s: (0, 0)),
        ),
        out_shape=shape((count, 2 * HD)),
        compiler_params=PARAMS,
        name="pack",
    )(where, key_rows, value_rows)


def pick_kernel(where, foreign, key, value, out):
    own = where[0] == 1
    out[:, 0:HD] = jnp.where(own, key[...], foreign[:, 0:HD])
    out[:, HD : 2 * HD] = jnp.where(own, value[...], foreign[:, HD : 2 * HD])


def pick(where, foreign, key_rows, value_rows, n):
    part = pl.BlockSpec((HALF, HD), lambda i, s: (n, s[0]))
    return call_blocks(pick_kernel, "pick", [None, part, part], [shape((HALF, 2 * HD))])(
        where, foreign, key_rows, value_rows
    )[0]


def pack_q_kernel(where, query, rates, sent):
    sent[0:BLK, :] = query[...]
    rate = jnp.where(where[0] == 0, rates[1:2, :], rates[0:1, :])
    parts = []
    for _ in range(3):
        part = rate.astype(BF)
        parts.append(part)
        rate = rate - part.astype(F32)
    row = lax.broadcasted_iota(jnp.int32, (RATE_ROWS, BLK), 0)
    tail = jnp.zeros((RATE_ROWS, BLK), F32)
    for n, part in enumerate(parts):
        tail = jnp.where(row == n, part.astype(F32), tail)
    sent[BLK : BLK + RATE_ROWS, :] = tail.astype(BF)


def factors(core, key, wg, wu, put):
    for c in range(2):
        rows = pl.ds(c * HALF, HALF)
        kc = rms(key(c))
        put(0, rows, slice(None), kc)
        for side in range(2):
            units = pl.ds(side * HALF, HALF)
            hg = mm_t(kc, wg[units, :])
            hu = mm_t(kc, wu[units, :])
            sig = jax.nn.sigmoid(hg)
            a = hg * sig
            put(1, rows, units, (a * hu).astype(BF))

            @pl.when(core == side)
            def _():
                put(2, rows, slice(None), hu * sig * (1.0 + hg * (1.0 - sig)))
                put(3, rows, slice(None), a)


def pre_own_kernel(where, own, own2, wg, wu, *outs):
    for n, kv in enumerate((own, own2)):

        def put(i, rows, columns, value):
            outs[4 * n + i][rows, columns] = value

        factors(where[1], lambda c: kv[c * HALF : (c + 1) * HALF, 0:HD], wg, wu, put)


def pick_factors(where, halves, mine, wg, wu, outs, work):
    def put(i, rows, columns, value):
        work[i][rows, columns] = value

    factors(where[1], lambda c: halves[c][:, 0:HD], wg, wu, put)
    bottom = where[0] == 0
    for i in range(4):
        outs[i][...] = jnp.where(bottom, mine[i][...], work[i][...])
        outs[4 + i][...] = jnp.where(bottom, work[i][...], mine[i][...])


def pre_kernel(where, own, for_a, for_b, own2, for2_a, for2_b, *rest):
    mine, (wg, wu), (low, high, mid, low2), outs = rest[:4], rest[4:6], rest[6:10], rest[10:18]
    bottom = where[0] == 0
    first = where[1] == 0
    for c, (f, f2) in enumerate(((for_a, for2_a), (for_b, for2_b))):
        rows = pl.ds(c * HALF, HALF)
        low[rows, :] = jnp.where(bottom, own[rows, :], f[...])
        high[rows, :] = jnp.where(bottom, f[...], own[rows, :])
        l2 = jnp.where(bottom, own2[rows, :], f2[...])
        low2[rows, :] = l2
        mid[rows, :] = jnp.where(first, l2, jnp.where(bottom, f2[...], own2[rows, :]))
    pick_factors(where, (for_a, for_b), mine, wg, wu, outs, rest[18:])


def pre_other_kernel(where, for2_a, for2_b, *rest):
    pick_factors(where, (for2_a, for2_b), rest[:4], *rest[4:6], rest[6:14], rest[14:])


FACTORS = [
    shape((BLK, HD)),
    shape((BLK, HD)),
    shape((BLK, HALF), F32),
    shape((BLK, HALF), F32),
]


def pre_own(where, own, own2, w_gate, w_up):
    head = pl.BlockSpec((HD, HD), lambda i, s: (s[0], 0))
    return call_blocks(pre_own_kernel, "pre_own", [None] * 2 + [head] * 2, FACTORS * 2)(
        where, own, own2, w_gate, w_up
    )


def pre(kernel, where, pairs, mine, w_gate, w_up, outs):
    head = pl.BlockSpec((HD, HD), lambda i, s: (s[0], 0))
    specs = [None] * (len(pairs) + 4) + [head] * 2
    work = [pltpu.VMEM(f.shape, f.dtype) for f in FACTORS]
    return call_blocks(kernel, "pre", specs, outs + FACTORS * 2, work)(
        where, *pairs, *mine, w_gate, w_up
    )


def attend(q, rate, tile_a, tile_b, tile_c, a_ok, b_ok, att, err):
    scale = 1.0 / math.sqrt(HD)
    p = lax.broadcasted_iota(jnp.int32, (HALF, HALF), 0)
    j = lax.broadcasted_iota(jnp.int32, (HALF, HALF), 1)
    causal = j <= p
    neg = jnp.float32(-jnp.inf)
    zero = jnp.zeros((HALF, HALF), BF)

    def key(tile):
        return tile[:, 0:HD]

    def value(tile):
        return tile[:, HD : 2 * HD]

    for c in range(2):
        rows = pl.ds(c * HALF, HALF)
        qc = q(rows)
        tiles = []
        for t in range(2):
            if t <= c:
                sc = mm_t(qc, key(tile_c(t))) * scale
            if t >= c:
                sa = mm_t(qc, key(tile_a(t))) * scale
                if a_ok is not None:
                    sa = jnp.where(a_ok, sa, neg)
            tiles.append(sc if t < c else sa if t > c else jnp.where(causal, sc, sa))
        for t in range(2):
            sb = mm_t(qc, key(tile_b(t))) * scale
            tiles.append(sb if b_ok is None else jnp.where(b_ok, sb, neg))
        top = functools.reduce(jnp.maximum, [jnp.max(s, -1, keepdims=True) for s in tiles])
        expo = [jnp.exp(s - top) for s in tiles]
        total = functools.reduce(jnp.add, [jnp.sum(e, -1, keepdims=True) for e in expo])
        inv = 1.0 / total
        w = [(e * inv).astype(BF) for e in expo]
        acc = mm_n(w[2], value(tile_b(0))) + mm_n(w[3], value(tile_b(1)))
        for t in range(2):
            if t <= c:
                acc += mm_n(
                    jnp.where(causal, w[t], zero) if t == c else w[t], value(tile_c(t))
                )
            if t >= c:
                acc += mm_n(
                    jnp.where(causal, zero, w[t]) if t == c else w[t], value(tile_a(t))
                )
        out = acc.astype(BF)
        att[rows, :] = out
        err[rows, :] = (-rate[c * HALF : (c + 1) * HALF] * out.astype(F32)).astype(BF)


def column(mine, side, rates, q_for):
    parts = q_for[BLK : BLK + RATE_ROWS, :].astype(F32)
    other = parts[0:1, :] + parts[1:2, :] + parts[2:3, :]
    own = jnp.where(side == 0, rates[0:1, :], rates[1:2, :])
    line = jnp.where(mine, own, other)
    return jnp.transpose(jnp.broadcast_to(line, (8, BLK)))[:, 0:1]


def rows_of(ref):
    return lambda t: ref[t * HALF : (t + 1) * HALF, :]


def upper_kernel(where, q_own, q_for, rates, a, b, c, att, err):
    mine = where[0] == 1
    q = lambda rows: jnp.where(mine, q_own[rows, :], q_for[rows, :])
    r = column(mine, where[0], rates, q_for)
    attend(q, r, rows_of(a), rows_of(b), rows_of(c), None, None, att, err)


def lower_kernel(
    where, q_own, q_for, rates, halo_a, halo_b, halo2_a, halo2_b, low2, c, att, err, b
):
    mine = where[0] == 0
    first = where[1] == 0
    inner = where[2] > 0
    for t, h in enumerate((halo2_a, halo2_b)):
        rows = pl.ds(t * HALF, HALF)
        b[rows, :] = jnp.where(first, h[...], low2[rows, :])
    q = lambda rows: jnp.where(mine, q_own[rows, :], q_for[rows, :])
    r = column(mine, where[0], rates, q_for)
    halo = (halo_a, halo_b)
    attend(
        q, r, lambda t: halo[t][...], rows_of(b), rows_of(c), inner, inner | ~first, att, err
    )


def back_products(errs, kns, slopes, acts, w):
    gate = up = None
    for e, kn, slope, act in zip(errs, kns, slopes, acts, strict=True):
        back = mm_n(e[...], w[...])
        g = mm_rows((back * slope[...]).astype(BF), kn[...])
        u = mm_rows((back * act[...]).astype(BF), kn[...])
        gate = g if gate is None else gate + g
        up = u if up is None else up + u
    return gate, up


def down_products(errs, gateds):
    acc = None
    for e, g in zip(errs, gateds, strict=True):
        d = mm_rows(e[...], g[...])
        acc = d if acc is None else acc + d
    return acc


def grad_first_kernel(where, e0, e1, h0, h1, k0, k1, g0, g1, s0, s1, a0, a1, w, total):
    gate, up = back_products((e0, e1), (k0, k1), (s0, s1), (a0, a1), w)
    total[0] = gate
    total[1] = up
    total[2] = down_products((h0, h1), (g0, g1))


def grad_second_kernel(
    zs, where, e0, e1, h0, h1, k0, k1, g0, g1, s0, s1, a0, a1, before, w, own, *rest
):
    sends, total = rest[:-1], rest[-1]
    gate, up = back_products((e0, e1), (k0, k1), (s0, s1), (a0, a1), w)
    total[0] = before[0] + gate
    total[1] = before[1] + up
    total[2] = before[2] + down_products((h0, h1), (g0, g1))
    rows = HALF // zs
    for d in range(zs):
        src = pl.ds(pl.multiple_of(lax.rem(where[2] + d, zs) * rows, rows), rows)
        for kind in range(3):
            if d == 0:
                own[kind] = total[kind, src, :]
            else:
                sends[d - 1][kind] = total[kind, src, :].astype(BF)


def update_kernel(where, own, *rest):
    got, olds, (first, last) = rest[:-5], rest[-5:-2], rest[-2:]
    for kind, out in enumerate((first.at[0], first.at[1], last.at[0])):
        grad = own[kind]
        for g in got:
            grad = grad + g[kind].astype(F32)
        old = olds[kind][...].astype(F32)
        raised = old - grad
        factor = jnp.sqrt(jnp.mean(old * old, -1, keepdims=True) + 1e-06) * lax.rsqrt(
            jnp.mean(raised * raised, -1, keepdims=True) + 1e-06
        )
        out[...] = (raised * factor).astype(BF)


def update(zs, where, own, got, olds):
    rows = HALF // zs
    old = pl.BlockSpec((rows, HD), lambda i, s: ((s[0] * 2 + s[1]) * zs + s[2], 0))
    return call_blocks(
        update_kernel,
        "update",
        [None] * zs + [old] * 3,
        [shape((2, rows, HD)), shape((1, rows, HD))],
    )(where, own, *got, *olds)


def gather(zs, where, pieces, kinds, full):
    rows = HALF // zs
    for side, some in ((where[1], pieces[:zs]), (1 - where[1], pieces[zs:])):
        for d in range(zs):
            at = side * HALF + lax.rem(where[2] - d + zs, zs) * rows
            for kind in range(kinds):
                full[pl.ds(pl.multiple_of(kind * HD + at, rows), rows), :] = some[d][kind]


def windows(where, count, put):
    y, core, z = where[0], where[1], where[2]
    step = math.gcd(count, HD)
    for n, side in enumerate((1 - y, y)):
        first = ((z * 2 + side) * 2 + core) * count
        for c in range(count // step):
            r = first + c * step
            put(n, c * step, step, lax.div(r, 2 * HD), pl.multiple_of(lax.rem(r, HD), step))


def read_first_kernel(zs, count, where, *rest):
    pieces, (q_for, q_own) = rest[: 2 * zs], rest[2 * zs : 2 * zs + 2]
    g_for, g_own, given, kept, full = rest[2 * zs + 2 :]
    gather(zs, where, pieces, 2, full)
    outs = (given, kept)

    def put(n, to, step, kind, row):
        at = pl.multiple_of(lax.min(kind, 1) * HD + row, step)
        outs[n][to : to + step, :] = full[pl.ds(at, step), :]

    windows(where, count, put)
    for q, g in ((q_for, g_for), (q_own, g_own)):
        for c in range(2):
            rows = pl.ds(c * HALF, HALF)
            qn = rms(q[rows, :])
            hg = mm_t(qn, full[0:HD, :])
            hu = mm_t(qn, full[HD : 2 * HD, :])
            g[rows, :] = (hg * jax.nn.sigmoid(hg) * hu).astype(BF)


def read_down_kernel(zs, count, where, *rest):
    pieces = rest[: 2 * zs]
    g_for, att_low, att_up, some_given, some_kept, sent, full, kept = rest[2 * zs :]
    gather(zs, where, pieces, 1, full)
    low = where[0] == 1
    sent[0:BLK, :] = (
        jnp.where(low, att_low[...], att_up[...]).astype(F32) + mm_t(g_for[...], full[...])
    ).astype(BF)
    outs, before = (sent, kept), (some_given, some_kept)

    def put(n, to, step, kind, row):
        rows = slice(to, to + step)
        at = slice(to + BLK, to + BLK + step) if n == 0 else rows
        outs[n][at, :] = jnp.where(kind == 2, full[pl.ds(row, step), :], before[n][rows, :])

    windows(where, count, put)


def read_own_kernel(where, g_own, att_low, att_up, w, out):
    low = where[0] == 0
    out[...] = (
        jnp.where(low, att_low[...], att_up[...]).astype(F32) + mm_t(g_own[...], w[...])
    ).astype(BF)


def read_own(where, g_own, att_low, att_up, w):
    whole = pl.BlockSpec((BLK, HD), lambda i, s: (0, 0))
    return pl.pallas_call(
        read_own_kernel,
        grid_spec=pltpu.PrefetchScalarGridSpec(
            num_scalar_prefetch=1,
            grid=(1,),
            in_specs=[whole] * 4,
            out_specs=pl.BlockSpec((BLK, HD), lambda i, s: (0, s[0])),
        ),
        out_shape=shape((BLK, H * HD)),
        compiler_params=PARAMS,
        name="read_own",
    )(where, g_own, att_low, att_up, w)


def place_kernel(count, where, got, kept, half_filled, out, weights):
    y, core, z = where[0], where[1], where[2]
    out[...] = got[0:BLK, :]
    step = math.gcd(count, HD)
    first = ((z * 2 + y) * 2 + core) * count
    for c in range(count // step):
        rows = slice(c * step, (c + 1) * step)
        head = lax.rem(lax.div(first + c * step, HD), 2)
        weights[rows, :] = jnp.where(
            head == y, kept[rows, :], got[BLK + c * step : BLK + (c + 1) * step, :]
        )


def place(where, count, got, kept, half_filled):
    def whole(rows):
        return pl.BlockSpec((rows, HD), lambda i, s: (0, 0))

    return pl.pallas_call(
        functools.partial(place_kernel, count),
        grid_spec=pltpu.PrefetchScalarGridSpec(
            num_scalar_prefetch=1,
            grid=(1,),
            in_specs=[whole(BLK + count), whole(count), pl.BlockSpec(memory_space=pl.ANY)],
            out_specs=[pl.BlockSpec((BLK, HD), lambda i, s: (0, 1 - s[0])), whole(count)],
        ),
        out_shape=[shape((BLK, H * HD)), shape((count, HD))],
        input_output_aliases={3: 0},
        compiler_params=PARAMS,
        name="place",
    )(where, got, kept, half_filled)


def local(queries, key_rows, value_rows, step_rates, w_gate, w_up, w_down):
    zs = lax.axis_size("z")
    z, y, core = lax.axis_index("z"), lax.axis_index("y"), lax.axis_index("core")
    where = jnp.stack([y, core, z]).astype(jnp.int32)
    rows = HALF // zs
    count = 3 * H * HD // (4 * zs)

    def swap(value, axis):
        return lax.ppermute(value, axis, SWAP)

    def shift(value, d, ring=True):
        return lax.ppermute(
            value, "z", [(i, (i + d) % zs) for i in range(zs) if ring or i + d < zs]
        )

    two = [shape((BLK, HD))] * 2

    def after(value, earlier):
        return lax.optimization_barrier((value, earlier))[0]

    q_other = pl.BlockSpec((BLK, HD), lambda i, s: (0, 1 - s[0]))
    sent_a = pack(where, key_rows, value_rows, 0, HALF, False)
    sent_b = pack(where, after(key_rows, sent_a), value_rows, HALF, HALF, False)
    sent_q = call_blocks(
        pack_q_kernel, "pack_q", [q_other, None], [shape((BLK + RATE_ROWS, HD))]
    )(where, after(queries, sent_b), step_rates)[0]
    own = pack(where, after(key_rows, sent_b), value_rows, 0, BLK, True)
    theirs = [swap(sent_a, "y"), swap(sent_b, "y")]
    q_for = swap(sent_q, "y")
    q_own = jnp.where(y == 0, queries[:, :HD], queries[:, HD:])
    own2 = swap(own, "core")
    gone = pick(where, theirs[0], key_rows, value_rows, 0)
    halo_a = shift(gone, 1, ring=False)
    theirs2 = [swap(after(theirs[0], gone), "core")]
    theirs[1], own2, theirs2[0] = lax.optimization_barrier((theirs[1], own2, theirs2[0]))
    gone = pick(where, theirs[1], key_rows, value_rows, 1)
    halo_b = shift(gone, 1, ring=False)
    theirs2.append(swap(after(theirs[1], gone), "core"))
    theirs2, halo_a = lax.optimization_barrier((theirs2, halo_a))
    mine = pre_own(where, own, own2, w_gate, w_up)
    kv_low, kv_high, kv_mid, kv_low2, *blocks = pre(
        pre_kernel,
        where,
        (own, *theirs, own2, *theirs2),
        mine[:4],
        w_gate,
        w_up,
        [shape((BLK, 2 * HD))] * 4,
    )
    theirs2, q_for, blocks = lax.optimization_barrier((theirs2, q_for, blocks))
    blocks += pre(pre_other_kernel, where, theirs2, mine[4:], w_gate, w_up, [])
    blocks, q_for, halo = lax.optimization_barrier((blocks, q_for, (halo_a, halo_b)))
    low, high, low2, high2 = (blocks[4 * n : 4 * n + 4] for n in range(4))
    halo2 = [swap(h, "core") for h in halo]

    att_up, err_up = call(upper_kernel, "attend_upper", two)(
        where, q_own, q_for, step_rates, kv_low, kv_mid, kv_high
    )
    err_up2 = swap(err_up, "core")
    att_low, err_low = call(
        lower_kernel, "attend_lower", two, [pltpu.VMEM((BLK, 2 * HD), BF)]
    )(where, q_own, q_for, step_rates, *halo, *halo2, kv_low2, kv_low)
    err_low2 = swap(err_low, "core")

    w_half = pl.BlockSpec((HD, HALF), lambda i, s: (s[0], s[1]))
    err_half = pl.BlockSpec((BLK, HALF), lambda i, s: (0, s[1]))

    def grads(kernel, name, outs, errs, pair, *more, scratch=()):
        specs = [None] * 2 + [err_half] * 2 + [None] * (8 + len(more)) + [w_half]
        factors = [pair[i][n] for n in range(4) for i in range(2)]
        return call_blocks(kernel, name, specs, outs, scratch)(
            where, *errs, *errs, *factors, *more, w_down
        )

    total = shape((3, HALF, HD), F32)
    first = grads(grad_first_kernel, "grad_first", [total], (err_up, err_up2), (high, high2))[0]
    own_sum, *sends = grads(
        functools.partial(grad_second_kernel, zs),
        "grad_second",
        [shape((3, rows, HD), F32)] + [shape((3, rows, HD))] * (zs - 1),
        (err_low, err_low2),
        (low, low2),
        first,
        scratch=[pltpu.VMEM(total.shape, F32)],
    )
    got = [shift(s, d) for d, s in enumerate(sends, 1)]
    piece_a, piece_b = update(zs, where, own_sum, got, (w_gate, w_up, w_down))

    def around(piece):
        return [piece] + [shift(piece, d) for d in range(1, zs)]

    def both(mine):
        return mine + [swap(p, "core") for p in mine]

    pieces_a = both(around(piece_a))
    pieces_b = around(piece_b)
    window = shape((count, HD))
    g_for, g_own, some_given, some_kept = call(
        functools.partial(read_first_kernel, zs, count),
        "read_first",
        two + [window] * 2,
        [pltpu.VMEM((2 * HD, HD), BF)],
    )(where, *pieces_a, q_for, q_own)
    g_for, pieces_b = lax.optimization_barrier((g_for, pieces_b))
    pieces_b = both(pieces_b)
    sent, full, kept = call(
        functools.partial(read_down_kernel, zs, count),
        "read_down",
        [shape((BLK + count, HD)), shape((HD, HD)), window],
    )(where, *pieces_b, g_for, att_low, att_up, some_given, some_kept)
    got_out = swap(sent, "y")
    half_filled = read_own(where, g_own, att_low, att_up, full)
    return tuple(place(where, count, got_out, kept, half_filled))


def solution(mesh):
    groups, ctx = mesh.devices.shape
    split = Mesh(mesh.devices.reshape(groups, ctx // 4, 2, 2), ("groups", "z", "y", "core"))
    tokens = ("groups", "z", "y", "core")
    return jax.shard_map(
        local,
        mesh=split,
        in_specs=(
            P(tokens, None),
            P(tokens, None),
            P(tokens, None),
            P(None, tokens),
            P("groups", None),
            P("groups", None),
            P("groups", None),
        ),
        out_specs=(P(tokens, None), P(tokens, None)),
        check_vma=False,
    )
```

time: 284 us -> 141 us (0.50)
  waiting for transfers between devices: 188 us -> 54.3 us
  Pallas kernels: 0 us -> 31.5 us
  matrix products: 26.9 us -> 0 us
  other arithmetic: 24.4 us -> 1.42 us
  starting transfers between devices: 15.5 us -> 35.3 us
  between operations: 14.2 us -> 1.27 us
    psum x1 -> x0, waiting for transfers between devices: 162 us -> none  [local(): summed = lax.psum(grads, 'ctx')]
    pallas_call x0 -> x18, Pallas kernels: none -> 31.5 us  [the longest x9 16.1 us: run(): pl.pallas_call(kernel, grid_spec=pltpu.PrefetchScalarGridSpec(num_scalar_...]
    ppermute x4 -> x30, waiting for transfers between devices: 25.5 us -> 54.3 us  [the longest x19 32 us: swap(): return lax.ppermute(value, axis, SWAP)]
    dot_general x10 -> x0, matrix products: 26.9 us -> none  [the longest x1 7.75 us: local(): jnp.einsum('hqk,khd->qhd', weights, v_block, preferred_element_type=jnp.f...]
    ppermute x4 -> x30, starting transfers between devices: 15.5 us -> 35.3 us  [the longest x11 25.9 us: shift(): lax.ppermute(value, 'z', [(i, (i + d) % zs) for i in range(zs) if ring or...]
    unnamed x36 -> x98, local copies, waits for them, and re-layouts: 6.35 us -> 17.1 us
    concatenate x3 -> x0, other arithmetic: 8.33 us -> none  [the longest x1 3.37 us: local(): jnp.concatenate([grad_gate.reshape(H * HD, HD), grad_up.reshape(H * HD, H...]
    convert_element_type x2 -> x0, other arithmetic: 6.93 us -> none  [the longest x1 5.05 us: normalize_rows(): return (raised * factor).astype(jnp.bfloat16)]
  transfers between devices with their start and end apart: 5 -> 30, of which waited for: 2 -> 14; matrix products, arithmetic and copies ran while one was open for 6% -> 1% of each run, Pallas kernels for 0% -> 18%
where the time goes in v2:
time: 141 us
  waiting for transfers between devices  54.3 us (39%)
  starting transfers between devices  35.3 us (25%)
  Pallas kernels  31.5 us (22%)
  local copies, waits for them, and re-layouts  17.1 us (12%)
  other arithmetic  1.42 us (1%)
    ppermute x19, waiting for transfers between devices, swap(): return lax.ppermute(value, axis, SWAP)  32 us
    ppermute x11, starting transfers between devices, shift(): lax.ppermute(value, 'z', [(i, (i + d) % zs) for i in range(zs) if ring or...  25.9 us
    ppermute x11, waiting for transfers between devices, shift(): lax.ppermute(value, 'z', [(i, (i + d) % zs) for i in range(zs) if ring or...  22.3 us
    unnamed x98, local copies, waits for them, and re-layouts  17.1 us
    pallas_call x9, Pallas kernels, run(): pl.pallas_call(kernel, grid_spec=pltpu.PrefetchScalarGridSpec(num_scalar_...  16.1 us
    pallas_call x4, Pallas kernels, run(): pl.pallas_call(kernel, in_specs=[SM] + [VM] * len(args), out_specs=[VM] *...  10.4 us
    ppermute x19, starting transfers between devices, swap(): return lax.ppermute(value, axis, SWAP)  9.36 us
  transfers between devices with their start and end apart: 30, of which 14 were waited for; matrix products, arithmetic and copies ran while one was open for 1% of the time, Pallas kernels for 18%

profile of v2, /device:TPU:0, one launch (start us, length us, event | category | flops | bytes accessed | tf_op | source)
XLA Modules:
  0.0 141.0 jit_solution(6705624288870890892)
XLA Ops:
  0.7 1.2 copy-done
  1.9 1.2 copy-done.2
  3.7 3.0 %collective-permute-start.2 = (bf16[256,1024]{1,0:T(8,128)(2,1)S(1)}, bf16[256,1024]{1,0:T(8,128)(2,1)S(1)}, u32[]{:S(2)}, u32[]{:S(2)}) collective-permute-start(bf16[256,1024]{1,0:T(8,128)(2,1)S(1)} %pack.3), channel_id=1, source_target_pairs={{0,2},{2,0},{1,3},{3,1},{4,6},{6,4},{5,7},{7,5},{8,10},{10,8},{9,1... | collective-permute-start | bytes 1572872 | tf_op jit(solution)/shard_map/ppermute | solution.py:493
  8.2 11.4 %collective-permute-done.2.foreign.for_a = bf16[256,1024]{1,0:T(8,128)(2,1)S(1)} collective-permute-done((bf16[256,1024]{1,0:T(8,128)(2,1)S(1)}, bf16[256,1024]{1,0:T(8,128)(2,1)S(1)}, u32[]{:S(2)}, u32[]{:S(2)}) %collective-permute-start.2) | collective-permute-done | bytes 524320 | tf_op jit(solution)/shard_map/ppermute | solution.py:493
  20.9 2.1 %collective-permute-start.6 = (bf16[528,512]{1,0:T(8,128)(2,1)S(1)}, bf16[528,512]{1,0:T(8,128)(2,1)S(1)}, u32[]{:S(2)}, u32[]{:S(2)}) collective-permute-start(bf16[528,512]{1,0:T(8,128)(2,1)S(1)} %pack_q.1), channel_id=1, source_target_pairs={{0,2},{2,0},{1,3},{3,1},{4,6},{6,4},{5,7},{7,5},{8,10},{10,8},{9,1... | collective-permute-start | bytes 1622024 | tf_op jit(solution)/shard_map/ppermute | solution.py:493
  23.0 3.5 %collective-permute-start.5 = (bf16[256,1024]{1,0:T(8,128)(2,1)S(1)}, bf16[256,1024]{1,0:T(8,128)(2,1)S(1)}, u32[]{:S(2)}, u32[]{:S(2)}) collective-permute-start(bf16[256,1024]{1,0:T(8,128)(2,1)S(1)} %pick.2), channel_id=1, source_target_pairs={{0,4},{4,8},{8,12},{1,5},{5,9},{9,13},{2,6},{6,10},{10,14},{3,7},{... | collective-permute-start | bytes 1572872 | tf_op jit(solution)/shard_map/ppermute | solution.py:496
  26.5 4.3 %collective-permute-done.foreign.for_b = bf16[256,1024]{1,0:T(8,128)(2,1)S(1)} collective-permute-done((bf16[256,1024]{1,0:T(8,128)(2,1)S(1)}, bf16[256,1024]{1,0:T(8,128)(2,1)S(1)}, u32[]{:S(2)}, u32[]{:S(2)}) %collective-permute-start) | collective-permute-done | bytes 524320 | tf_op jit(solution)/shard_map/ppermute | solution.py:493
  31.5 4.9 %collective-permute-start.7 = (bf16[256,1024]{1,0:T(8,128)(2,1)S(1)}, bf16[256,1024]{1,0:T(8,128)(2,1)}, u32[]{:S(2)}, u32[]{:S(2)}) collective-permute-start(bf16[256,1024]{1,0:T(8,128)(2,1)S(1)} %pick.3), channel_id=1, source_target_pairs={{0,4},{4,8},{8,12},{1,5},{5,9},{9,13},{2,6},{6,10},{10,14},{3,7},{... | collective-permute-start | bytes 1572872 | tf_op jit(solution)/shard_map/ppermute | solution.py:496
  36.4 3.7 %pre_own.1 = (bf16[512,512]{1,0:T(8,128)(2,1)S(1)}, bf16[512,512]{1,0:T(8,128)(2,1)S(1)}, f32[512,256]{1,0:T(8,128)S(1)}, f32[512,256]{1,0:T(8,128)S(1)}, bf16[5...) custom-call(s32[3]{0:T(128)S(1)} %pad_add_fusion.where, ...), custom_call_target="tpu_custom_call" | custom-call | tf_op jit(solution)/shard_map/pre_own/pallas_call | solution.py:70
  40.1 3.1 %pre.2 = (bf16[512,1024]{1,0:T(8,128)(2,1)S(1)}, bf16[512,1024]{1,0:T(8,128)(2,1)S(1)}, bf16[512,1024]{1,0:T(8,128)(2,1)S(1)}, bf16[512,1024]{1,0:T(8,128)(2,1)S...) custom-call(s32[3]{0:T(128)S(1)} %pad_add_fusion.where, ...), custom_call_target="tpu_custom_call" | custom-call | tf_op jit(solution)/shard_map/pre/pallas_call | solution.py:70
  43.2 1.0 copy-done.8
  44.1 1.0 copy-done.10
  45.1 1.0 copy-done.12
  46.1 1.0 copy-done.14
  47.1 0.8 copy-done.16
  48.7 2.8 %pre.3 = (bf16[512,512]{1,0:T(8,128)(2,1)S(1)}, bf16[512,512]{1,0:T(8,128)(2,1)S(1)}, f32[512,256]{1,0:T(8,128)S(1)}, f32[512,256]{1,0:T(8,128)S(1)}, bf16[512,5...) custom-call(s32[3]{0:T(128)S(1)} %pad_add_fusion.where, ...), custom_call_target="tpu_custom_call" | custom-call | tf_op jit(solution)/shard_map/pre/pallas_call | solution.py:70
  51.5 0.8 copy-done.32
  52.3 0.8 copy-done.34
  53.9 0.8 copy-done.38
  54.7 0.8 copy-done.40
  56.3 0.8 copy-done.44
  57.1 0.8 copy-done.46
  58.5 1.3 slice_select_fusion.q_own.rest_9_
  60.0 1.2 copy-done.11
  61.2 1.2 copy-done.13
  62.5 3.2 %attend_upper.1 = (bf16[512,512]{1,0:T(8,128)(2,1)S(1)}, bf16[512,512]{1,0:T(8,128)(2,1)S(1)}) custom-call(s32[3]{0:T(128)S(1)} %pad_add_fusion.where, bf16[512,512]{1,0:T(8,128)(2,1)S(1)} %slice_select_fusion.q_own.rest_9_, bf16[528,512]{1,0:T(8,128)(2,1)S(1)} %collective-permute-done.6.q_for.rest_8_, f32[2,512]{1,0:T(2,128)S(1)} %copy-done.48, ...), custom_call_target="tpu_custom_call" | custom-call | tf_op jit(solution)/shard_map/attend_upper/pallas_call | solution.py:51
  66.1 4.2 %attend_lower.1 = (bf16[512,512]{1,0:T(8,128)(2,1)S(1)}, bf16[512,512]{1,0:T(8,128)(2,1)S(1)}) custom-call(s32[3]{0:T(128)S(1)} %pad_add_fusion.where, bf16[512,512]{1,0:T(8,128)(2,1)S(1)} %slice_select_fusion.q_own.rest_9_, bf16[528,512]{1,0:T(8,128)(2,1)S(1)} %collective-permute-done.6.q_for.rest_8_, f32[2,512]{1,0:T(2,128)S(1)} %copy-done.48, ...), custom_call_target="tpu_custom_call" | custom-call | tf_op jit(solution)/shard_map/attend_lower/pallas_call | solution.py:51
  70.8 1.9 %grad_first.1.before = f32[3,256,512]{2,1,0:T(8,128)S(1)} custom-call(s32[3]{0:T(128)S(1)} %pad_add_fusion.where, bf16[512,512]{1,0:T(8,128)(2,1)S(1)} %get-tuple-element.155.e0.h0, bf16[512,512]{1,0:T(8,128)(2,1)S(1)} %collective-permute-done.11.e1.h1, bf16[512,512]{1,0:T(8,128)(2,1)S(1)} %get-tuple-element.155.e0.h0, ...), custom_call_target="tpu_custom_call" | custom-call | tf_op jit(solution)/shard_map/grad_first/pallas_call | solution.py:70
  72.8 2.1 %grad_second.1 = (f32[3,64,512]{2,1,0:T(8,128)S(1)}, bf16[3,64,512]{2,1,0:T(8,128)(2,1)S(1)}, bf16[3,64,512]{2,1,0:T(8,128)(2,1)S(1)}, bf16[3,64,512]{2,1,0:T(8,128)(2,1)S(1)}) custom-call(s32[3]{0:T(128)S(1)} %pad_add_fusion.where, bf16[512,512]{1,0:T(8,128)(2,1)S(1)} %get-tuple-element.144.e0.h0, bf16[512,512]{1,0:T(8,128)(2,1)S(1)} %collective-permute-done.10.e1.h1, ...), custom_call_target="tpu_custom_call" | custom-call | tf_op jit(solution)/shard_map/grad_second/pallas_call | solution.py:70
  74.9 1.2 collective-permute-start.12
  76.1 2.6 %collective-permute-start.13 = (bf16[3,64,512]{2,1,0:T(8,128)(2,1)S(1)}, bf16[3,64,512]{2,1,0:T(8,128)(2,1)S(1)}, u32[]{:S(2)}, u32[]{:S(2)}) collective-permute-start(bf16[3,64,512]{2,1,0:T(8,128)(2,1)S(1)} %get-tuple-element.166), channel_id=1, source_target_pairs={{0,8},{4,12},{8,0},{12,4},{1,9},{5,13},{9,1},{13,5},{2,10},{6,14},... | collective-permute-start | bytes 589832 | tf_op jit(solution)/shard_map/ppermute | solution.py:496
  78.7 1.3 collective-permute-start.14
  80.0 4.6 %collective-permute-done.12.rest_0_ = bf16[3,64,512]{2,1,0:T(8,128)(2,1)S(1)} collective-permute-done((bf16[3,64,512]{2,1,0:T(8,128)(2,1)S(1)}, bf16[3,64,512]{2,1,0:T(8,128)(2,1)S(1)}, u32[]{:S(2)}, u32[]{:S(2)}) %collective-permute-start.12) | collective-permute-done | bytes 196640 | tf_op jit(solution)/shard_map/ppermute | solution.py:496
  84.7 7.7 %collective-permute-done.13.rest_1_ = bf16[3,64,512]{2,1,0:T(8,128)(2,1)S(1)} collective-permute-done((bf16[3,64,512]{2,1,0:T(8,128)(2,1)S(1)}, bf16[3,64,512]{2,1,0:T(8,128)(2,1)S(1)}, u32[]{:S(2)}, u32[]{:S(2)}) %collective-permute-start.13) | collective-permute-done | bytes 196640 | tf_op jit(solution)/shard_map/ppermute | solution.py:496
  93.1 4.5 %collective-permute-start.15 = (bf16[2,64,512]{2,1,0:T(8,128)(2,1)S(1)}, bf16[2,64,512]{2,1,0:T(8,128)(2,1)S(1)}, u32[]{:S(2)}, u32[]{:S(2)}) collective-permute-start(bf16[2,64,512]{2,1,0:T(8,128)(2,1)S(1)} %get-tuple-element.168.rest_0_), channel_id=1, source_target_pairs={{0,4},{4,8},{8,12},{12,0},{1,5},{5,9},{9,13},{13,1},{2,6},{6,10},{... | collective-permute-start | bytes 393224 | tf_op jit(solution)/shard_map/ppermute | solution.py:496
  97.6 1.2 collective-permute-start.16
  98.9 1.2 collective-permute-start.17
  100.1 2.1 %collective-permute-done.15.rest_1_ = bf16[2,64,512]{2,1,0:T(8,128)(2,1)S(1)} collective-permute-done((bf16[2,64,512]{2,1,0:T(8,128)(2,1)S(1)}, bf16[2,64,512]{2,1,0:T(8,128)(2,1)S(1)}, u32[]{:S(2)}, u32[]{:S(2)}) %collective-permute-start.15) | collective-permute-done | bytes 131104 | tf_op jit(solution)/shard_map/ppermute | solution.py:496
  102.2 4.7 %collective-permute-done.16.rest_2_ = bf16[2,64,512]{2,1,0:T(8,128)(2,1)S(1)} collective-permute-done((bf16[2,64,512]{2,1,0:T(8,128)(2,1)S(1)}, bf16[2,64,512]{2,1,0:T(8,128)(2,1)S(1)}, u32[]{:S(2)}, u32[]{:S(2)}) %collective-permute-start.16) | collective-permute-done | bytes 131104 | tf_op jit(solution)/shard_map/ppermute | solution.py:496
  107.5 2.8 %collective-permute-start.22 = (bf16[1,64,512]{2,1,0:T(8,128)(2,1)S(1)}, bf16[1,64,512]{2,1,0:T(8,128)(2,1)S(1)}, u32[]{:S(2)}, u32[]{:S(2)}) collective-permute-start(bf16[1,64,512]{2,1,0:T(8,128)(2,1)S(1)} %get-tuple-element.171.rest_0_), channel_id=1, source_target_pairs={{0,4},{4,8},{8,12},{12,0},{1,5},{5,9},{9,13},{13,1},{2,6},{6,10},{... | collective-permute-start | bytes 196616 | tf_op jit(solution)/shard_map/ppermute | solution.py:496
  110.3 2.7 %collective-permute-start.23 = (bf16[1,64,512]{2,1,0:T(8,128)(2,1)S(1)}, bf16[1,64,512]{2,1,0:T(8,128)(2,1)S(1)}, u32[]{:S(2)}, u32[]{:S(2)}) collective-permute-start(bf16[1,64,512]{2,1,0:T(8,128)(2,1)S(1)} %get-tuple-element.171.rest_0_), channel_id=1, source_target_pairs={{0,8},{4,12},{8,0},{12,4},{1,9},{5,13},{9,1},{13,5},{2,10},{6,14},... | collective-permute-start | bytes 196616 | tf_op jit(solution)/shard_map/ppermute | solution.py:496
  113.0 1.9 %read_first.1 = (bf16[512,512]{1,0:T(8,128)(2,1)S(1)}, bf16[512,512]{1,0:T(8,128)(2,1)S(1)}, bf16[192,512]{1,0:T(8,128)(2,1)S(1)}, bf16[192,512]{1,0:T(8,128)(2,1)S(1)}) custom-call(s32[3]{0:T(128)S(1)} %pad_add_fusion.where, bf16[2,64,512]{2,1,0:T(8,128)(2,1)S(1)} %get-tuple-element.168.rest_0_, bf16[2,64,512]{2,1,0:T(8,128)(2,1)S(1)} %collective-permute-done.15.rest_1_, ...), custom_call_target="tpu_custom_call" | custom-call | tf_op jit(solution)/shard_map/read_first/pallas_call | solution.py:51
  115.4 2.2 %collective-permute-done.23.rest_2_ = bf16[1,64,512]{2,1,0:T(8,128)(2,1)S(1)} collective-permute-done((bf16[1,64,512]{2,1,0:T(8,128)(2,1)S(1)}, bf16[1,64,512]{2,1,0:T(8,128)(2,1)S(1)}, u32[]{:S(2)}, u32[]{:S(2)}) %collective-permute-start.23) | collective-permute-done | bytes 65568 | tf_op jit(solution)/shard_map/ppermute | solution.py:496
  120.0 1.1 read_down.1
  121.1 1.2 collective-permute-start.29
  122.3 1.8 %read_own.1.half_filled = bf16[512,1024]{1,0:T(8,128)(2,1)} custom-call(s32[3]{0:T(128)S(1)} %pad_add_fusion.where, bf16[512,512]{1,0:T(8,128)(2,1)S(1)} %get-tuple-element.182.g_own, bf16[512,512]{1,0:T(8,128)(2,1)S(1)} %get-tuple-element.176.rest_9_.att_low, bf16[512,512]{1,0:T(8,128)(2,1)S(1)} %get-tuple-element.177.rest_10_.att_up, ...), custom_call_target="tpu_custom_call" | custom-call | tf_op jit(solution)/shard_map/read_own/pallas_call | solution.py:439
  124.1 15.4 %collective-permute-done.29.got = bf16[704,512]{1,0:T(8,128)(2,1)S(1)} collective-permute-done((bf16[704,512]{1,0:T(8,128)(2,1)S(1)}, bf16[704,512]{1,0:T(8,128)(2,1)S(1)}, u32[]{:S(2)}, u32[]{:S(2)}) %collective-permute-start.29) | collective-permute-done | bytes 720928 | tf_op jit(solution)/shard_map/ppermute | solution.py:493
  139.5 1.4 %place.1 = (bf16[512,1024]{1,0:T(8,128)(2,1)}, bf16[192,512]{1,0:T(8,128)(2,1)}) custom-call(s32[3]{0:T(128)S(1)} %pad_add_fusion.where, bf16[704,512]{1,0:T(8,128)(2,1)S(1)} %collective-permute-done.29.got, bf16[192,512]{1,0:T(8,128)(2,1)S(1)} %get-tuple-element.181.kept, bf16[512,1024]{1,0:T(8,128)(2,1)} %read_own.1.half_filled), custom_call_target="tpu_custom_call", output_to_operand_aliasing={{0}: (3, {})} | custom-call | tf_op jit(solution)/shard_map/place/pallas_call | solution.py:470
  (130 shorter events, 12.0 us)
Async XLA Ops:
  3.7 15.8 %collective-permute-start.2 = (bf16[256,1024]{1,0:T(8,128)(2,1)S(1)}, bf16[256,1024]{1,0:T(8,128)(2,1)S(1)}, u32[]{:S(2)}, u32[]{:S(2)}) collective-permute-start(bf16[256,1024]{1,0:T(8,128)(2,1)S(1)} %pack.3), channel_id=1, source_target_pairs={{0,2},{2,0},{1,3},{3,1},{4,6},{6,4},{5,7},{7,5},{8,10},{10,8},{9,1... | collective-permute-start | bytes 1572872 | tf_op jit(solution)/shard_map/ppermute | solution.py:493
  8.0 12.2 %copy-start.7 = (bf16[512,1024]{1,0:T(8,128)(2,1)S(1)}, bf16[512,1024]{1,0:T(8,128)(2,1)}, u32[]{:S(2)}) copy-start(bf16[512,1024]{1,0:T(8,128)(2,1)} %query) | copy-start | bytes 3145732
  8.0 12.2 %copy-start.48 = (f32[2,512]{1,0:T(2,128)S(1)}, f32[2,512]{1,0:T(2,128)}, u32[]{:S(2)}) copy-start(f32[2,512]{1,0:T(2,128)} %rates.5) | copy-start | bytes 12292
  8.0 22.8 %collective-permute-start.1 = (bf16[512,1024]{1,0:T(8,128)(2,1)S(1)}, bf16[512,1024]{1,0:T(8,128)(2,1)S(1)}, u32[]{:S(2)}, u32[]{:S(2)}) collective-permute-start(bf16[512,1024]{1,0:T(8,128)(2,1)S(1)} %pack.5.own), channel_id=1, source_target_pairs={{0,1},{1,0},{2,3},{3,2},{4,5},{5,4},{6,7},{7,6},{8,9},{9,8},{10,11... | collective-permute-start | bytes 3145736 | tf_op jit(solution)/shard_map/ppermute | solution.py:493
  8.1 22.7 %collective-permute-start = (bf16[256,1024]{1,0:T(8,128)(2,1)S(1)}, bf16[256,1024]{1,0:T(8,128)(2,1)S(1)}, u32[]{:S(2)}, u32[]{:S(2)}) collective-permute-start(bf16[256,1024]{1,0:T(8,128)(2,1)S(1)} %pack.4), channel_id=1, source_target_pairs={{0,2},{2,0},{1,3},{3,1},{4,6},{6,4},{5,7},{7,5},{8,10},{10,8},{9,1... | collective-permute-start | bytes 1572872 | tf_op jit(solution)/shard_map/ppermute | solution.py:493
  19.5 11.2 %copy-start.3 = (bf16[512,1024]{1,0:T(8,128)(2,1)S(1)}, bf16[512,1024]{1,0:T(8,128)(2,1)}, u32[]{:S(2)}) copy-start(bf16[512,1024]{1,0:T(8,128)(2,1)} %value.9) | copy-start | bytes 3145732
  20.1 10.6 %copy-start.1 = (bf16[512,1024]{1,0:T(8,128)(2,1)S(1)}, bf16[512,1024]{1,0:T(8,128)(2,1)}, u32[]{:S(2)}) copy-start(bf16[512,1024]{1,0:T(8,128)(2,1)} %key.7) | copy-start | bytes 3145732
  20.2 10.6 %collective-permute-start.3 = (bf16[256,1024]{1,0:T(8,128)(2,1)S(1)}, bf16[256,1024]{1,0:T(8,128)(2,1)S(1)}, u32[]{:S(2)}, u32[]{:S(2)}) collective-permute-start(bf16[256,1024]{1,0:T(8,128)(2,1)S(1)} %collective-permute-done.2.foreign.for_a), channel_id=1, source_target_pairs={{0,1},{1,0},{2,3},{3,2},{4,5},{5,4},{6,7},{7,6},{8,9},{9,8},{10,11... | collective-permute-start | bytes 1572872 | tf_op jit(solution)/shard_map/ppermute | solution.py:493
  20.8 15.5 %copy-start.4 = (bf16[1024,512]{1,0:T(8,128)(2,1)S(1)}, bf16[1024,512]{1,0:T(8,128)(2,1)}, u32[]{:S(2)}) copy-start(bf16[1024,512]{1,0:T(8,128)(2,1)} %rest_3_.1) | copy-start | bytes 3145732
  20.9 15.5 %copy-start.5 = (bf16[1024,512]{1,0:T(8,128)(2,1)S(1)}, bf16[1024,512]{1,0:T(8,128)(2,1)}, u32[]{:S(2)}) copy-start(bf16[1024,512]{1,0:T(8,128)(2,1)} %rest_4_.5) | copy-start | bytes 3145732
  20.9 27.8 %collective-permute-start.6 = (bf16[528,512]{1,0:T(8,128)(2,1)S(1)}, bf16[528,512]{1,0:T(8,128)(2,1)S(1)}, u32[]{:S(2)}, u32[]{:S(2)}) collective-permute-start(bf16[528,512]{1,0:T(8,128)(2,1)S(1)} %pack_q.1), channel_id=1, source_target_pairs={{0,2},{2,0},{1,3},{3,1},{4,6},{6,4},{5,7},{7,5},{8,10},{10,8},{9,1... | collective-permute-start | bytes 1622024 | tf_op jit(solution)/shard_map/ppermute | solution.py:493
  23.0 17.1 %collective-permute-start.5 = (bf16[256,1024]{1,0:T(8,128)(2,1)S(1)}, bf16[256,1024]{1,0:T(8,128)(2,1)S(1)}, u32[]{:S(2)}, u32[]{:S(2)}) collective-permute-start(bf16[256,1024]{1,0:T(8,128)(2,1)S(1)} %pick.2), channel_id=1, source_target_pairs={{0,4},{4,8},{8,12},{1,5},{5,9},{9,13},{2,6},{6,10},{10,14},{3,7},{... | collective-permute-start | bytes 1572872 | tf_op jit(solution)/shard_map/ppermute | solution.py:496
  31.4 8.7 %collective-permute-start.4 = (bf16[256,1024]{1,0:T(8,128)(2,1)S(1)}, bf16[256,1024]{1,0:T(8,128)(2,1)S(1)}, u32[]{:S(2)}, u32[]{:S(2)}) collective-permute-start(bf16[256,1024]{1,0:T(8,128)(2,1)S(1)} %collective-permute-done.foreign.for_b), channel_id=1, source_target_pairs={{0,1},{1,0},{2,3},{3,2},{4,5},{5,4},{6,7},{7,6},{8,9},{9,8},{10,11... | collective-permute-start | bytes 1572872 | tf_op jit(solution)/shard_map/ppermute | solution.py:493
  31.5 26.5 %collective-permute-start.7 = (bf16[256,1024]{1,0:T(8,128)(2,1)S(1)}, bf16[256,1024]{1,0:T(8,128)(2,1)}, u32[]{:S(2)}, u32[]{:S(2)}) collective-permute-start(bf16[256,1024]{1,0:T(8,128)(2,1)S(1)} %pick.3), channel_id=1, source_target_pairs={{0,4},{4,8},{8,12},{1,5},{5,9},{9,13},{2,6},{6,10},{10,14},{3,7},{... | collective-permute-start | bytes 1572872 | tf_op jit(solution)/shard_map/ppermute | solution.py:496
  48.7 2.8 %copy-start.28 = (f32[512,256]{1,0:T(8,128)}, f32[512,256]{1,0:T(8,128)S(1)}, u32[]{:S(2)}) copy-start(f32[512,256]{1,0:T(8,128)S(1)} %get-tuple-element.160.s0) | copy-start | bytes 1572868
  48.7 2.8 %copy-start.30 = (f32[512,256]{1,0:T(8,128)}, f32[512,256]{1,0:T(8,128)S(1)}, u32[]{:S(2)}) copy-start(f32[512,256]{1,0:T(8,128)S(1)} %get-tuple-element.162.a0) | copy-start | bytes 1572868
  58.0 8.0 %collective-permute-start.8 = (bf16[256,1024]{1,0:T(8,128)(2,1)S(1)}, bf16[256,1024]{1,0:T(8,128)(2,1)}, u32[]{:S(2)}, u32[]{:S(2)}) collective-permute-start(bf16[256,1024]{1,0:T(8,128)(2,1)S(1)} %collective-permute-done.5.halo_a), channel_id=1, source_target_pairs={{0,1},{1,0},{2,3},{3,2},{4,5},{5,4},{6,7},{7,6},{8,9},{9,8},{10,11... | collective-permute-start | bytes 1572872 | tf_op jit(solution)/shard_map/ppermute | solution.py:493
  58.1 7.8 %collective-permute-start.9 = (bf16[256,1024]{1,0:T(8,128)(2,1)}, bf16[256,1024]{1,0:T(8,128)(2,1)}, u32[]{:S(2)}, u32[]{:S(2)}) collective-permute-start(bf16[256,1024]{1,0:T(8,128)(2,1)} %collective-permute-done.7.halo_b), channel_id=1, source_target_pairs={{0,1},{1,0},{2,3},{3,2},{4,5},{5,4},{6,7},{7,6},{8,9},{9,8},{10,11... | collective-permute-start | bytes 1572872 | tf_op jit(solution)/shard_map/ppermute | solution.py:493
  62.5 3.5 %copy-start.15 = (bf16[512,1024]{1,0:T(8,128)(2,1)S(1)}, bf16[512,1024]{1,0:T(8,128)(2,1)}, u32[]{:S(2)}) copy-start(bf16[512,1024]{1,0:T(8,128)(2,1)} %copy-done.14) | copy-start | bytes 3145732
  65.7 5.0 %collective-permute-start.11 = (bf16[512,512]{1,0:T(8,128)(2,1)S(1)}, bf16[512,512]{1,0:T(8,128)(2,1)S(1)}, u32[]{:S(2)}, u32[]{:S(2)}) collective-permute-start(bf16[512,512]{1,0:T(8,128)(2,1)S(1)} %get-tuple-element.155.e0.h0), channel_id=1, source_target_pairs={{0,1},{1,0},{2,3},{3,2},{4,5},{5,4},{6,7},{7,6},{8,9},{9,8},{10,11... | collective-permute-start | bytes 1572872 | tf_op jit(solution)/shard_map/ppermute | solution.py:493
  66.0 4.7 %copy-start.6 = (bf16[1024,512]{1,0:T(8,128)(2,1)S(1)}, bf16[1024,512]{1,0:T(8,128)(2,1)}, u32[]{:S(2)}) copy-start(bf16[1024,512]{1,0:T(8,128)(2,1)} %rest_5_.5) | copy-start | bytes 3145732
  66.0 4.7 %copy-start.25 = (bf16[512,512]{1,0:T(8,128)(2,1)S(1)}, bf16[512,512]{1,0:T(8,128)(2,1)}, u32[]{:S(2)}) copy-start(bf16[512,512]{1,0:T(8,128)(2,1)} %copy-done.24) | copy-start | bytes 1572868
  66.0 4.7 %copy-start.27 = (bf16[512,512]{1,0:T(8,128)(2,1)S(1)}, bf16[512,512]{1,0:T(8,128)(2,1)}, u32[]{:S(2)}) copy-start(bf16[512,512]{1,0:T(8,128)(2,1)} %copy-done.26) | copy-start | bytes 1572868
  66.0 4.7 %copy-start.29 = (f32[512,256]{1,0:T(8,128)S(1)}, f32[512,256]{1,0:T(8,128)}, u32[]{:S(2)}) copy-start(f32[512,256]{1,0:T(8,128)} %copy-done.28) | copy-start | bytes 1572868
  66.0 4.7 %copy-start.31 = (f32[512,256]{1,0:T(8,128)S(1)}, f32[512,256]{1,0:T(8,128)}, u32[]{:S(2)}) copy-start(f32[512,256]{1,0:T(8,128)} %copy-done.30) | copy-start | bytes 1572868
  66.0 4.7 %copy-start.41 = (bf16[512,512]{1,0:T(8,128)(2,1)S(1)}, bf16[512,512]{1,0:T(8,128)(2,1)}, u32[]{:S(2)}) copy-start(bf16[512,512]{1,0:T(8,128)(2,1)} %copy-done.40) | copy-start | bytes 1572868
  66.0 4.7 %copy-start.43 = (bf16[512,512]{1,0:T(8,128)(2,1)S(1)}, bf16[512,512]{1,0:T(8,128)(2,1)}, u32[]{:S(2)}) copy-start(bf16[512,512]{1,0:T(8,128)(2,1)} %copy-done.42) | copy-start | bytes 1572868
  66.0 4.7 %copy-start.45 = (f32[512,256]{1,0:T(8,128)S(1)}, f32[512,256]{1,0:T(8,128)}, u32[]{:S(2)}) copy-start(f32[512,256]{1,0:T(8,128)} %copy-done.44) | copy-start | bytes 1572868
  66.0 4.7 %copy-start.47 = (f32[512,256]{1,0:T(8,128)S(1)}, f32[512,256]{1,0:T(8,128)}, u32[]{:S(2)}) copy-start(f32[512,256]{1,0:T(8,128)} %copy-done.46) | copy-start | bytes 1572868
  70.3 2.4 %collective-permute-start.10 = (bf16[512,512]{1,0:T(8,128)(2,1)S(1)}, bf16[512,512]{1,0:T(8,128)(2,1)S(1)}, u32[]{:S(2)}, u32[]{:S(2)}) collective-permute-start(bf16[512,512]{1,0:T(8,128)(2,1)S(1)} %get-tuple-element.144.e0.h0), channel_id=1, source_target_pairs={{0,1},{1,0},{2,3},{3,2},{4,5},{5,4},{6,7},{7,6},{8,9},{9,8},{10,11... | collective-permute-start | bytes 1572872 | tf_op jit(solution)/shard_map/ppermute | solution.py:493
  74.9 9.7 %collective-permute-start.12 = (bf16[3,64,512]{2,1,0:T(8,128)(2,1)S(1)}, bf16[3,64,512]{2,1,0:T(8,128)(2,1)S(1)}, u32[]{:S(2)}, u32[]{:S(2)}) collective-permute-start(bf16[3,64,512]{2,1,0:T(8,128)(2,1)S(1)} %get-tuple-element.165), channel_id=1, source_target_pairs={{0,4},{4,8},{8,12},{12,0},{1,5},{5,9},{9,13},{13,1},{2,6},{6,10},{... | collective-permute-start | bytes 589832 | tf_op jit(solution)/shard_map/ppermute | solution.py:496
  76.1 16.2 %collective-permute-start.13 = (bf16[3,64,512]{2,1,0:T(8,128)(2,1)S(1)}, bf16[3,64,512]{2,1,0:T(8,128)(2,1)S(1)}, u32[]{:S(2)}, u32[]{:S(2)}) collective-permute-start(bf16[3,64,512]{2,1,0:T(8,128)(2,1)S(1)} %get-tuple-element.166), channel_id=1, source_target_pairs={{0,8},{4,12},{8,0},{12,4},{1,9},{5,13},{9,1},{13,5},{2,10},{6,14},... | collective-permute-start | bytes 589832 | tf_op jit(solution)/shard_map/ppermute | solution.py:496
  78.7 13.6 %collective-permute-start.14 = (bf16[3,64,512]{2,1,0:T(8,128)(2,1)S(1)}, bf16[3,64,512]{2,1,0:T(8,128)(2,1)S(1)}, u32[]{:S(2)}, u32[]{:S(2)}) collective-permute-start(bf16[3,64,512]{2,1,0:T(8,128)(2,1)S(1)} %get-tuple-element.167), channel_id=1, source_target_pairs={{0,12},{4,0},{8,4},{12,8},{1,13},{5,1},{9,5},{13,9},{2,14},{6,2},{... | collective-permute-start | bytes 589832 | tf_op jit(solution)/shard_map/ppermute | solution.py:496
  93.1 9.1 %collective-permute-start.15 = (bf16[2,64,512]{2,1,0:T(8,128)(2,1)S(1)}, bf16[2,64,512]{2,1,0:T(8,128)(2,1)S(1)}, u32[]{:S(2)}, u32[]{:S(2)}) collective-permute-start(bf16[2,64,512]{2,1,0:T(8,128)(2,1)S(1)} %get-tuple-element.168.rest_0_), channel_id=1, source_target_pairs={{0,4},{4,8},{8,12},{12,0},{1,5},{5,9},{9,13},{13,1},{2,6},{6,10},{... | collective-permute-start | bytes 393224 | tf_op jit(solution)/shard_map/ppermute | solution.py:496
  97.6 9.3 %collective-permute-start.16 = (bf16[2,64,512]{2,1,0:T(8,128)(2,1)S(1)}, bf16[2,64,512]{2,1,0:T(8,128)(2,1)S(1)}, u32[]{:S(2)}, u32[]{:S(2)}) collective-permute-start(bf16[2,64,512]{2,1,0:T(8,128)(2,1)S(1)} %get-tuple-element.168.rest_0_), channel_id=1, source_target_pairs={{0,8},{4,12},{8,0},{12,4},{1,9},{5,13},{9,1},{13,5},{2,10},{6,14},... | collective-permute-start | bytes 393224 | tf_op jit(solution)/shard_map/ppermute | solution.py:496
  98.9 8.1 %collective-permute-start.17 = (bf16[2,64,512]{2,1,0:T(8,128)(2,1)S(1)}, bf16[2,64,512]{2,1,0:T(8,128)(2,1)S(1)}, u32[]{:S(2)}, u32[]{:S(2)}) collective-permute-start(bf16[2,64,512]{2,1,0:T(8,128)(2,1)S(1)} %get-tuple-element.168.rest_0_), channel_id=1, source_target_pairs={{0,12},{4,0},{8,4},{12,8},{1,13},{5,1},{9,5},{13,9},{2,14},{6,2},{... | collective-permute-start | bytes 393224 | tf_op jit(solution)/shard_map/ppermute | solution.py:496
  100.1 10.2 %collective-permute-start.18 = (bf16[2,64,512]{2,1,0:T(8,128)(2,1)S(1)}, bf16[2,64,512]{2,1,0:T(8,128)(2,1)S(1)}, u32[]{:S(2)}, u32[]{:S(2)}) collective-permute-start(bf16[2,64,512]{2,1,0:T(8,128)(2,1)S(1)} %get-tuple-element.168.rest_0_), channel_id=1, source_target_pairs={{0,1},{1,0},{2,3},{3,2},{4,5},{5,4},{6,7},{7,6},{8,9},{9,8},{10,11... | collective-permute-start | bytes 393224 | tf_op jit(solution)/shard_map/ppermute | solution.py:493
  102.2 10.8 %collective-permute-start.19 = (bf16[2,64,512]{2,1,0:T(8,128)(2,1)S(1)}, bf16[2,64,512]{2,1,0:T(8,128)(2,1)S(1)}, u32[]{:S(2)}, u32[]{:S(2)}) collective-permute-start(bf16[2,64,512]{2,1,0:T(8,128)(2,1)S(1)} %collective-permute-done.15.rest_1_), channel_id=1, source_target_pairs={{0,1},{1,0},{2,3},{3,2},{4,5},{5,4},{6,7},{7,6},{8,9},{9,8},{10,11... | collective-permute-start | bytes 393224 | tf_op jit(solution)/shard_map/ppermute | solution.py:493
  107.0 6.0 %collective-permute-start.20 = (bf16[2,64,512]{2,1,0:T(8,128)(2,1)S(1)}, bf16[2,64,512]{2,1,0:T(8,128)(2,1)S(1)}, u32[]{:S(2)}, u32[]{:S(2)}) collective-permute-start(bf16[2,64,512]{2,1,0:T(8,128)(2,1)S(1)} %collective-permute-done.16.rest_2_), channel_id=1, source_target_pairs={{0,1},{1,0},{2,3},{3,2},{4,5},{5,4},{6,7},{7,6},{8,9},{9,8},{10,11... | collective-permute-start | bytes 393224 | tf_op jit(solution)/shard_map/ppermute | solution.py:493
  107.0 6.0 %collective-permute-start.21 = (bf16[2,64,512]{2,1,0:T(8,128)(2,1)S(1)}, bf16[2,64,512]{2,1,0:T(8,128)(2,1)S(1)}, u32[]{:S(2)}, u32[]{:S(2)}) collective-permute-start(bf16[2,64,512]{2,1,0:T(8,128)(2,1)S(1)} %collective-permute-done.17.rest_3_), channel_id=1, source_target_pairs={{0,1},{1,0},{2,3},{3,2},{4,5},{5,4},{6,7},{7,6},{8,9},{9,8},{10,11... | collective-permute-start | bytes 393224 | tf_op jit(solution)/shard_map/ppermute | solution.py:493
  107.5 7.9 %collective-permute-start.22 = (bf16[1,64,512]{2,1,0:T(8,128)(2,1)S(1)}, bf16[1,64,512]{2,1,0:T(8,128)(2,1)S(1)}, u32[]{:S(2)}, u32[]{:S(2)}) collective-permute-start(bf16[1,64,512]{2,1,0:T(8,128)(2,1)S(1)} %get-tuple-element.171.rest_0_), channel_id=1, source_target_pairs={{0,4},{4,8},{8,12},{12,0},{1,5},{5,9},{9,13},{13,1},{2,6},{6,10},{... | collective-permute-start | bytes 196616 | tf_op jit(solution)/shard_map/ppermute | solution.py:496
  110.3 7.3 %collective-permute-start.23 = (bf16[1,64,512]{2,1,0:T(8,128)(2,1)S(1)}, bf16[1,64,512]{2,1,0:T(8,128)(2,1)S(1)}, u32[]{:S(2)}, u32[]{:S(2)}) collective-permute-start(bf16[1,64,512]{2,1,0:T(8,128)(2,1)S(1)} %get-tuple-element.171.rest_0_), channel_id=1, source_target_pairs={{0,8},{4,12},{8,0},{12,4},{1,9},{5,13},{9,1},{13,5},{2,10},{6,14},... | collective-permute-start | bytes 196616 | tf_op jit(solution)/shard_map/ppermute | solution.py:496
  113.0 5.1 %collective-permute-start.24 = (bf16[1,64,512]{2,1,0:T(8,128)(2,1)S(1)}, bf16[1,64,512]{2,1,0:T(8,128)(2,1)S(1)}, u32[]{:S(2)}, u32[]{:S(2)}) collective-permute-start(bf16[1,64,512]{2,1,0:T(8,128)(2,1)S(1)} %get-tuple-element.171.rest_0_), channel_id=1, source_target_pairs={{0,12},{4,0},{8,4},{12,8},{1,13},{5,1},{9,5},{13,9},{2,14},{6,2},{... | collective-permute-start | bytes 196616 | tf_op jit(solution)/shard_map/ppermute | solution.py:496
  118.1 1.3 collective-permute-start.25
  118.1 1.4 %collective-permute-start.26 = (bf16[1,64,512]{2,1,0:T(8,128)(2,1)S(1)}, bf16[1,64,512]{2,1,0:T(8,128)(2,1)S(1)}, u32[]{:S(2)}, u32[]{:S(2)}) collective-permute-start(bf16[1,64,512]{2,1,0:T(8,128)(2,1)S(1)} %collective-permute-done.22.rest_1_), channel_id=1, source_target_pairs={{0,1},{1,0},{2,3},{3,2},{4,5},{5,4},{6,7},{7,6},{8,9},{9,8},{10,11... | collective-permute-start | bytes 196616 | tf_op jit(solution)/shard_map/ppermute | solution.py:493
  118.6 1.3 collective-permute-start.27
  118.6 1.4 collective-permute-start.28
  121.1 18.5 %collective-permute-start.29 = (bf16[704,512]{1,0:T(8,128)(2,1)S(1)}, bf16[704,512]{1,0:T(8,128)(2,1)S(1)}, u32[]{:S(2)}, u32[]{:S(2)}) collective-permute-start(bf16[704,512]{1,0:T(8,128)(2,1)S(1)} %get-tuple-element.180), channel_id=1, source_target_pairs={{0,2},{2,0},{1,3},{3,1},{4,6},{6,4},{5,7},{7,5},{8,10},{10,8},{9,1... | collective-permute-start | bytes 2162696 | tf_op jit(solution)/shard_map/ppermute | solution.py:493
  (31 other events, 49.6 us)

commit v3 on v2

--- a/solution.py
+++ b/solution.py
@@ -40,6 +40,10 @@
 def rms(x):
     v = x.astype(F32)
     return (v * lax.rsqrt(jnp.mean(v * v, -1, keepdims=True) + 1e-06)).astype(BF)
+
+
+def in_hbm(value):
+    return pltpu.with_memory_space_constraint(value, pltpu.HBM)
 
 
 def shape(dims, dtype=BF):
@@ -104,7 +108,7 @@
         out_shape=shape((count, 2 * HD)),
         compiler_params=PARAMS,
         name="pack",
-    )(where, key_rows, value_rows)
+    )(where, in_hbm(key_rows), in_hbm(value_rows))
 
 
 def pick_kernel(where, foreign, key, value, out):
@@ -116,7 +120,7 @@
 def pick(where, foreign, key_rows, value_rows, n):
     part = pl.BlockSpec((HALF, HD), lambda i, s: (n, s[0]))
     return call_blocks(pick_kernel, "pick", [None, part, part], [shape((HALF, 2 * HD))])(
-        where, foreign, key_rows, value_rows
+        where, foreign, in_hbm(key_rows), in_hbm(value_rows)
     )[0]
 
 
@@ -174,22 +178,8 @@
         outs[4 + i][...] = jnp.where(bottom, work[i][...], mine[i][...])
 
 
-def pre_kernel(where, own, for_a, for_b, own2, for2_a, for2_b, *rest):
-    mine, (wg, wu), (low, high, mid, low2), outs = rest[:4], rest[4:6], rest[6:10], rest[10:18]
-    bottom = where[0] == 0
-    first = where[1] == 0
-    for c, (f, f2) in enumerate(((for_a, for2_a), (for_b, for2_b))):
-        rows = pl.ds(c * HALF, HALF)
-        low[rows, :] = jnp.where(bottom, own[rows, :], f[...])
-        high[rows, :] = jnp.where(bottom, f[...], own[rows, :])
-        l2 = jnp.where(bottom, own2[rows, :], f2[...])
-        low2[rows, :] = l2
-        mid[rows, :] = jnp.where(first, l2, jnp.where(bottom, f2[...], own2[rows, :]))
-    pick_factors(where, (for_a, for_b), mine, wg, wu, outs, rest[18:])
-
-
-def pre_other_kernel(where, for2_a, for2_b, *rest):
-    pick_factors(where, (for2_a, for2_b), rest[:4], *rest[4:6], rest[6:14], rest[14:])
+def pre_kernel(where, *rest):
+    pick_factors(where, rest[:2], rest[2:6], *rest[6:8], rest[8:16], rest[16:])
 
 
 FACTORS = [
@@ -200,20 +190,14 @@
 ]
 
 
-def pre_own(where, own, own2, w_gate, w_up):
-    head = pl.BlockSpec((HD, HD), lambda i, s: (s[0], 0))
-    return call_blocks(pre_own_kernel, "pre_own", [None] * 2 + [head] * 2, FACTORS * 2)(
-        where, own, own2, w_gate, w_up
-    )
-
-
-def pre(kernel, where, pairs, mine, w_gate, w_up, outs):
-    head = pl.BlockSpec((HD, HD), lambda i, s: (s[0], 0))
-    specs = [None] * (len(pairs) + 4) + [head] * 2
+def pre_own(where, own, own2, wg, wu):
+    return call(pre_own_kernel, "pre_own", FACTORS * 2)(where, own, own2, wg, wu)
+
+
+def pre(where, halves, mine, wg, wu):
     work = [pltpu.VMEM(f.shape, f.dtype) for f in FACTORS]
-    return call_blocks(kernel, "pre", specs, outs + FACTORS * 2, work)(
-        where, *pairs, *mine, w_gate, w_up
-    )
+    outs = call(pre_kernel, "pre", FACTORS * 2, work)(where, *halves, *mine, wg, wu)
+    return outs[:4], outs[4:]
 
 
 def attend(q, rate, tile_a, tile_b, tile_c, a_ok, b_ok, att, err):
@@ -277,11 +261,23 @@
     return lambda t: ref[t * HALF : (t + 1) * HALF, :]
 
 
-def upper_kernel(where, q_own, q_for, rates, a, b, c, att, err):
+def upper_kernel(
+    where, q_own, q_for, rates, own, for_a, for_b, own2, for2_a, for2_b, *rest
+):
+    att, err, low, low2, high, mid = rest
+    bottom = where[0] == 0
+    first = where[1] == 0
+    for c, (f, f2) in enumerate(((for_a, for2_a), (for_b, for2_b))):
+        rows = pl.ds(c * HALF, HALF)
+        low[rows, :] = jnp.where(bottom, own[rows, :], f[...])
+        high[rows, :] = jnp.where(bottom, f[...], own[rows, :])
+        l2 = jnp.where(bottom, own2[rows, :], f2[...])
+        low2[rows, :] = l2
+        mid[rows, :] = jnp.where(first, l2, jnp.where(bottom, f2[...], own2[rows, :]))
     mine = where[0] == 1
     q = lambda rows: jnp.where(mine, q_own[rows, :], q_for[rows, :])
     r = column(mine, where[0], rates, q_for)
-    attend(q, r, rows_of(a), rows_of(b), rows_of(c), None, None, att, err)
+    attend(q, r, rows_of(low), rows_of(mid), rows_of(high), None, None, att, err)
 
 
 def lower_kernel(
@@ -301,40 +297,31 @@
     )
 
 
-def back_products(errs, kns, slopes, acts, w):
-    gate = up = None
-    for e, kn, slope, act in zip(errs, kns, slopes, acts, strict=True):
-        back = mm_n(e[...], w[...])
-        g = mm_rows((back * slope[...]).astype(BF), kn[...])
-        u = mm_rows((back * act[...]).astype(BF), kn[...])
-        gate = g if gate is None else gate + g
-        up = u if up is None else up + u
-    return gate, up
-
-
-def down_products(errs, gateds):
-    acc = None
-    for e, g in zip(errs, gateds, strict=True):
-        d = mm_rows(e[...], g[...])
-        acc = d if acc is None else acc + d
-    return acc
-
-
-def grad_first_kernel(where, e0, e1, h0, h1, k0, k1, g0, g1, s0, s1, a0, a1, w, total):
-    gate, up = back_products((e0, e1), (k0, k1), (s0, s1), (a0, a1), w)
-    total[0] = gate
-    total[1] = up
-    total[2] = down_products((h0, h1), (g0, g1))
+def half_of(core, ref):
+    return jnp.where(core == 0, ref[:, 0:HALF], ref[:, HALF:HD])
+
+
+def add_products(where, errs, kns, gateds, slopes, acts, w, total):
+    core = where[1]
+    w_half = half_of(core, w)
+    for e, kn, gated, slope, act in zip(errs, kns, gateds, slopes, acts, strict=True):
+        back = mm_n(e[...], w_half)
+        total[0] += mm_rows((back * slope[...]).astype(BF), kn[...])
+        total[1] += mm_rows((back * act[...]).astype(BF), kn[...])
+        total[2] += mm_rows(half_of(core, e), gated[...])
+
+
+def grad_first_kernel(where, e0, e1, k0, k1, g0, g1, s0, s1, a0, a1, w, total):
+    total[...] = jnp.zeros_like(total)
+    add_products(where, (e0, e1), (k0, k1), (g0, g1), (s0, s1), (a0, a1), w, total)
 
 
 def grad_second_kernel(
-    zs, where, e0, e1, h0, h1, k0, k1, g0, g1, s0, s1, a0, a1, before, w, own, *rest
+    zs, where, e0, e1, k0, k1, g0, g1, s0, s1, a0, a1, w, before, own, *rest
 ):
     sends, total = rest[:-1], rest[-1]
-    gate, up = back_products((e0, e1), (k0, k1), (s0, s1), (a0, a1), w)
-    total[0] = before[0] + gate
-    total[1] = before[1] + up
-    total[2] = before[2] + down_products((h0, h1), (g0, g1))
+    total[...] = before[...]
+    add_products(where, (e0, e1), (k0, k1), (g0, g1), (s0, s1), (a0, a1), w, total)
     rows = HALF // zs
     for d in range(zs):
         src = pl.ds(pl.multiple_of(lax.rem(where[2] + d, zs) * rows, rows), rows)
@@ -345,29 +332,20 @@
                 sends[d - 1][kind] = total[kind, src, :].astype(BF)
 
 
-def update_kernel(where, own, *rest):
+def update_kernel(zs, where, own, *rest):
     got, olds, (first, last) = rest[:-5], rest[-5:-2], rest[-2:]
+    rows = HALF // zs
+    mine = pl.ds(pl.multiple_of(where[1] * HALF + where[2] * rows, rows), rows)
     for kind, out in enumerate((first.at[0], first.at[1], last.at[0])):
         grad = own[kind]
         for g in got:
             grad = grad + g[kind].astype(F32)
-        old = olds[kind][...].astype(F32)
+        old = olds[kind][mine, :].astype(F32)
         raised = old - grad
         factor = jnp.sqrt(jnp.mean(old * old, -1, keepdims=True) + 1e-06) * lax.rsqrt(
             jnp.mean(raised * raised, -1, keepdims=True) + 1e-06
         )
         out[...] = (raised * factor).astype(BF)
-
-
-def update(zs, where, own, got, olds):
-    rows = HALF // zs
-    old = pl.BlockSpec((rows, HD), lambda i, s: ((s[0] * 2 + s[1]) * zs + s[2], 0))
-    return call_blocks(
-        update_kernel,
-        "update",
-        [None] * zs + [old] * 3,
-        [shape((2, rows, HD)), shape((1, rows, HD))],
-    )(where, own, *got, *olds)
 
 
 def gather(zs, where, pieces, kinds, full):
@@ -507,68 +485,60 @@
     sent_b = pack(where, after(key_rows, sent_a), value_rows, HALF, HALF, False)
     sent_q = call_blocks(
         pack_q_kernel, "pack_q", [q_other, None], [shape((BLK + RATE_ROWS, HD))]
-    )(where, after(queries, sent_b), step_rates)[0]
+    )(where, in_hbm(after(queries, sent_b)), step_rates)[0]
     own = pack(where, after(key_rows, sent_b), value_rows, 0, BLK, True)
     theirs = [swap(sent_a, "y"), swap(sent_b, "y")]
+    q_own = jnp.where(y == 0, queries[:, :HD], queries[:, HD:])
+    weights = [jnp.where(y == 0, w[:HD], w[HD:]) for w in (w_gate, w_up, w_down)]
+    theirs[0], sent_q, q_own, (wg, wu, wd) = lax.optimization_barrier(
+        (theirs[0], sent_q, q_own, weights)
+    )
     q_for = swap(sent_q, "y")
-    q_own = jnp.where(y == 0, queries[:, :HD], queries[:, HD:])
     own2 = swap(own, "core")
     gone = pick(where, theirs[0], key_rows, value_rows, 0)
     halo_a = shift(gone, 1, ring=False)
     theirs2 = [swap(after(theirs[0], gone), "core")]
-    theirs[1], own2, theirs2[0] = lax.optimization_barrier((theirs[1], own2, theirs2[0]))
+    mine = pre_own(where, own, own2, wg, wu)
+    theirs[1], mine, theirs2[0] = lax.optimization_barrier((theirs[1], mine, theirs2[0]))
     gone = pick(where, theirs[1], key_rows, value_rows, 1)
     halo_b = shift(gone, 1, ring=False)
     theirs2.append(swap(after(theirs[1], gone), "core"))
     theirs2, halo_a = lax.optimization_barrier((theirs2, halo_a))
-    mine = pre_own(where, own, own2, w_gate, w_up)
-    kv_low, kv_high, kv_mid, kv_low2, *blocks = pre(
-        pre_kernel,
-        where,
-        (own, *theirs, own2, *theirs2),
-        mine[:4],
-        w_gate,
-        w_up,
-        [shape((BLK, 2 * HD))] * 4,
-    )
-    theirs2, q_for, blocks = lax.optimization_barrier((theirs2, q_for, blocks))
-    blocks += pre(pre_other_kernel, where, theirs2, mine[4:], w_gate, w_up, [])
-    blocks, q_for, halo = lax.optimization_barrier((blocks, q_for, (halo_a, halo_b)))
-    low, high, low2, high2 = (blocks[4 * n : 4 * n + 4] for n in range(4))
+    low, high = pre(where, theirs, mine[:4], wg, wu)
+    theirs2, low, q_for = lax.optimization_barrier((theirs2, low, q_for))
+    low2, high2 = pre(where, theirs2, mine[4:], wg, wu)
+    low2, q_for, halo = lax.optimization_barrier((low2, q_for, (halo_a, halo_b)))
     halo2 = [swap(h, "core") for h in halo]
 
-    att_up, err_up = call(upper_kernel, "attend_upper", two)(
-        where, q_own, q_for, step_rates, kv_low, kv_mid, kv_high
-    )
+    pair = shape((BLK, 2 * HD))
+    att_up, err_up, kv_low, kv_low2 = call(
+        upper_kernel, "attend_upper", two + [pair] * 2, [pltpu.VMEM(pair.shape, BF)] * 2
+    )(where, q_own, q_for, step_rates, own, *theirs, own2, *theirs2)
     err_up2 = swap(err_up, "core")
     att_low, err_low = call(
         lower_kernel, "attend_lower", two, [pltpu.VMEM((BLK, 2 * HD), BF)]
     )(where, q_own, q_for, step_rates, *halo, *halo2, kv_low2, kv_low)
     err_low2 = swap(err_low, "core")
 
-    w_half = pl.BlockSpec((HD, HALF), lambda i, s: (s[0], s[1]))
-    err_half = pl.BlockSpec((BLK, HALF), lambda i, s: (0, s[1]))
-
-    def grads(kernel, name, outs, errs, pair, *more, scratch=()):
-        specs = [None] * 2 + [err_half] * 2 + [None] * (8 + len(more)) + [w_half]
-        factors = [pair[i][n] for n in range(4) for i in range(2)]
-        return call_blocks(kernel, name, specs, outs, scratch)(
-            where, *errs, *errs, *factors, *more, w_down
-        )
+    def factors_of(*blocks):
+        return [block[n] for n in range(4) for block in blocks]
 
     total = shape((3, HALF, HD), F32)
-    first = grads(grad_first_kernel, "grad_first", [total], (err_up, err_up2), (high, high2))[0]
-    own_sum, *sends = grads(
+    before = call(grad_first_kernel, "grad_first", [total])(
+        where, err_up, err_up2, *factors_of(high, high2), wd
+    )[0]
+    own_sum, *sends = call(
         functools.partial(grad_second_kernel, zs),
         "grad_second",
         [shape((3, rows, HD), F32)] + [shape((3, rows, HD))] * (zs - 1),
-        (err_low, err_low2),
-        (low, low2),
-        first,
-        scratch=[pltpu.VMEM(total.shape, F32)],
-    )
+        [pltpu.VMEM(total.shape, F32)],
+    )(where, err_low, err_low2, *factors_of(low, low2), wd, before)
     got = [shift(s, d) for d, s in enumerate(sends, 1)]
-    piece_a, piece_b = update(zs, where, own_sum, got, (w_gate, w_up, w_down))
+    piece_a, piece_b = call(
+        functools.partial(update_kernel, zs),
+        "update",
+        [shape((2, rows, HD)), shape((1, rows, HD))],
+    )(where, own_sum, *got, wg, wu, wd)
 
     def around(piece):
         return [piece] + [shift(piece, d) for d in range(1, zs)]

time: 141 us -> 130 us (0.922)
  local copies, waits for them, and re-layouts: 17.1 us -> 0.33 us
  Pallas kernels: 31.5 us -> 38.9 us
  starting transfers between devices: 35.3 us -> 31.3 us
  waiting for transfers between devices: 54.3 us -> 56.8 us
    unnamed x98 -> x8, local copies, waits for them, and re-layouts: 17.1 us -> 0.33 us
    pallas_call x4 -> x10, Pallas kernels: 10.4 us -> 24.1 us  [run(): pl.pallas_call(kernel, in_specs=[SM] + [VM] * len(args), out_specs=[VM] *...]
    pallas_call x9 -> x3, Pallas kernels: 16.1 us -> 4.9 us  [run(): pl.pallas_call(kernel, grid_spec=pltpu.PrefetchScalarGridSpec(num_scalar_...]
    ppermute x11, waiting for transfers between devices: 22.3 us -> 32.3 us  [shift(): lax.ppermute(value, 'z', [(i, (i + d) % zs) for i in range(zs) if ring or...]
    ppermute x19, waiting for transfers between devices: 32 us -> 24.5 us  [swap(): return lax.ppermute(value, axis, SWAP)]
    pallas_call x3, Pallas kernels: 1.77 us -> 6.63 us  [pack(): pl.pallas_call(pack_kernel, grid_spec=pltpu.PrefetchScalarGridSpec(num_sc...]
    ppermute x11, starting transfers between devices: 25.9 us -> 22.8 us  [shift(): lax.ppermute(value, 'z', [(i, (i + d) % zs) for i in range(zs) if ring or...]
  transfers between devices with their start and end apart: 30 -> 30, of which waited for: 14 -> 15; matrix products, arithmetic and copies ran while one was open for 1% -> 1% of each run, Pallas kernels for 18% -> 24%
where the time goes in v3:
time: 130 us
  waiting for transfers between devices  56.8 us (44%)
  Pallas kernels  38.9 us (30%)
  starting transfers between devices  31.3 us (24%)
  other arithmetic  1.7 us (1%)
    ppermute x11, waiting for transfers between devices, shift(): lax.ppermute(value, 'z', [(i, (i + d) % zs) for i in range(zs) if ring or...  32.3 us
    ppermute x19, waiting for transfers between devices, swap(): return lax.ppermute(value, axis, SWAP)  24.5 us
    pallas_call x10, Pallas kernels, run(): pl.pallas_call(kernel, in_specs=[SM] + [VM] * len(args), out_specs=[VM] *...  24.1 us
    ppermute x11, starting transfers between devices, shift(): lax.ppermute(value, 'z', [(i, (i + d) % zs) for i in range(zs) if ring or...  22.8 us
    ppermute x19, starting transfers between devices, swap(): return lax.ppermute(value, axis, SWAP)  8.54 us
    pallas_call x3, Pallas kernels, pack(): pl.pallas_call(pack_kernel, grid_spec=pltpu.PrefetchScalarGridSpec(num_sc...  6.63 us
    pallas_call x3, Pallas kernels, run(): pl.pallas_call(kernel, grid_spec=pltpu.PrefetchScalarGridSpec(num_scalar_...  4.9 us
  transfers between devices with their start and end apart: 30, of which 15 were waited for; matrix products, arithmetic and copies ran while one was open for 1% of the time, Pallas kernels for 24%

profile of v3, /device:TPU:0, one launch (start us, length us, event | category | flops | bytes accessed | tf_op | source)
XLA Modules:
  0.0 130.0 jit_solution(13815014040772577677)
XLA Ops:
  0.7 2.4 %pack.3 = bf16[256,1024]{1,0:T(8,128)(2,1)} custom-call(s32[3]{0:T(128)S(1)} %pad_add_fusion.where, bf16[512,1024]{1,0:T(8,128)(2,1)} %key.7, bf16[512,1024]{1,0:T(8,128)(2,1)} %value.9), custom_call_target="tpu_custom_call" | custom-call | tf_op jit(solution)/shard_map/pack/pallas_call | solution.py:100
  3.1 3.0 %collective-permute-start = (bf16[256,1024]{1,0:T(8,128)(2,1)}, bf16[256,1024]{1,0:T(8,128)(2,1)S(1)}, u32[]{:S(2)}, u32[]{:S(2)}) collective-permute-start(bf16[256,1024]{1,0:T(8,128)(2,1)} %pack.3), channel_id=1, source_target_pairs={{0,2},{2,0},{1,3},{3,1},{4,6},{6,4},{5,7},{7,5},{8,10},{10,8},{9,1... | collective-permute-start | bytes 1572872 | tf_op jit(solution)/shard_map/ppermute | solution.py:471
  6.1 2.4 %pack.4 = bf16[256,1024]{1,0:T(8,128)(2,1)} custom-call(s32[3]{0:T(128)S(1)} %pad_add_fusion.where, bf16[512,1024]{1,0:T(8,128)(2,1)} %key.7, bf16[512,1024]{1,0:T(8,128)(2,1)} %value.9), custom_call_target="tpu_custom_call" | custom-call | tf_op jit(solution)/shard_map/pack/pallas_call | solution.py:100
  8.5 1.8 %pack.5.own = bf16[512,1024]{1,0:T(8,128)(2,1)S(1)} custom-call(s32[3]{0:T(128)S(1)} %pad_add_fusion.where, bf16[512,1024]{1,0:T(8,128)(2,1)} %key.7, bf16[512,1024]{1,0:T(8,128)(2,1)} %value.9), custom_call_target="tpu_custom_call" | custom-call | tf_op jit(solution)/shard_map/pack/pallas_call | solution.py:100
  10.4 1.6 %pack_q.1 = bf16[528,512]{1,0:T(8,128)(2,1)S(1)} custom-call(s32[3]{0:T(128)S(1)} %pad_add_fusion.where, bf16[512,1024]{1,0:T(8,128)(2,1)} %query, f32[2,512]{1,0:T(2,128)S(1)} %copy-done), custom_call_target="tpu_custom_call" | custom-call | tf_op jit(solution)/shard_map/pack_q/pallas_call | solution.py:74
  12.1 1.5 %slice_select_fusion.2 = (bf16[512,512]{1,0:T(8,128)(2,1)S(1)}, bf16[512,512]{1,0:T(8,128)(2,1)S(1)}) fusion(bf16[1024,512]{1,0:T(8,128)(2,1)} %param.11, pred[]{:T(512)S(6)} %eq.2, bf16[512,1024]{1,0:T(8,128)(2,1)S(1)} %copy-done.1), kind=kLoop, calls=%fused_computation.2 | loop fusion | flops 524288 | bytes 3145729 | tf_op jit(solution)/shard_map/jit(_where)/select_n | solution.py:492
  13.6 0.3 copy-done.3
  14.1 5.0 %collective-permute-done.foreign.rest_0_.for_a = bf16[256,1024]{1,0:T(8,128)(2,1)S(1)} collective-permute-done((bf16[256,1024]{1,0:T(8,128)(2,1)}, bf16[256,1024]{1,0:T(8,128)(2,1)S(1)}, u32[]{:S(2)}, u32[]{:S(2)}) %collective-permute-start) | collective-permute-done | bytes 524320 | tf_op jit(solution)/shard_map/ppermute | solution.py:471
  19.0 1.6 %pick.2 = bf16[256,1024]{1,0:T(8,128)(2,1)S(1)} custom-call(s32[3]{0:T(128)S(1)} %pad_add_fusion.where, bf16[256,1024]{1,0:T(8,128)(2,1)S(1)} %collective-permute-done.foreign.rest_0_.for_a, bf16[512,1024]{1,0:T(8,128)(2,1)} %key.7, bf16[512,1024]{1,0:T(8,128)(2,1)} %value.9), custom_call_target="tpu_custom_call" | custom-call | tf_op jit(solution)/shard_map/pick/pallas_call | solution.py:74
  20.8 2.1 %collective-permute-start.6 = (bf16[528,512]{1,0:T(8,128)(2,1)S(1)}, bf16[528,512]{1,0:T(8,128)(2,1)S(1)}, u32[]{:S(2)}, u32[]{:S(2)}) collective-permute-start(bf16[528,512]{1,0:T(8,128)(2,1)S(1)} %pack_q.1), channel_id=1, source_target_pairs={{0,2},{2,0},{1,3},{3,1},{4,6},{6,4},{5,7},{7,5},{8,10},{10,8},{9,1... | collective-permute-start | bytes 1622024 | tf_op jit(solution)/shard_map/ppermute | solution.py:471
  22.9 3.5 %collective-permute-start.5 = (bf16[256,1024]{1,0:T(8,128)(2,1)S(1)}, bf16[256,1024]{1,0:T(8,128)(2,1)S(1)}, u32[]{:S(2)}, u32[]{:S(2)}) collective-permute-start(bf16[256,1024]{1,0:T(8,128)(2,1)S(1)} %pick.2), channel_id=1, source_target_pairs={{0,4},{4,8},{8,12},{1,5},{5,9},{9,13},{2,6},{6,10},{10,14},{3,7},{... | collective-permute-start | bytes 1572872 | tf_op jit(solution)/shard_map/ppermute | solution.py:474
  26.4 3.7 %pre_own.1 = (bf16[512,512]{1,0:T(8,128)(2,1)S(1)}, bf16[512,512]{1,0:T(8,128)(2,1)S(1)}, f32[512,256]{1,0:T(8,128)S(1)}, f32[512,256]{1,0:T(8,128)S(1)}, bf16[5...) custom-call(s32[3]{0:T(128)S(1)} %pad_add_fusion.where, ...), custom_call_target="tpu_custom_call" | custom-call | tf_op jit(solution)/shard_map/pre_own/pallas_call | solution.py:55
  30.3 1.6 %pick.3 = bf16[256,1024]{1,0:T(8,128)(2,1)S(1)} custom-call(s32[3]{0:T(128)S(1)} %pad_add_fusion.where, bf16[256,1024]{1,0:T(8,128)(2,1)S(1)} %collective-permute-done.1.foreign.rest_1_.for_b, bf16[512,1024]{1,0:T(8,128)(2,1)} %key.7, bf16[512,1024]{1,0:T(8,128)(2,1)} %value.9), custom_call_target="tpu_custom_call" | custom-call | tf_op jit(solution)/shard_map/pick/pallas_call | solution.py:74
  32.0 4.1 %collective-permute-start.7 = (bf16[256,1024]{1,0:T(8,128)(2,1)S(1)}, bf16[256,1024]{1,0:T(8,128)(2,1)S(1)}, u32[]{:S(2)}, u32[]{:S(2)}) collective-permute-start(bf16[256,1024]{1,0:T(8,128)(2,1)S(1)} %pick.3), channel_id=1, source_target_pairs={{0,4},{4,8},{8,12},{1,5},{5,9},{9,13},{2,6},{6,10},{10,14},{3,7},{... | collective-permute-start | bytes 1572872 | tf_op jit(solution)/shard_map/ppermute | solution.py:474
  36.1 2.6 %pre.2 = (bf16[512,512]{1,0:T(8,128)(2,1)S(1)}, bf16[512,512]{1,0:T(8,128)(2,1)S(1)}, f32[512,256]{1,0:T(8,128)S(1)}, f32[512,256]{1,0:T(8,128)S(1)}, bf16[512,5...) custom-call(s32[3]{0:T(128)S(1)} %pad_add_fusion.where, ...), custom_call_target="tpu_custom_call" | custom-call | tf_op jit(solution)/shard_map/pre/pallas_call | solution.py:55
  38.7 2.4 %collective-permute-done.6.q_for.rest_8_ = bf16[528,512]{1,0:T(8,128)(2,1)S(1)} collective-permute-done((bf16[528,512]{1,0:T(8,128)(2,1)S(1)}, bf16[528,512]{1,0:T(8,128)(2,1)S(1)}, u32[]{:S(2)}, u32[]{:S(2)}) %collective-permute-start.6) | collective-permute-done | bytes 540704 | tf_op jit(solution)/shard_map/ppermute | solution.py:471
  41.0 2.8 %pre.3 = (bf16[512,512]{1,0:T(8,128)(2,1)S(1)}, bf16[512,512]{1,0:T(8,128)(2,1)S(1)}, f32[512,256]{1,0:T(8,128)S(1)}, f32[512,256]{1,0:T(8,128)S(1)}, bf16[512,5...) custom-call(s32[3]{0:T(128)S(1)} %pad_add_fusion.where, ...), custom_call_target="tpu_custom_call" | custom-call | tf_op jit(solution)/shard_map/pre/pallas_call | solution.py:55
  43.8 5.3 %collective-permute-done.7.halo_b = bf16[256,1024]{1,0:T(8,128)(2,1)S(1)} collective-permute-done((bf16[256,1024]{1,0:T(8,128)(2,1)S(1)}, bf16[256,1024]{1,0:T(8,128)(2,1)S(1)}, u32[]{:S(2)}, u32[]{:S(2)}) %collective-permute-start.7) | collective-permute-done | bytes 524320 | tf_op jit(solution)/shard_map/ppermute | solution.py:474
  49.1 0.5 collective-permute-start.9
  49.6 3.3 %attend_upper.1 = (bf16[512,512]{1,0:T(8,128)(2,1)S(1)}, bf16[512,512]{1,0:T(8,128)(2,1)S(1)}, bf16[512,1024]{1,0:T(8,128)(2,1)S(1)}, bf16[512,1024]{1,0:T(8,128)(2,1)S(1)}) custom-call(s32[3]{0:T(128)S(1)} %pad_add_fusion.where, bf16[512,512]{1,0:T(8,128)(2,1)S(1)} %get-tuple-element.90.q_own.rest_9_, ...), custom_call_target="tpu_custom_call" | custom-call | tf_op jit(solution)/shard_map/attend_upper/pallas_call | solution.py:55
  53.0 3.2 %attend_lower.1 = (bf16[512,512]{1,0:T(8,128)(2,1)S(1)}, bf16[512,512]{1,0:T(8,128)(2,1)S(1)}) custom-call(s32[3]{0:T(128)S(1)} %pad_add_fusion.where, bf16[512,512]{1,0:T(8,128)(2,1)S(1)} %get-tuple-element.90.q_own.rest_9_, bf16[528,512]{1,0:T(8,128)(2,1)S(1)} %collective-permute-done.6.q_for.rest_8_, f32[2,512]{1,0:T(2,128)S(1)} %copy-done, ...), custom_call_target="tpu_custom_call" | custom-call | tf_op jit(solution)/shard_map/attend_lower/pallas_call | solution.py:55
  56.2 0.5 collective-permute-start.10
  56.8 2.3 %grad_first.1.before = f32[3,256,512]{2,1,0:T(8,128)S(1)} custom-call(s32[3]{0:T(128)S(1)} %pad_add_fusion.where, bf16[512,512]{1,0:T(8,128)(2,1)S(1)} %get-tuple-element.145.e0, bf16[512,512]{1,0:T(8,128)(2,1)S(1)} %collective-permute-done.11.e1, bf16[512,512]{1,0:T(8,128)(2,1)S(1)} %get-tuple-element.146.k0, bf16[512,512]{1,0:T(8,128)(2,1)S(1)} %get-tuple-element.147.k1, ...), custom_call_target="tpu_custom_call" | custom-call | tf_op jit(solution)/shard_map/grad_first/pallas_call | solution.py:55
  59.0 2.5 %grad_second.1 = (f32[3,64,512]{2,1,0:T(8,128)S(1)}, bf16[3,64,512]{2,1,0:T(8,128)(2,1)S(1)}, bf16[3,64,512]{2,1,0:T(8,128)(2,1)S(1)}, bf16[3,64,512]{2,1,0:T(8,128)(2,1)S(1)}) custom-call(s32[3]{0:T(128)S(1)} %pad_add_fusion.where, bf16[512,512]{1,0:T(8,128)(2,1)S(1)} %get-tuple-element.135.e0, bf16[512,512]{1,0:T(8,128)(2,1)S(1)} %collective-permute-done.10.e1, ...), custom_call_target="tpu_custom_call" | custom-call | tf_op jit(solution)/shard_map/grad_second/pallas_call | solution.py:55
  61.6 2.6 %collective-permute-start.12 = (bf16[3,64,512]{2,1,0:T(8,128)(2,1)S(1)}, bf16[3,64,512]{2,1,0:T(8,128)(2,1)S(1)}, u32[]{:S(2)}, u32[]{:S(2)}) collective-permute-start(bf16[3,64,512]{2,1,0:T(8,128)(2,1)S(1)} %get-tuple-element.155), channel_id=1, source_target_pairs={{0,4},{4,8},{8,12},{12,0},{1,5},{5,9},{9,13},{13,1},{2,6},{6,10},{... | collective-permute-start | bytes 589832 | tf_op jit(solution)/shard_map/ppermute | solution.py:474
  64.1 2.6 %collective-permute-start.13 = (bf16[3,64,512]{2,1,0:T(8,128)(2,1)S(1)}, bf16[3,64,512]{2,1,0:T(8,128)(2,1)S(1)}, u32[]{:S(2)}, u32[]{:S(2)}) collective-permute-start(bf16[3,64,512]{2,1,0:T(8,128)(2,1)S(1)} %get-tuple-element.156), channel_id=1, source_target_pairs={{0,8},{4,12},{8,0},{12,4},{1,9},{5,13},{9,1},{13,5},{2,10},{6,14},... | collective-permute-start | bytes 589832 | tf_op jit(solution)/shard_map/ppermute | solution.py:474
  66.7 1.3 %collective-permute-start.14 = (bf16[3,64,512]{2,1,0:T(8,128)(2,1)S(1)}, bf16[3,64,512]{2,1,0:T(8,128)(2,1)S(1)}, u32[]{:S(2)}, u32[]{:S(2)}) collective-permute-start(bf16[3,64,512]{2,1,0:T(8,128)(2,1)S(1)} %get-tuple-element.157), channel_id=1, source_target_pairs={{0,12},{4,0},{8,4},{12,8},{1,13},{5,1},{9,5},{13,9},{2,14},{6,2},{... | collective-permute-start | bytes 589832 | tf_op jit(solution)/shard_map/ppermute | solution.py:474
  68.0 3.9 %collective-permute-done.12.rest_0_ = bf16[3,64,512]{2,1,0:T(8,128)(2,1)S(1)} collective-permute-done((bf16[3,64,512]{2,1,0:T(8,128)(2,1)S(1)}, bf16[3,64,512]{2,1,0:T(8,128)(2,1)S(1)}, u32[]{:S(2)}, u32[]{:S(2)}) %collective-permute-start.12) | collective-permute-done | bytes 196640 | tf_op jit(solution)/shard_map/ppermute | solution.py:474
  72.0 7.8 %collective-permute-done.13.rest_1_ = bf16[3,64,512]{2,1,0:T(8,128)(2,1)S(1)} collective-permute-done((bf16[3,64,512]{2,1,0:T(8,128)(2,1)S(1)}, bf16[3,64,512]{2,1,0:T(8,128)(2,1)S(1)}, u32[]{:S(2)}, u32[]{:S(2)}) %collective-permute-start.13) | collective-permute-done | bytes 196640 | tf_op jit(solution)/shard_map/ppermute | solution.py:474
  79.8 0.8 update.1
  80.6 5.8 %collective-permute-start.17 = (bf16[2,64,512]{2,1,0:T(8,128)(2,1)S(1)}, bf16[2,64,512]{2,1,0:T(8,128)(2,1)S(1)}, u32[]{:S(2)}, u32[]{:S(2)}) collective-permute-start(bf16[2,64,512]{2,1,0:T(8,128)(2,1)S(1)} %get-tuple-element.158.rest_0_), channel_id=1, source_target_pairs={{0,12},{4,0},{8,4},{12,8},{1,13},{5,1},{9,5},{13,9},{2,14},{6,2},{... | collective-permute-start | bytes 393224 | tf_op jit(solution)/shard_map/ppermute | solution.py:474
  86.3 0.4 collective-permute-start.16
  87.0 3.3 %collective-permute-done.17.rest_3_ = bf16[2,64,512]{2,1,0:T(8,128)(2,1)S(1)} collective-permute-done((bf16[2,64,512]{2,1,0:T(8,128)(2,1)S(1)}, bf16[2,64,512]{2,1,0:T(8,128)(2,1)S(1)}, u32[]{:S(2)}, u32[]{:S(2)}) %collective-permute-start.17) | collective-permute-done | bytes 131104 | tf_op jit(solution)/shard_map/ppermute | solution.py:474
  90.3 8.3 %collective-permute-done.16.rest_2_ = bf16[2,64,512]{2,1,0:T(8,128)(2,1)S(1)} collective-permute-done((bf16[2,64,512]{2,1,0:T(8,128)(2,1)S(1)}, bf16[2,64,512]{2,1,0:T(8,128)(2,1)S(1)}, u32[]{:S(2)}, u32[]{:S(2)}) %collective-permute-start.16) | collective-permute-done | bytes 131104 | tf_op jit(solution)/shard_map/ppermute | solution.py:474
  98.6 0.5 collective-permute-start.19
  99.1 0.4 collective-permute-start.23
  99.5 2.0 %collective-permute-start.22 = (bf16[1,64,512]{2,1,0:T(8,128)(2,1)S(1)}, bf16[1,64,512]{2,1,0:T(8,128)(2,1)S(1)}, u32[]{:S(2)}, u32[]{:S(2)}) collective-permute-start(bf16[1,64,512]{2,1,0:T(8,128)(2,1)S(1)} %get-tuple-element.161.rest_0_), channel_id=1, source_target_pairs={{0,4},{4,8},{8,12},{12,0},{1,5},{5,9},{9,13},{13,1},{2,6},{6,10},{... | collective-permute-start | bytes 196616 | tf_op jit(solution)/shard_map/ppermute | solution.py:474
  101.5 1.9 %read_first.1 = (bf16[512,512]{1,0:T(8,128)(2,1)S(1)}, bf16[512,512]{1,0:T(8,128)(2,1)S(1)}, bf16[192,512]{1,0:T(8,128)(2,1)S(1)}, bf16[192,512]{1,0:T(8,128)(2,1)S(1)}) custom-call(s32[3]{0:T(128)S(1)} %pad_add_fusion.where, bf16[2,64,512]{2,1,0:T(8,128)(2,1)S(1)} %get-tuple-element.158.rest_0_, bf16[2,64,512]{2,1,0:T(8,128)(2,1)S(1)} %collective-permute-done.15.rest_1_, ...), custom_call_target="tpu_custom_call" | custom-call | tf_op jit(solution)/shard_map/read_first/pallas_call | solution.py:55
  103.4 1.0 collective-permute-done.24.rest_3_
  104.4 2.7 %collective-permute-done.23.rest_2_ = bf16[1,64,512]{2,1,0:T(8,128)(2,1)S(1)} collective-permute-done((bf16[1,64,512]{2,1,0:T(8,128)(2,1)S(1)}, bf16[1,64,512]{2,1,0:T(8,128)(2,1)S(1)}, u32[]{:S(2)}, u32[]{:S(2)}) %collective-permute-start.23) | collective-permute-done | bytes 65568 | tf_op jit(solution)/shard_map/ppermute | solution.py:474
  107.1 0.5 collective-permute-start.26
  107.6 0.5 collective-permute-start.28
  108.5 0.4 collective-permute-done.27.rest_6_
  109.0 1.1 read_down.1
  110.1 0.6 collective-permute-start.29
  110.6 1.8 %read_own.1.half_filled = bf16[512,1024]{1,0:T(8,128)(2,1)} custom-call(s32[3]{0:T(128)S(1)} %pad_add_fusion.where, bf16[512,512]{1,0:T(8,128)(2,1)S(1)} %get-tuple-element.172.g_own, bf16[512,512]{1,0:T(8,128)(2,1)S(1)} %get-tuple-element.166.rest_9_.att_low, bf16[512,512]{1,0:T(8,128)(2,1)S(1)} %get-tuple-element.167.rest_10_.att_up, ...), custom_call_target="tpu_custom_call" | custom-call | tf_op jit(solution)/shard_map/read_own/pallas_call | solution.py:417
  112.5 16.1 %collective-permute-done.29.got = bf16[704,512]{1,0:T(8,128)(2,1)S(1)} collective-permute-done((bf16[704,512]{1,0:T(8,128)(2,1)S(1)}, bf16[704,512]{1,0:T(8,128)(2,1)S(1)}, u32[]{:S(2)}, u32[]{:S(2)}) %collective-permute-start.29) | collective-permute-done | bytes 720928 | tf_op jit(solution)/shard_map/ppermute | solution.py:471
  128.5 1.4 %place.1 = (bf16[512,1024]{1,0:T(8,128)(2,1)}, bf16[192,512]{1,0:T(8,128)(2,1)}) custom-call(s32[3]{0:T(128)S(1)} %pad_add_fusion.where, bf16[704,512]{1,0:T(8,128)(2,1)S(1)} %collective-permute-done.29.got, bf16[192,512]{1,0:T(8,128)(2,1)S(1)} %get-tuple-element.171.kept, bf16[512,1024]{1,0:T(8,128)(2,1)} %read_own.1.half_filled), custom_call_target="tpu_custom_call", output_to_operand_aliasing={{0}: (3, {})} | custom-call | tf_op jit(solution)/shard_map/place/pallas_call | solution.py:448
  (41 shorter events, 1.5 us)
Async XLA Ops:
  3.1 15.9 %collective-permute-start = (bf16[256,1024]{1,0:T(8,128)(2,1)}, bf16[256,1024]{1,0:T(8,128)(2,1)S(1)}, u32[]{:S(2)}, u32[]{:S(2)}) collective-permute-start(bf16[256,1024]{1,0:T(8,128)(2,1)} %pack.3), channel_id=1, source_target_pairs={{0,2},{2,0},{1,3},{3,1},{4,6},{6,4},{5,7},{7,5},{8,10},{10,8},{9,1... | collective-permute-start | bytes 1572872 | tf_op jit(solution)/shard_map/ppermute | solution.py:471
  8.5 1.9 %copy-start = (f32[2,512]{1,0:T(2,128)S(1)}, f32[2,512]{1,0:T(2,128)}, u32[]{:S(2)}) copy-start(f32[2,512]{1,0:T(2,128)} %rates.5) | copy-start | bytes 12292
  8.5 21.8 %collective-permute-start.1 = (bf16[256,1024]{1,0:T(8,128)(2,1)}, bf16[256,1024]{1,0:T(8,128)(2,1)S(1)}, u32[]{:S(2)}, u32[]{:S(2)}) collective-permute-start(bf16[256,1024]{1,0:T(8,128)(2,1)} %pack.4), channel_id=1, source_target_pairs={{0,2},{2,0},{1,3},{3,1},{4,6},{6,4},{5,7},{7,5},{8,10},{10,8},{9,1... | collective-permute-start | bytes 1572872 | tf_op jit(solution)/shard_map/ppermute | solution.py:471
  10.3 16.1 %collective-permute-start.2 = (bf16[512,1024]{1,0:T(8,128)(2,1)S(1)}, bf16[512,1024]{1,0:T(8,128)(2,1)S(1)}, u32[]{:S(2)}, u32[]{:S(2)}) collective-permute-start(bf16[512,1024]{1,0:T(8,128)(2,1)S(1)} %pack.5.own), channel_id=1, source_target_pairs={{0,1},{1,0},{2,3},{3,2},{4,5},{5,4},{6,7},{7,6},{8,9},{9,8},{10,11... | collective-permute-start | bytes 3145736 | tf_op jit(solution)/shard_map/ppermute | solution.py:471
  10.4 1.7 %copy-start.1 = (bf16[512,1024]{1,0:T(8,128)(2,1)S(1)}, bf16[512,1024]{1,0:T(8,128)(2,1)}, u32[]{:S(2)}) copy-start(bf16[512,1024]{1,0:T(8,128)(2,1)} %query) | copy-start | bytes 3145732
  12.1 1.5 %copy-start.2 = (bf16[1024,512]{1,0:T(8,128)(2,1)S(1)}, bf16[1024,512]{1,0:T(8,128)(2,1)}, u32[]{:S(2)}) copy-start(bf16[1024,512]{1,0:T(8,128)(2,1)} %param.13) | copy-start | bytes 3145732
  12.1 1.8 %copy-start.3 = (bf16[1024,512]{1,0:T(8,128)(2,1)S(1)}, bf16[1024,512]{1,0:T(8,128)(2,1)}, u32[]{:S(2)}) copy-start(bf16[1024,512]{1,0:T(8,128)(2,1)} %param.12) | copy-start | bytes 3145732
  20.7 9.6 %collective-permute-start.3 = (bf16[256,1024]{1,0:T(8,128)(2,1)S(1)}, bf16[256,1024]{1,0:T(8,128)(2,1)S(1)}, u32[]{:S(2)}, u32[]{:S(2)}) collective-permute-start(bf16[256,1024]{1,0:T(8,128)(2,1)S(1)} %collective-permute-done.foreign.rest_0_.for_a), channel_id=1, source_target_pairs={{0,1},{1,0},{2,3},{3,2},{4,5},{5,4},{6,7},{7,6},{8,9},{9,8},{10,11... | collective-permute-start | bytes 1572872 | tf_op jit(solution)/shard_map/ppermute | solution.py:471
  20.8 20.3 %collective-permute-start.6 = (bf16[528,512]{1,0:T(8,128)(2,1)S(1)}, bf16[528,512]{1,0:T(8,128)(2,1)S(1)}, u32[]{:S(2)}, u32[]{:S(2)}) collective-permute-start(bf16[528,512]{1,0:T(8,128)(2,1)S(1)} %pack_q.1), channel_id=1, source_target_pairs={{0,2},{2,0},{1,3},{3,1},{4,6},{6,4},{5,7},{7,5},{8,10},{10,8},{9,1... | collective-permute-start | bytes 1622024 | tf_op jit(solution)/shard_map/ppermute | solution.py:471
  22.9 15.8 %collective-permute-start.5 = (bf16[256,1024]{1,0:T(8,128)(2,1)S(1)}, bf16[256,1024]{1,0:T(8,128)(2,1)S(1)}, u32[]{:S(2)}, u32[]{:S(2)}) collective-permute-start(bf16[256,1024]{1,0:T(8,128)(2,1)S(1)} %pick.2), channel_id=1, source_target_pairs={{0,4},{4,8},{8,12},{1,5},{5,9},{9,13},{2,6},{6,10},{10,14},{3,7},{... | collective-permute-start | bytes 1572872 | tf_op jit(solution)/shard_map/ppermute | solution.py:474
  31.9 6.7 %collective-permute-start.4 = (bf16[256,1024]{1,0:T(8,128)(2,1)S(1)}, bf16[256,1024]{1,0:T(8,128)(2,1)S(1)}, u32[]{:S(2)}, u32[]{:S(2)}) collective-permute-start(bf16[256,1024]{1,0:T(8,128)(2,1)S(1)} %collective-permute-done.1.foreign.rest_1_.for_b), channel_id=1, source_target_pairs={{0,1},{1,0},{2,3},{3,2},{4,5},{5,4},{6,7},{7,6},{8,9},{9,8},{10,11... | collective-permute-start | bytes 1572872 | tf_op jit(solution)/shard_map/ppermute | solution.py:471
  32.0 17.1 %collective-permute-start.7 = (bf16[256,1024]{1,0:T(8,128)(2,1)S(1)}, bf16[256,1024]{1,0:T(8,128)(2,1)S(1)}, u32[]{:S(2)}, u32[]{:S(2)}) collective-permute-start(bf16[256,1024]{1,0:T(8,128)(2,1)S(1)} %pick.3), channel_id=1, source_target_pairs={{0,4},{4,8},{8,12},{1,5},{5,9},{9,13},{2,6},{6,10},{10,14},{3,7},{... | collective-permute-start | bytes 1572872 | tf_op jit(solution)/shard_map/ppermute | solution.py:474
  49.1 3.9 %collective-permute-start.8 = (bf16[256,1024]{1,0:T(8,128)(2,1)S(1)}, bf16[256,1024]{1,0:T(8,128)(2,1)S(1)}, u32[]{:S(2)}, u32[]{:S(2)}) collective-permute-start(bf16[256,1024]{1,0:T(8,128)(2,1)S(1)} %collective-permute-done.5.halo_a), channel_id=1, source_target_pairs={{0,1},{1,0},{2,3},{3,2},{4,5},{5,4},{6,7},{7,6},{8,9},{9,8},{10,11... | collective-permute-start | bytes 1572872 | tf_op jit(solution)/shard_map/ppermute | solution.py:471
  49.1 3.9 %collective-permute-start.9 = (bf16[256,1024]{1,0:T(8,128)(2,1)S(1)}, bf16[256,1024]{1,0:T(8,128)(2,1)S(1)}, u32[]{:S(2)}, u32[]{:S(2)}) collective-permute-start(bf16[256,1024]{1,0:T(8,128)(2,1)S(1)} %collective-permute-done.7.halo_b), channel_id=1, source_target_pairs={{0,1},{1,0},{2,3},{3,2},{4,5},{5,4},{6,7},{7,6},{8,9},{9,8},{10,11... | collective-permute-start | bytes 1572872 | tf_op jit(solution)/shard_map/ppermute | solution.py:471
  52.9 3.9 %collective-permute-start.11 = (bf16[512,512]{1,0:T(8,128)(2,1)S(1)}, bf16[512,512]{1,0:T(8,128)(2,1)S(1)}, u32[]{:S(2)}, u32[]{:S(2)}) collective-permute-start(bf16[512,512]{1,0:T(8,128)(2,1)S(1)} %get-tuple-element.145.e0), channel_id=1, source_target_pairs={{0,1},{1,0},{2,3},{3,2},{4,5},{5,4},{6,7},{7,6},{8,9},{9,8},{10,11... | collective-permute-start | bytes 1572872 | tf_op jit(solution)/shard_map/ppermute | solution.py:471
  56.2 2.8 %collective-permute-start.10 = (bf16[512,512]{1,0:T(8,128)(2,1)S(1)}, bf16[512,512]{1,0:T(8,128)(2,1)S(1)}, u32[]{:S(2)}, u32[]{:S(2)}) collective-permute-start(bf16[512,512]{1,0:T(8,128)(2,1)S(1)} %get-tuple-element.135.e0), channel_id=1, source_target_pairs={{0,1},{1,0},{2,3},{3,2},{4,5},{5,4},{6,7},{7,6},{8,9},{9,8},{10,11... | collective-permute-start | bytes 1572872 | tf_op jit(solution)/shard_map/ppermute | solution.py:471
  61.6 10.4 %collective-permute-start.12 = (bf16[3,64,512]{2,1,0:T(8,128)(2,1)S(1)}, bf16[3,64,512]{2,1,0:T(8,128)(2,1)S(1)}, u32[]{:S(2)}, u32[]{:S(2)}) collective-permute-start(bf16[3,64,512]{2,1,0:T(8,128)(2,1)S(1)} %get-tuple-element.155), channel_id=1, source_target_pairs={{0,4},{4,8},{8,12},{12,0},{1,5},{5,9},{9,13},{13,1},{2,6},{6,10},{... | collective-permute-start | bytes 589832 | tf_op jit(solution)/shard_map/ppermute | solution.py:474
  64.1 15.7 %collective-permute-start.13 = (bf16[3,64,512]{2,1,0:T(8,128)(2,1)S(1)}, bf16[3,64,512]{2,1,0:T(8,128)(2,1)S(1)}, u32[]{:S(2)}, u32[]{:S(2)}) collective-permute-start(bf16[3,64,512]{2,1,0:T(8,128)(2,1)S(1)} %get-tuple-element.156), channel_id=1, source_target_pairs={{0,8},{4,12},{8,0},{12,4},{1,9},{5,13},{9,1},{13,5},{2,10},{6,14},... | collective-permute-start | bytes 589832 | tf_op jit(solution)/shard_map/ppermute | solution.py:474
  66.7 13.1 %collective-permute-start.14 = (bf16[3,64,512]{2,1,0:T(8,128)(2,1)S(1)}, bf16[3,64,512]{2,1,0:T(8,128)(2,1)S(1)}, u32[]{:S(2)}, u32[]{:S(2)}) collective-permute-start(bf16[3,64,512]{2,1,0:T(8,128)(2,1)S(1)} %get-tuple-element.157), channel_id=1, source_target_pairs={{0,12},{4,0},{8,4},{12,8},{1,13},{5,1},{9,5},{13,9},{2,14},{6,2},{... | collective-permute-start | bytes 589832 | tf_op jit(solution)/shard_map/ppermute | solution.py:474
  80.6 9.7 %collective-permute-start.17 = (bf16[2,64,512]{2,1,0:T(8,128)(2,1)S(1)}, bf16[2,64,512]{2,1,0:T(8,128)(2,1)S(1)}, u32[]{:S(2)}, u32[]{:S(2)}) collective-permute-start(bf16[2,64,512]{2,1,0:T(8,128)(2,1)S(1)} %get-tuple-element.158.rest_0_), channel_id=1, source_target_pairs={{0,12},{4,0},{8,4},{12,8},{1,13},{5,1},{9,5},{13,9},{2,14},{6,2},{... | collective-permute-start | bytes 393224 | tf_op jit(solution)/shard_map/ppermute | solution.py:474
  86.3 12.3 %collective-permute-start.16 = (bf16[2,64,512]{2,1,0:T(8,128)(2,1)S(1)}, bf16[2,64,512]{2,1,0:T(8,128)(2,1)S(1)}, u32[]{:S(2)}, u32[]{:S(2)}) collective-permute-start(bf16[2,64,512]{2,1,0:T(8,128)(2,1)S(1)} %get-tuple-element.158.rest_0_), channel_id=1, source_target_pairs={{0,8},{4,12},{8,0},{12,4},{1,9},{5,13},{9,1},{13,5},{2,10},{6,14},... | collective-permute-start | bytes 393224 | tf_op jit(solution)/shard_map/ppermute | solution.py:474
  86.8 11.8 %collective-permute-start.15 = (bf16[2,64,512]{2,1,0:T(8,128)(2,1)S(1)}, bf16[2,64,512]{2,1,0:T(8,128)(2,1)S(1)}, u32[]{:S(2)}, u32[]{:S(2)}) collective-permute-start(bf16[2,64,512]{2,1,0:T(8,128)(2,1)S(1)} %get-tuple-element.158.rest_0_), channel_id=1, source_target_pairs={{0,4},{4,8},{8,12},{12,0},{1,5},{5,9},{9,13},{13,1},{2,6},{6,10},{... | collective-permute-start | bytes 393224 | tf_op jit(solution)/shard_map/ppermute | solution.py:474
  87.0 12.1 %collective-permute-start.18 = (bf16[2,64,512]{2,1,0:T(8,128)(2,1)S(1)}, bf16[2,64,512]{2,1,0:T(8,128)(2,1)S(1)}, u32[]{:S(2)}, u32[]{:S(2)}) collective-permute-start(bf16[2,64,512]{2,1,0:T(8,128)(2,1)S(1)} %get-tuple-element.158.rest_0_), channel_id=1, source_target_pairs={{0,1},{1,0},{2,3},{3,2},{4,5},{5,4},{6,7},{7,6},{8,9},{9,8},{10,11... | collective-permute-start | bytes 393224 | tf_op jit(solution)/shard_map/ppermute | solution.py:471
  90.3 9.2 %collective-permute-start.21 = (bf16[2,64,512]{2,1,0:T(8,128)(2,1)S(1)}, bf16[2,64,512]{2,1,0:T(8,128)(2,1)S(1)}, u32[]{:S(2)}, u32[]{:S(2)}) collective-permute-start(bf16[2,64,512]{2,1,0:T(8,128)(2,1)S(1)} %collective-permute-done.17.rest_3_), channel_id=1, source_target_pairs={{0,1},{1,0},{2,3},{3,2},{4,5},{5,4},{6,7},{7,6},{8,9},{9,8},{10,11... | collective-permute-start | bytes 393224 | tf_op jit(solution)/shard_map/ppermute | solution.py:471
  98.6 2.9 %collective-permute-start.20 = (bf16[2,64,512]{2,1,0:T(8,128)(2,1)S(1)}, bf16[2,64,512]{2,1,0:T(8,128)(2,1)S(1)}, u32[]{:S(2)}, u32[]{:S(2)}) collective-permute-start(bf16[2,64,512]{2,1,0:T(8,128)(2,1)S(1)} %collective-permute-done.16.rest_2_), channel_id=1, source_target_pairs={{0,1},{1,0},{2,3},{3,2},{4,5},{5,4},{6,7},{7,6},{8,9},{9,8},{10,11... | collective-permute-start | bytes 393224 | tf_op jit(solution)/shard_map/ppermute | solution.py:471
  98.6 2.9 %collective-permute-start.19 = (bf16[2,64,512]{2,1,0:T(8,128)(2,1)S(1)}, bf16[2,64,512]{2,1,0:T(8,128)(2,1)S(1)}, u32[]{:S(2)}, u32[]{:S(2)}) collective-permute-start(bf16[2,64,512]{2,1,0:T(8,128)(2,1)S(1)} %collective-permute-done.15.rest_1_), channel_id=1, source_target_pairs={{0,1},{1,0},{2,3},{3,2},{4,5},{5,4},{6,7},{7,6},{8,9},{9,8},{10,11... | collective-permute-start | bytes 393224 | tf_op jit(solution)/shard_map/ppermute | solution.py:471
  99.1 5.3 %collective-permute-start.24 = (bf16[1,64,512]{2,1,0:T(8,128)(2,1)S(1)}, bf16[1,64,512]{2,1,0:T(8,128)(2,1)S(1)}, u32[]{:S(2)}, u32[]{:S(2)}) collective-permute-start(bf16[1,64,512]{2,1,0:T(8,128)(2,1)S(1)} %get-tuple-element.161.rest_0_), channel_id=1, source_target_pairs={{0,12},{4,0},{8,4},{12,8},{1,13},{5,1},{9,5},{13,9},{2,14},{6,2},{... | collective-permute-start | bytes 196616 | tf_op jit(solution)/shard_map/ppermute | solution.py:474
  99.1 8.0 %collective-permute-start.23 = (bf16[1,64,512]{2,1,0:T(8,128)(2,1)S(1)}, bf16[1,64,512]{2,1,0:T(8,128)(2,1)S(1)}, u32[]{:S(2)}, u32[]{:S(2)}) collective-permute-start(bf16[1,64,512]{2,1,0:T(8,128)(2,1)S(1)} %get-tuple-element.161.rest_0_), channel_id=1, source_target_pairs={{0,8},{4,12},{8,0},{12,4},{1,9},{5,13},{9,1},{13,5},{2,10},{6,14},... | collective-permute-start | bytes 196616 | tf_op jit(solution)/shard_map/ppermute | solution.py:474
  99.5 7.6 %collective-permute-start.22 = (bf16[1,64,512]{2,1,0:T(8,128)(2,1)S(1)}, bf16[1,64,512]{2,1,0:T(8,128)(2,1)S(1)}, u32[]{:S(2)}, u32[]{:S(2)}) collective-permute-start(bf16[1,64,512]{2,1,0:T(8,128)(2,1)S(1)} %get-tuple-element.161.rest_0_), channel_id=1, source_target_pairs={{0,4},{4,8},{8,12},{12,0},{1,5},{5,9},{9,13},{13,1},{2,6},{6,10},{... | collective-permute-start | bytes 196616 | tf_op jit(solution)/shard_map/ppermute | solution.py:474
  107.1 1.3 collective-permute-start.25
  107.1 1.4 %collective-permute-start.26 = (bf16[1,64,512]{2,1,0:T(8,128)(2,1)S(1)}, bf16[1,64,512]{2,1,0:T(8,128)(2,1)S(1)}, u32[]{:S(2)}, u32[]{:S(2)}) collective-permute-start(bf16[1,64,512]{2,1,0:T(8,128)(2,1)S(1)} %collective-permute-done.22.rest_1_), channel_id=1, source_target_pairs={{0,1},{1,0},{2,3},{3,2},{4,5},{5,4},{6,7},{7,6},{8,9},{9,8},{10,11... | collective-permute-start | bytes 196616 | tf_op jit(solution)/shard_map/ppermute | solution.py:471
  107.6 1.3 collective-permute-start.27
  107.6 1.4 %collective-permute-start.28 = (bf16[1,64,512]{2,1,0:T(8,128)(2,1)S(1)}, bf16[1,64,512]{2,1,0:T(8,128)(2,1)S(1)}, u32[]{:S(2)}, u32[]{:S(2)}) collective-permute-start(bf16[1,64,512]{2,1,0:T(8,128)(2,1)S(1)} %collective-permute-done.24.rest_3_), channel_id=1, source_target_pairs={{0,1},{1,0},{2,3},{3,2},{4,5},{5,4},{6,7},{7,6},{8,9},{9,8},{10,11... | collective-permute-start | bytes 196616 | tf_op jit(solution)/shard_map/ppermute | solution.py:471
  110.1 18.5 %collective-permute-start.29 = (bf16[704,512]{1,0:T(8,128)(2,1)S(1)}, bf16[704,512]{1,0:T(8,128)(2,1)S(1)}, u32[]{:S(2)}, u32[]{:S(2)}) collective-permute-start(bf16[704,512]{1,0:T(8,128)(2,1)S(1)} %get-tuple-element.170), channel_id=1, source_target_pairs={{0,2},{2,0},{1,3},{3,1},{4,6},{6,4},{5,7},{7,5},{8,10},{10,8},{9,1... | collective-permute-start | bytes 2162696 | tf_op jit(solution)/shard_map/ppermute | solution.py:471

commit v4 on v3

--- a/solution.py
+++ b/solution.py
@@ -88,39 +88,38 @@
     return run
 
 
-def pack_kernel(where, key, value, out):
-    out[:, 0:HD] = key[...]
-    out[:, HD : 2 * HD] = value[...]
+def pack_kernel(first, count, own, where, key, value, out, sems):
+    column = where[0] if own else 1 - where[0]
+    source = (pl.ds(first, count), pl.ds(pl.multiple_of(column * HD, HD), HD))
+    copies = [
+        pltpu.make_async_copy(ref.at[source], out.at[:, pl.ds(n * HD, HD)], sems.at[n])
+        for n, ref in enumerate((key, value))
+    ]
+    for copy in copies:
+        copy.start()
+    for copy in copies:
+        copy.wait()
 
 
 def pack(where, key_rows, value_rows, first, count, own):
-    def block(i, s):
-        return (first // count, s[0] if own else 1 - s[0])
-
     return pl.pallas_call(
-        pack_kernel,
-        grid_spec=pltpu.PrefetchScalarGridSpec(
-            num_scalar_prefetch=1,
-            grid=(1,),
-            in_specs=[pl.BlockSpec((count, HD), block)] * 2,
-            out_specs=pl.BlockSpec((count, 2 * HD), lambda i, s: (0, 0)),
-        ),
+        functools.partial(pack_kernel, first, count, own),
+        in_specs=[SM] + [pl.BlockSpec(memory_space=pl.ANY)] * 2,
+        out_specs=VM,
         out_shape=shape((count, 2 * HD)),
+        scratch_shapes=[pltpu.SemaphoreType.DMA((2,))],
         compiler_params=PARAMS,
         name="pack",
     )(where, in_hbm(key_rows), in_hbm(value_rows))
 
 
-def pick_kernel(where, foreign, key, value, out):
-    own = where[0] == 1
-    out[:, 0:HD] = jnp.where(own, key[...], foreign[:, 0:HD])
-    out[:, HD : 2 * HD] = jnp.where(own, value[...], foreign[:, HD : 2 * HD])
-
-
-def pick(where, foreign, key_rows, value_rows, n):
-    part = pl.BlockSpec((HALF, HD), lambda i, s: (n, s[0]))
-    return call_blocks(pick_kernel, "pick", [None, part, part], [shape((HALF, 2 * HD))])(
-        where, foreign, in_hbm(key_rows), in_hbm(value_rows)
+def pick_kernel(n, where, foreign, own, out):
+    out[...] = jnp.where(where[0] == 0, foreign[...], own[n * HALF : (n + 1) * HALF, :])
+
+
+def pick(where, foreign, own, n):
+    return call(functools.partial(pick_kernel, n), "pick", [shape((HALF, 2 * HD))])(
+        where, foreign, own
     )[0]
 
 
@@ -333,9 +332,11 @@
 
 
 def update_kernel(zs, where, own, *rest):
-    got, olds, (first, last) = rest[:-5], rest[-5:-2], rest[-2:]
+    got, olds, (first, last, placed) = rest[:-6], rest[-6:-3], rest[-3:]
     rows = HALF // zs
-    mine = pl.ds(pl.multiple_of(where[1] * HALF + where[2] * rows, rows), rows)
+    at = where[1] * HALF + where[2] * rows
+    mine = pl.ds(pl.multiple_of(at, rows), rows)
+    number = where[0] * 2 * zs + where[1] * zs + where[2]
     for kind, out in enumerate((first.at[0], first.at[1], last.at[0])):
         grad = own[kind]
         for g in got:
@@ -345,7 +346,18 @@
         factor = jnp.sqrt(jnp.mean(old * old, -1, keepdims=True) + 1e-06) * lax.rsqrt(
             jnp.mean(raised * raised, -1, keepdims=True) + 1e-06
         )
-        out[...] = (raised * factor).astype(BF)
+        new = (raised * factor).astype(BF)
+        out[...] = new
+        placed[lax.rem(kind * 4 * zs + number, 3)] = new
+
+
+def owners(zs, slot):
+    pairs = []
+    for owner in range(4 * zs):
+        head, piece = divmod((3 * owner + slot) % (4 * zs), 2 * zs)
+        core, z = divmod(piece, zs)
+        pairs.append(((z * 2 + head) * 2 + core, owner))
+    return pairs
 
 
 def gather(zs, where, pieces, kinds, full):
@@ -357,27 +369,9 @@
                 full[pl.ds(pl.multiple_of(kind * HD + at, rows), rows), :] = some[d][kind]
 
 
-def windows(where, count, put):
-    y, core, z = where[0], where[1], where[2]
-    step = math.gcd(count, HD)
-    for n, side in enumerate((1 - y, y)):
-        first = ((z * 2 + side) * 2 + core) * count
-        for c in range(count // step):
-            r = first + c * step
-            put(n, c * step, step, lax.div(r, 2 * HD), pl.multiple_of(lax.rem(r, HD), step))
-
-
-def read_first_kernel(zs, count, where, *rest):
-    pieces, (q_for, q_own) = rest[: 2 * zs], rest[2 * zs : 2 * zs + 2]
-    g_for, g_own, given, kept, full = rest[2 * zs + 2 :]
+def read_first_kernel(zs, where, *rest):
+    pieces, (q_for, q_own, g_for, g_own, full) = rest[: 2 * zs], rest[2 * zs :]
     gather(zs, where, pieces, 2, full)
-    outs = (given, kept)
-
-    def put(n, to, step, kind, row):
-        at = pl.multiple_of(lax.min(kind, 1) * HD + row, step)
-        outs[n][to : to + step, :] = full[pl.ds(at, step), :]
-
-    windows(where, count, put)
     for q, g in ((q_for, g_for), (q_own, g_own)):
         for c in range(2):
             rows = pl.ds(c * HALF, HALF)
@@ -387,22 +381,14 @@
             g[rows, :] = (hg * jax.nn.sigmoid(hg) * hu).astype(BF)
 
 
-def read_down_kernel(zs, count, where, *rest):
+def read_down_kernel(zs, where, *rest):
     pieces = rest[: 2 * zs]
-    g_for, att_low, att_up, some_given, some_kept, sent, full, kept = rest[2 * zs :]
+    g_for, att_low, att_up, out, full = rest[2 * zs :]
     gather(zs, where, pieces, 1, full)
     low = where[0] == 1
-    sent[0:BLK, :] = (
+    out[...] = (
         jnp.where(low, att_low[...], att_up[...]).astype(F32) + mm_t(g_for[...], full[...])
     ).astype(BF)
-    outs, before = (sent, kept), (some_given, some_kept)
-
-    def put(n, to, step, kind, row):
-        rows = slice(to, to + step)
-        at = slice(to + BLK, to + BLK + step) if n == 0 else rows
-        outs[n][at, :] = jnp.where(kind == 2, full[pl.ds(row, step), :], before[n][rows, :])
-
-    windows(where, count, put)
 
 
 def read_own_kernel(where, g_own, att_low, att_up, w, out):
@@ -428,36 +414,25 @@
     )(where, g_own, att_low, att_up, w)
 
 
-def place_kernel(count, where, got, kept, half_filled, out, weights):
-    y, core, z = where[0], where[1], where[2]
-    out[...] = got[0:BLK, :]
-    step = math.gcd(count, HD)
-    first = ((z * 2 + y) * 2 + core) * count
-    for c in range(count // step):
-        rows = slice(c * step, (c + 1) * step)
-        head = lax.rem(lax.div(first + c * step, HD), 2)
-        weights[rows, :] = jnp.where(
-            head == y, kept[rows, :], got[BLK + c * step : BLK + (c + 1) * step, :]
-        )
-
-
-def place(where, count, got, kept, half_filled):
-    def whole(rows):
-        return pl.BlockSpec((rows, HD), lambda i, s: (0, 0))
-
+def place_kernel(where, got, half_filled, out, sem):
+    column = pl.ds(pl.multiple_of((1 - where[0]) * HD, HD), HD)
+    copy = pltpu.make_async_copy(got, out.at[:, column], sem)
+    copy.start()
+    copy.wait()
+
+
+def place(where, got, half_filled):
+    anyspec = pl.BlockSpec(memory_space=pl.ANY)
     return pl.pallas_call(
-        functools.partial(place_kernel, count),
-        grid_spec=pltpu.PrefetchScalarGridSpec(
-            num_scalar_prefetch=1,
-            grid=(1,),
-            in_specs=[whole(BLK + count), whole(count), pl.BlockSpec(memory_space=pl.ANY)],
-            out_specs=[pl.BlockSpec((BLK, HD), lambda i, s: (0, 1 - s[0])), whole(count)],
-        ),
-        out_shape=[shape((BLK, H * HD)), shape((count, HD))],
-        input_output_aliases={3: 0},
+        place_kernel,
+        in_specs=[SM, VM, anyspec],
+        out_specs=anyspec,
+        out_shape=shape((BLK, H * HD)),
+        scratch_shapes=[pltpu.SemaphoreType.DMA],
+        input_output_aliases={2: 0},
         compiler_params=PARAMS,
         name="place",
-    )(where, got, kept, half_filled)
+    )(where, got, half_filled)
 
 
 def local(queries, key_rows, value_rows, step_rates, w_gate, w_up, w_down):
@@ -465,7 +440,6 @@
     z, y, core = lax.axis_index("z"), lax.axis_index("y"), lax.axis_index("core")
     where = jnp.stack([y, core, z]).astype(jnp.int32)
     rows = HALF // zs
-    count = 3 * H * HD // (4 * zs)
 
     def swap(value, axis):
         return lax.ppermute(value, axis, SWAP)
@@ -495,25 +469,26 @@
     )
     q_for = swap(sent_q, "y")
     own2 = swap(own, "core")
-    gone = pick(where, theirs[0], key_rows, value_rows, 0)
+    gone = pick(where, theirs[0], own, 0)
     halo_a = shift(gone, 1, ring=False)
     theirs2 = [swap(after(theirs[0], gone), "core")]
     mine = pre_own(where, own, own2, wg, wu)
     theirs[1], mine, theirs2[0] = lax.optimization_barrier((theirs[1], mine, theirs2[0]))
-    gone = pick(where, theirs[1], key_rows, value_rows, 1)
+    gone = pick(where, theirs[1], own, 1)
     halo_b = shift(gone, 1, ring=False)
     theirs2.append(swap(after(theirs[1], gone), "core"))
     theirs2, halo_a = lax.optimization_barrier((theirs2, halo_a))
     low, high = pre(where, theirs, mine[:4], wg, wu)
     theirs2, low, q_for = lax.optimization_barrier((theirs2, low, q_for))
     low2, high2 = pre(where, theirs2, mine[4:], wg, wu)
-    low2, q_for, halo = lax.optimization_barrier((low2, q_for, (halo_a, halo_b)))
-    halo2 = [swap(h, "core") for h in halo]
+    low2, q_for = lax.optimization_barrier((low2, q_for))
 
     pair = shape((BLK, 2 * HD))
     att_up, err_up, kv_low, kv_low2 = call(
         upper_kernel, "attend_upper", two + [pair] * 2, [pltpu.VMEM(pair.shape, BF)] * 2
     )(where, q_own, q_for, step_rates, own, *theirs, own2, *theirs2)
+    err_up, halo = lax.optimization_barrier((err_up, (halo_a, halo_b)))
+    halo2 = [swap(h, "core") for h in halo]
     err_up2 = swap(err_up, "core")
     att_low, err_low = call(
         lower_kernel, "attend_lower", two, [pltpu.VMEM((BLK, 2 * HD), BF)]
@@ -534,10 +509,10 @@
         [pltpu.VMEM(total.shape, F32)],
     )(where, err_low, err_low2, *factors_of(low, low2), wd, before)
     got = [shift(s, d) for d, s in enumerate(sends, 1)]
-    piece_a, piece_b = call(
+    piece_a, piece_b, placed = call(
         functools.partial(update_kernel, zs),
         "update",
-        [shape((2, rows, HD)), shape((1, rows, HD))],
+        [shape((2, rows, HD)), shape((1, rows, HD)), shape((3, rows, HD))],
     )(where, own_sum, *got, wg, wu, wd)
 
     def around(piece):
@@ -548,23 +523,21 @@
 
     pieces_a = both(around(piece_a))
     pieces_b = around(piece_b)
-    window = shape((count, HD))
-    g_for, g_own, some_given, some_kept = call(
-        functools.partial(read_first_kernel, zs, count),
-        "read_first",
-        two + [window] * 2,
-        [pltpu.VMEM((2 * HD, HD), BF)],
+    g_for, g_own = call(
+        functools.partial(read_first_kernel, zs), "read_first", two, [pltpu.VMEM((2 * HD, HD), BF)]
     )(where, *pieces_a, q_for, q_own)
+    own_rows = [
+        lax.ppermute(placed[slot], ("z", "y", "core"), owners(zs, slot)) for slot in range(3)
+    ]
     g_for, pieces_b = lax.optimization_barrier((g_for, pieces_b))
     pieces_b = both(pieces_b)
-    sent, full, kept = call(
-        functools.partial(read_down_kernel, zs, count),
-        "read_down",
-        [shape((BLK + count, HD)), shape((HD, HD)), window],
-    )(where, *pieces_b, g_for, att_low, att_up, some_given, some_kept)
-    got_out = swap(sent, "y")
+    out_for, full = call(
+        functools.partial(read_down_kernel, zs), "read_down", [shape((BLK, HD)), shape((HD, HD))]
+    )(where, *pieces_b, g_for, att_low, att_up)
+    out_got = swap(out_for, "y")
     half_filled = read_own(where, g_own, att_low, att_up, full)
-    return tuple(place(where, count, got_out, kept, half_filled))
+    half_filled, own_rows = lax.optimization_barrier((half_filled, own_rows))
+    return place(where, out_got, half_filled), jnp.concatenate(own_rows, 0)
 
 
 def solution(mesh):

time: 130 us -> 126 us (0.969)
  the two profiles are of different devices: /device:TPU:0 before, /device:TPU:16 now
where the time goes in v4:
time: 126 us
  waiting for transfers between devices  49.8 us (40%)
  Pallas kernels  36.6 us (29%)
  starting transfers between devices  35.8 us (28%)
  other arithmetic  2.39 us (2%)
    ppermute x11, waiting for transfers between devices, shift(): lax.ppermute(value, 'z', [(i, (i + d) % zs) for i in range(zs) if ring or...  31.3 us
    pallas_call x12, Pallas kernels, run(): pl.pallas_call(kernel, in_specs=[SM] + [VM] * len(args), out_specs=[VM] *...  25.3 us
    ppermute x11, starting transfers between devices, shift(): lax.ppermute(value, 'z', [(i, (i + d) % zs) for i in range(zs) if ring or...  19.4 us
    ppermute x19, waiting for transfers between devices, swap(): return lax.ppermute(value, axis, SWAP)  12.6 us
    ppermute x3, starting transfers between devices, local(): lax.ppermute(placed[slot], ('z', 'y', 'core'), owners(zs, slot))  10.2 us
    pallas_call x3, Pallas kernels, pack(): pl.pallas_call(functools.partial(pack_kernel, first, count, own), in_spec...  6.53 us
    ppermute x19, starting transfers between devices, swap(): return lax.ppermute(value, axis, SWAP)  6.26 us
    ppermute x3, waiting for transfers between devices, local(): lax.ppermute(placed[slot], ('z', 'y', 'core'), owners(zs, slot))  5.9 us
  transfers between devices with their start and end apart: 33, of which 19 were waited for; matrix products, arithmetic and copies ran while one was open for 2% of the time, Pallas kernels for 23%

profile of v4, /device:TPU:16, one launch (start us, length us, event | category | flops | bytes accessed | tf_op | source)
XLA Modules:
  0.0 126.1 jit_solution(2583234167072759887)
XLA Ops:
  0.7 2.4 %pack.3 = bf16[256,1024]{1,0:T(8,128)(2,1)} custom-call(s32[3]{0:T(128)S(1)} %pad_add_fusion.where, bf16[512,1024]{1,0:T(8,128)(2,1)} %key.3, bf16[512,1024]{1,0:T(8,128)(2,1)} %value.5), custom_call_target="tpu_custom_call" | custom-call | tf_op jit(solution)/shard_map/pack/pallas_call | solution.py:105
  3.1 1.6 %collective-permute-start = (bf16[256,1024]{1,0:T(8,128)(2,1)}, bf16[256,1024]{1,0:T(8,128)(2,1)S(1)}, u32[]{:S(2)}, u32[]{:S(2)}) collective-permute-start(bf16[256,1024]{1,0:T(8,128)(2,1)} %pack.3), channel_id=1, source_target_pairs={{0,2},{2,0},{1,3},{3,1},{4,6},{6,4},{5,7},{7,5},{8,10},{10,8},{9,1... | collective-permute-start | bytes 1572872 | tf_op jit(solution)/shard_map/ppermute | solution.py:445
  4.7 2.4 %pack.4 = bf16[256,1024]{1,0:T(8,128)(2,1)} custom-call(s32[3]{0:T(128)S(1)} %pad_add_fusion.where, bf16[512,1024]{1,0:T(8,128)(2,1)} %key.3, bf16[512,1024]{1,0:T(8,128)(2,1)} %value.5), custom_call_target="tpu_custom_call" | custom-call | tf_op jit(solution)/shard_map/pack/pallas_call | solution.py:105
  7.7 1.8 %pack.5.own = bf16[512,1024]{1,0:T(8,128)(2,1)S(1)} custom-call(s32[3]{0:T(128)S(1)} %pad_add_fusion.where, bf16[512,1024]{1,0:T(8,128)(2,1)} %key.3, bf16[512,1024]{1,0:T(8,128)(2,1)} %value.5), custom_call_target="tpu_custom_call" | custom-call | tf_op jit(solution)/shard_map/pack/pallas_call | solution.py:105
  9.5 1.6 %pack_q.1 = bf16[528,512]{1,0:T(8,128)(2,1)S(1)} custom-call(s32[3]{0:T(128)S(1)} %pad_add_fusion.where, bf16[512,1024]{1,0:T(8,128)(2,1)} %query, f32[2,512]{1,0:T(2,128)S(1)} %copy-done), custom_call_target="tpu_custom_call" | custom-call | tf_op jit(solution)/shard_map/pack_q/pallas_call | solution.py:74
  11.2 1.5 %slice_select_fusion.2 = (bf16[512,512]{1,0:T(8,128)(2,1)S(1)}, bf16[512,512]{1,0:T(8,128)(2,1)S(1)}) fusion(bf16[1024,512]{1,0:T(8,128)(2,1)} %param.11, pred[]{:T(512)S(6)} %eq.2, bf16[512,1024]{1,0:T(8,128)(2,1)S(1)} %copy-done.1), kind=kLoop, calls=%fused_computation.2 | loop fusion | flops 524288 | bytes 3145729 | tf_op jit(solution)/shard_map/jit(_where)/select_n | solution.py:466
  13.2 5.0 %collective-permute-done.foreign.rest_0_.for_a = bf16[256,1024]{1,0:T(8,128)(2,1)S(1)} collective-permute-done((bf16[256,1024]{1,0:T(8,128)(2,1)}, bf16[256,1024]{1,0:T(8,128)(2,1)S(1)}, u32[]{:S(2)}, u32[]{:S(2)}) %collective-permute-start) | collective-permute-done | bytes 524320 | tf_op jit(solution)/shard_map/ppermute | solution.py:445
  18.2 0.6 pick.2
  18.9 1.6 %collective-permute-start.6 = (bf16[528,512]{1,0:T(8,128)(2,1)S(1)}, bf16[528,512]{1,0:T(8,128)(2,1)S(1)}, u32[]{:S(2)}, u32[]{:S(2)}) collective-permute-start(bf16[528,512]{1,0:T(8,128)(2,1)S(1)} %pack_q.1), channel_id=1, source_target_pairs={{0,2},{2,0},{1,3},{3,1},{4,6},{6,4},{5,7},{7,5},{8,10},{10,8},{9,1... | collective-permute-start | bytes 1622024 | tf_op jit(solution)/shard_map/ppermute | solution.py:445
  20.5 3.5 %collective-permute-start.5 = (bf16[256,1024]{1,0:T(8,128)(2,1)S(1)}, bf16[256,1024]{1,0:T(8,128)(2,1)S(1)}, u32[]{:S(2)}, u32[]{:S(2)}) collective-permute-start(bf16[256,1024]{1,0:T(8,128)(2,1)S(1)} %pick.2), channel_id=1, source_target_pairs={{0,4},{4,8},{8,12},{1,5},{5,9},{9,13},{2,6},{6,10},{10,14},{3,7},{... | collective-permute-start | bytes 1572872 | tf_op jit(solution)/shard_map/ppermute | solution.py:448
  23.9 3.7 %pre_own.1 = (bf16[512,512]{1,0:T(8,128)(2,1)S(1)}, bf16[512,512]{1,0:T(8,128)(2,1)S(1)}, f32[512,256]{1,0:T(8,128)S(1)}, f32[512,256]{1,0:T(8,128)S(1)}, bf16[5...) custom-call(s32[3]{0:T(128)S(1)} %pad_add_fusion.where, ...), custom_call_target="tpu_custom_call" | custom-call | tf_op jit(solution)/shard_map/pre_own/pallas_call | solution.py:55
  27.7 1.8 %collective-permute-done.1.foreign.rest_1_.for_b = bf16[256,1024]{1,0:T(8,128)(2,1)S(1)} collective-permute-done((bf16[256,1024]{1,0:T(8,128)(2,1)}, bf16[256,1024]{1,0:T(8,128)(2,1)S(1)}, u32[]{:S(2)}, u32[]{:S(2)}) %collective-permute-start.1) | collective-permute-done | bytes 524320 | tf_op jit(solution)/shard_map/ppermute | solution.py:445
  29.4 0.6 pick.3
  30.1 3.5 %collective-permute-start.7 = (bf16[256,1024]{1,0:T(8,128)(2,1)S(1)}, bf16[256,1024]{1,0:T(8,128)(2,1)S(1)}, u32[]{:S(2)}, u32[]{:S(2)}) collective-permute-start(bf16[256,1024]{1,0:T(8,128)(2,1)S(1)} %pick.3), channel_id=1, source_target_pairs={{0,4},{4,8},{8,12},{1,5},{5,9},{9,13},{2,6},{6,10},{10,14},{3,7},{... | collective-permute-start | bytes 1572872 | tf_op jit(solution)/shard_map/ppermute | solution.py:448
  33.6 2.6 %pre.2 = (bf16[512,512]{1,0:T(8,128)(2,1)S(1)}, bf16[512,512]{1,0:T(8,128)(2,1)S(1)}, f32[512,256]{1,0:T(8,128)S(1)}, f32[512,256]{1,0:T(8,128)S(1)}, bf16[512,5...) custom-call(s32[3]{0:T(128)S(1)} %pad_add_fusion.where, ...), custom_call_target="tpu_custom_call" | custom-call | tf_op jit(solution)/shard_map/pre/pallas_call | solution.py:55
  36.2 0.9 collective-permute-done.5.halo_a
  37.1 2.8 %collective-permute-done.6.q_for.rest_8_ = bf16[528,512]{1,0:T(8,128)(2,1)S(1)} collective-permute-done((bf16[528,512]{1,0:T(8,128)(2,1)S(1)}, bf16[528,512]{1,0:T(8,128)(2,1)S(1)}, u32[]{:S(2)}, u32[]{:S(2)}) %collective-permute-start.6) | collective-permute-done | bytes 540704 | tf_op jit(solution)/shard_map/ppermute | solution.py:445
  39.9 2.8 %pre.3 = (bf16[512,512]{1,0:T(8,128)(2,1)S(1)}, bf16[512,512]{1,0:T(8,128)(2,1)S(1)}, f32[512,256]{1,0:T(8,128)S(1)}, f32[512,256]{1,0:T(8,128)S(1)}, bf16[512,5...) custom-call(s32[3]{0:T(128)S(1)} %pad_add_fusion.where, ...), custom_call_target="tpu_custom_call" | custom-call | tf_op jit(solution)/shard_map/pre/pallas_call | solution.py:55
  42.7 3.3 %attend_upper.1 = (bf16[512,512]{1,0:T(8,128)(2,1)S(1)}, bf16[512,512]{1,0:T(8,128)(2,1)S(1)}, bf16[512,1024]{1,0:T(8,128)(2,1)S(1)}, bf16[512,1024]{1,0:T(8,128)(2,1)S(1)}) custom-call(s32[3]{0:T(128)S(1)} %pad_add_fusion.where, bf16[512,512]{1,0:T(8,128)(2,1)S(1)} %get-tuple-element.93.q_own.rest_9_, ...), custom_call_target="tpu_custom_call" | custom-call | tf_op jit(solution)/shard_map/attend_upper/pallas_call | solution.py:55
  46.0 1.6 %collective-permute-done.7.halo_b = bf16[256,1024]{1,0:T(8,128)(2,1)S(1)} collective-permute-done((bf16[256,1024]{1,0:T(8,128)(2,1)S(1)}, bf16[256,1024]{1,0:T(8,128)(2,1)S(1)}, u32[]{:S(2)}, u32[]{:S(2)}) %collective-permute-start.7) | collective-permute-done | bytes 524320 | tf_op jit(solution)/shard_map/ppermute | solution.py:448
  48.1 1.4 %collective-permute-done.8.halo2_a = bf16[256,1024]{1,0:T(8,128)(2,1)S(1)} collective-permute-done((bf16[256,1024]{1,0:T(8,128)(2,1)S(1)}, bf16[256,1024]{1,0:T(8,128)(2,1)S(1)}, u32[]{:S(2)}, u32[]{:S(2)}) %collective-permute-start.8) | collective-permute-done | bytes 524320 | tf_op jit(solution)/shard_map/ppermute | solution.py:445
  49.5 0.7 collective-permute-done.9.halo2_b
  50.2 3.2 %attend_lower.1 = (bf16[512,512]{1,0:T(8,128)(2,1)S(1)}, bf16[512,512]{1,0:T(8,128)(2,1)S(1)}) custom-call(s32[3]{0:T(128)S(1)} %pad_add_fusion.where, bf16[512,512]{1,0:T(8,128)(2,1)S(1)} %get-tuple-element.93.q_own.rest_9_, bf16[528,512]{1,0:T(8,128)(2,1)S(1)} %collective-permute-done.6.q_for.rest_8_, f32[2,512]{1,0:T(2,128)S(1)} %copy-done, ...), custom_call_target="tpu_custom_call" | custom-call | tf_op jit(solution)/shard_map/attend_lower/pallas_call | solution.py:55
  53.7 2.3 %grad_first.1.before = f32[3,256,512]{2,1,0:T(8,128)S(1)} custom-call(s32[3]{0:T(128)S(1)} %pad_add_fusion.where, bf16[512,512]{1,0:T(8,128)(2,1)S(1)} %get-tuple-element.149.e0, bf16[512,512]{1,0:T(8,128)(2,1)S(1)} %collective-permute-done.11.e1, bf16[512,512]{1,0:T(8,128)(2,1)S(1)} %get-tuple-element.150.k0, bf16[512,512]{1,0:T(8,128)(2,1)S(1)} %get-tuple-element.151.k1, ...), custom_call_target="tpu_custom_call" | custom-call | tf_op jit(solution)/shard_map/grad_first/pallas_call | solution.py:55
  55.9 2.5 %grad_second.1 = (f32[3,64,512]{2,1,0:T(8,128)S(1)}, bf16[3,64,512]{2,1,0:T(8,128)(2,1)S(1)}, bf16[3,64,512]{2,1,0:T(8,128)(2,1)S(1)}, bf16[3,64,512]{2,1,0:T(8,128)(2,1)S(1)}) custom-call(s32[3]{0:T(128)S(1)} %pad_add_fusion.where, bf16[512,512]{1,0:T(8,128)(2,1)S(1)} %get-tuple-element.139.e0, bf16[512,512]{1,0:T(8,128)(2,1)S(1)} %collective-permute-done.10.e1, ...), custom_call_target="tpu_custom_call" | custom-call | tf_op jit(solution)/shard_map/grad_second/pallas_call | solution.py:55
  58.4 1.6 %collective-permute-start.12 = (bf16[3,64,512]{2,1,0:T(8,128)(2,1)S(1)}, bf16[3,64,512]{2,1,0:T(8,128)(2,1)S(1)}, u32[]{:S(2)}, u32[]{:S(2)}) collective-permute-start(bf16[3,64,512]{2,1,0:T(8,128)(2,1)S(1)} %get-tuple-element.159), channel_id=1, source_target_pairs={{0,4},{4,8},{8,12},{12,0},{1,5},{5,9},{9,13},{13,1},{2,6},{6,10},{... | collective-permute-start | bytes 589832 | tf_op jit(solution)/shard_map/ppermute | solution.py:448
  60.4 1.2 collective-permute-start.14
  61.6 13.0 %collective-permute-done.12.rest_0_ = bf16[3,64,512]{2,1,0:T(8,128)(2,1)S(1)} collective-permute-done((bf16[3,64,512]{2,1,0:T(8,128)(2,1)S(1)}, bf16[3,64,512]{2,1,0:T(8,128)(2,1)S(1)}, u32[]{:S(2)}, u32[]{:S(2)}) %collective-permute-start.12) | collective-permute-done | bytes 196640 | tf_op jit(solution)/shard_map/ppermute | solution.py:448
  74.7 2.5 %collective-permute-done.14.rest_2_ = bf16[3,64,512]{2,1,0:T(8,128)(2,1)S(1)} collective-permute-done((bf16[3,64,512]{2,1,0:T(8,128)(2,1)S(1)}, bf16[3,64,512]{2,1,0:T(8,128)(2,1)S(1)}, u32[]{:S(2)}, u32[]{:S(2)}) %collective-permute-start.14) | collective-permute-done | bytes 196640 | tf_op jit(solution)/shard_map/ppermute | solution.py:448
  77.2 0.8 update.1
  78.0 2.5 %collective-permute-start.17 = (bf16[2,64,512]{2,1,0:T(8,128)(2,1)S(1)}, bf16[2,64,512]{2,1,0:T(8,128)(2,1)S(1)}, u32[]{:S(2)}, u32[]{:S(2)}) collective-permute-start(bf16[2,64,512]{2,1,0:T(8,128)(2,1)S(1)} %get-tuple-element.162.rest_0_), channel_id=1, source_target_pairs={{0,12},{4,0},{8,4},{12,8},{1,13},{5,1},{9,5},{13,9},{2,14},{6,2},{... | collective-permute-start | bytes 393224 | tf_op jit(solution)/shard_map/ppermute | solution.py:448
  80.5 2.5 %collective-permute-start.16 = (bf16[2,64,512]{2,1,0:T(8,128)(2,1)S(1)}, bf16[2,64,512]{2,1,0:T(8,128)(2,1)S(1)}, u32[]{:S(2)}, u32[]{:S(2)}) collective-permute-start(bf16[2,64,512]{2,1,0:T(8,128)(2,1)S(1)} %get-tuple-element.162.rest_0_), channel_id=1, source_target_pairs={{0,8},{4,12},{8,0},{12,4},{1,9},{5,13},{9,1},{13,5},{2,10},{6,14},... | collective-permute-start | bytes 393224 | tf_op jit(solution)/shard_map/ppermute | solution.py:448
  83.0 7.0 %collective-permute-done.17.rest_3_ = bf16[2,64,512]{2,1,0:T(8,128)(2,1)S(1)} collective-permute-done((bf16[2,64,512]{2,1,0:T(8,128)(2,1)S(1)}, bf16[2,64,512]{2,1,0:T(8,128)(2,1)S(1)}, u32[]{:S(2)}, u32[]{:S(2)}) %collective-permute-start.17) | collective-permute-done | bytes 131104 | tf_op jit(solution)/shard_map/ppermute | solution.py:448
  90.0 1.9 %collective-permute-done.16.rest_2_ = bf16[2,64,512]{2,1,0:T(8,128)(2,1)S(1)} collective-permute-done((bf16[2,64,512]{2,1,0:T(8,128)(2,1)S(1)}, bf16[2,64,512]{2,1,0:T(8,128)(2,1)S(1)}, u32[]{:S(2)}, u32[]{:S(2)}) %collective-permute-start.16) | collective-permute-done | bytes 131104 | tf_op jit(solution)/shard_map/ppermute | solution.py:448
  91.9 1.7 %collective-permute-done.15.rest_1_ = bf16[2,64,512]{2,1,0:T(8,128)(2,1)S(1)} collective-permute-done((bf16[2,64,512]{2,1,0:T(8,128)(2,1)S(1)}, bf16[2,64,512]{2,1,0:T(8,128)(2,1)S(1)}, u32[]{:S(2)}, u32[]{:S(2)}) %collective-permute-start.15) | collective-permute-done | bytes 131104 | tf_op jit(solution)/shard_map/ppermute | solution.py:448
  93.5 2.5 %collective-permute-start.23 = (bf16[1,64,512]{2,1,0:T(8,128)(2,1)S(1)}, bf16[1,64,512]{2,1,0:T(8,128)(2,1)S(1)}, u32[]{:S(2)}, u32[]{:S(2)}) collective-permute-start(bf16[1,64,512]{2,1,0:T(8,128)(2,1)S(1)} %get-tuple-element.165.rest_0_), channel_id=1, source_target_pairs={{0,8},{4,12},{8,0},{12,4},{1,9},{5,13},{9,1},{13,5},{2,10},{6,14},... | collective-permute-start | bytes 196616 | tf_op jit(solution)/shard_map/ppermute | solution.py:448
  96.0 1.8 %collective-permute-start.22 = (bf16[1,64,512]{2,1,0:T(8,128)(2,1)S(1)}, bf16[1,64,512]{2,1,0:T(8,128)(2,1)S(1)}, u32[]{:S(2)}, u32[]{:S(2)}) collective-permute-start(bf16[1,64,512]{2,1,0:T(8,128)(2,1)S(1)} %get-tuple-element.165.rest_0_), channel_id=1, source_target_pairs={{0,4},{4,8},{8,12},{12,0},{1,5},{5,9},{9,13},{13,1},{2,6},{6,10},{... | collective-permute-start | bytes 196616 | tf_op jit(solution)/shard_map/ppermute | solution.py:448
  97.8 1.9 %read_first.1 = (bf16[512,512]{1,0:T(8,128)(2,1)S(1)}, bf16[512,512]{1,0:T(8,128)(2,1)S(1)}) custom-call(s32[3]{0:T(128)S(1)} %pad_add_fusion.where, bf16[2,64,512]{2,1,0:T(8,128)(2,1)S(1)} %get-tuple-element.162.rest_0_, bf16[2,64,512]{2,1,0:T(8,128)(2,1)S(1)} %collective-permute-done.15.rest_1_, bf16[2,64,512]{2,1,0:T(8,128)(2,1)S(1)} %collective-permute-done.16.rest_2_, ...), custom_call_target="tpu_custom_call" | custom-call | tf_op jit(solution)/shard_map/read_first/pallas_call | solution.py:55
  99.8 0.9 collective-permute-done.23.rest_2_
  100.6 1.8 %collective-permute-done.22.rest_1_ = bf16[1,64,512]{2,1,0:T(8,128)(2,1)S(1)} collective-permute-done((bf16[1,64,512]{2,1,0:T(8,128)(2,1)S(1)}, bf16[1,64,512]{2,1,0:T(8,128)(2,1)S(1)}, u32[]{:S(2)}, u32[]{:S(2)}) %collective-permute-start.22) | collective-permute-done | bytes 65568 | tf_op jit(solution)/shard_map/ppermute | solution.py:448
  104.4 1.1 read_down.1
  106.0 3.4 %collective-permute-start.32 = (bf16[64,512]{1,0:T(8,128)(2,1)S(1)}, bf16[64,512]{1,0:T(8,128)(2,1)S(1)}, u32[]{:S(2)}, u32[]{:S(2)}) collective-permute-start(bf16[64,512]{1,0:T(8,128)(2,1)S(1)} %get-tuple-element.180), channel_id=1, source_target_pairs={{8,0},{5,1},{2,2},{14,3},{11,4},{4,5},{1,6},{13,7},{10,8},{7,9},{0... | collective-permute-start | bytes 196616 | tf_op jit(solution)/shard_map/ppermute | solution.py:530
  109.4 1.9 %collective-permute-start.31 = (bf16[64,512]{1,0:T(8,128)(2,1)S(1)}, bf16[64,512]{1,0:T(8,128)(2,1)S(1)}, u32[]{:S(2)}, u32[]{:S(2)}) collective-permute-start(bf16[64,512]{1,0:T(8,128)(2,1)S(1)} %get-tuple-element.181), channel_id=1, source_target_pairs={{4,0},{1,1},{13,2},{10,3},{7,4},{0,5},{12,6},{9,7},{6,8},{3,9},{15... | collective-permute-start | bytes 196616 | tf_op jit(solution)/shard_map/ppermute | solution.py:530
  111.4 4.8 %collective-permute-start.30 = (bf16[64,512]{1,0:T(8,128)(2,1)S(1)}, bf16[64,512]{1,0:T(8,128)(2,1)S(1)}, u32[]{:S(2)}, u32[]{:S(2)}) collective-permute-start(bf16[64,512]{1,0:T(8,128)(2,1)S(1)} %get-tuple-element.182), channel_id=1, source_target_pairs={{0,0},{12,1},{9,2},{6,3},{3,4},{15,5},{8,6},{5,7},{2,8},{14,9},{11... | collective-permute-start | bytes 196616 | tf_op jit(solution)/shard_map/ppermute | solution.py:530
  116.2 1.8 %read_own.1.half_filled = bf16[512,1024]{1,0:T(8,128)(2,1)} custom-call(s32[3]{0:T(128)S(1)} %pad_add_fusion.where, bf16[512,512]{1,0:T(8,128)(2,1)S(1)} %get-tuple-element.173.g_own, bf16[512,512]{1,0:T(8,128)(2,1)S(1)} %get-tuple-element.170.rest_9_.att_low, bf16[512,512]{1,0:T(8,128)(2,1)S(1)} %get-tuple-element.171.rest_10_.att_up, ...), custom_call_target="tpu_custom_call" | custom-call | tf_op jit(solution)/shard_map/read_own/pallas_call | solution.py:403
  118.0 5.9 %collective-permute-done.32 = bf16[64,512]{1,0:T(8,128)(2,1)S(1)} collective-permute-done((bf16[64,512]{1,0:T(8,128)(2,1)S(1)}, bf16[64,512]{1,0:T(8,128)(2,1)S(1)}, u32[]{:S(2)}, u32[]{:S(2)}) %collective-permute-start.32) | collective-permute-done | bytes 65568 | tf_op jit(solution)/shard_map/ppermute | solution.py:530
  123.9 0.7 pad_maximum_fusion
  124.6 1.3 %place.1 = bf16[512,1024]{1,0:T(8,128)(2,1)} custom-call(s32[3]{0:T(128)S(1)} %pad_add_fusion.where, bf16[512,512]{1,0:T(8,128)(2,1)S(1)} %collective-permute-done.29.got, bf16[512,1024]{1,0:T(8,128)(2,1)} %read_own.1.half_filled), custom_call_target="tpu_custom_call", output_to_operand_aliasing={{}: (2, {})} | custom-call | tf_op jit(solution)/shard_map/place/pallas_call | solution.py:426
  (49 shorter events, 4.9 us)
Async XLA Ops:
  3.1 15.1 %collective-permute-start = (bf16[256,1024]{1,0:T(8,128)(2,1)}, bf16[256,1024]{1,0:T(8,128)(2,1)S(1)}, u32[]{:S(2)}, u32[]{:S(2)}) collective-permute-start(bf16[256,1024]{1,0:T(8,128)(2,1)} %pack.3), channel_id=1, source_target_pairs={{0,2},{2,0},{1,3},{3,1},{4,6},{6,4},{5,7},{7,5},{8,10},{10,8},{9,1... | collective-permute-start | bytes 1572872 | tf_op jit(solution)/shard_map/ppermute | solution.py:445
  7.1 2.4 %copy-start = (f32[2,512]{1,0:T(2,128)S(1)}, f32[2,512]{1,0:T(2,128)}, u32[]{:S(2)}) copy-start(f32[2,512]{1,0:T(2,128)} %rates.5) | copy-start | bytes 12292
  7.1 22.3 %collective-permute-start.1 = (bf16[256,1024]{1,0:T(8,128)(2,1)}, bf16[256,1024]{1,0:T(8,128)(2,1)S(1)}, u32[]{:S(2)}, u32[]{:S(2)}) collective-permute-start(bf16[256,1024]{1,0:T(8,128)(2,1)} %pack.4), channel_id=1, source_target_pairs={{0,2},{2,0},{1,3},{3,1},{4,6},{6,4},{5,7},{7,5},{8,10},{10,8},{9,1... | collective-permute-start | bytes 1572872 | tf_op jit(solution)/shard_map/ppermute | solution.py:445
  9.4 14.5 %collective-permute-start.2 = (bf16[512,1024]{1,0:T(8,128)(2,1)S(1)}, bf16[512,1024]{1,0:T(8,128)(2,1)S(1)}, u32[]{:S(2)}, u32[]{:S(2)}) collective-permute-start(bf16[512,1024]{1,0:T(8,128)(2,1)S(1)} %pack.5.own), channel_id=1, source_target_pairs={{0,1},{1,0},{2,3},{3,2},{4,5},{5,4},{6,7},{7,6},{8,9},{9,8},{10,11... | collective-permute-start | bytes 3145736 | tf_op jit(solution)/shard_map/ppermute | solution.py:445
  9.5 1.7 %copy-start.1 = (bf16[512,1024]{1,0:T(8,128)(2,1)S(1)}, bf16[512,1024]{1,0:T(8,128)(2,1)}, u32[]{:S(2)}) copy-start(bf16[512,1024]{1,0:T(8,128)(2,1)} %query) | copy-start | bytes 3145732
  11.2 1.5 %copy-start.2 = (bf16[1024,512]{1,0:T(8,128)(2,1)S(1)}, bf16[1024,512]{1,0:T(8,128)(2,1)}, u32[]{:S(2)}) copy-start(bf16[1024,512]{1,0:T(8,128)(2,1)} %param.13) | copy-start | bytes 3145732
  11.2 1.8 %copy-start.3 = (bf16[1024,512]{1,0:T(8,128)(2,1)S(1)}, bf16[1024,512]{1,0:T(8,128)(2,1)}, u32[]{:S(2)}) copy-start(bf16[1024,512]{1,0:T(8,128)(2,1)} %param.12) | copy-start | bytes 3145732
  18.8 10.6 %collective-permute-start.3 = (bf16[256,1024]{1,0:T(8,128)(2,1)S(1)}, bf16[256,1024]{1,0:T(8,128)(2,1)S(1)}, u32[]{:S(2)}, u32[]{:S(2)}) collective-permute-start(bf16[256,1024]{1,0:T(8,128)(2,1)S(1)} %collective-permute-done.foreign.rest_0_.for_a), channel_id=1, source_target_pairs={{0,1},{1,0},{2,3},{3,2},{4,5},{5,4},{6,7},{7,6},{8,9},{9,8},{10,11... | collective-permute-start | bytes 1572872 | tf_op jit(solution)/shard_map/ppermute | solution.py:445
  18.9 21.0 %collective-permute-start.6 = (bf16[528,512]{1,0:T(8,128)(2,1)S(1)}, bf16[528,512]{1,0:T(8,128)(2,1)S(1)}, u32[]{:S(2)}, u32[]{:S(2)}) collective-permute-start(bf16[528,512]{1,0:T(8,128)(2,1)S(1)} %pack_q.1), channel_id=1, source_target_pairs={{0,2},{2,0},{1,3},{3,1},{4,6},{6,4},{5,7},{7,5},{8,10},{10,8},{9,1... | collective-permute-start | bytes 1622024 | tf_op jit(solution)/shard_map/ppermute | solution.py:445
  20.5 16.6 %collective-permute-start.5 = (bf16[256,1024]{1,0:T(8,128)(2,1)S(1)}, bf16[256,1024]{1,0:T(8,128)(2,1)S(1)}, u32[]{:S(2)}, u32[]{:S(2)}) collective-permute-start(bf16[256,1024]{1,0:T(8,128)(2,1)S(1)} %pick.2), channel_id=1, source_target_pairs={{0,4},{4,8},{8,12},{1,5},{5,9},{9,13},{2,6},{6,10},{10,14},{3,7},{... | collective-permute-start | bytes 1572872 | tf_op jit(solution)/shard_map/ppermute | solution.py:448
  30.0 7.1 %collective-permute-start.4 = (bf16[256,1024]{1,0:T(8,128)(2,1)S(1)}, bf16[256,1024]{1,0:T(8,128)(2,1)S(1)}, u32[]{:S(2)}, u32[]{:S(2)}) collective-permute-start(bf16[256,1024]{1,0:T(8,128)(2,1)S(1)} %collective-permute-done.1.foreign.rest_1_.for_b), channel_id=1, source_target_pairs={{0,1},{1,0},{2,3},{3,2},{4,5},{5,4},{6,7},{7,6},{8,9},{9,8},{10,11... | collective-permute-start | bytes 1572872 | tf_op jit(solution)/shard_map/ppermute | solution.py:445
  30.1 17.5 %collective-permute-start.7 = (bf16[256,1024]{1,0:T(8,128)(2,1)S(1)}, bf16[256,1024]{1,0:T(8,128)(2,1)S(1)}, u32[]{:S(2)}, u32[]{:S(2)}) collective-permute-start(bf16[256,1024]{1,0:T(8,128)(2,1)S(1)} %pick.3), channel_id=1, source_target_pairs={{0,4},{4,8},{8,12},{1,5},{5,9},{9,13},{2,6},{6,10},{10,14},{3,7},{... | collective-permute-start | bytes 1572872 | tf_op jit(solution)/shard_map/ppermute | solution.py:448
  47.6 1.9 %collective-permute-start.8 = (bf16[256,1024]{1,0:T(8,128)(2,1)S(1)}, bf16[256,1024]{1,0:T(8,128)(2,1)S(1)}, u32[]{:S(2)}, u32[]{:S(2)}) collective-permute-start(bf16[256,1024]{1,0:T(8,128)(2,1)S(1)} %collective-permute-done.5.halo_a), channel_id=1, source_target_pairs={{0,1},{1,0},{2,3},{3,2},{4,5},{5,4},{6,7},{7,6},{8,9},{9,8},{10,11... | collective-permute-start | bytes 1572872 | tf_op jit(solution)/shard_map/ppermute | solution.py:445
  47.6 2.7 %collective-permute-start.9 = (bf16[256,1024]{1,0:T(8,128)(2,1)S(1)}, bf16[256,1024]{1,0:T(8,128)(2,1)S(1)}, u32[]{:S(2)}, u32[]{:S(2)}) collective-permute-start(bf16[256,1024]{1,0:T(8,128)(2,1)S(1)} %collective-permute-done.7.halo_b), channel_id=1, source_target_pairs={{0,1},{1,0},{2,3},{3,2},{4,5},{5,4},{6,7},{7,6},{8,9},{9,8},{10,11... | collective-permute-start | bytes 1572872 | tf_op jit(solution)/shard_map/ppermute | solution.py:445
  48.1 5.6 %collective-permute-start.11 = (bf16[512,512]{1,0:T(8,128)(2,1)S(1)}, bf16[512,512]{1,0:T(8,128)(2,1)S(1)}, u32[]{:S(2)}, u32[]{:S(2)}) collective-permute-start(bf16[512,512]{1,0:T(8,128)(2,1)S(1)} %get-tuple-element.149.e0), channel_id=1, source_target_pairs={{0,1},{1,0},{2,3},{3,2},{4,5},{5,4},{6,7},{7,6},{8,9},{9,8},{10,11... | collective-permute-start | bytes 1572872 | tf_op jit(solution)/shard_map/ppermute | solution.py:445
  53.5 2.5 %collective-permute-start.10 = (bf16[512,512]{1,0:T(8,128)(2,1)S(1)}, bf16[512,512]{1,0:T(8,128)(2,1)S(1)}, u32[]{:S(2)}, u32[]{:S(2)}) collective-permute-start(bf16[512,512]{1,0:T(8,128)(2,1)S(1)} %get-tuple-element.139.e0), channel_id=1, source_target_pairs={{0,1},{1,0},{2,3},{3,2},{4,5},{5,4},{6,7},{7,6},{8,9},{9,8},{10,11... | collective-permute-start | bytes 1572872 | tf_op jit(solution)/shard_map/ppermute | solution.py:445
  58.4 16.2 %collective-permute-start.12 = (bf16[3,64,512]{2,1,0:T(8,128)(2,1)S(1)}, bf16[3,64,512]{2,1,0:T(8,128)(2,1)S(1)}, u32[]{:S(2)}, u32[]{:S(2)}) collective-permute-start(bf16[3,64,512]{2,1,0:T(8,128)(2,1)S(1)} %get-tuple-element.159), channel_id=1, source_target_pairs={{0,4},{4,8},{8,12},{12,0},{1,5},{5,9},{9,13},{13,1},{2,6},{6,10},{... | collective-permute-start | bytes 589832 | tf_op jit(solution)/shard_map/ppermute | solution.py:448
  60.1 14.6 %collective-permute-start.13 = (bf16[3,64,512]{2,1,0:T(8,128)(2,1)S(1)}, bf16[3,64,512]{2,1,0:T(8,128)(2,1)S(1)}, u32[]{:S(2)}, u32[]{:S(2)}) collective-permute-start(bf16[3,64,512]{2,1,0:T(8,128)(2,1)S(1)} %get-tuple-element.160), channel_id=1, source_target_pairs={{0,8},{4,12},{8,0},{12,4},{1,9},{5,13},{9,1},{13,5},{2,10},{6,14},... | collective-permute-start | bytes 589832 | tf_op jit(solution)/shard_map/ppermute | solution.py:448
  60.4 16.8 %collective-permute-start.14 = (bf16[3,64,512]{2,1,0:T(8,128)(2,1)S(1)}, bf16[3,64,512]{2,1,0:T(8,128)(2,1)S(1)}, u32[]{:S(2)}, u32[]{:S(2)}) collective-permute-start(bf16[3,64,512]{2,1,0:T(8,128)(2,1)S(1)} %get-tuple-element.161), channel_id=1, source_target_pairs={{0,12},{4,0},{8,4},{12,8},{1,13},{5,1},{9,5},{13,9},{2,14},{6,2},{... | collective-permute-start | bytes 589832 | tf_op jit(solution)/shard_map/ppermute | solution.py:448
  78.0 12.0 %collective-permute-start.17 = (bf16[2,64,512]{2,1,0:T(8,128)(2,1)S(1)}, bf16[2,64,512]{2,1,0:T(8,128)(2,1)S(1)}, u32[]{:S(2)}, u32[]{:S(2)}) collective-permute-start(bf16[2,64,512]{2,1,0:T(8,128)(2,1)S(1)} %get-tuple-element.162.rest_0_), channel_id=1, source_target_pairs={{0,12},{4,0},{8,4},{12,8},{1,13},{5,1},{9,5},{13,9},{2,14},{6,2},{... | collective-permute-start | bytes 393224 | tf_op jit(solution)/shard_map/ppermute | solution.py:448
  80.5 11.4 %collective-permute-start.16 = (bf16[2,64,512]{2,1,0:T(8,128)(2,1)S(1)}, bf16[2,64,512]{2,1,0:T(8,128)(2,1)S(1)}, u32[]{:S(2)}, u32[]{:S(2)}) collective-permute-start(bf16[2,64,512]{2,1,0:T(8,128)(2,1)S(1)} %get-tuple-element.162.rest_0_), channel_id=1, source_target_pairs={{0,8},{4,12},{8,0},{12,4},{1,9},{5,13},{9,1},{13,5},{2,10},{6,14},... | collective-permute-start | bytes 393224 | tf_op jit(solution)/shard_map/ppermute | solution.py:448
  83.0 10.5 %collective-permute-start.15 = (bf16[2,64,512]{2,1,0:T(8,128)(2,1)S(1)}, bf16[2,64,512]{2,1,0:T(8,128)(2,1)S(1)}, u32[]{:S(2)}, u32[]{:S(2)}) collective-permute-start(bf16[2,64,512]{2,1,0:T(8,128)(2,1)S(1)} %get-tuple-element.162.rest_0_), channel_id=1, source_target_pairs={{0,4},{4,8},{8,12},{12,0},{1,5},{5,9},{9,13},{13,1},{2,6},{6,10},{... | collective-permute-start | bytes 393224 | tf_op jit(solution)/shard_map/ppermute | solution.py:448
  83.0 10.6 %collective-permute-start.18 = (bf16[2,64,512]{2,1,0:T(8,128)(2,1)S(1)}, bf16[2,64,512]{2,1,0:T(8,128)(2,1)S(1)}, u32[]{:S(2)}, u32[]{:S(2)}) collective-permute-start(bf16[2,64,512]{2,1,0:T(8,128)(2,1)S(1)} %get-tuple-element.162.rest_0_), channel_id=1, source_target_pairs={{0,1},{1,0},{2,3},{3,2},{4,5},{5,4},{6,7},{7,6},{8,9},{9,8},{10,11... | collective-permute-start | bytes 393224 | tf_op jit(solution)/shard_map/ppermute | solution.py:445
  90.0 6.0 %collective-permute-start.21 = (bf16[2,64,512]{2,1,0:T(8,128)(2,1)S(1)}, bf16[2,64,512]{2,1,0:T(8,128)(2,1)S(1)}, u32[]{:S(2)}, u32[]{:S(2)}) collective-permute-start(bf16[2,64,512]{2,1,0:T(8,128)(2,1)S(1)} %collective-permute-done.17.rest_3_), channel_id=1, source_target_pairs={{0,1},{1,0},{2,3},{3,2},{4,5},{5,4},{6,7},{7,6},{8,9},{9,8},{10,11... | collective-permute-start | bytes 393224 | tf_op jit(solution)/shard_map/ppermute | solution.py:445
  91.9 5.9 %collective-permute-start.20 = (bf16[2,64,512]{2,1,0:T(8,128)(2,1)S(1)}, bf16[2,64,512]{2,1,0:T(8,128)(2,1)S(1)}, u32[]{:S(2)}, u32[]{:S(2)}) collective-permute-start(bf16[2,64,512]{2,1,0:T(8,128)(2,1)S(1)} %collective-permute-done.16.rest_2_), channel_id=1, source_target_pairs={{0,1},{1,0},{2,3},{3,2},{4,5},{5,4},{6,7},{7,6},{8,9},{9,8},{10,11... | collective-permute-start | bytes 393224 | tf_op jit(solution)/shard_map/ppermute | solution.py:445
  93.5 4.3 %collective-permute-start.19 = (bf16[2,64,512]{2,1,0:T(8,128)(2,1)S(1)}, bf16[2,64,512]{2,1,0:T(8,128)(2,1)S(1)}, u32[]{:S(2)}, u32[]{:S(2)}) collective-permute-start(bf16[2,64,512]{2,1,0:T(8,128)(2,1)S(1)} %collective-permute-done.15.rest_1_), channel_id=1, source_target_pairs={{0,1},{1,0},{2,3},{3,2},{4,5},{5,4},{6,7},{7,6},{8,9},{9,8},{10,11... | collective-permute-start | bytes 393224 | tf_op jit(solution)/shard_map/ppermute | solution.py:445
  93.5 6.2 %collective-permute-start.24 = (bf16[1,64,512]{2,1,0:T(8,128)(2,1)S(1)}, bf16[1,64,512]{2,1,0:T(8,128)(2,1)S(1)}, u32[]{:S(2)}, u32[]{:S(2)}) collective-permute-start(bf16[1,64,512]{2,1,0:T(8,128)(2,1)S(1)} %get-tuple-element.165.rest_0_), channel_id=1, source_target_pairs={{0,12},{4,0},{8,4},{12,8},{1,13},{5,1},{9,5},{13,9},{2,14},{6,2},{... | collective-permute-start | bytes 196616 | tf_op jit(solution)/shard_map/ppermute | solution.py:448
  93.5 7.1 %collective-permute-start.23 = (bf16[1,64,512]{2,1,0:T(8,128)(2,1)S(1)}, bf16[1,64,512]{2,1,0:T(8,128)(2,1)S(1)}, u32[]{:S(2)}, u32[]{:S(2)}) collective-permute-start(bf16[1,64,512]{2,1,0:T(8,128)(2,1)S(1)} %get-tuple-element.165.rest_0_), channel_id=1, source_target_pairs={{0,8},{4,12},{8,0},{12,4},{1,9},{5,13},{9,1},{13,5},{2,10},{6,14},... | collective-permute-start | bytes 196616 | tf_op jit(solution)/shard_map/ppermute | solution.py:448
  96.0 6.4 %collective-permute-start.22 = (bf16[1,64,512]{2,1,0:T(8,128)(2,1)S(1)}, bf16[1,64,512]{2,1,0:T(8,128)(2,1)S(1)}, u32[]{:S(2)}, u32[]{:S(2)}) collective-permute-start(bf16[1,64,512]{2,1,0:T(8,128)(2,1)S(1)} %get-tuple-element.165.rest_0_), channel_id=1, source_target_pairs={{0,4},{4,8},{8,12},{12,0},{1,5},{5,9},{9,13},{13,1},{2,6},{6,10},{... | collective-permute-start | bytes 196616 | tf_op jit(solution)/shard_map/ppermute | solution.py:448
  102.5 1.3 collective-permute-start.25
  102.5 1.4 %collective-permute-start.26 = (bf16[1,64,512]{2,1,0:T(8,128)(2,1)S(1)}, bf16[1,64,512]{2,1,0:T(8,128)(2,1)S(1)}, u32[]{:S(2)}, u32[]{:S(2)}) collective-permute-start(bf16[1,64,512]{2,1,0:T(8,128)(2,1)S(1)} %collective-permute-done.22.rest_1_), channel_id=1, source_target_pairs={{0,1},{1,0},{2,3},{3,2},{4,5},{5,4},{6,7},{7,6},{8,9},{9,8},{10,11... | collective-permute-start | bytes 196616 | tf_op jit(solution)/shard_map/ppermute | solution.py:445
  103.0 1.3 collective-permute-start.27
  103.0 1.4 %collective-permute-start.28 = (bf16[1,64,512]{2,1,0:T(8,128)(2,1)S(1)}, bf16[1,64,512]{2,1,0:T(8,128)(2,1)S(1)}, u32[]{:S(2)}, u32[]{:S(2)}) collective-permute-start(bf16[1,64,512]{2,1,0:T(8,128)(2,1)S(1)} %collective-permute-done.24.rest_3_), channel_id=1, source_target_pairs={{0,1},{1,0},{2,3},{3,2},{4,5},{5,4},{6,7},{7,6},{8,9},{9,8},{10,11... | collective-permute-start | bytes 196616 | tf_op jit(solution)/shard_map/ppermute | solution.py:445
  105.4 19.2 %collective-permute-start.29 = (bf16[512,512]{1,0:T(8,128)(2,1)S(1)}, bf16[512,512]{1,0:T(8,128)(2,1)S(1)}, u32[]{:S(2)}, u32[]{:S(2)}) collective-permute-start(bf16[512,512]{1,0:T(8,128)(2,1)S(1)} %get-tuple-element.172), channel_id=1, source_target_pairs={{0,2},{2,0},{1,3},{3,1},{4,6},{6,4},{5,7},{7,5},{8,10},{10,8},{9,1... | collective-permute-start | bytes 1572872 | tf_op jit(solution)/shard_map/ppermute | solution.py:445
  106.0 17.9 %collective-permute-start.32 = (bf16[64,512]{1,0:T(8,128)(2,1)S(1)}, bf16[64,512]{1,0:T(8,128)(2,1)S(1)}, u32[]{:S(2)}, u32[]{:S(2)}) collective-permute-start(bf16[64,512]{1,0:T(8,128)(2,1)S(1)} %get-tuple-element.180), channel_id=1, source_target_pairs={{8,0},{5,1},{2,2},{14,3},{11,4},{4,5},{1,6},{13,7},{10,8},{7,9},{0... | collective-permute-start | bytes 196616 | tf_op jit(solution)/shard_map/ppermute | solution.py:530
  109.4 14.5 %collective-permute-start.31 = (bf16[64,512]{1,0:T(8,128)(2,1)S(1)}, bf16[64,512]{1,0:T(8,128)(2,1)S(1)}, u32[]{:S(2)}, u32[]{:S(2)}) collective-permute-start(bf16[64,512]{1,0:T(8,128)(2,1)S(1)} %get-tuple-element.181), channel_id=1, source_target_pairs={{4,0},{1,1},{13,2},{10,3},{7,4},{0,5},{12,6},{9,7},{6,8},{3,9},{15... | collective-permute-start | bytes 196616 | tf_op jit(solution)/shard_map/ppermute | solution.py:530
  111.4 12.5 %collective-permute-start.30 = (bf16[64,512]{1,0:T(8,128)(2,1)S(1)}, bf16[64,512]{1,0:T(8,128)(2,1)S(1)}, u32[]{:S(2)}, u32[]{:S(2)}) collective-permute-start(bf16[64,512]{1,0:T(8,128)(2,1)S(1)} %get-tuple-element.182), channel_id=1, source_target_pairs={{0,0},{12,1},{9,2},{6,3},{3,4},{15,5},{8,6},{5,7},{2,8},{14,9},{11... | collective-permute-start | bytes 196616 | tf_op jit(solution)/shard_map/ppermute | solution.py:530

commit v5 on v4

--- a/solution.py
+++ b/solution.py
@@ -332,12 +332,12 @@
 
 
 def update_kernel(zs, where, own, *rest):
-    got, olds, (first, last, placed) = rest[:-6], rest[-6:-3], rest[-3:]
+    got, olds, (piece, placed) = rest[:-5], rest[-5:-2], rest[-2:]
     rows = HALF // zs
     at = where[1] * HALF + where[2] * rows
     mine = pl.ds(pl.multiple_of(at, rows), rows)
     number = where[0] * 2 * zs + where[1] * zs + where[2]
-    for kind, out in enumerate((first.at[0], first.at[1], last.at[0])):
+    for kind in range(3):
         grad = own[kind]
         for g in got:
             grad = grad + g[kind].astype(F32)
@@ -347,7 +347,7 @@
             jnp.mean(raised * raised, -1, keepdims=True) + 1e-06
         )
         new = (raised * factor).astype(BF)
-        out[...] = new
+        piece[kind] = new
         placed[lax.rem(kind * 4 * zs + number, 3)] = new
 
 
@@ -369,49 +369,42 @@
                 full[pl.ds(pl.multiple_of(kind * HD + at, rows), rows), :] = some[d][kind]
 
 
-def read_first_kernel(zs, where, *rest):
-    pieces, (q_for, q_own, g_for, g_own, full) = rest[: 2 * zs], rest[2 * zs :]
-    gather(zs, where, pieces, 2, full)
-    for q, g in ((q_for, g_for), (q_own, g_own)):
-        for c in range(2):
-            rows = pl.ds(c * HALF, HALF)
-            qn = rms(q[rows, :])
-            hg = mm_t(qn, full[0:HD, :])
-            hu = mm_t(qn, full[HD : 2 * HD, :])
-            g[rows, :] = (hg * jax.nn.sigmoid(hg) * hu).astype(BF)
-
-
-def read_down_kernel(zs, where, *rest):
-    pieces = rest[: 2 * zs]
-    g_for, att_low, att_up, out, full = rest[2 * zs :]
-    gather(zs, where, pieces, 1, full)
+def read(q, att, full, out):
+    for c in range(2):
+        rows = pl.ds(c * HALF, HALF)
+        qn = rms(q[rows, :])
+        hg = mm_t(qn, full[0:HD, :])
+        hu = mm_t(qn, full[HD : 2 * HD, :])
+        g = (hg * jax.nn.sigmoid(hg) * hu).astype(BF)
+        out[rows, :] = (att(rows).astype(F32) + mm_t(g, full[2 * HD : 3 * HD, :])).astype(BF)
+
+
+def read_foreign_kernel(zs, where, *rest):
+    pieces, (q, att_low, att_up, out, full) = rest[: 2 * zs], rest[2 * zs :]
+    gather(zs, where, pieces, 3, full)
     low = where[0] == 1
-    out[...] = (
-        jnp.where(low, att_low[...], att_up[...]).astype(F32) + mm_t(g_for[...], full[...])
-    ).astype(BF)
-
-
-def read_own_kernel(where, g_own, att_low, att_up, w, out):
+    read(q, lambda rows: jnp.where(low, att_low[rows, :], att_up[rows, :]), full, out)
+
+
+def read_own_kernel(where, q, att_low, att_up, full, out, work, sem):
     low = where[0] == 0
-    out[...] = (
-        jnp.where(low, att_low[...], att_up[...]).astype(F32) + mm_t(g_own[...], w[...])
-    ).astype(BF)
-
-
-def read_own(where, g_own, att_low, att_up, w):
-    whole = pl.BlockSpec((BLK, HD), lambda i, s: (0, 0))
+    read(q, lambda rows: jnp.where(low, att_low[rows, :], att_up[rows, :]), full, work)
+    column = pl.ds(pl.multiple_of(where[0] * HD, HD), HD)
+    copy = pltpu.make_async_copy(work, out.at[:, column], sem)
+    copy.start()
+    copy.wait()
+
+
+def read_own(where, q, att_low, att_up, full):
     return pl.pallas_call(
         read_own_kernel,
-        grid_spec=pltpu.PrefetchScalarGridSpec(
-            num_scalar_prefetch=1,
-            grid=(1,),
-            in_specs=[whole] * 4,
-            out_specs=pl.BlockSpec((BLK, HD), lambda i, s: (0, s[0])),
-        ),
+        in_specs=[SM] + [VM] * 4,
+        out_specs=pl.BlockSpec(memory_space=pl.ANY),
         out_shape=shape((BLK, H * HD)),
+        scratch_shapes=[pltpu.VMEM((BLK, HD), BF), pltpu.SemaphoreType.DMA],
         compiler_params=PARAMS,
         name="read_own",
-    )(where, g_own, att_low, att_up, w)
+    )(where, q, att_low, att_up, full)
 
 
 def place_kernel(where, got, half_filled, out, sem):
@@ -509,33 +502,21 @@
         [pltpu.VMEM(total.shape, F32)],
     )(where, err_low, err_low2, *factors_of(low, low2), wd, before)
     got = [shift(s, d) for d, s in enumerate(sends, 1)]
-    piece_a, piece_b, placed = call(
-        functools.partial(update_kernel, zs),
-        "update",
-        [shape((2, rows, HD)), shape((1, rows, HD)), shape((3, rows, HD))],
+    piece, placed = call(
+        functools.partial(update_kernel, zs), "update", [shape((3, rows, HD))] * 2
     )(where, own_sum, *got, wg, wu, wd)
-
-    def around(piece):
-        return [piece] + [shift(piece, d) for d in range(1, zs)]
-
-    def both(mine):
-        return mine + [swap(p, "core") for p in mine]
-
-    pieces_a = both(around(piece_a))
-    pieces_b = around(piece_b)
-    g_for, g_own = call(
-        functools.partial(read_first_kernel, zs), "read_first", two, [pltpu.VMEM((2 * HD, HD), BF)]
-    )(where, *pieces_a, q_for, q_own)
+    pieces = [piece] + [shift(piece, d) for d in range(1, zs)]
+    pieces += [swap(p, "core") for p in pieces]
+    out_for, full = call(
+        functools.partial(read_foreign_kernel, zs),
+        "read_foreign",
+        [shape((BLK, HD)), shape((3 * HD, HD))],
+    )(where, *pieces, q_for, att_low, att_up)
+    out_got = swap(out_for, "y")
     own_rows = [
         lax.ppermute(placed[slot], ("z", "y", "core"), owners(zs, slot)) for slot in range(3)
     ]
-    g_for, pieces_b = lax.optimization_barrier((g_for, pieces_b))
-    pieces_b = both(pieces_b)
-    out_for, full = call(
-        functools.partial(read_down_kernel, zs), "read_down", [shape((BLK, HD)), shape((HD, HD))]
-    )(where, *pieces_b, g_for, att_low, att_up)
-    out_got = swap(out_for, "y")
-    half_filled = read_own(where, g_own, att_low, att_up, full)
+    half_filled = read_own(where, q_own, att_low, att_up, full)
     half_filled, own_rows = lax.optimization_barrier((half_filled, own_rows))
     return place(where, out_got, half_filled), jnp.concatenate(own_rows, 0)
 

time: 126 us -> 123 us (0.976)
  the two profiles are of different devices: /device:TPU:16 before, /device:TPU:0 now
where the time goes in v5:
time: 123 us; the launch traced here: 121 us
  waiting for transfers between devices  47 us (38%)
  Pallas kernels  36.4 us (30%)
  starting transfers between devices  34.1 us (28%)
  other arithmetic  2.39 us (2%)
    ppermute x8, waiting for transfers between devices, shift(): lax.ppermute(value, 'z', [(i, (i + d) % zs) for i in range(zs) if ring or...  30.2 us
    pallas_call x11, Pallas kernels, run(): pl.pallas_call(kernel, in_specs=[SM] + [VM] * len(args), out_specs=[VM] *...  24.2 us
    ppermute x8, starting transfers between devices, shift(): lax.ppermute(value, 'z', [(i, (i + d) % zs) for i in range(zs) if ring or...  20.5 us
    ppermute x15, waiting for transfers between devices, swap(): return lax.ppermute(value, axis, SWAP)  14.8 us
    ppermute x15, starting transfers between devices, swap(): return lax.ppermute(value, axis, SWAP)  7.23 us
    pallas_call x3, Pallas kernels, pack(): pl.pallas_call(functools.partial(pack_kernel, first, count, own), in_spec...  6.53 us
    ppermute x3, starting transfers between devices, local(): lax.ppermute(placed[slot], ('z', 'y', 'core'), owners(zs, slot))  6.41 us
    pallas_call x1, Pallas kernels, read_own(): pl.pallas_call(read_own_kernel, in_specs=[SM] + [VM] * 4, out_specs=pl.Bl...  2.61 us
  transfers between devices with their start and end apart: 26, of which 14 were waited for; matrix products, arithmetic and copies ran while one was open for 2% of the time, Pallas kernels for 23%

profile of v5, /device:TPU:0, one launch (start us, length us, event | category | flops | bytes accessed | tf_op | source)
XLA Modules:
  0.0 121.3 jit_solution(10748512402123517220)
XLA Ops:
  0.7 2.4 %pack.3 = bf16[256,1024]{1,0:T(8,128)(2,1)} custom-call(s32[3]{0:T(128)S(1)} %pad_add_fusion.where, bf16[512,1024]{1,0:T(8,128)(2,1)} %key.3, bf16[512,1024]{1,0:T(8,128)(2,1)} %value.5), custom_call_target="tpu_custom_call" | custom-call | tf_op jit(solution)/shard_map/pack/pallas_call | solution.py:105
  3.1 3.0 %collective-permute-start = (bf16[256,1024]{1,0:T(8,128)(2,1)}, bf16[256,1024]{1,0:T(8,128)(2,1)S(1)}, u32[]{:S(2)}, u32[]{:S(2)}) collective-permute-start(bf16[256,1024]{1,0:T(8,128)(2,1)} %pack.3), channel_id=1, source_target_pairs={{0,2},{2,0},{1,3},{3,1},{4,6},{6,4},{5,7},{7,5},{8,10},{10,8},{9,1... | collective-permute-start | bytes 1572872 | tf_op jit(solution)/shard_map/ppermute | solution.py:438
  6.1 2.4 %pack.4 = bf16[256,1024]{1,0:T(8,128)(2,1)} custom-call(s32[3]{0:T(128)S(1)} %pad_add_fusion.where, bf16[512,1024]{1,0:T(8,128)(2,1)} %key.3, bf16[512,1024]{1,0:T(8,128)(2,1)} %value.5), custom_call_target="tpu_custom_call" | custom-call | tf_op jit(solution)/shard_map/pack/pallas_call | solution.py:105
  8.6 1.8 %pack.5.own = bf16[512,1024]{1,0:T(8,128)(2,1)S(1)} custom-call(s32[3]{0:T(128)S(1)} %pad_add_fusion.where, bf16[512,1024]{1,0:T(8,128)(2,1)} %key.3, bf16[512,1024]{1,0:T(8,128)(2,1)} %value.5), custom_call_target="tpu_custom_call" | custom-call | tf_op jit(solution)/shard_map/pack/pallas_call | solution.py:105
  10.5 1.6 %pack_q.1 = bf16[528,512]{1,0:T(8,128)(2,1)S(1)} custom-call(s32[3]{0:T(128)S(1)} %pad_add_fusion.where, bf16[512,1024]{1,0:T(8,128)(2,1)} %query, f32[2,512]{1,0:T(2,128)S(1)} %copy-done), custom_call_target="tpu_custom_call" | custom-call | tf_op jit(solution)/shard_map/pack_q/pallas_call | solution.py:74
  12.2 1.5 %slice_select_fusion.2 = (bf16[512,512]{1,0:T(8,128)(2,1)S(1)}, bf16[512,512]{1,0:T(8,128)(2,1)S(1)}) fusion(bf16[1024,512]{1,0:T(8,128)(2,1)} %param.11, pred[]{:T(512)S(6)} %eq.2, bf16[512,1024]{1,0:T(8,128)(2,1)S(1)} %copy-done.1), kind=kLoop, calls=%fused_computation.2 | loop fusion | flops 524288 | bytes 3145729 | tf_op jit(solution)/shard_map/jit(_where)/select_n | solution.py:459
  13.7 0.3 copy-done.3
  14.1 5.0 %collective-permute-done.foreign.rest_0_.for_a = bf16[256,1024]{1,0:T(8,128)(2,1)S(1)} collective-permute-done((bf16[256,1024]{1,0:T(8,128)(2,1)}, bf16[256,1024]{1,0:T(8,128)(2,1)S(1)}, u32[]{:S(2)}, u32[]{:S(2)}) %collective-permute-start) | collective-permute-done | bytes 524320 | tf_op jit(solution)/shard_map/ppermute | solution.py:438
  19.1 0.6 pick.2
  19.8 2.1 %collective-permute-start.6 = (bf16[528,512]{1,0:T(8,128)(2,1)S(1)}, bf16[528,512]{1,0:T(8,128)(2,1)S(1)}, u32[]{:S(2)}, u32[]{:S(2)}) collective-permute-start(bf16[528,512]{1,0:T(8,128)(2,1)S(1)} %pack_q.1), channel_id=1, source_target_pairs={{0,2},{2,0},{1,3},{3,1},{4,6},{6,4},{5,7},{7,5},{8,10},{10,8},{9,1... | collective-permute-start | bytes 1622024 | tf_op jit(solution)/shard_map/ppermute | solution.py:438
  21.9 3.5 %collective-permute-start.5 = (bf16[256,1024]{1,0:T(8,128)(2,1)S(1)}, bf16[256,1024]{1,0:T(8,128)(2,1)S(1)}, u32[]{:S(2)}, u32[]{:S(2)}) collective-permute-start(bf16[256,1024]{1,0:T(8,128)(2,1)S(1)} %pick.2), channel_id=1, source_target_pairs={{0,4},{4,8},{8,12},{1,5},{5,9},{9,13},{2,6},{6,10},{10,14},{3,7},{... | collective-permute-start | bytes 1572872 | tf_op jit(solution)/shard_map/ppermute | solution.py:441
  25.4 3.7 %pre_own.1 = (bf16[512,512]{1,0:T(8,128)(2,1)S(1)}, bf16[512,512]{1,0:T(8,128)(2,1)S(1)}, f32[512,256]{1,0:T(8,128)S(1)}, f32[512,256]{1,0:T(8,128)S(1)}, bf16[5...) custom-call(s32[3]{0:T(128)S(1)} %pad_add_fusion.where, ...), custom_call_target="tpu_custom_call" | custom-call | tf_op jit(solution)/shard_map/pre_own/pallas_call | solution.py:55
  29.1 1.2 collective-permute-done.1.foreign.rest_1_.for_b
  30.3 0.6 pick.3
  31.0 4.1 %collective-permute-start.7 = (bf16[256,1024]{1,0:T(8,128)(2,1)S(1)}, bf16[256,1024]{1,0:T(8,128)(2,1)S(1)}, u32[]{:S(2)}, u32[]{:S(2)}) collective-permute-start(bf16[256,1024]{1,0:T(8,128)(2,1)S(1)} %pick.3), channel_id=1, source_target_pairs={{0,4},{4,8},{8,12},{1,5},{5,9},{9,13},{2,6},{6,10},{10,14},{3,7},{... | collective-permute-start | bytes 1572872 | tf_op jit(solution)/shard_map/ppermute | solution.py:441
  35.1 2.6 %pre.2 = (bf16[512,512]{1,0:T(8,128)(2,1)S(1)}, bf16[512,512]{1,0:T(8,128)(2,1)S(1)}, f32[512,256]{1,0:T(8,128)S(1)}, f32[512,256]{1,0:T(8,128)S(1)}, bf16[512,5...) custom-call(s32[3]{0:T(128)S(1)} %pad_add_fusion.where, ...), custom_call_target="tpu_custom_call" | custom-call | tf_op jit(solution)/shard_map/pre/pallas_call | solution.py:55
  37.7 3.4 %collective-permute-done.6.q_for.rest_8_ = bf16[528,512]{1,0:T(8,128)(2,1)S(1)} collective-permute-done((bf16[528,512]{1,0:T(8,128)(2,1)S(1)}, bf16[528,512]{1,0:T(8,128)(2,1)S(1)}, u32[]{:S(2)}, u32[]{:S(2)}) %collective-permute-start.6) | collective-permute-done | bytes 540704 | tf_op jit(solution)/shard_map/ppermute | solution.py:438
  41.1 2.8 %pre.3 = (bf16[512,512]{1,0:T(8,128)(2,1)S(1)}, bf16[512,512]{1,0:T(8,128)(2,1)S(1)}, f32[512,256]{1,0:T(8,128)S(1)}, f32[512,256]{1,0:T(8,128)S(1)}, bf16[512,5...) custom-call(s32[3]{0:T(128)S(1)} %pad_add_fusion.where, ...), custom_call_target="tpu_custom_call" | custom-call | tf_op jit(solution)/shard_map/pre/pallas_call | solution.py:55
  43.9 3.3 %attend_upper.1 = (bf16[512,512]{1,0:T(8,128)(2,1)S(1)}, bf16[512,512]{1,0:T(8,128)(2,1)S(1)}, bf16[512,1024]{1,0:T(8,128)(2,1)S(1)}, bf16[512,1024]{1,0:T(8,128)(2,1)S(1)}) custom-call(s32[3]{0:T(128)S(1)} %pad_add_fusion.where, bf16[512,512]{1,0:T(8,128)(2,1)S(1)} %get-tuple-element.85.q_own.q, bf16[528,512]{1,0:T(8,128)(2,1)S(1)} %collective-permute-done.6.q_for.rest_8_, ...), custom_call_target="tpu_custom_call" | custom-call | tf_op jit(solution)/shard_map/attend_upper/pallas_call | solution.py:55
  47.2 0.9 collective-permute-done.7.halo_b
  48.1 0.5 collective-permute-start.9
  48.6 1.4 %collective-permute-done.8.halo2_a = bf16[256,1024]{1,0:T(8,128)(2,1)S(1)} collective-permute-done((bf16[256,1024]{1,0:T(8,128)(2,1)S(1)}, bf16[256,1024]{1,0:T(8,128)(2,1)S(1)}, u32[]{:S(2)}, u32[]{:S(2)}) %collective-permute-start.8) | collective-permute-done | bytes 524320 | tf_op jit(solution)/shard_map/ppermute | solution.py:438
  50.0 0.7 collective-permute-done.9.halo2_b
  50.8 3.2 %attend_lower.1 = (bf16[512,512]{1,0:T(8,128)(2,1)S(1)}, bf16[512,512]{1,0:T(8,128)(2,1)S(1)}) custom-call(s32[3]{0:T(128)S(1)} %pad_add_fusion.where, bf16[512,512]{1,0:T(8,128)(2,1)S(1)} %get-tuple-element.85.q_own.q, bf16[528,512]{1,0:T(8,128)(2,1)S(1)} %collective-permute-done.6.q_for.rest_8_, f32[2,512]{1,0:T(2,128)S(1)} %copy-done, ...), custom_call_target="tpu_custom_call" | custom-call | tf_op jit(solution)/shard_map/attend_lower/pallas_call | solution.py:55
  54.2 2.3 %grad_first.1.before = f32[3,256,512]{2,1,0:T(8,128)S(1)} custom-call(s32[3]{0:T(128)S(1)} %pad_add_fusion.where, bf16[512,512]{1,0:T(8,128)(2,1)S(1)} %get-tuple-element.141.e0, bf16[512,512]{1,0:T(8,128)(2,1)S(1)} %collective-permute-done.11.e1, bf16[512,512]{1,0:T(8,128)(2,1)S(1)} %get-tuple-element.142.k0, bf16[512,512]{1,0:T(8,128)(2,1)S(1)} %get-tuple-element.143.k1, ...), custom_call_target="tpu_custom_call" | custom-call | tf_op jit(solution)/shard_map/grad_first/pallas_call | solution.py:55
  56.5 2.5 %grad_second.1 = (f32[3,64,512]{2,1,0:T(8,128)S(1)}, bf16[3,64,512]{2,1,0:T(8,128)(2,1)S(1)}, bf16[3,64,512]{2,1,0:T(8,128)(2,1)S(1)}, bf16[3,64,512]{2,1,0:T(8,128)(2,1)S(1)}) custom-call(s32[3]{0:T(128)S(1)} %pad_add_fusion.where, bf16[512,512]{1,0:T(8,128)(2,1)S(1)} %get-tuple-element.131.e0, bf16[512,512]{1,0:T(8,128)(2,1)S(1)} %collective-permute-done.10.e1, ...), custom_call_target="tpu_custom_call" | custom-call | tf_op jit(solution)/shard_map/grad_second/pallas_call | solution.py:55
  59.0 2.6 %collective-permute-start.12 = (bf16[3,64,512]{2,1,0:T(8,128)(2,1)S(1)}, bf16[3,64,512]{2,1,0:T(8,128)(2,1)S(1)}, u32[]{:S(2)}, u32[]{:S(2)}) collective-permute-start(bf16[3,64,512]{2,1,0:T(8,128)(2,1)S(1)} %get-tuple-element.151), channel_id=1, source_target_pairs={{0,4},{4,8},{8,12},{12,0},{1,5},{5,9},{9,13},{13,1},{2,6},{6,10},{... | collective-permute-start | bytes 589832 | tf_op jit(solution)/shard_map/ppermute | solution.py:441
  61.5 2.6 %collective-permute-start.13 = (bf16[3,64,512]{2,1,0:T(8,128)(2,1)S(1)}, bf16[3,64,512]{2,1,0:T(8,128)(2,1)S(1)}, u32[]{:S(2)}, u32[]{:S(2)}) collective-permute-start(bf16[3,64,512]{2,1,0:T(8,128)(2,1)S(1)} %get-tuple-element.152), channel_id=1, source_target_pairs={{0,8},{4,12},{8,0},{12,4},{1,9},{5,13},{9,1},{13,5},{2,10},{6,14},... | collective-permute-start | bytes 589832 | tf_op jit(solution)/shard_map/ppermute | solution.py:441
  64.1 1.3 %collective-permute-start.14 = (bf16[3,64,512]{2,1,0:T(8,128)(2,1)S(1)}, bf16[3,64,512]{2,1,0:T(8,128)(2,1)S(1)}, u32[]{:S(2)}, u32[]{:S(2)}) collective-permute-start(bf16[3,64,512]{2,1,0:T(8,128)(2,1)S(1)} %get-tuple-element.153), channel_id=1, source_target_pairs={{0,12},{4,0},{8,4},{12,8},{1,13},{5,1},{9,5},{13,9},{2,14},{6,2},{... | collective-permute-start | bytes 589832 | tf_op jit(solution)/shard_map/ppermute | solution.py:441
  65.5 4.0 %collective-permute-done.12.rest_0_ = bf16[3,64,512]{2,1,0:T(8,128)(2,1)S(1)} collective-permute-done((bf16[3,64,512]{2,1,0:T(8,128)(2,1)S(1)}, bf16[3,64,512]{2,1,0:T(8,128)(2,1)S(1)}, u32[]{:S(2)}, u32[]{:S(2)}) %collective-permute-start.12) | collective-permute-done | bytes 196640 | tf_op jit(solution)/shard_map/ppermute | solution.py:441
  69.4 8.1 %collective-permute-done.13.rest_1_ = bf16[3,64,512]{2,1,0:T(8,128)(2,1)S(1)} collective-permute-done((bf16[3,64,512]{2,1,0:T(8,128)(2,1)S(1)}, bf16[3,64,512]{2,1,0:T(8,128)(2,1)S(1)}, u32[]{:S(2)}, u32[]{:S(2)}) %collective-permute-start.13) | collective-permute-done | bytes 196640 | tf_op jit(solution)/shard_map/ppermute | solution.py:441
  77.5 0.8 update.1
  78.3 5.8 %collective-permute-start.17 = (bf16[3,64,512]{2,1,0:T(8,128)(2,1)S(1)}, bf16[3,64,512]{2,1,0:T(8,128)(2,1)S(1)}, u32[]{:S(2)}, u32[]{:S(2)}) collective-permute-start(bf16[3,64,512]{2,1,0:T(8,128)(2,1)S(1)} %get-tuple-element.154.rest_0_), channel_id=1, source_target_pairs={{0,12},{4,0},{8,4},{12,8},{1,13},{5,1},{9,5},{13,9},{2,14},{6,2},{... | collective-permute-start | bytes 589832 | tf_op jit(solution)/shard_map/ppermute | solution.py:441
  84.1 0.4 collective-permute-start.16
  84.7 4.7 %collective-permute-done.17.rest_3_ = bf16[3,64,512]{2,1,0:T(8,128)(2,1)S(1)} collective-permute-done((bf16[3,64,512]{2,1,0:T(8,128)(2,1)S(1)}, bf16[3,64,512]{2,1,0:T(8,128)(2,1)S(1)}, u32[]{:S(2)}, u32[]{:S(2)}) %collective-permute-start.17) | collective-permute-done | bytes 196640 | tf_op jit(solution)/shard_map/ppermute | solution.py:441
  89.5 12.5 %collective-permute-done.16.rest_2_ = bf16[3,64,512]{2,1,0:T(8,128)(2,1)S(1)} collective-permute-done((bf16[3,64,512]{2,1,0:T(8,128)(2,1)S(1)}, bf16[3,64,512]{2,1,0:T(8,128)(2,1)S(1)}, u32[]{:S(2)}, u32[]{:S(2)}) %collective-permute-start.16) | collective-permute-done | bytes 196640 | tf_op jit(solution)/shard_map/ppermute | solution.py:441
  102.0 0.5 collective-permute-start.19
  102.5 0.9 collective-permute-done.20.rest_6_
  103.7 1.9 %read_foreign.1 = (bf16[512,512]{1,0:T(8,128)(2,1)S(1)}, bf16[1536,512]{1,0:T(8,128)(2,1)S(1)}) custom-call(s32[3]{0:T(128)S(1)} %pad_add_fusion.where, bf16[3,64,512]{2,1,0:T(8,128)(2,1)S(1)} %get-tuple-element.154.rest_0_, bf16[3,64,512]{2,1,0:T(8,128)(2,1)S(1)} %collective-permute-done.15.rest_1_, ...), custom_call_target="tpu_custom_call" | custom-call | tf_op jit(solution)/shard_map/read_foreign/pallas_call | solution.py:55
  105.6 0.6 collective-permute-start.22
  106.2 3.8 %collective-permute-start.25 = (bf16[64,512]{1,0:T(8,128)(2,1)S(1)}, bf16[64,512]{1,0:T(8,128)(2,1)S(1)}, u32[]{:S(2)}, u32[]{:S(2)}) collective-permute-start(bf16[64,512]{1,0:T(8,128)(2,1)S(1)} %get-tuple-element.164), channel_id=1, source_target_pairs={{8,0},{5,1},{2,2},{14,3},{11,4},{4,5},{1,6},{13,7},{10,8},{7,9},{0... | collective-permute-start | bytes 196616 | tf_op jit(solution)/shard_map/ppermute | solution.py:517
  110.0 1.9 %collective-permute-start.24 = (bf16[64,512]{1,0:T(8,128)(2,1)S(1)}, bf16[64,512]{1,0:T(8,128)(2,1)S(1)}, u32[]{:S(2)}, u32[]{:S(2)}) collective-permute-start(bf16[64,512]{1,0:T(8,128)(2,1)S(1)} %get-tuple-element.165), channel_id=1, source_target_pairs={{4,0},{1,1},{13,2},{10,3},{7,4},{0,5},{12,6},{9,7},{6,8},{3,9},{15... | collective-permute-start | bytes 196616 | tf_op jit(solution)/shard_map/ppermute | solution.py:517
  112.0 0.7 collective-permute-start.23
  112.6 2.6 %read_own.1.half_filled = bf16[512,1024]{1,0:T(8,128)(2,1)} custom-call(s32[3]{0:T(128)S(1)} %pad_add_fusion.where, bf16[512,512]{1,0:T(8,128)(2,1)S(1)} %get-tuple-element.85.q_own.q, bf16[512,512]{1,0:T(8,128)(2,1)S(1)} %get-tuple-element.155.rest_9_.att_low, bf16[512,512]{1,0:T(8,128)(2,1)S(1)} %get-tuple-element.156.rest_10_.att_up, ...), custom_call_target="tpu_custom_call" | custom-call | tf_op jit(solution)/shard_map/read_own/pallas_call | solution.py:399
  115.3 1.9 %collective-permute-done.24 = bf16[64,512]{1,0:T(8,128)(2,1)S(1)} collective-permute-done((bf16[64,512]{1,0:T(8,128)(2,1)S(1)}, bf16[64,512]{1,0:T(8,128)(2,1)S(1)}, u32[]{:S(2)}, u32[]{:S(2)}) %collective-permute-start.24) | collective-permute-done | bytes 65568 | tf_op jit(solution)/shard_map/ppermute | solution.py:517
  117.2 0.7 pad_maximum_fusion
  117.9 1.9 %collective-permute-done.22.got = bf16[512,512]{1,0:T(8,128)(2,1)S(1)} collective-permute-done((bf16[512,512]{1,0:T(8,128)(2,1)S(1)}, bf16[512,512]{1,0:T(8,128)(2,1)S(1)}, u32[]{:S(2)}, u32[]{:S(2)}) %collective-permute-start.22) | collective-permute-done | bytes 524320 | tf_op jit(solution)/shard_map/ppermute | solution.py:438
  119.8 1.3 %place.1 = bf16[512,1024]{1,0:T(8,128)(2,1)} custom-call(s32[3]{0:T(128)S(1)} %pad_add_fusion.where, bf16[512,512]{1,0:T(8,128)(2,1)S(1)} %collective-permute-done.22.got, bf16[512,1024]{1,0:T(8,128)(2,1)} %read_own.1.half_filled), custom_call_target="tpu_custom_call", output_to_operand_aliasing={{}: (2, {})} | custom-call | tf_op jit(solution)/shard_map/place/pallas_call | solution.py:419
  (34 shorter events, 1.2 us)
Async XLA Ops:
  3.1 16.0 %collective-permute-start = (bf16[256,1024]{1,0:T(8,128)(2,1)}, bf16[256,1024]{1,0:T(8,128)(2,1)S(1)}, u32[]{:S(2)}, u32[]{:S(2)}) collective-permute-start(bf16[256,1024]{1,0:T(8,128)(2,1)} %pack.3), channel_id=1, source_target_pairs={{0,2},{2,0},{1,3},{3,1},{4,6},{6,4},{5,7},{7,5},{8,10},{10,8},{9,1... | collective-permute-start | bytes 1572872 | tf_op jit(solution)/shard_map/ppermute | solution.py:438
  8.5 1.9 %copy-start = (f32[2,512]{1,0:T(2,128)S(1)}, f32[2,512]{1,0:T(2,128)}, u32[]{:S(2)}) copy-start(f32[2,512]{1,0:T(2,128)} %rates.5) | copy-start | bytes 12292
  8.5 21.8 %collective-permute-start.1 = (bf16[256,1024]{1,0:T(8,128)(2,1)}, bf16[256,1024]{1,0:T(8,128)(2,1)S(1)}, u32[]{:S(2)}, u32[]{:S(2)}) collective-permute-start(bf16[256,1024]{1,0:T(8,128)(2,1)} %pack.4), channel_id=1, source_target_pairs={{0,2},{2,0},{1,3},{3,1},{4,6},{6,4},{5,7},{7,5},{8,10},{10,8},{9,1... | collective-permute-start | bytes 1572872 | tf_op jit(solution)/shard_map/ppermute | solution.py:438
  10.4 15.0 %collective-permute-start.2 = (bf16[512,1024]{1,0:T(8,128)(2,1)S(1)}, bf16[512,1024]{1,0:T(8,128)(2,1)S(1)}, u32[]{:S(2)}, u32[]{:S(2)}) collective-permute-start(bf16[512,1024]{1,0:T(8,128)(2,1)S(1)} %pack.5.own), channel_id=1, source_target_pairs={{0,1},{1,0},{2,3},{3,2},{4,5},{5,4},{6,7},{7,6},{8,9},{9,8},{10,11... | collective-permute-start | bytes 3145736 | tf_op jit(solution)/shard_map/ppermute | solution.py:438
  10.5 1.7 %copy-start.1 = (bf16[512,1024]{1,0:T(8,128)(2,1)S(1)}, bf16[512,1024]{1,0:T(8,128)(2,1)}, u32[]{:S(2)}) copy-start(bf16[512,1024]{1,0:T(8,128)(2,1)} %query) | copy-start | bytes 3145732
  12.2 1.5 %copy-start.2 = (bf16[1024,512]{1,0:T(8,128)(2,1)S(1)}, bf16[1024,512]{1,0:T(8,128)(2,1)}, u32[]{:S(2)}) copy-start(bf16[1024,512]{1,0:T(8,128)(2,1)} %param.13) | copy-start | bytes 3145732
  12.2 1.8 %copy-start.3 = (bf16[1024,512]{1,0:T(8,128)(2,1)S(1)}, bf16[1024,512]{1,0:T(8,128)(2,1)}, u32[]{:S(2)}) copy-start(bf16[1024,512]{1,0:T(8,128)(2,1)} %param.12) | copy-start | bytes 3145732
  19.7 10.6 %collective-permute-start.3 = (bf16[256,1024]{1,0:T(8,128)(2,1)S(1)}, bf16[256,1024]{1,0:T(8,128)(2,1)S(1)}, u32[]{:S(2)}, u32[]{:S(2)}) collective-permute-start(bf16[256,1024]{1,0:T(8,128)(2,1)S(1)} %collective-permute-done.foreign.rest_0_.for_a), channel_id=1, source_target_pairs={{0,1},{1,0},{2,3},{3,2},{4,5},{5,4},{6,7},{7,6},{8,9},{9,8},{10,11... | collective-permute-start | bytes 1572872 | tf_op jit(solution)/shard_map/ppermute | solution.py:438
  19.8 21.3 %collective-permute-start.6 = (bf16[528,512]{1,0:T(8,128)(2,1)S(1)}, bf16[528,512]{1,0:T(8,128)(2,1)S(1)}, u32[]{:S(2)}, u32[]{:S(2)}) collective-permute-start(bf16[528,512]{1,0:T(8,128)(2,1)S(1)} %pack_q.1), channel_id=1, source_target_pairs={{0,2},{2,0},{1,3},{3,1},{4,6},{6,4},{5,7},{7,5},{8,10},{10,8},{9,1... | collective-permute-start | bytes 1622024 | tf_op jit(solution)/shard_map/ppermute | solution.py:438
  21.9 15.8 %collective-permute-start.5 = (bf16[256,1024]{1,0:T(8,128)(2,1)S(1)}, bf16[256,1024]{1,0:T(8,128)(2,1)S(1)}, u32[]{:S(2)}, u32[]{:S(2)}) collective-permute-start(bf16[256,1024]{1,0:T(8,128)(2,1)S(1)} %pick.2), channel_id=1, source_target_pairs={{0,4},{4,8},{8,12},{1,5},{5,9},{9,13},{2,6},{6,10},{10,14},{3,7},{... | collective-permute-start | bytes 1572872 | tf_op jit(solution)/shard_map/ppermute | solution.py:441
  30.9 6.7 %collective-permute-start.4 = (bf16[256,1024]{1,0:T(8,128)(2,1)S(1)}, bf16[256,1024]{1,0:T(8,128)(2,1)S(1)}, u32[]{:S(2)}, u32[]{:S(2)}) collective-permute-start(bf16[256,1024]{1,0:T(8,128)(2,1)S(1)} %collective-permute-done.1.foreign.rest_1_.for_b), channel_id=1, source_target_pairs={{0,1},{1,0},{2,3},{3,2},{4,5},{5,4},{6,7},{7,6},{8,9},{9,8},{10,11... | collective-permute-start | bytes 1572872 | tf_op jit(solution)/shard_map/ppermute | solution.py:438
  31.0 17.1 %collective-permute-start.7 = (bf16[256,1024]{1,0:T(8,128)(2,1)S(1)}, bf16[256,1024]{1,0:T(8,128)(2,1)S(1)}, u32[]{:S(2)}, u32[]{:S(2)}) collective-permute-start(bf16[256,1024]{1,0:T(8,128)(2,1)S(1)} %pick.3), channel_id=1, source_target_pairs={{0,4},{4,8},{8,12},{1,5},{5,9},{9,13},{2,6},{6,10},{10,14},{3,7},{... | collective-permute-start | bytes 1572872 | tf_op jit(solution)/shard_map/ppermute | solution.py:441
  48.1 1.9 %collective-permute-start.8 = (bf16[256,1024]{1,0:T(8,128)(2,1)S(1)}, bf16[256,1024]{1,0:T(8,128)(2,1)S(1)}, u32[]{:S(2)}, u32[]{:S(2)}) collective-permute-start(bf16[256,1024]{1,0:T(8,128)(2,1)S(1)} %collective-permute-done.5.halo_a), channel_id=1, source_target_pairs={{0,1},{1,0},{2,3},{3,2},{4,5},{5,4},{6,7},{7,6},{8,9},{9,8},{10,11... | collective-permute-start | bytes 1572872 | tf_op jit(solution)/shard_map/ppermute | solution.py:438
  48.1 2.7 %collective-permute-start.9 = (bf16[256,1024]{1,0:T(8,128)(2,1)S(1)}, bf16[256,1024]{1,0:T(8,128)(2,1)S(1)}, u32[]{:S(2)}, u32[]{:S(2)}) collective-permute-start(bf16[256,1024]{1,0:T(8,128)(2,1)S(1)} %collective-permute-done.7.halo_b), channel_id=1, source_target_pairs={{0,1},{1,0},{2,3},{3,2},{4,5},{5,4},{6,7},{7,6},{8,9},{9,8},{10,11... | collective-permute-start | bytes 1572872 | tf_op jit(solution)/shard_map/ppermute | solution.py:438
  48.6 5.6 %collective-permute-start.11 = (bf16[512,512]{1,0:T(8,128)(2,1)S(1)}, bf16[512,512]{1,0:T(8,128)(2,1)S(1)}, u32[]{:S(2)}, u32[]{:S(2)}) collective-permute-start(bf16[512,512]{1,0:T(8,128)(2,1)S(1)} %get-tuple-element.141.e0), channel_id=1, source_target_pairs={{0,1},{1,0},{2,3},{3,2},{4,5},{5,4},{6,7},{7,6},{8,9},{9,8},{10,11... | collective-permute-start | bytes 1572872 | tf_op jit(solution)/shard_map/ppermute | solution.py:438
  54.0 2.5 %collective-permute-start.10 = (bf16[512,512]{1,0:T(8,128)(2,1)S(1)}, bf16[512,512]{1,0:T(8,128)(2,1)S(1)}, u32[]{:S(2)}, u32[]{:S(2)}) collective-permute-start(bf16[512,512]{1,0:T(8,128)(2,1)S(1)} %get-tuple-element.131.e0), channel_id=1, source_target_pairs={{0,1},{1,0},{2,3},{3,2},{4,5},{5,4},{6,7},{7,6},{8,9},{9,8},{10,11... | collective-permute-start | bytes 1572872 | tf_op jit(solution)/shard_map/ppermute | solution.py:438
  59.0 10.5 %collective-permute-start.12 = (bf16[3,64,512]{2,1,0:T(8,128)(2,1)S(1)}, bf16[3,64,512]{2,1,0:T(8,128)(2,1)S(1)}, u32[]{:S(2)}, u32[]{:S(2)}) collective-permute-start(bf16[3,64,512]{2,1,0:T(8,128)(2,1)S(1)} %get-tuple-element.151), channel_id=1, source_target_pairs={{0,4},{4,8},{8,12},{12,0},{1,5},{5,9},{9,13},{13,1},{2,6},{6,10},{... | collective-permute-start | bytes 589832 | tf_op jit(solution)/shard_map/ppermute | solution.py:441
  61.5 16.0 %collective-permute-start.13 = (bf16[3,64,512]{2,1,0:T(8,128)(2,1)S(1)}, bf16[3,64,512]{2,1,0:T(8,128)(2,1)S(1)}, u32[]{:S(2)}, u32[]{:S(2)}) collective-permute-start(bf16[3,64,512]{2,1,0:T(8,128)(2,1)S(1)} %get-tuple-element.152), channel_id=1, source_target_pairs={{0,8},{4,12},{8,0},{12,4},{1,9},{5,13},{9,1},{13,5},{2,10},{6,14},... | collective-permute-start | bytes 589832 | tf_op jit(solution)/shard_map/ppermute | solution.py:441
  64.1 13.4 %collective-permute-start.14 = (bf16[3,64,512]{2,1,0:T(8,128)(2,1)S(1)}, bf16[3,64,512]{2,1,0:T(8,128)(2,1)S(1)}, u32[]{:S(2)}, u32[]{:S(2)}) collective-permute-start(bf16[3,64,512]{2,1,0:T(8,128)(2,1)S(1)} %get-tuple-element.153), channel_id=1, source_target_pairs={{0,12},{4,0},{8,4},{12,8},{1,13},{5,1},{9,5},{13,9},{2,14},{6,2},{... | collective-permute-start | bytes 589832 | tf_op jit(solution)/shard_map/ppermute | solution.py:441
  78.3 11.2 %collective-permute-start.17 = (bf16[3,64,512]{2,1,0:T(8,128)(2,1)S(1)}, bf16[3,64,512]{2,1,0:T(8,128)(2,1)S(1)}, u32[]{:S(2)}, u32[]{:S(2)}) collective-permute-start(bf16[3,64,512]{2,1,0:T(8,128)(2,1)S(1)} %get-tuple-element.154.rest_0_), channel_id=1, source_target_pairs={{0,12},{4,0},{8,4},{12,8},{1,13},{5,1},{9,5},{13,9},{2,14},{6,2},{... | collective-permute-start | bytes 589832 | tf_op jit(solution)/shard_map/ppermute | solution.py:441
  84.1 17.9 %collective-permute-start.16 = (bf16[3,64,512]{2,1,0:T(8,128)(2,1)S(1)}, bf16[3,64,512]{2,1,0:T(8,128)(2,1)S(1)}, u32[]{:S(2)}, u32[]{:S(2)}) collective-permute-start(bf16[3,64,512]{2,1,0:T(8,128)(2,1)S(1)} %get-tuple-element.154.rest_0_), channel_id=1, source_target_pairs={{0,8},{4,12},{8,0},{12,4},{1,9},{5,13},{9,1},{13,5},{2,10},{6,14},... | collective-permute-start | bytes 589832 | tf_op jit(solution)/shard_map/ppermute | solution.py:441
  84.5 17.5 %collective-permute-start.15 = (bf16[3,64,512]{2,1,0:T(8,128)(2,1)S(1)}, bf16[3,64,512]{2,1,0:T(8,128)(2,1)S(1)}, u32[]{:S(2)}, u32[]{:S(2)}) collective-permute-start(bf16[3,64,512]{2,1,0:T(8,128)(2,1)S(1)} %get-tuple-element.154.rest_0_), channel_id=1, source_target_pairs={{0,4},{4,8},{8,12},{12,0},{1,5},{5,9},{9,13},{13,1},{2,6},{6,10},{... | collective-permute-start | bytes 589832 | tf_op jit(solution)/shard_map/ppermute | solution.py:441
  84.7 17.8 %collective-permute-start.18 = (bf16[3,64,512]{2,1,0:T(8,128)(2,1)S(1)}, bf16[3,64,512]{2,1,0:T(8,128)(2,1)S(1)}, u32[]{:S(2)}, u32[]{:S(2)}) collective-permute-start(bf16[3,64,512]{2,1,0:T(8,128)(2,1)S(1)} %get-tuple-element.154.rest_0_), channel_id=1, source_target_pairs={{0,1},{1,0},{2,3},{3,2},{4,5},{5,4},{6,7},{7,6},{8,9},{9,8},{10,11... | collective-permute-start | bytes 589832 | tf_op jit(solution)/shard_map/ppermute | solution.py:438
  89.5 13.0 %collective-permute-start.21 = (bf16[3,64,512]{2,1,0:T(8,128)(2,1)S(1)}, bf16[3,64,512]{2,1,0:T(8,128)(2,1)S(1)}, u32[]{:S(2)}, u32[]{:S(2)}) collective-permute-start(bf16[3,64,512]{2,1,0:T(8,128)(2,1)S(1)} %collective-permute-done.17.rest_3_), channel_id=1, source_target_pairs={{0,1},{1,0},{2,3},{3,2},{4,5},{5,4},{6,7},{7,6},{8,9},{9,8},{10,11... | collective-permute-start | bytes 589832 | tf_op jit(solution)/shard_map/ppermute | solution.py:438
  102.0 1.4 %collective-permute-start.20 = (bf16[3,64,512]{2,1,0:T(8,128)(2,1)S(1)}, bf16[3,64,512]{2,1,0:T(8,128)(2,1)S(1)}, u32[]{:S(2)}, u32[]{:S(2)}) collective-permute-start(bf16[3,64,512]{2,1,0:T(8,128)(2,1)S(1)} %collective-permute-done.16.rest_2_), channel_id=1, source_target_pairs={{0,1},{1,0},{2,3},{3,2},{4,5},{5,4},{6,7},{7,6},{8,9},{9,8},{10,11... | collective-permute-start | bytes 589832 | tf_op jit(solution)/shard_map/ppermute | solution.py:438
  102.0 1.7 %collective-permute-start.19 = (bf16[3,64,512]{2,1,0:T(8,128)(2,1)S(1)}, bf16[3,64,512]{2,1,0:T(8,128)(2,1)S(1)}, u32[]{:S(2)}, u32[]{:S(2)}) collective-permute-start(bf16[3,64,512]{2,1,0:T(8,128)(2,1)S(1)} %collective-permute-done.15.rest_1_), channel_id=1, source_target_pairs={{0,1},{1,0},{2,3},{3,2},{4,5},{5,4},{6,7},{7,6},{8,9},{9,8},{10,11... | collective-permute-start | bytes 589832 | tf_op jit(solution)/shard_map/ppermute | solution.py:438
  105.6 14.1 %collective-permute-start.22 = (bf16[512,512]{1,0:T(8,128)(2,1)S(1)}, bf16[512,512]{1,0:T(8,128)(2,1)S(1)}, u32[]{:S(2)}, u32[]{:S(2)}) collective-permute-start(bf16[512,512]{1,0:T(8,128)(2,1)S(1)} %get-tuple-element.157), channel_id=1, source_target_pairs={{0,2},{2,0},{1,3},{3,1},{4,6},{6,4},{5,7},{7,5},{8,10},{10,8},{9,1... | collective-permute-start | bytes 1572872 | tf_op jit(solution)/shard_map/ppermute | solution.py:438
  106.2 9.1 %collective-permute-start.25 = (bf16[64,512]{1,0:T(8,128)(2,1)S(1)}, bf16[64,512]{1,0:T(8,128)(2,1)S(1)}, u32[]{:S(2)}, u32[]{:S(2)}) collective-permute-start(bf16[64,512]{1,0:T(8,128)(2,1)S(1)} %get-tuple-element.164), channel_id=1, source_target_pairs={{8,0},{5,1},{2,2},{14,3},{11,4},{4,5},{1,6},{13,7},{10,8},{7,9},{0... | collective-permute-start | bytes 196616 | tf_op jit(solution)/shard_map/ppermute | solution.py:517
  110.0 7.1 %collective-permute-start.24 = (bf16[64,512]{1,0:T(8,128)(2,1)S(1)}, bf16[64,512]{1,0:T(8,128)(2,1)S(1)}, u32[]{:S(2)}, u32[]{:S(2)}) collective-permute-start(bf16[64,512]{1,0:T(8,128)(2,1)S(1)} %get-tuple-element.165), channel_id=1, source_target_pairs={{4,0},{1,1},{13,2},{10,3},{7,4},{0,5},{12,6},{9,7},{6,8},{3,9},{15... | collective-permute-start | bytes 196616 | tf_op jit(solution)/shard_map/ppermute | solution.py:517
  112.0 5.2 %collective-permute-start.23 = (bf16[64,512]{1,0:T(8,128)(2,1)S(1)}, bf16[64,512]{1,0:T(8,128)(2,1)S(1)}, u32[]{:S(2)}, u32[]{:S(2)}) collective-permute-start(bf16[64,512]{1,0:T(8,128)(2,1)S(1)} %get-tuple-element.166), channel_id=1, source_target_pairs={{0,0},{12,1},{9,2},{6,3},{3,4},{15,5},{8,6},{5,7},{2,8},{14,9},{11... | collective-permute-start | bytes 196616 | tf_op jit(solution)/shard_map/ppermute | solution.py:517

commit v6 on v5

--- a/solution.py
+++ b/solution.py
@@ -280,20 +280,23 @@
 
 
 def lower_kernel(
-    where, q_own, q_for, rates, halo_a, halo_b, halo2_a, halo2_b, low2, c, att, err, b
+    where, q_own, q_for, rates, halo_a, halo_b, halo2_a, halo2_b, low2, c, att_up, *rest
 ):
-    mine = where[0] == 0
+    att_own, att_for, err, att, b = rest
+    bottom = where[0] == 0
     first = where[1] == 0
     inner = where[2] > 0
     for t, h in enumerate((halo2_a, halo2_b)):
         rows = pl.ds(t * HALF, HALF)
         b[rows, :] = jnp.where(first, h[...], low2[rows, :])
-    q = lambda rows: jnp.where(mine, q_own[rows, :], q_for[rows, :])
-    r = column(mine, where[0], rates, q_for)
+    q = lambda rows: jnp.where(bottom, q_own[rows, :], q_for[rows, :])
+    r = column(bottom, where[0], rates, q_for)
     halo = (halo_a, halo_b)
     attend(
         q, r, lambda t: halo[t][...], rows_of(b), rows_of(c), inner, inner | ~first, att, err
     )
+    att_own[...] = jnp.where(bottom, att[...], att_up[...])
+    att_for[...] = jnp.where(bottom, att_up[...], att[...])
 
 
 def half_of(core, ref):
@@ -332,11 +335,9 @@
 
 
 def update_kernel(zs, where, own, *rest):
-    got, olds, (piece, placed) = rest[:-5], rest[-5:-2], rest[-2:]
+    got, olds, piece = rest[:-4], rest[-4:-1], rest[-1]
     rows = HALF // zs
-    at = where[1] * HALF + where[2] * rows
-    mine = pl.ds(pl.multiple_of(at, rows), rows)
-    number = where[0] * 2 * zs + where[1] * zs + where[2]
+    mine = pl.ds(pl.multiple_of(where[1] * HALF + where[2] * rows, rows), rows)
     for kind in range(3):
         grad = own[kind]
         for g in got:
@@ -346,18 +347,7 @@
         factor = jnp.sqrt(jnp.mean(old * old, -1, keepdims=True) + 1e-06) * lax.rsqrt(
             jnp.mean(raised * raised, -1, keepdims=True) + 1e-06
         )
-        new = (raised * factor).astype(BF)
-        piece[kind] = new
-        placed[lax.rem(kind * 4 * zs + number, 3)] = new
-
-
-def owners(zs, slot):
-    pairs = []
-    for owner in range(4 * zs):
-        head, piece = divmod((3 * owner + slot) % (4 * zs), 2 * zs)
-        core, z = divmod(piece, zs)
-        pairs.append(((z * 2 + head) * 2 + core, owner))
-    return pairs
+        piece[kind] = (raised * factor).astype(BF)
 
 
 def gather(zs, where, pieces, kinds, full):
@@ -376,56 +366,71 @@
         hg = mm_t(qn, full[0:HD, :])
         hu = mm_t(qn, full[HD : 2 * HD, :])
         g = (hg * jax.nn.sigmoid(hg) * hu).astype(BF)
-        out[rows, :] = (att(rows).astype(F32) + mm_t(g, full[2 * HD : 3 * HD, :])).astype(BF)
-
-
-def read_foreign_kernel(zs, where, *rest):
-    pieces, (q, att_low, att_up, out, full) = rest[: 2 * zs], rest[2 * zs :]
-    gather(zs, where, pieces, 3, full)
-    low = where[0] == 1
-    read(q, lambda rows: jnp.where(low, att_low[rows, :], att_up[rows, :]), full, out)
-
-
-def read_own_kernel(where, q, att_low, att_up, full, out, work, sem):
-    low = where[0] == 0
-    read(q, lambda rows: jnp.where(low, att_low[rows, :], att_up[rows, :]), full, work)
-    column = pl.ds(pl.multiple_of(where[0] * HD, HD), HD)
+        fast = mm_t(g, full[2 * HD : 3 * HD, :])
+        out[rows, :] = (att[rows, :].astype(F32) + fast).astype(BF)
+
+
+def write_head(head, work, out, sem):
+    column = pl.ds(pl.multiple_of(head * HD, HD), HD)
     copy = pltpu.make_async_copy(work, out.at[:, column], sem)
     copy.start()
     copy.wait()
 
 
-def read_own(where, q, att_low, att_up, full):
+def read_own_kernel(zs, where, *rest):
+    pieces, (q, att, out, full, work, sem) = rest[: 2 * zs], rest[2 * zs :]
+    gather(zs, where, pieces, 3, full)
+    read(q, att, full, work)
+    write_head(where[0], work, out, sem)
+
+
+def read_own(zs, where, pieces, q, att):
     return pl.pallas_call(
-        read_own_kernel,
-        in_specs=[SM] + [VM] * 4,
-        out_specs=pl.BlockSpec(memory_space=pl.ANY),
-        out_shape=shape((BLK, H * HD)),
+        functools.partial(read_own_kernel, zs),
+        in_specs=[SM] + [VM] * (2 * zs + 2),
+        out_specs=[pl.BlockSpec(memory_space=pl.ANY), VM],
+        out_shape=[shape((BLK, H * HD)), shape((3 * HD, HD))],
         scratch_shapes=[pltpu.VMEM((BLK, HD), BF), pltpu.SemaphoreType.DMA],
         compiler_params=PARAMS,
         name="read_own",
-    )(where, q, att_low, att_up, full)
-
-
-def place_kernel(where, got, half_filled, out, sem):
-    column = pl.ds(pl.multiple_of((1 - where[0]) * HD, HD), HD)
-    copy = pltpu.make_async_copy(got, out.at[:, column], sem)
-    copy.start()
-    copy.wait()
-
-
-def place(where, got, half_filled):
+    )(where, *pieces, q, att)
+
+
+def read_other_kernel(zs, count, where, *rest):
+    pieces, (q, att, mine, half_filled, out, weights, full, work, sem) = (
+        rest[: 2 * zs],
+        rest[2 * zs :],
+    )
+    y, core, z = where[0], where[1], where[2]
+    gather(zs, where, pieces, 3, full)
+    read(q, att, full, work)
+    step = math.gcd(count, HD)
+    first = ((z * 2 + y) * 2 + core) * count
+    for c in range(count // step):
+        r = first + c * step
+        head = lax.rem(lax.div(r, HD), 2)
+        at = lax.div(r, 2 * HD) * HD + lax.rem(r, HD)
+        rows = pl.ds(pl.multiple_of(at, step), step)
+        weights[c * step : (c + 1) * step, :] = jnp.where(head == y, mine[rows, :], full[rows, :])
+    write_head(1 - y, work, out, sem)
+
+
+def read_other(zs, where, count, pieces, q, att, mine, half_filled):
     anyspec = pl.BlockSpec(memory_space=pl.ANY)
     return pl.pallas_call(
-        place_kernel,
-        in_specs=[SM, VM, anyspec],
-        out_specs=anyspec,
-        out_shape=shape((BLK, H * HD)),
-        scratch_shapes=[pltpu.SemaphoreType.DMA],
-        input_output_aliases={2: 0},
+        functools.partial(read_other_kernel, zs, count),
+        in_specs=[SM] + [VM] * (2 * zs + 3) + [anyspec],
+        out_specs=[anyspec, VM],
+        out_shape=[shape((BLK, H * HD)), shape((count, HD))],
+        scratch_shapes=[
+            pltpu.VMEM((3 * HD, HD), BF),
+            pltpu.VMEM((BLK, HD), BF),
+            pltpu.SemaphoreType.DMA,
+        ],
+        input_output_aliases={2 * zs + 4: 0},
         compiler_params=PARAMS,
-        name="place",
-    )(where, got, half_filled)
+        name="read_other",
+    )(where, *pieces, q, att, mine, half_filled)
 
 
 def local(queries, key_rows, value_rows, step_rates, w_gate, w_up, w_down):
@@ -456,6 +461,7 @@
     own = pack(where, after(key_rows, sent_b), value_rows, 0, BLK, True)
     theirs = [swap(sent_a, "y"), swap(sent_b, "y")]
     q_own = jnp.where(y == 0, queries[:, :HD], queries[:, HD:])
+    q_rest = jnp.where(y == 0, queries[:, HD:], queries[:, :HD])
     weights = [jnp.where(y == 0, w[:HD], w[HD:]) for w in (w_gate, w_up, w_down)]
     theirs[0], sent_q, q_own, (wg, wu, wd) = lax.optimization_barrier(
         (theirs[0], sent_q, q_own, weights)
@@ -483,9 +489,12 @@
     err_up, halo = lax.optimization_barrier((err_up, (halo_a, halo_b)))
     halo2 = [swap(h, "core") for h in halo]
     err_up2 = swap(err_up, "core")
-    att_low, err_low = call(
-        lower_kernel, "attend_lower", two, [pltpu.VMEM((BLK, 2 * HD), BF)]
-    )(where, q_own, q_for, step_rates, *halo, *halo2, kv_low2, kv_low)
+    att_own, att_for, err_low = call(
+        lower_kernel,
+        "attend_lower",
+        [shape((BLK, HD))] * 3,
+        [pltpu.VMEM((BLK, HD), BF), pltpu.VMEM((BLK, 2 * HD), BF)],
+    )(where, q_own, q_for, step_rates, *halo, *halo2, kv_low2, kv_low, att_up)
     err_low2 = swap(err_low, "core")
 
     def factors_of(*blocks):
@@ -502,23 +511,20 @@
         [pltpu.VMEM(total.shape, F32)],
     )(where, err_low, err_low2, *factors_of(low, low2), wd, before)
     got = [shift(s, d) for d, s in enumerate(sends, 1)]
-    piece, placed = call(
-        functools.partial(update_kernel, zs), "update", [shape((3, rows, HD))] * 2
-    )(where, own_sum, *got, wg, wu, wd)
+    att_back = swap(after(att_for, own_sum), "y")
+    got, att_back = lax.optimization_barrier((got, att_back))
+    piece = call(functools.partial(update_kernel, zs), "update", [shape((3, rows, HD))])(
+        where, own_sum, *got, wg, wu, wd
+    )[0]
     pieces = [piece] + [shift(piece, d) for d in range(1, zs)]
-    pieces += [swap(p, "core") for p in pieces]
-    out_for, full = call(
-        functools.partial(read_foreign_kernel, zs),
-        "read_foreign",
-        [shape((BLK, HD)), shape((3 * HD, HD))],
-    )(where, *pieces, q_for, att_low, att_up)
-    out_got = swap(out_for, "y")
-    own_rows = [
-        lax.ppermute(placed[slot], ("z", "y", "core"), owners(zs, slot)) for slot in range(3)
-    ]
-    half_filled = read_own(where, q_own, att_low, att_up, full)
-    half_filled, own_rows = lax.optimization_barrier((half_filled, own_rows))
-    return place(where, out_got, half_filled), jnp.concatenate(own_rows, 0)
+    others = [swap(p, "y") for p in pieces]
+    pieces2 = [swap(p, "core") for p in pieces]
+    others2 = [swap(p, "core") for p in others]
+    half_filled, full = read_own(zs, where, pieces + pieces2, q_own, att_own)
+    count = 3 * H * HD // (4 * zs)
+    return tuple(
+        read_other(zs, where, count, others + others2, q_rest, att_back, full, half_filled)
+    )
 
 
 def solution(mesh):

time: 123 us -> 120 us (0.976); the launches traced: 121 us -> 120 us
  starting transfers between devices: 34.1 us -> 32.8 us
    ppermute x3 -> x0, starting transfers between devices: 6.41 us -> none  [local(): lax.ppermute(placed[slot], ('z', 'y', 'core'), owners(zs, slot))]
    ppermute x15 -> x23, waiting for transfers between devices: 14.8 us -> 20.6 us  [swap(): return lax.ppermute(value, axis, SWAP)]
    ppermute x15 -> x23, starting transfers between devices: 7.23 us -> 12.8 us  [swap(): return lax.ppermute(value, axis, SWAP)]
    ppermute x8, waiting for transfers between devices: 30.2 us -> 26.9 us  [shift(): lax.ppermute(value, 'z', [(i, (i + d) % zs) for i in range(zs) if ring or...]
    pallas_call x2, Pallas kernels: 3.95 us -> 6.04 us  [the longest x1 3.35 us: read_other(): pl.pallas_call(functools.partial(read_other_kernel, zs, count), in_specs=...]
    ppermute x3 -> x0, waiting for transfers between devices: 1.91 us -> none  [local(): lax.ppermute(placed[slot], ('z', 'y', 'core'), owners(zs, slot))]
    pallas_call x11 -> x10, Pallas kernels: 24.2 us -> 22.3 us  [run(): pl.pallas_call(kernel, in_specs=[SM] + [VM] * len(args), out_specs=[VM] *...]
  transfers between devices with their start and end apart: 26 -> 31, of which waited for: 14 -> 12; matrix products, arithmetic and copies ran while one was open for 2% -> 1% of each run, Pallas kernels for 23% -> 23%
where the time goes in v6:
time: 120 us
  waiting for transfers between devices  47.5 us (40%)
  Pallas kernels  36.5 us (30%)
  starting transfers between devices  32.8 us (27%)
  other arithmetic  1.76 us (1%)
    ppermute x8, waiting for transfers between devices, shift(): lax.ppermute(value, 'z', [(i, (i + d) % zs) for i in range(zs) if ring or...  26.9 us
    pallas_call x10, Pallas kernels, run(): pl.pallas_call(kernel, in_specs=[SM] + [VM] * len(args), out_specs=[VM] *...  22.3 us
    ppermute x23, waiting for transfers between devices, swap(): return lax.ppermute(value, axis, SWAP)  20.6 us
    ppermute x8, starting transfers between devices, shift(): lax.ppermute(value, 'z', [(i, (i + d) % zs) for i in range(zs) if ring or...  20.1 us
    ppermute x23, starting transfers between devices, swap(): return lax.ppermute(value, axis, SWAP)  12.8 us
    pallas_call x3, Pallas kernels, pack(): pl.pallas_call(functools.partial(pack_kernel, first, count, own), in_spec...  6.52 us
    pallas_call x1, Pallas kernels, read_other(): pl.pallas_call(functools.partial(read_other_kernel, zs, count), in_specs=...  3.35 us
    pallas_call x1, Pallas kernels, read_own(): pl.pallas_call(functools.partial(read_own_kernel, zs), in_specs=[SM] + [V...  2.69 us
  transfers between devices with their start and end apart: 31, of which 12 were waited for; matrix products, arithmetic and copies ran while one was open for 1% of the time, Pallas kernels for 23%

profile of v6, /device:TPU:0, one launch (start us, length us, event | category | flops | bytes accessed | tf_op | source)
XLA Modules:
  0.0 120.0 jit_solution(1841779165891478136)
XLA Ops:
  0.7 2.4 %pack.3 = bf16[256,1024]{1,0:T(8,128)(2,1)} custom-call(s32[3]{0:T(128)S(1)} %pad_add_fusion.where, bf16[512,1024]{1,0:T(8,128)(2,1)} %key.3, bf16[512,1024]{1,0:T(8,128)(2,1)} %value.5), custom_call_target="tpu_custom_call" | custom-call | tf_op jit(solution)/shard_map/pack/pallas_call | solution.py:105
  3.1 3.0 %collective-permute-start = (bf16[256,1024]{1,0:T(8,128)(2,1)}, bf16[256,1024]{1,0:T(8,128)(2,1)S(1)}, u32[]{:S(2)}, u32[]{:S(2)}) collective-permute-start(bf16[256,1024]{1,0:T(8,128)(2,1)} %pack.3), channel_id=1, source_target_pairs={{0,2},{2,0},{1,3},{3,1},{4,6},{6,4},{5,7},{7,5},{8,10},{10,8},{9,1... | collective-permute-start | bytes 1572872 | tf_op jit(solution)/shard_map/ppermute | solution.py:443
  6.1 2.4 %pack.4 = bf16[256,1024]{1,0:T(8,128)(2,1)} custom-call(s32[3]{0:T(128)S(1)} %pad_add_fusion.where, bf16[512,1024]{1,0:T(8,128)(2,1)} %key.3, bf16[512,1024]{1,0:T(8,128)(2,1)} %value.5), custom_call_target="tpu_custom_call" | custom-call | tf_op jit(solution)/shard_map/pack/pallas_call | solution.py:105
  8.6 1.8 %pack.5.own = bf16[512,1024]{1,0:T(8,128)(2,1)S(1)} custom-call(s32[3]{0:T(128)S(1)} %pad_add_fusion.where, bf16[512,1024]{1,0:T(8,128)(2,1)} %key.3, bf16[512,1024]{1,0:T(8,128)(2,1)} %value.5), custom_call_target="tpu_custom_call" | custom-call | tf_op jit(solution)/shard_map/pack/pallas_call | solution.py:105
  10.5 1.6 %pack_q.1 = bf16[528,512]{1,0:T(8,128)(2,1)S(1)} custom-call(s32[3]{0:T(128)S(1)} %pad_add_fusion.where, bf16[512,1024]{1,0:T(8,128)(2,1)} %query, f32[2,512]{1,0:T(2,128)S(1)} %copy-done), custom_call_target="tpu_custom_call" | custom-call | tf_op jit(solution)/shard_map/pack_q/pallas_call | solution.py:74
  12.2 1.5 %slice_select_fusion = (bf16[512,512]{1,0:T(8,128)(2,1)S(1)}, bf16[512,512]{1,0:T(8,128)(2,1)S(1)}) fusion(bf16[1024,512]{1,0:T(8,128)(2,1)S(1)} %copy-done.2, pred[]{:T(512)S(6)} %eq.2, bf16[1024,512]{1,0:T(8,128)(2,1)} %param.12), kind=kLoop, calls=%fused_computation | loop fusion | flops 524288 | bytes 3145729 | tf_op jit(solution)/shard_map/jit(_where)/select_n | solution.py:465
  13.7 0.3 copy-done.3
  14.2 4.9 %collective-permute-done.foreign.rest_0_.for_a = bf16[256,1024]{1,0:T(8,128)(2,1)S(1)} collective-permute-done((bf16[256,1024]{1,0:T(8,128)(2,1)}, bf16[256,1024]{1,0:T(8,128)(2,1)S(1)}, u32[]{:S(2)}, u32[]{:S(2)}) %collective-permute-start) | collective-permute-done | bytes 524320 | tf_op jit(solution)/shard_map/ppermute | solution.py:443
  19.1 0.6 pick.2
  19.8 2.1 %collective-permute-start.6 = (bf16[528,512]{1,0:T(8,128)(2,1)S(1)}, bf16[528,512]{1,0:T(8,128)(2,1)S(1)}, u32[]{:S(2)}, u32[]{:S(2)}) collective-permute-start(bf16[528,512]{1,0:T(8,128)(2,1)S(1)} %pack_q.1), channel_id=1, source_target_pairs={{0,2},{2,0},{1,3},{3,1},{4,6},{6,4},{5,7},{7,5},{8,10},{10,8},{9,1... | collective-permute-start | bytes 1622024 | tf_op jit(solution)/shard_map/ppermute | solution.py:443
  21.9 3.5 %collective-permute-start.5 = (bf16[256,1024]{1,0:T(8,128)(2,1)S(1)}, bf16[256,1024]{1,0:T(8,128)(2,1)S(1)}, u32[]{:S(2)}, u32[]{:S(2)}) collective-permute-start(bf16[256,1024]{1,0:T(8,128)(2,1)S(1)} %pick.2), channel_id=1, source_target_pairs={{0,4},{4,8},{8,12},{1,5},{5,9},{9,13},{2,6},{6,10},{10,14},{3,7},{... | collective-permute-start | bytes 1572872 | tf_op jit(solution)/shard_map/ppermute | solution.py:446
  25.4 3.7 %pre_own.1 = (bf16[512,512]{1,0:T(8,128)(2,1)S(1)}, bf16[512,512]{1,0:T(8,128)(2,1)S(1)}, f32[512,256]{1,0:T(8,128)S(1)}, f32[512,256]{1,0:T(8,128)S(1)}, bf16[5...) custom-call(s32[3]{0:T(128)S(1)} %pad_add_fusion.where, ...), custom_call_target="tpu_custom_call" | custom-call | tf_op jit(solution)/shard_map/pre_own/pallas_call | solution.py:55
  29.1 1.2 %collective-permute-done.1.foreign.rest_1_.for_b = bf16[256,1024]{1,0:T(8,128)(2,1)S(1)} collective-permute-done((bf16[256,1024]{1,0:T(8,128)(2,1)}, bf16[256,1024]{1,0:T(8,128)(2,1)S(1)}, u32[]{:S(2)}, u32[]{:S(2)}) %collective-permute-start.1) | collective-permute-done | bytes 524320 | tf_op jit(solution)/shard_map/ppermute | solution.py:443
  30.3 0.6 pick.3
  31.0 4.1 %collective-permute-start.7 = (bf16[256,1024]{1,0:T(8,128)(2,1)S(1)}, bf16[256,1024]{1,0:T(8,128)(2,1)S(1)}, u32[]{:S(2)}, u32[]{:S(2)}) collective-permute-start(bf16[256,1024]{1,0:T(8,128)(2,1)S(1)} %pick.3), channel_id=1, source_target_pairs={{0,4},{4,8},{8,12},{1,5},{5,9},{9,13},{2,6},{6,10},{10,14},{3,7},{... | collective-permute-start | bytes 1572872 | tf_op jit(solution)/shard_map/ppermute | solution.py:446
  35.1 2.6 %pre.2 = (bf16[512,512]{1,0:T(8,128)(2,1)S(1)}, bf16[512,512]{1,0:T(8,128)(2,1)S(1)}, f32[512,256]{1,0:T(8,128)S(1)}, f32[512,256]{1,0:T(8,128)S(1)}, bf16[512,5...) custom-call(s32[3]{0:T(128)S(1)} %pad_add_fusion.where, ...), custom_call_target="tpu_custom_call" | custom-call | tf_op jit(solution)/shard_map/pre/pallas_call | solution.py:55
  37.7 3.4 %collective-permute-done.6.q_for = bf16[528,512]{1,0:T(8,128)(2,1)S(1)} collective-permute-done((bf16[528,512]{1,0:T(8,128)(2,1)S(1)}, bf16[528,512]{1,0:T(8,128)(2,1)S(1)}, u32[]{:S(2)}, u32[]{:S(2)}) %collective-permute-start.6) | collective-permute-done | bytes 540704 | tf_op jit(solution)/shard_map/ppermute | solution.py:443
  41.1 2.8 %pre.3 = (bf16[512,512]{1,0:T(8,128)(2,1)S(1)}, bf16[512,512]{1,0:T(8,128)(2,1)S(1)}, f32[512,256]{1,0:T(8,128)S(1)}, f32[512,256]{1,0:T(8,128)S(1)}, bf16[512,5...) custom-call(s32[3]{0:T(128)S(1)} %pad_add_fusion.where, ...), custom_call_target="tpu_custom_call" | custom-call | tf_op jit(solution)/shard_map/pre/pallas_call | solution.py:55
  43.9 3.3 %attend_upper.1 = (bf16[512,512]{1,0:T(8,128)(2,1)S(1)}, bf16[512,512]{1,0:T(8,128)(2,1)S(1)}, bf16[512,1024]{1,0:T(8,128)(2,1)S(1)}, bf16[512,1024]{1,0:T(8,128)(2,1)S(1)}) custom-call(s32[3]{0:T(128)S(1)} %pad_add_fusion.where, bf16[512,512]{1,0:T(8,128)(2,1)S(1)} %get-tuple-element.85.q_own.rest_8_, bf16[528,512]{1,0:T(8,128)(2,1)S(1)} %collective-permute-done.6.q_for, ...), custom_call_target="tpu_custom_call" | custom-call | tf_op jit(solution)/shard_map/attend_upper/pallas_call | solution.py:55
  47.2 0.9 collective-permute-done.7.halo_b
  48.1 0.5 collective-permute-start.9
  48.6 1.4 %collective-permute-done.8.halo2_a = bf16[256,1024]{1,0:T(8,128)(2,1)S(1)} collective-permute-done((bf16[256,1024]{1,0:T(8,128)(2,1)S(1)}, bf16[256,1024]{1,0:T(8,128)(2,1)S(1)}, u32[]{:S(2)}, u32[]{:S(2)}) %collective-permute-start.8) | collective-permute-done | bytes 524320 | tf_op jit(solution)/shard_map/ppermute | solution.py:443
  50.0 0.7 collective-permute-done.9.halo2_b
  50.8 3.2 %attend_lower.1 = (bf16[512,512]{1,0:T(8,128)(2,1)S(1)}, bf16[512,512]{1,0:T(8,128)(2,1)S(1)}, bf16[512,512]{1,0:T(8,128)(2,1)S(1)}) custom-call(s32[3]{0:T(128)S(1)} %pad_add_fusion.where, bf16[512,512]{1,0:T(8,128)(2,1)S(1)} %get-tuple-element.85.q_own.rest_8_, bf16[528,512]{1,0:T(8,128)(2,1)S(1)} %collective-permute-done.6.q_for, f32[2,512]{1,0:T(2,128)S(1)} %copy-done, ...), custom_call_target="tpu_custom_call" | custom-call | tf_op jit(solution)/shard_map/attend_lower/pallas_call | solution.py:55
  54.0 0.2 collective-permute-start.10
  54.2 2.3 %grad_first.1.before = f32[3,256,512]{2,1,0:T(8,128)S(1)} custom-call(s32[3]{0:T(128)S(1)} %pad_add_fusion.where, bf16[512,512]{1,0:T(8,128)(2,1)S(1)} %get-tuple-element.142.e0, bf16[512,512]{1,0:T(8,128)(2,1)S(1)} %collective-permute-done.11.e1, bf16[512,512]{1,0:T(8,128)(2,1)S(1)} %get-tuple-element.143.k0, bf16[512,512]{1,0:T(8,128)(2,1)S(1)} %get-tuple-element.144.k1, ...), custom_call_target="tpu_custom_call" | custom-call | tf_op jit(solution)/shard_map/grad_first/pallas_call | solution.py:55
  56.5 2.5 %grad_second.1 = (f32[3,64,512]{2,1,0:T(8,128)S(1)}, bf16[3,64,512]{2,1,0:T(8,128)(2,1)S(1)}, bf16[3,64,512]{2,1,0:T(8,128)(2,1)S(1)}, bf16[3,64,512]{2,1,0:T(8,128)(2,1)S(1)}) custom-call(s32[3]{0:T(128)S(1)} %pad_add_fusion.where, bf16[512,512]{1,0:T(8,128)(2,1)S(1)} %get-tuple-element.132.e0, bf16[512,512]{1,0:T(8,128)(2,1)S(1)} %collective-permute-done.10.e1, ...), custom_call_target="tpu_custom_call" | custom-call | tf_op jit(solution)/shard_map/grad_second/pallas_call | solution.py:55
  59.0 1.0 collective-permute-start.15
  60.0 2.1 %collective-permute-start.12 = (bf16[3,64,512]{2,1,0:T(8,128)(2,1)S(1)}, bf16[3,64,512]{2,1,0:T(8,128)(2,1)S(1)}, u32[]{:S(2)}, u32[]{:S(2)}) collective-permute-start(bf16[3,64,512]{2,1,0:T(8,128)(2,1)S(1)} %get-tuple-element.152), channel_id=1, source_target_pairs={{0,4},{4,8},{8,12},{12,0},{1,5},{5,9},{9,13},{13,1},{2,6},{6,10},{... | collective-permute-start | bytes 589832 | tf_op jit(solution)/shard_map/ppermute | solution.py:446
  62.0 2.6 %collective-permute-start.13 = (bf16[3,64,512]{2,1,0:T(8,128)(2,1)S(1)}, bf16[3,64,512]{2,1,0:T(8,128)(2,1)S(1)}, u32[]{:S(2)}, u32[]{:S(2)}) collective-permute-start(bf16[3,64,512]{2,1,0:T(8,128)(2,1)S(1)} %get-tuple-element.153), channel_id=1, source_target_pairs={{0,8},{4,12},{8,0},{12,4},{1,9},{5,13},{9,1},{13,5},{2,10},{6,14},... | collective-permute-start | bytes 589832 | tf_op jit(solution)/shard_map/ppermute | solution.py:446
  64.7 1.3 %collective-permute-start.14 = (bf16[3,64,512]{2,1,0:T(8,128)(2,1)S(1)}, bf16[3,64,512]{2,1,0:T(8,128)(2,1)S(1)}, u32[]{:S(2)}, u32[]{:S(2)}) collective-permute-start(bf16[3,64,512]{2,1,0:T(8,128)(2,1)S(1)} %get-tuple-element.154), channel_id=1, source_target_pairs={{0,12},{4,0},{8,4},{12,8},{1,13},{5,1},{9,5},{13,9},{2,14},{6,2},{... | collective-permute-start | bytes 589832 | tf_op jit(solution)/shard_map/ppermute | solution.py:446
  66.0 3.9 %collective-permute-done.12.rest_0_ = bf16[3,64,512]{2,1,0:T(8,128)(2,1)S(1)} collective-permute-done((bf16[3,64,512]{2,1,0:T(8,128)(2,1)S(1)}, bf16[3,64,512]{2,1,0:T(8,128)(2,1)S(1)}, u32[]{:S(2)}, u32[]{:S(2)}) %collective-permute-start.12) | collective-permute-done | bytes 196640 | tf_op jit(solution)/shard_map/ppermute | solution.py:446
  69.9 7.9 %collective-permute-done.13.rest_1_ = bf16[3,64,512]{2,1,0:T(8,128)(2,1)S(1)} collective-permute-done((bf16[3,64,512]{2,1,0:T(8,128)(2,1)S(1)}, bf16[3,64,512]{2,1,0:T(8,128)(2,1)S(1)}, u32[]{:S(2)}, u32[]{:S(2)}) %collective-permute-start.13) | collective-permute-done | bytes 196640 | tf_op jit(solution)/shard_map/ppermute | solution.py:446
  77.8 0.8 update.1.rest_0_
  78.6 5.8 %collective-permute-start.21 = (bf16[3,64,512]{2,1,0:T(8,128)(2,1)S(1)}, bf16[3,64,512]{2,1,0:T(8,128)(2,1)S(1)}, u32[]{:S(2)}, u32[]{:S(2)}) collective-permute-start(bf16[3,64,512]{2,1,0:T(8,128)(2,1)S(1)} %update.1.rest_0_), channel_id=1, source_target_pairs={{0,12},{4,0},{8,4},{12,8},{1,13},{5,1},{9,5},{13,9},{2,14},{6,2},{... | collective-permute-start | bytes 589832 | tf_op jit(solution)/shard_map/ppermute | solution.py:446
  84.4 0.4 collective-permute-start.19
  84.8 0.3 collective-permute-start.17
  85.1 1.5 %collective-permute-start.16 = (bf16[3,64,512]{2,1,0:T(8,128)(2,1)S(1)}, bf16[3,64,512]{2,1,0:T(8,128)(2,1)S(1)}, u32[]{:S(2)}, u32[]{:S(2)}) collective-permute-start(bf16[3,64,512]{2,1,0:T(8,128)(2,1)S(1)} %update.1.rest_0_), channel_id=1, source_target_pairs={{0,2},{2,0},{1,3},{3,1},{4,6},{6,4},{5,7},{7,5},{8,10},{10,8},{9,1... | collective-permute-start | bytes 589832 | tf_op jit(solution)/shard_map/ppermute | solution.py:443
  86.6 3.2 %collective-permute-done.21.rest_3_ = bf16[3,64,512]{2,1,0:T(8,128)(2,1)S(1)} collective-permute-done((bf16[3,64,512]{2,1,0:T(8,128)(2,1)S(1)}, bf16[3,64,512]{2,1,0:T(8,128)(2,1)S(1)}, u32[]{:S(2)}, u32[]{:S(2)}) %collective-permute-start.21) | collective-permute-done | bytes 196640 | tf_op jit(solution)/shard_map/ppermute | solution.py:446
  89.8 1.5 %collective-permute-start.22 = (bf16[3,64,512]{2,1,0:T(8,128)(2,1)S(1)}, bf16[3,64,512]{2,1,0:T(8,128)(2,1)S(1)}, u32[]{:S(2)}, u32[]{:S(2)}) collective-permute-start(bf16[3,64,512]{2,1,0:T(8,128)(2,1)S(1)} %collective-permute-done.21.rest_3_), channel_id=1, source_target_pairs={{0,2},{2,0},{1,3},{3,1},{4,6},{6,4},{5,7},{7,5},{8,10},{10,8},{9,1... | collective-permute-start | bytes 589832 | tf_op jit(solution)/shard_map/ppermute | solution.py:443
  91.3 11.0 %collective-permute-done.19.rest_2_ = bf16[3,64,512]{2,1,0:T(8,128)(2,1)S(1)} collective-permute-done((bf16[3,64,512]{2,1,0:T(8,128)(2,1)S(1)}, bf16[3,64,512]{2,1,0:T(8,128)(2,1)S(1)}, u32[]{:S(2)}, u32[]{:S(2)}) %collective-permute-start.19) | collective-permute-done | bytes 196640 | tf_op jit(solution)/shard_map/ppermute | solution.py:446
  102.2 1.5 %collective-permute-start.20 = (bf16[3,64,512]{2,1,0:T(8,128)(2,1)S(1)}, bf16[3,64,512]{2,1,0:T(8,128)(2,1)S(1)}, u32[]{:S(2)}, u32[]{:S(2)}) collective-permute-start(bf16[3,64,512]{2,1,0:T(8,128)(2,1)S(1)} %collective-permute-done.19.rest_2_), channel_id=1, source_target_pairs={{0,2},{2,0},{1,3},{3,1},{4,6},{6,4},{5,7},{7,5},{8,10},{10,8},{9,1... | collective-permute-start | bytes 589832 | tf_op jit(solution)/shard_map/ppermute | solution.py:443
  103.7 0.5 collective-permute-start.18
  104.3 0.5 collective-permute-start.23
  104.9 5.1 %collective-permute-done.20.rest_2_ = bf16[3,64,512]{2,1,0:T(8,128)(2,1)S(1)} collective-permute-done((bf16[3,64,512]{2,1,0:T(8,128)(2,1)S(1)}, bf16[3,64,512]{2,1,0:T(8,128)(2,1)S(1)}, u32[]{:S(2)}, u32[]{:S(2)}) %collective-permute-start.20) | collective-permute-done | bytes 196640 | tf_op jit(solution)/shard_map/ppermute | solution.py:443
  109.9 3.8 %collective-permute-done.18.rest_1_ = bf16[3,64,512]{2,1,0:T(8,128)(2,1)S(1)} collective-permute-done((bf16[3,64,512]{2,1,0:T(8,128)(2,1)S(1)}, bf16[3,64,512]{2,1,0:T(8,128)(2,1)S(1)}, u32[]{:S(2)}, u32[]{:S(2)}) %collective-permute-start.18) | collective-permute-done | bytes 196640 | tf_op jit(solution)/shard_map/ppermute | solution.py:443
  113.8 2.7 %read_own.1 = (bf16[512,1024]{1,0:T(8,128)(2,1)}, bf16[1536,512]{1,0:T(8,128)(2,1)S(1)}) custom-call(s32[3]{0:T(128)S(1)} %pad_add_fusion.where, bf16[3,64,512]{2,1,0:T(8,128)(2,1)S(1)} %update.1.rest_0_, bf16[3,64,512]{2,1,0:T(8,128)(2,1)S(1)} %collective-permute-done.17.rest_1_, bf16[3,64,512]{2,1,0:T(8,128)(2,1)S(1)} %collective-permute-done.19.rest_2_, ...), custom_call_target="tpu_custom_call" | custom-call | tf_op jit(solution)/shard_map/read_own/pallas_call | solution.py:388
  116.5 3.3 %read_other.1 = (bf16[512,1024]{1,0:T(8,128)(2,1)}, bf16[192,512]{1,0:T(8,128)(2,1)}) custom-call(s32[3]{0:T(128)S(1)} %pad_add_fusion.where, bf16[3,64,512]{2,1,0:T(8,128)(2,1)S(1)} %collective-permute-done.16.rest_0_, bf16[3,64,512]{2,1,0:T(8,128)(2,1)S(1)} %collective-permute-done.18.rest_1_, ...), custom_call_target="tpu_custom_call", output_to_operand_aliasing={{0}: (12, {})} | custom-call | tf_op jit(solution)/shard_map/read_other/pallas_call | solution.py:420
  (41 shorter events, 0.7 us)
Async XLA Ops:
  3.1 16.0 %collective-permute-start = (bf16[256,1024]{1,0:T(8,128)(2,1)}, bf16[256,1024]{1,0:T(8,128)(2,1)S(1)}, u32[]{:S(2)}, u32[]{:S(2)}) collective-permute-start(bf16[256,1024]{1,0:T(8,128)(2,1)} %pack.3), channel_id=1, source_target_pairs={{0,2},{2,0},{1,3},{3,1},{4,6},{6,4},{5,7},{7,5},{8,10},{10,8},{9,1... | collective-permute-start | bytes 1572872 | tf_op jit(solution)/shard_map/ppermute | solution.py:443
  8.5 1.9 %copy-start = (f32[2,512]{1,0:T(2,128)S(1)}, f32[2,512]{1,0:T(2,128)}, u32[]{:S(2)}) copy-start(f32[2,512]{1,0:T(2,128)} %rates.5) | copy-start | bytes 12292
  8.5 21.8 %collective-permute-start.1 = (bf16[256,1024]{1,0:T(8,128)(2,1)}, bf16[256,1024]{1,0:T(8,128)(2,1)S(1)}, u32[]{:S(2)}, u32[]{:S(2)}) collective-permute-start(bf16[256,1024]{1,0:T(8,128)(2,1)} %pack.4), channel_id=1, source_target_pairs={{0,2},{2,0},{1,3},{3,1},{4,6},{6,4},{5,7},{7,5},{8,10},{10,8},{9,1... | collective-permute-start | bytes 1572872 | tf_op jit(solution)/shard_map/ppermute | solution.py:443
  10.4 15.0 %collective-permute-start.2 = (bf16[512,1024]{1,0:T(8,128)(2,1)S(1)}, bf16[512,1024]{1,0:T(8,128)(2,1)S(1)}, u32[]{:S(2)}, u32[]{:S(2)}) collective-permute-start(bf16[512,1024]{1,0:T(8,128)(2,1)S(1)} %pack.5.own), channel_id=1, source_target_pairs={{0,1},{1,0},{2,3},{3,2},{4,5},{5,4},{6,7},{7,6},{8,9},{9,8},{10,11... | collective-permute-start | bytes 3145736 | tf_op jit(solution)/shard_map/ppermute | solution.py:443
  10.5 1.7 %copy-start.2 = (bf16[1024,512]{1,0:T(8,128)(2,1)S(1)}, bf16[1024,512]{1,0:T(8,128)(2,1)}, u32[]{:S(2)}) copy-start(bf16[1024,512]{1,0:T(8,128)(2,1)} %param.13) | copy-start | bytes 3145732
  12.1 1.5 %copy-start.1 = (bf16[512,1024]{1,0:T(8,128)(2,1)S(1)}, bf16[512,1024]{1,0:T(8,128)(2,1)}, u32[]{:S(2)}) copy-start(bf16[512,1024]{1,0:T(8,128)(2,1)} %query) | copy-start | bytes 3145732
  12.2 1.8 %copy-start.3 = (bf16[1024,512]{1,0:T(8,128)(2,1)S(1)}, bf16[1024,512]{1,0:T(8,128)(2,1)}, u32[]{:S(2)}) copy-start(bf16[1024,512]{1,0:T(8,128)(2,1)} %param.11) | copy-start | bytes 3145732
  19.7 10.6 %collective-permute-start.3 = (bf16[256,1024]{1,0:T(8,128)(2,1)S(1)}, bf16[256,1024]{1,0:T(8,128)(2,1)S(1)}, u32[]{:S(2)}, u32[]{:S(2)}) collective-permute-start(bf16[256,1024]{1,0:T(8,128)(2,1)S(1)} %collective-permute-done.foreign.rest_0_.for_a), channel_id=1, source_target_pairs={{0,1},{1,0},{2,3},{3,2},{4,5},{5,4},{6,7},{7,6},{8,9},{9,8},{10,11... | collective-permute-start | bytes 1572872 | tf_op jit(solution)/shard_map/ppermute | solution.py:443
  19.8 21.3 %collective-permute-start.6 = (bf16[528,512]{1,0:T(8,128)(2,1)S(1)}, bf16[528,512]{1,0:T(8,128)(2,1)S(1)}, u32[]{:S(2)}, u32[]{:S(2)}) collective-permute-start(bf16[528,512]{1,0:T(8,128)(2,1)S(1)} %pack_q.1), channel_id=1, source_target_pairs={{0,2},{2,0},{1,3},{3,1},{4,6},{6,4},{5,7},{7,5},{8,10},{10,8},{9,1... | collective-permute-start | bytes 1622024 | tf_op jit(solution)/shard_map/ppermute | solution.py:443
  21.9 15.8 %collective-permute-start.5 = (bf16[256,1024]{1,0:T(8,128)(2,1)S(1)}, bf16[256,1024]{1,0:T(8,128)(2,1)S(1)}, u32[]{:S(2)}, u32[]{:S(2)}) collective-permute-start(bf16[256,1024]{1,0:T(8,128)(2,1)S(1)} %pick.2), channel_id=1, source_target_pairs={{0,4},{4,8},{8,12},{1,5},{5,9},{9,13},{2,6},{6,10},{10,14},{3,7},{... | collective-permute-start | bytes 1572872 | tf_op jit(solution)/shard_map/ppermute | solution.py:446
  30.9 6.7 %collective-permute-start.4 = (bf16[256,1024]{1,0:T(8,128)(2,1)S(1)}, bf16[256,1024]{1,0:T(8,128)(2,1)S(1)}, u32[]{:S(2)}, u32[]{:S(2)}) collective-permute-start(bf16[256,1024]{1,0:T(8,128)(2,1)S(1)} %collective-permute-done.1.foreign.rest_1_.for_b), channel_id=1, source_target_pairs={{0,1},{1,0},{2,3},{3,2},{4,5},{5,4},{6,7},{7,6},{8,9},{9,8},{10,11... | collective-permute-start | bytes 1572872 | tf_op jit(solution)/shard_map/ppermute | solution.py:443
  31.0 17.1 %collective-permute-start.7 = (bf16[256,1024]{1,0:T(8,128)(2,1)S(1)}, bf16[256,1024]{1,0:T(8,128)(2,1)S(1)}, u32[]{:S(2)}, u32[]{:S(2)}) collective-permute-start(bf16[256,1024]{1,0:T(8,128)(2,1)S(1)} %pick.3), channel_id=1, source_target_pairs={{0,4},{4,8},{8,12},{1,5},{5,9},{9,13},{2,6},{6,10},{10,14},{3,7},{... | collective-permute-start | bytes 1572872 | tf_op jit(solution)/shard_map/ppermute | solution.py:446
  48.1 1.9 %collective-permute-start.8 = (bf16[256,1024]{1,0:T(8,128)(2,1)S(1)}, bf16[256,1024]{1,0:T(8,128)(2,1)S(1)}, u32[]{:S(2)}, u32[]{:S(2)}) collective-permute-start(bf16[256,1024]{1,0:T(8,128)(2,1)S(1)} %collective-permute-done.5.halo_a), channel_id=1, source_target_pairs={{0,1},{1,0},{2,3},{3,2},{4,5},{5,4},{6,7},{7,6},{8,9},{9,8},{10,11... | collective-permute-start | bytes 1572872 | tf_op jit(solution)/shard_map/ppermute | solution.py:443
  48.1 2.7 %collective-permute-start.9 = (bf16[256,1024]{1,0:T(8,128)(2,1)S(1)}, bf16[256,1024]{1,0:T(8,128)(2,1)S(1)}, u32[]{:S(2)}, u32[]{:S(2)}) collective-permute-start(bf16[256,1024]{1,0:T(8,128)(2,1)S(1)} %collective-permute-done.7.halo_b), channel_id=1, source_target_pairs={{0,1},{1,0},{2,3},{3,2},{4,5},{5,4},{6,7},{7,6},{8,9},{9,8},{10,11... | collective-permute-start | bytes 1572872 | tf_op jit(solution)/shard_map/ppermute | solution.py:443
  48.6 5.6 %collective-permute-start.11 = (bf16[512,512]{1,0:T(8,128)(2,1)S(1)}, bf16[512,512]{1,0:T(8,128)(2,1)S(1)}, u32[]{:S(2)}, u32[]{:S(2)}) collective-permute-start(bf16[512,512]{1,0:T(8,128)(2,1)S(1)} %get-tuple-element.142.e0), channel_id=1, source_target_pairs={{0,1},{1,0},{2,3},{3,2},{4,5},{5,4},{6,7},{7,6},{8,9},{9,8},{10,11... | collective-permute-start | bytes 1572872 | tf_op jit(solution)/shard_map/ppermute | solution.py:443
  54.0 2.5 %collective-permute-start.10 = (bf16[512,512]{1,0:T(8,128)(2,1)S(1)}, bf16[512,512]{1,0:T(8,128)(2,1)S(1)}, u32[]{:S(2)}, u32[]{:S(2)}) collective-permute-start(bf16[512,512]{1,0:T(8,128)(2,1)S(1)} %get-tuple-element.132.e0), channel_id=1, source_target_pairs={{0,1},{1,0},{2,3},{3,2},{4,5},{5,4},{6,7},{7,6},{8,9},{9,8},{10,11... | collective-permute-start | bytes 1572872 | tf_op jit(solution)/shard_map/ppermute | solution.py:443
  59.0 18.8 %collective-permute-start.15 = (bf16[512,512]{1,0:T(8,128)(2,1)S(1)}, bf16[512,512]{1,0:T(8,128)(2,1)S(1)}, u32[]{:S(2)}, u32[]{:S(2)}) collective-permute-start(bf16[512,512]{1,0:T(8,128)(2,1)S(1)} %get-tuple-element.156), channel_id=1, source_target_pairs={{0,2},{2,0},{1,3},{3,1},{4,6},{6,4},{5,7},{7,5},{8,10},{10,8},{9,1... | collective-permute-start | bytes 1572872 | tf_op jit(solution)/shard_map/ppermute | solution.py:443
  60.0 10.0 %collective-permute-start.12 = (bf16[3,64,512]{2,1,0:T(8,128)(2,1)S(1)}, bf16[3,64,512]{2,1,0:T(8,128)(2,1)S(1)}, u32[]{:S(2)}, u32[]{:S(2)}) collective-permute-start(bf16[3,64,512]{2,1,0:T(8,128)(2,1)S(1)} %get-tuple-element.152), channel_id=1, source_target_pairs={{0,4},{4,8},{8,12},{12,0},{1,5},{5,9},{9,13},{13,1},{2,6},{6,10},{... | collective-permute-start | bytes 589832 | tf_op jit(solution)/shard_map/ppermute | solution.py:446
  62.0 15.8 %collective-permute-start.13 = (bf16[3,64,512]{2,1,0:T(8,128)(2,1)S(1)}, bf16[3,64,512]{2,1,0:T(8,128)(2,1)S(1)}, u32[]{:S(2)}, u32[]{:S(2)}) collective-permute-start(bf16[3,64,512]{2,1,0:T(8,128)(2,1)S(1)} %get-tuple-element.153), channel_id=1, source_target_pairs={{0,8},{4,12},{8,0},{12,4},{1,9},{5,13},{9,1},{13,5},{2,10},{6,14},... | collective-permute-start | bytes 589832 | tf_op jit(solution)/shard_map/ppermute | solution.py:446
  64.7 13.1 %collective-permute-start.14 = (bf16[3,64,512]{2,1,0:T(8,128)(2,1)S(1)}, bf16[3,64,512]{2,1,0:T(8,128)(2,1)S(1)}, u32[]{:S(2)}, u32[]{:S(2)}) collective-permute-start(bf16[3,64,512]{2,1,0:T(8,128)(2,1)S(1)} %get-tuple-element.154), channel_id=1, source_target_pairs={{0,12},{4,0},{8,4},{12,8},{1,13},{5,1},{9,5},{13,9},{2,14},{6,2},{... | collective-permute-start | bytes 589832 | tf_op jit(solution)/shard_map/ppermute | solution.py:446
  78.6 11.2 %collective-permute-start.21 = (bf16[3,64,512]{2,1,0:T(8,128)(2,1)S(1)}, bf16[3,64,512]{2,1,0:T(8,128)(2,1)S(1)}, u32[]{:S(2)}, u32[]{:S(2)}) collective-permute-start(bf16[3,64,512]{2,1,0:T(8,128)(2,1)S(1)} %update.1.rest_0_), channel_id=1, source_target_pairs={{0,12},{4,0},{8,4},{12,8},{1,13},{5,1},{9,5},{13,9},{2,14},{6,2},{... | collective-permute-start | bytes 589832 | tf_op jit(solution)/shard_map/ppermute | solution.py:446
  84.4 5.4 %collective-permute-start.27 = (bf16[3,64,512]{2,1,0:T(8,128)(2,1)S(1)}, bf16[3,64,512]{2,1,0:T(8,128)(2,1)S(1)}, u32[]{:S(2)}, u32[]{:S(2)}) collective-permute-start(bf16[3,64,512]{2,1,0:T(8,128)(2,1)S(1)} %update.1.rest_0_), channel_id=1, source_target_pairs={{0,1},{1,0},{2,3},{3,2},{4,5},{5,4},{6,7},{7,6},{8,9},{9,8},{10,11... | collective-permute-start | bytes 589832 | tf_op jit(solution)/shard_map/ppermute | solution.py:443
  84.4 17.9 %collective-permute-start.19 = (bf16[3,64,512]{2,1,0:T(8,128)(2,1)S(1)}, bf16[3,64,512]{2,1,0:T(8,128)(2,1)S(1)}, u32[]{:S(2)}, u32[]{:S(2)}) collective-permute-start(bf16[3,64,512]{2,1,0:T(8,128)(2,1)S(1)} %update.1.rest_0_), channel_id=1, source_target_pairs={{0,8},{4,12},{8,0},{12,4},{1,9},{5,13},{9,1},{13,5},{2,10},{6,14},... | collective-permute-start | bytes 589832 | tf_op jit(solution)/shard_map/ppermute | solution.py:446
  84.8 17.4 %collective-permute-start.17 = (bf16[3,64,512]{2,1,0:T(8,128)(2,1)S(1)}, bf16[3,64,512]{2,1,0:T(8,128)(2,1)S(1)}, u32[]{:S(2)}, u32[]{:S(2)}) collective-permute-start(bf16[3,64,512]{2,1,0:T(8,128)(2,1)S(1)} %update.1.rest_0_), channel_id=1, source_target_pairs={{0,4},{4,8},{8,12},{12,0},{1,5},{5,9},{9,13},{13,1},{2,6},{6,10},{... | collective-permute-start | bytes 589832 | tf_op jit(solution)/shard_map/ppermute | solution.py:446
  85.1 18.7 %collective-permute-start.16 = (bf16[3,64,512]{2,1,0:T(8,128)(2,1)S(1)}, bf16[3,64,512]{2,1,0:T(8,128)(2,1)S(1)}, u32[]{:S(2)}, u32[]{:S(2)}) collective-permute-start(bf16[3,64,512]{2,1,0:T(8,128)(2,1)S(1)} %update.1.rest_0_), channel_id=1, source_target_pairs={{0,2},{2,0},{1,3},{3,1},{4,6},{6,4},{5,7},{7,5},{8,10},{10,8},{9,1... | collective-permute-start | bytes 589832 | tf_op jit(solution)/shard_map/ppermute | solution.py:443
  89.8 14.5 %collective-permute-start.30 = (bf16[3,64,512]{2,1,0:T(8,128)(2,1)S(1)}, bf16[3,64,512]{2,1,0:T(8,128)(2,1)S(1)}, u32[]{:S(2)}, u32[]{:S(2)}) collective-permute-start(bf16[3,64,512]{2,1,0:T(8,128)(2,1)S(1)} %collective-permute-done.21.rest_3_), channel_id=1, source_target_pairs={{0,1},{1,0},{2,3},{3,2},{4,5},{5,4},{6,7},{7,6},{8,9},{9,8},{10,11... | collective-permute-start | bytes 589832 | tf_op jit(solution)/shard_map/ppermute | solution.py:443
  89.8 14.5 %collective-permute-start.22 = (bf16[3,64,512]{2,1,0:T(8,128)(2,1)S(1)}, bf16[3,64,512]{2,1,0:T(8,128)(2,1)S(1)}, u32[]{:S(2)}, u32[]{:S(2)}) collective-permute-start(bf16[3,64,512]{2,1,0:T(8,128)(2,1)S(1)} %collective-permute-done.21.rest_3_), channel_id=1, source_target_pairs={{0,2},{2,0},{1,3},{3,1},{4,6},{6,4},{5,7},{7,5},{8,10},{10,8},{9,1... | collective-permute-start | bytes 589832 | tf_op jit(solution)/shard_map/ppermute | solution.py:443
  102.2 2.6 %collective-permute-start.29 = (bf16[3,64,512]{2,1,0:T(8,128)(2,1)S(1)}, bf16[3,64,512]{2,1,0:T(8,128)(2,1)S(1)}, u32[]{:S(2)}, u32[]{:S(2)}) collective-permute-start(bf16[3,64,512]{2,1,0:T(8,128)(2,1)S(1)} %collective-permute-done.19.rest_2_), channel_id=1, source_target_pairs={{0,1},{1,0},{2,3},{3,2},{4,5},{5,4},{6,7},{7,6},{8,9},{9,8},{10,11... | collective-permute-start | bytes 589832 | tf_op jit(solution)/shard_map/ppermute | solution.py:443
  102.2 7.7 %collective-permute-start.20 = (bf16[3,64,512]{2,1,0:T(8,128)(2,1)S(1)}, bf16[3,64,512]{2,1,0:T(8,128)(2,1)S(1)}, u32[]{:S(2)}, u32[]{:S(2)}) collective-permute-start(bf16[3,64,512]{2,1,0:T(8,128)(2,1)S(1)} %collective-permute-done.19.rest_2_), channel_id=1, source_target_pairs={{0,2},{2,0},{1,3},{3,1},{4,6},{6,4},{5,7},{7,5},{8,10},{10,8},{9,1... | collective-permute-start | bytes 589832 | tf_op jit(solution)/shard_map/ppermute | solution.py:443
  103.7 10.0 %collective-permute-start.18 = (bf16[3,64,512]{2,1,0:T(8,128)(2,1)S(1)}, bf16[3,64,512]{2,1,0:T(8,128)(2,1)S(1)}, u32[]{:S(2)}, u32[]{:S(2)}) collective-permute-start(bf16[3,64,512]{2,1,0:T(8,128)(2,1)S(1)} %collective-permute-done.17.rest_1_), channel_id=1, source_target_pairs={{0,2},{2,0},{1,3},{3,1},{4,6},{6,4},{5,7},{7,5},{8,10},{10,8},{9,1... | collective-permute-start | bytes 589832 | tf_op jit(solution)/shard_map/ppermute | solution.py:443
  104.3 9.5 %collective-permute-start.28 = (bf16[3,64,512]{2,1,0:T(8,128)(2,1)S(1)}, bf16[3,64,512]{2,1,0:T(8,128)(2,1)S(1)}, u32[]{:S(2)}, u32[]{:S(2)}) collective-permute-start(bf16[3,64,512]{2,1,0:T(8,128)(2,1)S(1)} %collective-permute-done.17.rest_1_), channel_id=1, source_target_pairs={{0,1},{1,0},{2,3},{3,2},{4,5},{5,4},{6,7},{7,6},{8,9},{9,8},{10,11... | collective-permute-start | bytes 589832 | tf_op jit(solution)/shard_map/ppermute | solution.py:443
  104.3 12.2 %collective-permute-start.23 = (bf16[3,64,512]{2,1,0:T(8,128)(2,1)S(1)}, bf16[3,64,512]{2,1,0:T(8,128)(2,1)S(1)}, u32[]{:S(2)}, u32[]{:S(2)}) collective-permute-start(bf16[3,64,512]{2,1,0:T(8,128)(2,1)S(1)} %collective-permute-done.16.rest_0_), channel_id=1, source_target_pairs={{0,1},{1,0},{2,3},{3,2},{4,5},{5,4},{6,7},{7,6},{8,9},{9,8},{10,11... | collective-permute-start | bytes 589832 | tf_op jit(solution)/shard_map/ppermute | solution.py:443
  104.8 11.7 %collective-permute-start.26 = (bf16[3,64,512]{2,1,0:T(8,128)(2,1)S(1)}, bf16[3,64,512]{2,1,0:T(8,128)(2,1)S(1)}, u32[]{:S(2)}, u32[]{:S(2)}) collective-permute-start(bf16[3,64,512]{2,1,0:T(8,128)(2,1)S(1)} %collective-permute-done.22.rest_3_), channel_id=1, source_target_pairs={{0,1},{1,0},{2,3},{3,2},{4,5},{5,4},{6,7},{7,6},{8,9},{9,8},{10,11... | collective-permute-start | bytes 589832 | tf_op jit(solution)/shard_map/ppermute | solution.py:443
  109.9 6.6 %collective-permute-start.25 = (bf16[3,64,512]{2,1,0:T(8,128)(2,1)S(1)}, bf16[3,64,512]{2,1,0:T(8,128)(2,1)S(1)}, u32[]{:S(2)}, u32[]{:S(2)}) collective-permute-start(bf16[3,64,512]{2,1,0:T(8,128)(2,1)S(1)} %collective-permute-done.20.rest_2_), channel_id=1, source_target_pairs={{0,1},{1,0},{2,3},{3,2},{4,5},{5,4},{6,7},{7,6},{8,9},{9,8},{10,11... | collective-permute-start | bytes 589832 | tf_op jit(solution)/shard_map/ppermute | solution.py:443
  113.8 2.7 %collective-permute-start.24 = (bf16[3,64,512]{2,1,0:T(8,128)(2,1)S(1)}, bf16[3,64,512]{2,1,0:T(8,128)(2,1)S(1)}, u32[]{:S(2)}, u32[]{:S(2)}) collective-permute-start(bf16[3,64,512]{2,1,0:T(8,128)(2,1)S(1)} %collective-permute-done.18.rest_1_), channel_id=1, source_target_pairs={{0,1},{1,0},{2,3},{3,2},{4,5},{5,4},{6,7},{7,6},{8,9},{9,8},{10,11... | collective-permute-start | bytes 589832 | tf_op jit(solution)/shard_map/ppermute | solution.py:443

commit v7 on v6

--- a/solution.py
+++ b/solution.py
@@ -359,51 +359,50 @@
                 full[pl.ds(pl.multiple_of(kind * HD + at, rows), rows), :] = some[d][kind]
 
 
-def read(q, att, full, out):
+def read(qn, att, full, out, head, work, sems):
+    column = pl.ds(pl.multiple_of(head * HD, HD), HD)
+    copies = []
     for c in range(2):
         rows = pl.ds(c * HALF, HALF)
-        qn = rms(q[rows, :])
-        hg = mm_t(qn, full[0:HD, :])
-        hu = mm_t(qn, full[HD : 2 * HD, :])
+        x = qn(rows)
+        hg = mm_t(x, full[0:HD, :])
+        hu = mm_t(x, full[HD : 2 * HD, :])
         g = (hg * jax.nn.sigmoid(hg) * hu).astype(BF)
         fast = mm_t(g, full[2 * HD : 3 * HD, :])
-        out[rows, :] = (att[rows, :].astype(F32) + fast).astype(BF)
-
-
-def write_head(head, work, out, sem):
-    column = pl.ds(pl.multiple_of(head * HD, HD), HD)
-    copy = pltpu.make_async_copy(work, out.at[:, column], sem)
-    copy.start()
-    copy.wait()
+        work[rows, :] = (att[rows, :].astype(F32) + fast).astype(BF)
+        copy = pltpu.make_async_copy(work.at[rows, :], out.at[rows, column], sems.at[c])
+        copy.start()
+        copies.append(copy)
+    for copy in copies:
+        copy.wait()
 
 
 def read_own_kernel(zs, where, *rest):
-    pieces, (q, att, out, full, work, sem) = rest[: 2 * zs], rest[2 * zs :]
+    pieces, (q, att, q_rest, out, full, qn_rest, work, sems) = rest[: 2 * zs], rest[2 * zs :]
     gather(zs, where, pieces, 3, full)
-    read(q, att, full, work)
-    write_head(where[0], work, out, sem)
-
-
-def read_own(zs, where, pieces, q, att):
+    qn_rest[...] = rms(q_rest[...])
+    read(lambda rows: rms(q[rows, :]), att, full, out, where[0], work, sems)
+
+
+def read_own(zs, where, pieces, q, att, q_rest):
     return pl.pallas_call(
         functools.partial(read_own_kernel, zs),
-        in_specs=[SM] + [VM] * (2 * zs + 2),
-        out_specs=[pl.BlockSpec(memory_space=pl.ANY), VM],
-        out_shape=[shape((BLK, H * HD)), shape((3 * HD, HD))],
-        scratch_shapes=[pltpu.VMEM((BLK, HD), BF), pltpu.SemaphoreType.DMA],
+        in_specs=[SM] + [VM] * (2 * zs + 3),
+        out_specs=[pl.BlockSpec(memory_space=pl.ANY), VM, VM],
+        out_shape=[shape((BLK, H * HD)), shape((3 * HD, HD)), shape((BLK, HD))],
+        scratch_shapes=[pltpu.VMEM((BLK, HD), BF), pltpu.SemaphoreType.DMA((2,))],
         compiler_params=PARAMS,
         name="read_own",
-    )(where, *pieces, q, att)
+    )(where, *pieces, q, att, q_rest)
 
 
 def read_other_kernel(zs, count, where, *rest):
-    pieces, (q, att, mine, half_filled, out, weights, full, work, sem) = (
+    pieces, (qn, att, mine, half_filled, out, weights, full, work, sems) = (
         rest[: 2 * zs],
         rest[2 * zs :],
     )
     y, core, z = where[0], where[1], where[2]
     gather(zs, where, pieces, 3, full)
-    read(q, att, full, work)
     step = math.gcd(count, HD)
     first = ((z * 2 + y) * 2 + core) * count
     for c in range(count // step):
@@ -412,10 +411,10 @@
         at = lax.div(r, 2 * HD) * HD + lax.rem(r, HD)
         rows = pl.ds(pl.multiple_of(at, step), step)
         weights[c * step : (c + 1) * step, :] = jnp.where(head == y, mine[rows, :], full[rows, :])
-    write_head(1 - y, work, out, sem)
-
-
-def read_other(zs, where, count, pieces, q, att, mine, half_filled):
+    read(lambda rows: qn[rows, :], att, full, out, 1 - y, work, sems)
+
+
+def read_other(zs, where, count, pieces, qn, att, mine, half_filled):
     anyspec = pl.BlockSpec(memory_space=pl.ANY)
     return pl.pallas_call(
         functools.partial(read_other_kernel, zs, count),
@@ -425,12 +424,12 @@
         scratch_shapes=[
             pltpu.VMEM((3 * HD, HD), BF),
             pltpu.VMEM((BLK, HD), BF),
-            pltpu.SemaphoreType.DMA,
+            pltpu.SemaphoreType.DMA((2,)),
         ],
         input_output_aliases={2 * zs + 4: 0},
         compiler_params=PARAMS,
         name="read_other",
-    )(where, *pieces, q, att, mine, half_filled)
+    )(where, *pieces, qn, att, mine, half_filled)
 
 
 def local(queries, key_rows, value_rows, step_rates, w_gate, w_up, w_down):
@@ -516,14 +515,35 @@
     piece = call(functools.partial(update_kernel, zs), "update", [shape((3, rows, HD))])(
         where, own_sum, *got, wg, wu, wd
     )[0]
-    pieces = [piece] + [shift(piece, d) for d in range(1, zs)]
-    others = [swap(p, "y") for p in pieces]
-    pieces2 = [swap(p, "core") for p in pieces]
-    others2 = [swap(p, "core") for p in others]
-    half_filled, full = read_own(zs, where, pieces + pieces2, q_own, att_own)
+    order = [zs - 1, *range(1, zs - 1)]
+    pieces = {0: piece} | {d: shift(piece, d) for d in order}
+    others = {0: swap(piece, "y")}
+    last = 0
+    for d in order:
+        if d == order[-1]:
+            pieces[d], pieces[last] = lax.optimization_barrier((pieces[d], pieces[last]))
+        elif d != order[0]:
+            pieces[d], others[last] = lax.optimization_barrier((pieces[d], others[last]))
+        others[d] = swap(pieces[d], "y")
+        last = d
+    final = order[-1]
+    soon = [0, *order[:-1]]
+    gate = (pieces[final], others[soon[-1]])
+    arrived = after([pieces[d] for d in soon], gate)
+    pieces2 = {d: swap(p, "core") for d, p in zip(soon, arrived, strict=True)}
+    pieces2[final] = swap(after(pieces[final], gate), "core")
+    arrived = after([others[d] for d in soon], gate)
+    others2 = {d: swap(p, "core") for d, p in zip(soon, arrived, strict=True)}
+    listed = lambda some: [some[d] for d in range(zs)]
+    half_filled, full, qn_rest = read_own(
+        zs, where, listed(pieces) + listed(pieces2), q_own, att_own, q_rest
+    )
+    others2[final] = swap(after(others[final], full), "core")
     count = 3 * H * HD // (4 * zs)
     return tuple(
-        read_other(zs, where, count, others + others2, q_rest, att_back, full, half_filled)
+        read_other(
+            zs, where, count, listed(others) + listed(others2), qn_rest, att_back, full, half_filled
+        )
     )
 
 

time: 120 us -> 120 us (level)
  the two profiles are of different devices: /device:TPU:0 before, /device:TPU:13 now
where the time goes in v7:
time: 120 us
  starting transfers between devices  41 us (34%)
  waiting for transfers between devices  39.1 us (33%)
  Pallas kernels  36.4 us (30%)
  other arithmetic  1.76 us (1%)
    ppermute x23, starting transfers between devices, swap(): return lax.ppermute(value, axis, SWAP)  28.6 us
    ppermute x8, waiting for transfers between devices, shift(): lax.ppermute(value, 'z', [(i, (i + d) % zs) for i in range(zs) if ring or...  28.5 us
    pallas_call x10, Pallas kernels, run(): pl.pallas_call(kernel, in_specs=[SM] + [VM] * len(args), out_specs=[VM] *...  22.3 us
    ppermute x8, starting transfers between devices, shift(): lax.ppermute(value, 'z', [(i, (i + d) % zs) for i in range(zs) if ring or...  12.4 us
    ppermute x23, waiting for transfers between devices, swap(): return lax.ppermute(value, axis, SWAP)  10.6 us
    pallas_call x3, Pallas kernels, pack(): pl.pallas_call(functools.partial(pack_kernel, first, count, own), in_spec...  6.52 us
    pallas_call x1, Pallas kernels, read_other(): pl.pallas_call(functools.partial(read_other_kernel, zs, count), in_specs=...  3.27 us
    pallas_call x1, Pallas kernels, read_own(): pl.pallas_call(functools.partial(read_own_kernel, zs), in_specs=[SM] + [V...  2.64 us
  transfers between devices with their start and end apart: 31, of which 16 were waited for; matrix products, arithmetic and copies ran while one was open for 1% of the time, Pallas kernels for 23%

profile of v7, /device:TPU:13, one launch (start us, length us, event | category | flops | bytes accessed | tf_op | source)
XLA Modules:
  0.0 119.6 jit_solution(14478894893859415544)
XLA Ops:
  0.7 2.4 %pack.3 = bf16[256,1024]{1,0:T(8,128)(2,1)} custom-call(s32[3]{0:T(128)S(1)} %pad_add_fusion.where, bf16[512,1024]{1,0:T(8,128)(2,1)} %key.3, bf16[512,1024]{1,0:T(8,128)(2,1)} %value.5), custom_call_target="tpu_custom_call" | custom-call | tf_op jit(solution)/shard_map/pack/pallas_call | solution.py:105
  3.4 2.4 %pack.4 = bf16[256,1024]{1,0:T(8,128)(2,1)} custom-call(s32[3]{0:T(128)S(1)} %pad_add_fusion.where, bf16[512,1024]{1,0:T(8,128)(2,1)} %key.3, bf16[512,1024]{1,0:T(8,128)(2,1)} %value.5), custom_call_target="tpu_custom_call" | custom-call | tf_op jit(solution)/shard_map/pack/pallas_call | solution.py:105
  5.8 1.3 %collective-permute-start.1 = (bf16[256,1024]{1,0:T(8,128)(2,1)}, bf16[256,1024]{1,0:T(8,128)(2,1)S(1)}, u32[]{:S(2)}, u32[]{:S(2)}) collective-permute-start(bf16[256,1024]{1,0:T(8,128)(2,1)} %pack.4), channel_id=1, source_target_pairs={{0,2},{2,0},{1,3},{3,1},{4,6},{6,4},{5,7},{7,5},{8,10},{10,8},{9,1... | collective-permute-start | bytes 1572872 | tf_op jit(solution)/shard_map/ppermute | solution.py:442
  7.1 1.8 %pack.5.own = bf16[512,1024]{1,0:T(8,128)(2,1)S(1)} custom-call(s32[3]{0:T(128)S(1)} %pad_add_fusion.where, bf16[512,1024]{1,0:T(8,128)(2,1)} %key.3, bf16[512,1024]{1,0:T(8,128)(2,1)} %value.5), custom_call_target="tpu_custom_call" | custom-call | tf_op jit(solution)/shard_map/pack/pallas_call | solution.py:105
  8.9 1.3 %collective-permute-start.2 = (bf16[512,1024]{1,0:T(8,128)(2,1)S(1)}, bf16[512,1024]{1,0:T(8,128)(2,1)S(1)}, u32[]{:S(2)}, u32[]{:S(2)}) collective-permute-start(bf16[512,1024]{1,0:T(8,128)(2,1)S(1)} %pack.5.own), channel_id=1, source_target_pairs={{0,1},{1,0},{2,3},{3,2},{4,5},{5,4},{6,7},{7,6},{8,9},{9,8},{10,11... | collective-permute-start | bytes 3145736 | tf_op jit(solution)/shard_map/ppermute | solution.py:442
  10.2 1.6 %pack_q.1 = bf16[528,512]{1,0:T(8,128)(2,1)S(1)} custom-call(s32[3]{0:T(128)S(1)} %pad_add_fusion.where, bf16[512,1024]{1,0:T(8,128)(2,1)} %query, f32[2,512]{1,0:T(2,128)S(1)} %copy-done), custom_call_target="tpu_custom_call" | custom-call | tf_op jit(solution)/shard_map/pack_q/pallas_call | solution.py:74
  11.8 1.5 %slice_select_fusion = (bf16[512,512]{1,0:T(8,128)(2,1)S(1)}, bf16[512,512]{1,0:T(8,128)(2,1)S(1)}) fusion(bf16[1024,512]{1,0:T(8,128)(2,1)S(1)} %copy-done.2, pred[]{:T(512)S(6)} %eq.2, bf16[1024,512]{1,0:T(8,128)(2,1)} %param.12), kind=kLoop, calls=%fused_computation | loop fusion | flops 524288 | bytes 3145729 | tf_op jit(solution)/shard_map/jit(_where)/select_n | solution.py:464
  13.8 2.3 %collective-permute-done.foreign.rest_0_.for_a = bf16[256,1024]{1,0:T(8,128)(2,1)S(1)} collective-permute-done((bf16[256,1024]{1,0:T(8,128)(2,1)}, bf16[256,1024]{1,0:T(8,128)(2,1)S(1)}, u32[]{:S(2)}, u32[]{:S(2)}) %collective-permute-start) | collective-permute-done | bytes 524320 | tf_op jit(solution)/shard_map/ppermute | solution.py:442
  16.2 0.6 pick.2
  16.8 2.8 %collective-permute-start.3 = (bf16[256,1024]{1,0:T(8,128)(2,1)S(1)}, bf16[256,1024]{1,0:T(8,128)(2,1)S(1)}, u32[]{:S(2)}, u32[]{:S(2)}) collective-permute-start(bf16[256,1024]{1,0:T(8,128)(2,1)S(1)} %collective-permute-done.foreign.rest_0_.for_a), channel_id=1, source_target_pairs={{0,1},{1,0},{2,3},{3,2},{4,5},{5,4},{6,7},{7,6},{8,9},{9,8},{10,11... | collective-permute-start | bytes 1572872 | tf_op jit(solution)/shard_map/ppermute | solution.py:442
  19.8 3.2 %collective-permute-start.5 = (bf16[256,1024]{1,0:T(8,128)(2,1)S(1)}, bf16[256,1024]{1,0:T(8,128)(2,1)S(1)}, u32[]{:S(2)}, u32[]{:S(2)}) collective-permute-start(bf16[256,1024]{1,0:T(8,128)(2,1)S(1)} %pick.2), channel_id=1, source_target_pairs={{0,4},{4,8},{8,12},{1,5},{5,9},{9,13},{2,6},{6,10},{10,14},{3,7},{... | collective-permute-start | bytes 1572872 | tf_op jit(solution)/shard_map/ppermute | solution.py:445
  23.0 3.7 %pre_own.1 = (bf16[512,512]{1,0:T(8,128)(2,1)S(1)}, bf16[512,512]{1,0:T(8,128)(2,1)S(1)}, f32[512,256]{1,0:T(8,128)S(1)}, f32[512,256]{1,0:T(8,128)S(1)}, bf16[5...) custom-call(s32[3]{0:T(128)S(1)} %pad_add_fusion.where, ...), custom_call_target="tpu_custom_call" | custom-call | tf_op jit(solution)/shard_map/pre_own/pallas_call | solution.py:55
  26.7 0.7 collective-permute-done.1.foreign.rest_1_.for_b
  27.4 0.6 pick.3
  28.0 2.8 %collective-permute-start.4 = (bf16[256,1024]{1,0:T(8,128)(2,1)S(1)}, bf16[256,1024]{1,0:T(8,128)(2,1)S(1)}, u32[]{:S(2)}, u32[]{:S(2)}) collective-permute-start(bf16[256,1024]{1,0:T(8,128)(2,1)S(1)} %collective-permute-done.1.foreign.rest_1_.for_b), channel_id=1, source_target_pairs={{0,1},{1,0},{2,3},{3,2},{4,5},{5,4},{6,7},{7,6},{8,9},{9,8},{10,11... | collective-permute-start | bytes 1572872 | tf_op jit(solution)/shard_map/ppermute | solution.py:442
  30.8 3.2 %collective-permute-start.7 = (bf16[256,1024]{1,0:T(8,128)(2,1)S(1)}, bf16[256,1024]{1,0:T(8,128)(2,1)S(1)}, u32[]{:S(2)}, u32[]{:S(2)}) collective-permute-start(bf16[256,1024]{1,0:T(8,128)(2,1)S(1)} %pick.3), channel_id=1, source_target_pairs={{0,4},{4,8},{8,12},{1,5},{5,9},{9,13},{2,6},{6,10},{10,14},{3,7},{... | collective-permute-start | bytes 1572872 | tf_op jit(solution)/shard_map/ppermute | solution.py:445
  34.0 2.6 %pre.2 = (bf16[512,512]{1,0:T(8,128)(2,1)S(1)}, bf16[512,512]{1,0:T(8,128)(2,1)S(1)}, f32[512,256]{1,0:T(8,128)S(1)}, f32[512,256]{1,0:T(8,128)S(1)}, bf16[512,5...) custom-call(s32[3]{0:T(128)S(1)} %pad_add_fusion.where, ...), custom_call_target="tpu_custom_call" | custom-call | tf_op jit(solution)/shard_map/pre/pallas_call | solution.py:55
  36.6 2.4 %collective-permute-done.6.q_for = bf16[528,512]{1,0:T(8,128)(2,1)S(1)} collective-permute-done((bf16[528,512]{1,0:T(8,128)(2,1)S(1)}, bf16[528,512]{1,0:T(8,128)(2,1)S(1)}, u32[]{:S(2)}, u32[]{:S(2)}) %collective-permute-start.6) | collective-permute-done | bytes 540704 | tf_op jit(solution)/shard_map/ppermute | solution.py:442
  39.0 2.8 %pre.3 = (bf16[512,512]{1,0:T(8,128)(2,1)S(1)}, bf16[512,512]{1,0:T(8,128)(2,1)S(1)}, f32[512,256]{1,0:T(8,128)S(1)}, f32[512,256]{1,0:T(8,128)S(1)}, bf16[512,5...) custom-call(s32[3]{0:T(128)S(1)} %pad_add_fusion.where, ...), custom_call_target="tpu_custom_call" | custom-call | tf_op jit(solution)/shard_map/pre/pallas_call | solution.py:55
  41.8 3.3 %attend_upper.1 = (bf16[512,512]{1,0:T(8,128)(2,1)S(1)}, bf16[512,512]{1,0:T(8,128)(2,1)S(1)}, bf16[512,1024]{1,0:T(8,128)(2,1)S(1)}, bf16[512,1024]{1,0:T(8,128)(2,1)S(1)}) custom-call(s32[3]{0:T(128)S(1)} %pad_add_fusion.where, bf16[512,512]{1,0:T(8,128)(2,1)S(1)} %get-tuple-element.98.q_own.rest_8_, bf16[528,512]{1,0:T(8,128)(2,1)S(1)} %collective-permute-done.6.q_for, ...), custom_call_target="tpu_custom_call" | custom-call | tf_op jit(solution)/shard_map/attend_upper/pallas_call | solution.py:55
  45.1 1.5 %collective-permute-done.7.halo_b = bf16[256,1024]{1,0:T(8,128)(2,1)S(1)} collective-permute-done((bf16[256,1024]{1,0:T(8,128)(2,1)S(1)}, bf16[256,1024]{1,0:T(8,128)(2,1)S(1)}, u32[]{:S(2)}, u32[]{:S(2)}) %collective-permute-start.7) | collective-permute-done | bytes 524320 | tf_op jit(solution)/shard_map/ppermute | solution.py:445
  46.6 0.6 collective-permute-start.8
  47.7 1.0 collective-permute-done.8.halo2_a
  48.8 0.7 collective-permute-done.9.halo2_b
  49.5 3.2 %attend_lower.1 = (bf16[512,512]{1,0:T(8,128)(2,1)S(1)}, bf16[512,512]{1,0:T(8,128)(2,1)S(1)}, bf16[512,512]{1,0:T(8,128)(2,1)S(1)}) custom-call(s32[3]{0:T(128)S(1)} %pad_add_fusion.where, bf16[512,512]{1,0:T(8,128)(2,1)S(1)} %get-tuple-element.98.q_own.rest_8_, bf16[528,512]{1,0:T(8,128)(2,1)S(1)} %collective-permute-done.6.q_for, f32[2,512]{1,0:T(2,128)S(1)} %copy-done, ...), custom_call_target="tpu_custom_call" | custom-call | tf_op jit(solution)/shard_map/attend_lower/pallas_call | solution.py:55
  53.2 2.3 %grad_first.1.before = f32[3,256,512]{2,1,0:T(8,128)S(1)} custom-call(s32[3]{0:T(128)S(1)} %pad_add_fusion.where, bf16[512,512]{1,0:T(8,128)(2,1)S(1)} %get-tuple-element.155.e0, bf16[512,512]{1,0:T(8,128)(2,1)S(1)} %collective-permute-done.11.e1, bf16[512,512]{1,0:T(8,128)(2,1)S(1)} %get-tuple-element.156.k0, bf16[512,512]{1,0:T(8,128)(2,1)S(1)} %get-tuple-element.157.k1, ...), custom_call_target="tpu_custom_call" | custom-call | tf_op jit(solution)/shard_map/grad_first/pallas_call | solution.py:55
  55.5 2.5 %grad_second.1 = (f32[3,64,512]{2,1,0:T(8,128)S(1)}, bf16[3,64,512]{2,1,0:T(8,128)(2,1)S(1)}, bf16[3,64,512]{2,1,0:T(8,128)(2,1)S(1)}, bf16[3,64,512]{2,1,0:T(8,128)(2,1)S(1)}) custom-call(s32[3]{0:T(128)S(1)} %pad_add_fusion.where, bf16[512,512]{1,0:T(8,128)(2,1)S(1)} %get-tuple-element.145.e0, bf16[512,512]{1,0:T(8,128)(2,1)S(1)} %collective-permute-done.10.e1, ...), custom_call_target="tpu_custom_call" | custom-call | tf_op jit(solution)/shard_map/grad_second/pallas_call | solution.py:55
  58.0 1.3 %collective-permute-start.15 = (bf16[512,512]{1,0:T(8,128)(2,1)S(1)}, bf16[512,512]{1,0:T(8,128)(2,1)S(1)}, u32[]{:S(2)}, u32[]{:S(2)}) collective-permute-start(bf16[512,512]{1,0:T(8,128)(2,1)S(1)} %get-tuple-element.169), channel_id=1, source_target_pairs={{0,2},{2,0},{1,3},{3,1},{4,6},{6,4},{5,7},{7,5},{8,10},{10,8},{9,1... | collective-permute-start | bytes 1572872 | tf_op jit(solution)/shard_map/ppermute | solution.py:442
  59.3 1.3 %collective-permute-start.12 = (bf16[3,64,512]{2,1,0:T(8,128)(2,1)S(1)}, bf16[3,64,512]{2,1,0:T(8,128)(2,1)S(1)}, u32[]{:S(2)}, u32[]{:S(2)}) collective-permute-start(bf16[3,64,512]{2,1,0:T(8,128)(2,1)S(1)} %get-tuple-element.165), channel_id=1, source_target_pairs={{0,4},{4,8},{8,12},{12,0},{1,5},{5,9},{9,13},{13,1},{2,6},{6,10},{... | collective-permute-start | bytes 589832 | tf_op jit(solution)/shard_map/ppermute | solution.py:445
  60.6 1.0 collective-permute-start.13
  61.6 1.5 %collective-permute-start.14 = (bf16[3,64,512]{2,1,0:T(8,128)(2,1)S(1)}, bf16[3,64,512]{2,1,0:T(8,128)(2,1)S(1)}, u32[]{:S(2)}, u32[]{:S(2)}) collective-permute-start(bf16[3,64,512]{2,1,0:T(8,128)(2,1)S(1)} %get-tuple-element.167), channel_id=1, source_target_pairs={{0,12},{4,0},{8,4},{12,8},{1,13},{5,1},{9,5},{13,9},{2,14},{6,2},{... | collective-permute-start | bytes 589832 | tf_op jit(solution)/shard_map/ppermute | solution.py:445
  63.0 2.3 %collective-permute-done.12.rest_0_ = bf16[3,64,512]{2,1,0:T(8,128)(2,1)S(1)} collective-permute-done((bf16[3,64,512]{2,1,0:T(8,128)(2,1)S(1)}, bf16[3,64,512]{2,1,0:T(8,128)(2,1)S(1)}, u32[]{:S(2)}, u32[]{:S(2)}) %collective-permute-start.12) | collective-permute-done | bytes 196640 | tf_op jit(solution)/shard_map/ppermute | solution.py:445
  65.3 11.7 %collective-permute-done.13.rest_1_ = bf16[3,64,512]{2,1,0:T(8,128)(2,1)S(1)} collective-permute-done((bf16[3,64,512]{2,1,0:T(8,128)(2,1)S(1)}, bf16[3,64,512]{2,1,0:T(8,128)(2,1)S(1)}, u32[]{:S(2)}, u32[]{:S(2)}) %collective-permute-start.13) | collective-permute-done | bytes 196640 | tf_op jit(solution)/shard_map/ppermute | solution.py:445
  77.0 2.6 %collective-permute-done.14.rest_2_ = bf16[3,64,512]{2,1,0:T(8,128)(2,1)S(1)} collective-permute-done((bf16[3,64,512]{2,1,0:T(8,128)(2,1)S(1)}, bf16[3,64,512]{2,1,0:T(8,128)(2,1)S(1)}, u32[]{:S(2)}, u32[]{:S(2)}) %collective-permute-start.14) | collective-permute-done | bytes 196640 | tf_op jit(solution)/shard_map/ppermute | solution.py:445
  79.6 0.8 update.1.rest_0_
  80.5 1.5 %collective-permute-start.17 = (bf16[3,64,512]{2,1,0:T(8,128)(2,1)S(1)}, bf16[3,64,512]{2,1,0:T(8,128)(2,1)S(1)}, u32[]{:S(2)}, u32[]{:S(2)}) collective-permute-start(bf16[3,64,512]{2,1,0:T(8,128)(2,1)S(1)} %update.1.rest_0_), channel_id=1, source_target_pairs={{0,4},{4,8},{8,12},{12,0},{1,5},{5,9},{9,13},{13,1},{2,6},{6,10},{... | collective-permute-start | bytes 589832 | tf_op jit(solution)/shard_map/ppermute | solution.py:445
  81.9 5.4 %collective-permute-done.18.rest_3_ = bf16[3,64,512]{2,1,0:T(8,128)(2,1)S(1)} collective-permute-done((bf16[3,64,512]{2,1,0:T(8,128)(2,1)S(1)}, bf16[3,64,512]{2,1,0:T(8,128)(2,1)S(1)}, u32[]{:S(2)}, u32[]{:S(2)}) %collective-permute-start.18) | collective-permute-done | bytes 196640 | tf_op jit(solution)/shard_map/ppermute | solution.py:445
  87.6 0.7 collective-permute-start.21
  88.2 3.6 %collective-permute-done.17.rest_1_ = bf16[3,64,512]{2,1,0:T(8,128)(2,1)S(1)} collective-permute-done((bf16[3,64,512]{2,1,0:T(8,128)(2,1)S(1)}, bf16[3,64,512]{2,1,0:T(8,128)(2,1)S(1)}, u32[]{:S(2)}, u32[]{:S(2)}) %collective-permute-start.17) | collective-permute-done | bytes 196640 | tf_op jit(solution)/shard_map/ppermute | solution.py:445
  92.4 1.2 %collective-permute-start.16 = (bf16[3,64,512]{2,1,0:T(8,128)(2,1)S(1)}, bf16[3,64,512]{2,1,0:T(8,128)(2,1)S(1)}, u32[]{:S(2)}, u32[]{:S(2)}) collective-permute-start(bf16[3,64,512]{2,1,0:T(8,128)(2,1)S(1)} %update.1.rest_0_), channel_id=1, source_target_pairs={{0,2},{2,0},{1,3},{3,1},{4,6},{6,4},{5,7},{7,5},{8,10},{10,8},{9,1... | collective-permute-start | bytes 589832 | tf_op jit(solution)/shard_map/ppermute | solution.py:442
  93.6 1.4 %collective-permute-done.21.rest_2_ = bf16[3,64,512]{2,1,0:T(8,128)(2,1)S(1)} collective-permute-done((bf16[3,64,512]{2,1,0:T(8,128)(2,1)S(1)}, bf16[3,64,512]{2,1,0:T(8,128)(2,1)S(1)}, u32[]{:S(2)}, u32[]{:S(2)}) %collective-permute-start.21) | collective-permute-done | bytes 196640 | tf_op jit(solution)/shard_map/ppermute | solution.py:445
  95.0 1.6 %collective-permute-done.20.rest_1_ = bf16[3,64,512]{2,1,0:T(8,128)(2,1)S(1)} collective-permute-done((bf16[3,64,512]{2,1,0:T(8,128)(2,1)S(1)}, bf16[3,64,512]{2,1,0:T(8,128)(2,1)S(1)}, u32[]{:S(2)}, u32[]{:S(2)}) %collective-permute-start.20) | collective-permute-done | bytes 196640 | tf_op jit(solution)/shard_map/ppermute | solution.py:442
  96.7 10.6 %collective-permute-start.25 = (bf16[3,64,512]{2,1,0:T(8,128)(2,1)S(1)}, bf16[3,64,512]{2,1,0:T(8,128)(2,1)S(1)}, u32[]{:S(2)}, u32[]{:S(2)}) collective-permute-start(bf16[3,64,512]{2,1,0:T(8,128)(2,1)S(1)} %update.1.rest_0_), channel_id=1, source_target_pairs={{0,1},{1,0},{2,3},{3,2},{4,5},{5,4},{6,7},{7,6},{8,9},{9,8},{10,11... | collective-permute-start | bytes 589832 | tf_op jit(solution)/shard_map/ppermute | solution.py:442
  108.3 1.5 %collective-permute-start.23 = (bf16[3,64,512]{2,1,0:T(8,128)(2,1)S(1)}, bf16[3,64,512]{2,1,0:T(8,128)(2,1)S(1)}, u32[]{:S(2)}, u32[]{:S(2)}) collective-permute-start(bf16[3,64,512]{2,1,0:T(8,128)(2,1)S(1)} %collective-permute-done.16.rest_0_), channel_id=1, source_target_pairs={{0,1},{1,0},{2,3},{3,2},{4,5},{5,4},{6,7},{7,6},{8,9},{9,8},{10,11... | collective-permute-start | bytes 589832 | tf_op jit(solution)/shard_map/ppermute | solution.py:442
  110.4 2.6 %read_own.1 = (bf16[512,1024]{1,0:T(8,128)(2,1)}, bf16[1536,512]{1,0:T(8,128)(2,1)S(1)}, bf16[512,512]{1,0:T(8,128)(2,1)S(1)}) custom-call(s32[3]{0:T(128)S(1)} %pad_add_fusion.where, bf16[3,64,512]{2,1,0:T(8,128)(2,1)S(1)} %update.1.rest_0_, bf16[3,64,512]{2,1,0:T(8,128)(2,1)S(1)} %collective-permute-done.17.rest_1_, ...), custom_call_target="tpu_custom_call" | custom-call | tf_op jit(solution)/shard_map/read_own/pallas_call | solution.py:388
  113.0 2.0 %collective-permute-start.29 = (bf16[3,64,512]{2,1,0:T(8,128)(2,1)S(1)}, bf16[3,64,512]{2,1,0:T(8,128)(2,1)S(1)}, u32[]{:S(2)}, u32[]{:S(2)}) collective-permute-start(bf16[3,64,512]{2,1,0:T(8,128)(2,1)S(1)} %collective-permute-done.22.rest_2_), channel_id=1, source_target_pairs={{0,1},{1,0},{2,3},{3,2},{4,5},{5,4},{6,7},{7,6},{8,9},{9,8},{10,11... | collective-permute-start | bytes 589832 | tf_op jit(solution)/shard_map/ppermute | solution.py:442
  115.1 1.1 collective-permute-done.29.rest_6_
  116.1 3.3 %read_other.1 = (bf16[512,1024]{1,0:T(8,128)(2,1)}, bf16[192,512]{1,0:T(8,128)(2,1)}) custom-call(s32[3]{0:T(128)S(1)} %pad_add_fusion.where, bf16[3,64,512]{2,1,0:T(8,128)(2,1)S(1)} %collective-permute-done.16.rest_0_, bf16[3,64,512]{2,1,0:T(8,128)(2,1)S(1)} %collective-permute-done.20.rest_1_, ...), custom_call_target="tpu_custom_call", output_to_operand_aliasing={{0}: (12, {})} | custom-call | tf_op jit(solution)/shard_map/read_other/pallas_call | solution.py:419
  (41 shorter events, 4.5 us)
Async XLA Ops:
  3.1 13.1 %collective-permute-start = (bf16[256,1024]{1,0:T(8,128)(2,1)}, bf16[256,1024]{1,0:T(8,128)(2,1)S(1)}, u32[]{:S(2)}, u32[]{:S(2)}) collective-permute-start(bf16[256,1024]{1,0:T(8,128)(2,1)} %pack.3), channel_id=1, source_target_pairs={{0,2},{2,0},{1,3},{3,1},{4,6},{6,4},{5,7},{7,5},{8,10},{10,8},{9,1... | collective-permute-start | bytes 1572872 | tf_op jit(solution)/shard_map/ppermute | solution.py:442
  5.8 4.4 %copy-start = (f32[2,512]{1,0:T(2,128)S(1)}, f32[2,512]{1,0:T(2,128)}, u32[]{:S(2)}) copy-start(f32[2,512]{1,0:T(2,128)} %rates.5) | copy-start | bytes 12292
  5.8 21.6 %collective-permute-start.1 = (bf16[256,1024]{1,0:T(8,128)(2,1)}, bf16[256,1024]{1,0:T(8,128)(2,1)S(1)}, u32[]{:S(2)}, u32[]{:S(2)}) collective-permute-start(bf16[256,1024]{1,0:T(8,128)(2,1)} %pack.4), channel_id=1, source_target_pairs={{0,2},{2,0},{1,3},{3,1},{4,6},{6,4},{5,7},{7,5},{8,10},{10,8},{9,1... | collective-permute-start | bytes 1572872 | tf_op jit(solution)/shard_map/ppermute | solution.py:442
  8.9 14.1 %collective-permute-start.2 = (bf16[512,1024]{1,0:T(8,128)(2,1)S(1)}, bf16[512,1024]{1,0:T(8,128)(2,1)S(1)}, u32[]{:S(2)}, u32[]{:S(2)}) collective-permute-start(bf16[512,1024]{1,0:T(8,128)(2,1)S(1)} %pack.5.own), channel_id=1, source_target_pairs={{0,1},{1,0},{2,3},{3,2},{4,5},{5,4},{6,7},{7,6},{8,9},{9,8},{10,11... | collective-permute-start | bytes 3145736 | tf_op jit(solution)/shard_map/ppermute | solution.py:442
  10.2 1.6 %copy-start.2 = (bf16[1024,512]{1,0:T(8,128)(2,1)S(1)}, bf16[1024,512]{1,0:T(8,128)(2,1)}, u32[]{:S(2)}) copy-start(bf16[1024,512]{1,0:T(8,128)(2,1)} %param.13) | copy-start | bytes 3145732
  11.8 1.5 %copy-start.1 = (bf16[512,1024]{1,0:T(8,128)(2,1)S(1)}, bf16[512,1024]{1,0:T(8,128)(2,1)}, u32[]{:S(2)}) copy-start(bf16[512,1024]{1,0:T(8,128)(2,1)} %query) | copy-start | bytes 3145732
  11.8 1.8 %copy-start.3 = (bf16[1024,512]{1,0:T(8,128)(2,1)S(1)}, bf16[1024,512]{1,0:T(8,128)(2,1)}, u32[]{:S(2)}) copy-start(bf16[1024,512]{1,0:T(8,128)(2,1)} %param.11) | copy-start | bytes 3145732
  16.8 10.6 %collective-permute-start.3 = (bf16[256,1024]{1,0:T(8,128)(2,1)S(1)}, bf16[256,1024]{1,0:T(8,128)(2,1)S(1)}, u32[]{:S(2)}, u32[]{:S(2)}) collective-permute-start(bf16[256,1024]{1,0:T(8,128)(2,1)S(1)} %collective-permute-done.foreign.rest_0_.for_a), channel_id=1, source_target_pairs={{0,1},{1,0},{2,3},{3,2},{4,5},{5,4},{6,7},{7,6},{8,9},{9,8},{10,11... | collective-permute-start | bytes 1572872 | tf_op jit(solution)/shard_map/ppermute | solution.py:442
  19.5 19.5 %collective-permute-start.6 = (bf16[528,512]{1,0:T(8,128)(2,1)S(1)}, bf16[528,512]{1,0:T(8,128)(2,1)S(1)}, u32[]{:S(2)}, u32[]{:S(2)}) collective-permute-start(bf16[528,512]{1,0:T(8,128)(2,1)S(1)} %pack_q.1), channel_id=1, source_target_pairs={{0,2},{2,0},{1,3},{3,1},{4,6},{6,4},{5,7},{7,5},{8,10},{10,8},{9,1... | collective-permute-start | bytes 1622024 | tf_op jit(solution)/shard_map/ppermute | solution.py:442
  19.8 16.8 %collective-permute-start.5 = (bf16[256,1024]{1,0:T(8,128)(2,1)S(1)}, bf16[256,1024]{1,0:T(8,128)(2,1)S(1)}, u32[]{:S(2)}, u32[]{:S(2)}) collective-permute-start(bf16[256,1024]{1,0:T(8,128)(2,1)S(1)} %pick.2), channel_id=1, source_target_pairs={{0,4},{4,8},{8,12},{1,5},{5,9},{9,13},{2,6},{6,10},{10,14},{3,7},{... | collective-permute-start | bytes 1572872 | tf_op jit(solution)/shard_map/ppermute | solution.py:445
  28.0 8.6 %collective-permute-start.4 = (bf16[256,1024]{1,0:T(8,128)(2,1)S(1)}, bf16[256,1024]{1,0:T(8,128)(2,1)S(1)}, u32[]{:S(2)}, u32[]{:S(2)}) collective-permute-start(bf16[256,1024]{1,0:T(8,128)(2,1)S(1)} %collective-permute-done.1.foreign.rest_1_.for_b), channel_id=1, source_target_pairs={{0,1},{1,0},{2,3},{3,2},{4,5},{5,4},{6,7},{7,6},{8,9},{9,8},{10,11... | collective-permute-start | bytes 1572872 | tf_op jit(solution)/shard_map/ppermute | solution.py:442
  30.8 15.8 %collective-permute-start.7 = (bf16[256,1024]{1,0:T(8,128)(2,1)S(1)}, bf16[256,1024]{1,0:T(8,128)(2,1)S(1)}, u32[]{:S(2)}, u32[]{:S(2)}) collective-permute-start(bf16[256,1024]{1,0:T(8,128)(2,1)S(1)} %pick.3), channel_id=1, source_target_pairs={{0,4},{4,8},{8,12},{1,5},{5,9},{9,13},{2,6},{6,10},{10,14},{3,7},{... | collective-permute-start | bytes 1572872 | tf_op jit(solution)/shard_map/ppermute | solution.py:445
  46.6 2.2 %collective-permute-start.8 = (bf16[256,1024]{1,0:T(8,128)(2,1)S(1)}, bf16[256,1024]{1,0:T(8,128)(2,1)S(1)}, u32[]{:S(2)}, u32[]{:S(2)}) collective-permute-start(bf16[256,1024]{1,0:T(8,128)(2,1)S(1)} %collective-permute-done.5.halo_a), channel_id=1, source_target_pairs={{0,1},{1,0},{2,3},{3,2},{4,5},{5,4},{6,7},{7,6},{8,9},{9,8},{10,11... | collective-permute-start | bytes 1572872 | tf_op jit(solution)/shard_map/ppermute | solution.py:442
  47.2 2.3 %collective-permute-start.9 = (bf16[256,1024]{1,0:T(8,128)(2,1)S(1)}, bf16[256,1024]{1,0:T(8,128)(2,1)S(1)}, u32[]{:S(2)}, u32[]{:S(2)}) collective-permute-start(bf16[256,1024]{1,0:T(8,128)(2,1)S(1)} %collective-permute-done.7.halo_b), channel_id=1, source_target_pairs={{0,1},{1,0},{2,3},{3,2},{4,5},{5,4},{6,7},{7,6},{8,9},{9,8},{10,11... | collective-permute-start | bytes 1572872 | tf_op jit(solution)/shard_map/ppermute | solution.py:442
  47.2 6.0 %collective-permute-start.11 = (bf16[512,512]{1,0:T(8,128)(2,1)S(1)}, bf16[512,512]{1,0:T(8,128)(2,1)S(1)}, u32[]{:S(2)}, u32[]{:S(2)}) collective-permute-start(bf16[512,512]{1,0:T(8,128)(2,1)S(1)} %get-tuple-element.155.e0), channel_id=1, source_target_pairs={{0,1},{1,0},{2,3},{3,2},{4,5},{5,4},{6,7},{7,6},{8,9},{9,8},{10,11... | collective-permute-start | bytes 1572872 | tf_op jit(solution)/shard_map/ppermute | solution.py:442
  52.8 2.7 %collective-permute-start.10 = (bf16[512,512]{1,0:T(8,128)(2,1)S(1)}, bf16[512,512]{1,0:T(8,128)(2,1)S(1)}, u32[]{:S(2)}, u32[]{:S(2)}) collective-permute-start(bf16[512,512]{1,0:T(8,128)(2,1)S(1)} %get-tuple-element.145.e0), channel_id=1, source_target_pairs={{0,1},{1,0},{2,3},{3,2},{4,5},{5,4},{6,7},{7,6},{8,9},{9,8},{10,11... | collective-permute-start | bytes 1572872 | tf_op jit(solution)/shard_map/ppermute | solution.py:442
  58.0 21.7 %collective-permute-start.15 = (bf16[512,512]{1,0:T(8,128)(2,1)S(1)}, bf16[512,512]{1,0:T(8,128)(2,1)S(1)}, u32[]{:S(2)}, u32[]{:S(2)}) collective-permute-start(bf16[512,512]{1,0:T(8,128)(2,1)S(1)} %get-tuple-element.169), channel_id=1, source_target_pairs={{0,2},{2,0},{1,3},{3,1},{4,6},{6,4},{5,7},{7,5},{8,10},{10,8},{9,1... | collective-permute-start | bytes 1572872 | tf_op jit(solution)/shard_map/ppermute | solution.py:442
  59.3 6.0 %collective-permute-start.12 = (bf16[3,64,512]{2,1,0:T(8,128)(2,1)S(1)}, bf16[3,64,512]{2,1,0:T(8,128)(2,1)S(1)}, u32[]{:S(2)}, u32[]{:S(2)}) collective-permute-start(bf16[3,64,512]{2,1,0:T(8,128)(2,1)S(1)} %get-tuple-element.165), channel_id=1, source_target_pairs={{0,4},{4,8},{8,12},{12,0},{1,5},{5,9},{9,13},{13,1},{2,6},{6,10},{... | collective-permute-start | bytes 589832 | tf_op jit(solution)/shard_map/ppermute | solution.py:445
  60.6 16.5 %collective-permute-start.13 = (bf16[3,64,512]{2,1,0:T(8,128)(2,1)S(1)}, bf16[3,64,512]{2,1,0:T(8,128)(2,1)S(1)}, u32[]{:S(2)}, u32[]{:S(2)}) collective-permute-start(bf16[3,64,512]{2,1,0:T(8,128)(2,1)S(1)} %get-tuple-element.166), channel_id=1, source_target_pairs={{0,8},{4,12},{8,0},{12,4},{1,9},{5,13},{9,1},{13,5},{2,10},{6,14},... | collective-permute-start | bytes 589832 | tf_op jit(solution)/shard_map/ppermute | solution.py:445
  61.6 18.0 %collective-permute-start.14 = (bf16[3,64,512]{2,1,0:T(8,128)(2,1)S(1)}, bf16[3,64,512]{2,1,0:T(8,128)(2,1)S(1)}, u32[]{:S(2)}, u32[]{:S(2)}) collective-permute-start(bf16[3,64,512]{2,1,0:T(8,128)(2,1)S(1)} %get-tuple-element.167), channel_id=1, source_target_pairs={{0,12},{4,0},{8,4},{12,8},{1,13},{5,1},{9,5},{13,9},{2,14},{6,2},{... | collective-permute-start | bytes 589832 | tf_op jit(solution)/shard_map/ppermute | solution.py:445
  80.4 6.9 %collective-permute-start.18 = (bf16[3,64,512]{2,1,0:T(8,128)(2,1)S(1)}, bf16[3,64,512]{2,1,0:T(8,128)(2,1)S(1)}, u32[]{:S(2)}, u32[]{:S(2)}) collective-permute-start(bf16[3,64,512]{2,1,0:T(8,128)(2,1)S(1)} %update.1.rest_0_), channel_id=1, source_target_pairs={{0,12},{4,0},{8,4},{12,8},{1,13},{5,1},{9,5},{13,9},{2,14},{6,2},{... | collective-permute-start | bytes 589832 | tf_op jit(solution)/shard_map/ppermute | solution.py:445
  80.5 11.4 %collective-permute-start.17 = (bf16[3,64,512]{2,1,0:T(8,128)(2,1)S(1)}, bf16[3,64,512]{2,1,0:T(8,128)(2,1)S(1)}, u32[]{:S(2)}, u32[]{:S(2)}) collective-permute-start(bf16[3,64,512]{2,1,0:T(8,128)(2,1)S(1)} %update.1.rest_0_), channel_id=1, source_target_pairs={{0,4},{4,8},{8,12},{12,0},{1,5},{5,9},{9,13},{13,1},{2,6},{6,10},{... | collective-permute-start | bytes 589832 | tf_op jit(solution)/shard_map/ppermute | solution.py:445
  87.3 4.8 %collective-permute-start.19 = (bf16[3,64,512]{2,1,0:T(8,128)(2,1)S(1)}, bf16[3,64,512]{2,1,0:T(8,128)(2,1)S(1)}, u32[]{:S(2)}, u32[]{:S(2)}) collective-permute-start(bf16[3,64,512]{2,1,0:T(8,128)(2,1)S(1)} %collective-permute-done.18.rest_3_), channel_id=1, source_target_pairs={{0,2},{2,0},{1,3},{3,1},{4,6},{6,4},{5,7},{7,5},{8,10},{10,8},{9,1... | collective-permute-start | bytes 589832 | tf_op jit(solution)/shard_map/ppermute | solution.py:442
  87.6 7.5 %collective-permute-start.21 = (bf16[3,64,512]{2,1,0:T(8,128)(2,1)S(1)}, bf16[3,64,512]{2,1,0:T(8,128)(2,1)S(1)}, u32[]{:S(2)}, u32[]{:S(2)}) collective-permute-start(bf16[3,64,512]{2,1,0:T(8,128)(2,1)S(1)} %update.1.rest_0_), channel_id=1, source_target_pairs={{0,8},{4,12},{8,0},{12,4},{1,9},{5,13},{9,1},{13,5},{2,10},{6,14},... | collective-permute-start | bytes 589832 | tf_op jit(solution)/shard_map/ppermute | solution.py:445
  92.1 4.5 %collective-permute-start.20 = (bf16[3,64,512]{2,1,0:T(8,128)(2,1)S(1)}, bf16[3,64,512]{2,1,0:T(8,128)(2,1)S(1)}, u32[]{:S(2)}, u32[]{:S(2)}) collective-permute-start(bf16[3,64,512]{2,1,0:T(8,128)(2,1)S(1)} %collective-permute-done.17.rest_1_), channel_id=1, source_target_pairs={{0,2},{2,0},{1,3},{3,1},{4,6},{6,4},{5,7},{7,5},{8,10},{10,8},{9,1... | collective-permute-start | bytes 589832 | tf_op jit(solution)/shard_map/ppermute | solution.py:442
  92.4 15.4 %collective-permute-start.16 = (bf16[3,64,512]{2,1,0:T(8,128)(2,1)S(1)}, bf16[3,64,512]{2,1,0:T(8,128)(2,1)S(1)}, u32[]{:S(2)}, u32[]{:S(2)}) collective-permute-start(bf16[3,64,512]{2,1,0:T(8,128)(2,1)S(1)} %update.1.rest_0_), channel_id=1, source_target_pairs={{0,2},{2,0},{1,3},{3,1},{4,6},{6,4},{5,7},{7,5},{8,10},{10,8},{9,1... | collective-permute-start | bytes 589832 | tf_op jit(solution)/shard_map/ppermute | solution.py:442
  96.7 11.6 %collective-permute-start.25 = (bf16[3,64,512]{2,1,0:T(8,128)(2,1)S(1)}, bf16[3,64,512]{2,1,0:T(8,128)(2,1)S(1)}, u32[]{:S(2)}, u32[]{:S(2)}) collective-permute-start(bf16[3,64,512]{2,1,0:T(8,128)(2,1)S(1)} %update.1.rest_0_), channel_id=1, source_target_pairs={{0,1},{1,0},{2,3},{3,2},{4,5},{5,4},{6,7},{7,6},{8,9},{9,8},{10,11... | collective-permute-start | bytes 589832 | tf_op jit(solution)/shard_map/ppermute | solution.py:442
  107.2 2.6 %collective-permute-start.26 = (bf16[3,64,512]{2,1,0:T(8,128)(2,1)S(1)}, bf16[3,64,512]{2,1,0:T(8,128)(2,1)S(1)}, u32[]{:S(2)}, u32[]{:S(2)}) collective-permute-start(bf16[3,64,512]{2,1,0:T(8,128)(2,1)S(1)} %collective-permute-done.17.rest_1_), channel_id=1, source_target_pairs={{0,1},{1,0},{2,3},{3,2},{4,5},{5,4},{6,7},{7,6},{8,9},{9,8},{10,11... | collective-permute-start | bytes 589832 | tf_op jit(solution)/shard_map/ppermute | solution.py:442
  107.2 2.7 %collective-permute-start.28 = (bf16[3,64,512]{2,1,0:T(8,128)(2,1)S(1)}, bf16[3,64,512]{2,1,0:T(8,128)(2,1)S(1)}, u32[]{:S(2)}, u32[]{:S(2)}) collective-permute-start(bf16[3,64,512]{2,1,0:T(8,128)(2,1)S(1)} %collective-permute-done.18.rest_3_), channel_id=1, source_target_pairs={{0,1},{1,0},{2,3},{3,2},{4,5},{5,4},{6,7},{7,6},{8,9},{9,8},{10,11... | collective-permute-start | bytes 589832 | tf_op jit(solution)/shard_map/ppermute | solution.py:442
  107.7 2.6 %collective-permute-start.27 = (bf16[3,64,512]{2,1,0:T(8,128)(2,1)S(1)}, bf16[3,64,512]{2,1,0:T(8,128)(2,1)S(1)}, u32[]{:S(2)}, u32[]{:S(2)}) collective-permute-start(bf16[3,64,512]{2,1,0:T(8,128)(2,1)S(1)} %collective-permute-done.21.rest_2_), channel_id=1, source_target_pairs={{0,1},{1,0},{2,3},{3,2},{4,5},{5,4},{6,7},{7,6},{8,9},{9,8},{10,11... | collective-permute-start | bytes 589832 | tf_op jit(solution)/shard_map/ppermute | solution.py:442
  107.8 5.3 %collective-permute-start.22 = (bf16[3,64,512]{2,1,0:T(8,128)(2,1)S(1)}, bf16[3,64,512]{2,1,0:T(8,128)(2,1)S(1)}, u32[]{:S(2)}, u32[]{:S(2)}) collective-permute-start(bf16[3,64,512]{2,1,0:T(8,128)(2,1)S(1)} %collective-permute-done.21.rest_2_), channel_id=1, source_target_pairs={{0,2},{2,0},{1,3},{3,1},{4,6},{6,4},{5,7},{7,5},{8,10},{10,8},{9,1... | collective-permute-start | bytes 589832 | tf_op jit(solution)/shard_map/ppermute | solution.py:442
  108.3 6.8 %collective-permute-start.23 = (bf16[3,64,512]{2,1,0:T(8,128)(2,1)S(1)}, bf16[3,64,512]{2,1,0:T(8,128)(2,1)S(1)}, u32[]{:S(2)}, u32[]{:S(2)}) collective-permute-start(bf16[3,64,512]{2,1,0:T(8,128)(2,1)S(1)} %collective-permute-done.16.rest_0_), channel_id=1, source_target_pairs={{0,1},{1,0},{2,3},{3,2},{4,5},{5,4},{6,7},{7,6},{8,9},{9,8},{10,11... | collective-permute-start | bytes 589832 | tf_op jit(solution)/shard_map/ppermute | solution.py:442
  109.9 5.2 %collective-permute-start.24 = (bf16[3,64,512]{2,1,0:T(8,128)(2,1)S(1)}, bf16[3,64,512]{2,1,0:T(8,128)(2,1)S(1)}, u32[]{:S(2)}, u32[]{:S(2)}) collective-permute-start(bf16[3,64,512]{2,1,0:T(8,128)(2,1)S(1)} %collective-permute-done.20.rest_1_), channel_id=1, source_target_pairs={{0,1},{1,0},{2,3},{3,2},{4,5},{5,4},{6,7},{7,6},{8,9},{9,8},{10,11... | collective-permute-start | bytes 589832 | tf_op jit(solution)/shard_map/ppermute | solution.py:442
  109.9 5.2 %collective-permute-start.30 = (bf16[3,64,512]{2,1,0:T(8,128)(2,1)S(1)}, bf16[3,64,512]{2,1,0:T(8,128)(2,1)S(1)}, u32[]{:S(2)}, u32[]{:S(2)}) collective-permute-start(bf16[3,64,512]{2,1,0:T(8,128)(2,1)S(1)} %collective-permute-done.19.rest_3_), channel_id=1, source_target_pairs={{0,1},{1,0},{2,3},{3,2},{4,5},{5,4},{6,7},{7,6},{8,9},{9,8},{10,11... | collective-permute-start | bytes 589832 | tf_op jit(solution)/shard_map/ppermute | solution.py:442
  113.0 3.1 %collective-permute-start.29 = (bf16[3,64,512]{2,1,0:T(8,128)(2,1)S(1)}, bf16[3,64,512]{2,1,0:T(8,128)(2,1)S(1)}, u32[]{:S(2)}, u32[]{:S(2)}) collective-permute-start(bf16[3,64,512]{2,1,0:T(8,128)(2,1)S(1)} %collective-permute-done.22.rest_2_), channel_id=1, source_target_pairs={{0,1},{1,0},{2,3},{3,2},{4,5},{5,4},{6,7},{7,6},{8,9},{9,8},{10,11... | collective-permute-start | bytes 589832 | tf_op jit(solution)/shard_map/ppermute | solution.py:442

commit v8 on v7

--- a/solution.py
+++ b/solution.py
@@ -515,34 +515,20 @@
     piece = call(functools.partial(update_kernel, zs), "update", [shape((3, rows, HD))])(
         where, own_sum, *got, wg, wu, wd
     )[0]
-    order = [zs - 1, *range(1, zs - 1)]
-    pieces = {0: piece} | {d: shift(piece, d) for d in order}
-    others = {0: swap(piece, "y")}
-    last = 0
-    for d in order:
-        if d == order[-1]:
-            pieces[d], pieces[last] = lax.optimization_barrier((pieces[d], pieces[last]))
-        elif d != order[0]:
-            pieces[d], others[last] = lax.optimization_barrier((pieces[d], others[last]))
-        others[d] = swap(pieces[d], "y")
-        last = d
-    final = order[-1]
-    soon = [0, *order[:-1]]
-    gate = (pieces[final], others[soon[-1]])
-    arrived = after([pieces[d] for d in soon], gate)
-    pieces2 = {d: swap(p, "core") for d, p in zip(soon, arrived, strict=True)}
-    pieces2[final] = swap(after(pieces[final], gate), "core")
-    arrived = after([others[d] for d in soon], gate)
-    others2 = {d: swap(p, "core") for d, p in zip(soon, arrived, strict=True)}
-    listed = lambda some: [some[d] for d in range(zs)]
-    half_filled, full, qn_rest = read_own(
-        zs, where, listed(pieces) + listed(pieces2), q_own, att_own, q_rest
-    )
-    others2[final] = swap(after(others[final], full), "core")
+    order = [*range(2, zs - 1), 1, zs - 1]
+    pieces = {d: shift(piece, d) for d in order}
+    pieces = [piece] + [pieces[d] for d in range(1, zs)]
+    others = {d: swap(pieces[d], "y") for d in [*order, 0]}
+    others = [others[d] for d in range(zs)]
+    gate = [*pieces[1:], others[0], others[zs - 1], others[1]]
+    pieces2 = [swap(after(p, gate), "core") for p in pieces]
+    pieces2, others = lax.optimization_barrier((pieces2, others))
+    others2 = [swap(p, "core") for d, p in enumerate(others)]
+    half_filled, full, qn_rest = read_own(zs, where, pieces + pieces2, q_own, att_own, q_rest)
     count = 3 * H * HD // (4 * zs)
     return tuple(
         read_other(
-            zs, where, count, listed(others) + listed(others2), qn_rest, att_back, full, half_filled
+            zs, where, count, others + others2, qn_rest, att_back, full, half_filled
         )
     )
 

time: 120 us -> 116 us (0.967)
  the two profiles are of different devices: /device:TPU:13 before, /device:TPU:0 now
where the time goes in v8:
time: 116 us; the launch traced here: 115 us
  waiting for transfers between devices  40.3 us (35%)
  Pallas kernels  36.4 us (31%)
  starting transfers between devices  35.5 us (31%)
  other arithmetic  1.76 us (2%)
    ppermute x8, waiting for transfers between devices, shift(): lax.ppermute(value, 'z', [(i, (i + d) % zs) for i in range(zs) if ring or...  25.2 us
    pallas_call x10, Pallas kernels, run(): pl.pallas_call(kernel, in_specs=[SM] + [VM] * len(args), out_specs=[VM] *...  22.3 us
    ppermute x8, starting transfers between devices, shift(): lax.ppermute(value, 'z', [(i, (i + d) % zs) for i in range(zs) if ring or...  20.2 us
    ppermute x23, starting transfers between devices, swap(): return lax.ppermute(value, axis, SWAP)  15.3 us
    ppermute x23, waiting for transfers between devices, swap(): return lax.ppermute(value, axis, SWAP)  15.1 us
    pallas_call x3, Pallas kernels, pack(): pl.pallas_call(functools.partial(pack_kernel, first, count, own), in_spec...  6.52 us
    pallas_call x1, Pallas kernels, read_other(): pl.pallas_call(functools.partial(read_other_kernel, zs, count), in_specs=...  3.28 us
    pallas_call x1, Pallas kernels, read_own(): pl.pallas_call(functools.partial(read_own_kernel, zs), in_specs=[SM] + [V...  2.64 us
  transfers between devices with their start and end apart: 31, of which 12 were waited for; matrix products, arithmetic and copies ran while one was open for 1% of the time, Pallas kernels for 24%

profile of v8, /device:TPU:0, one launch (start us, length us, event | category | flops | bytes accessed | tf_op | source)
XLA Modules:
  0.0 115.5 jit_solution(15340803204415547944)
XLA Ops:
  0.7 2.4 %pack.3 = bf16[256,1024]{1,0:T(8,128)(2,1)} custom-call(s32[3]{0:T(128)S(1)} %pad_add_fusion.where, bf16[512,1024]{1,0:T(8,128)(2,1)} %key.3, bf16[512,1024]{1,0:T(8,128)(2,1)} %value.5), custom_call_target="tpu_custom_call" | custom-call | tf_op jit(solution)/shard_map/pack/pallas_call | solution.py:105
  3.1 3.0 %collective-permute-start = (bf16[256,1024]{1,0:T(8,128)(2,1)}, bf16[256,1024]{1,0:T(8,128)(2,1)S(1)}, u32[]{:S(2)}, u32[]{:S(2)}) collective-permute-start(bf16[256,1024]{1,0:T(8,128)(2,1)} %pack.3), channel_id=1, source_target_pairs={{0,2},{2,0},{1,3},{3,1},{4,6},{6,4},{5,7},{7,5},{8,10},{10,8},{9,1... | collective-permute-start | bytes 1572872 | tf_op jit(solution)/shard_map/ppermute | solution.py:442
  6.1 2.4 %pack.4 = bf16[256,1024]{1,0:T(8,128)(2,1)} custom-call(s32[3]{0:T(128)S(1)} %pad_add_fusion.where, bf16[512,1024]{1,0:T(8,128)(2,1)} %key.3, bf16[512,1024]{1,0:T(8,128)(2,1)} %value.5), custom_call_target="tpu_custom_call" | custom-call | tf_op jit(solution)/shard_map/pack/pallas_call | solution.py:105
  8.6 1.8 %pack.5.own = bf16[512,1024]{1,0:T(8,128)(2,1)S(1)} custom-call(s32[3]{0:T(128)S(1)} %pad_add_fusion.where, bf16[512,1024]{1,0:T(8,128)(2,1)} %key.3, bf16[512,1024]{1,0:T(8,128)(2,1)} %value.5), custom_call_target="tpu_custom_call" | custom-call | tf_op jit(solution)/shard_map/pack/pallas_call | solution.py:105
  10.5 1.6 %pack_q.1 = bf16[528,512]{1,0:T(8,128)(2,1)S(1)} custom-call(s32[3]{0:T(128)S(1)} %pad_add_fusion.where, bf16[512,1024]{1,0:T(8,128)(2,1)} %query, f32[2,512]{1,0:T(2,128)S(1)} %copy-done), custom_call_target="tpu_custom_call" | custom-call | tf_op jit(solution)/shard_map/pack_q/pallas_call | solution.py:74
  12.2 1.5 %slice_select_fusion = (bf16[512,512]{1,0:T(8,128)(2,1)S(1)}, bf16[512,512]{1,0:T(8,128)(2,1)S(1)}) fusion(bf16[1024,512]{1,0:T(8,128)(2,1)S(1)} %copy-done.2, pred[]{:T(512)S(6)} %eq.2, bf16[1024,512]{1,0:T(8,128)(2,1)} %param.12), kind=kLoop, calls=%fused_computation | loop fusion | flops 524288 | bytes 3145729 | tf_op jit(solution)/shard_map/jit(_where)/select_n | solution.py:464
  14.2 4.9 %collective-permute-done.foreign.rest_0_.for_a = bf16[256,1024]{1,0:T(8,128)(2,1)S(1)} collective-permute-done((bf16[256,1024]{1,0:T(8,128)(2,1)}, bf16[256,1024]{1,0:T(8,128)(2,1)S(1)}, u32[]{:S(2)}, u32[]{:S(2)}) %collective-permute-start) | collective-permute-done | bytes 524320 | tf_op jit(solution)/shard_map/ppermute | solution.py:442
  19.1 0.6 pick.2
  19.8 2.1 %collective-permute-start.6 = (bf16[528,512]{1,0:T(8,128)(2,1)S(1)}, bf16[528,512]{1,0:T(8,128)(2,1)S(1)}, u32[]{:S(2)}, u32[]{:S(2)}) collective-permute-start(bf16[528,512]{1,0:T(8,128)(2,1)S(1)} %pack_q.1), channel_id=1, source_target_pairs={{0,2},{2,0},{1,3},{3,1},{4,6},{6,4},{5,7},{7,5},{8,10},{10,8},{9,1... | collective-permute-start | bytes 1622024 | tf_op jit(solution)/shard_map/ppermute | solution.py:442
  21.9 3.5 %collective-permute-start.5 = (bf16[256,1024]{1,0:T(8,128)(2,1)S(1)}, bf16[256,1024]{1,0:T(8,128)(2,1)S(1)}, u32[]{:S(2)}, u32[]{:S(2)}) collective-permute-start(bf16[256,1024]{1,0:T(8,128)(2,1)S(1)} %pick.2), channel_id=1, source_target_pairs={{0,4},{4,8},{8,12},{1,5},{5,9},{9,13},{2,6},{6,10},{10,14},{3,7},{... | collective-permute-start | bytes 1572872 | tf_op jit(solution)/shard_map/ppermute | solution.py:445
  25.4 3.7 %pre_own.1 = (bf16[512,512]{1,0:T(8,128)(2,1)S(1)}, bf16[512,512]{1,0:T(8,128)(2,1)S(1)}, f32[512,256]{1,0:T(8,128)S(1)}, f32[512,256]{1,0:T(8,128)S(1)}, bf16[5...) custom-call(s32[3]{0:T(128)S(1)} %pad_add_fusion.where, ...), custom_call_target="tpu_custom_call" | custom-call | tf_op jit(solution)/shard_map/pre_own/pallas_call | solution.py:55
  29.1 1.2 %collective-permute-done.1.foreign.rest_1_.for_b = bf16[256,1024]{1,0:T(8,128)(2,1)S(1)} collective-permute-done((bf16[256,1024]{1,0:T(8,128)(2,1)}, bf16[256,1024]{1,0:T(8,128)(2,1)S(1)}, u32[]{:S(2)}, u32[]{:S(2)}) %collective-permute-start.1) | collective-permute-done | bytes 524320 | tf_op jit(solution)/shard_map/ppermute | solution.py:442
  30.3 0.6 pick.3
  31.0 4.1 %collective-permute-start.7 = (bf16[256,1024]{1,0:T(8,128)(2,1)S(1)}, bf16[256,1024]{1,0:T(8,128)(2,1)S(1)}, u32[]{:S(2)}, u32[]{:S(2)}) collective-permute-start(bf16[256,1024]{1,0:T(8,128)(2,1)S(1)} %pick.3), channel_id=1, source_target_pairs={{0,4},{4,8},{8,12},{1,5},{5,9},{9,13},{2,6},{6,10},{10,14},{3,7},{... | collective-permute-start | bytes 1572872 | tf_op jit(solution)/shard_map/ppermute | solution.py:445
  35.1 2.6 %pre.2 = (bf16[512,512]{1,0:T(8,128)(2,1)S(1)}, bf16[512,512]{1,0:T(8,128)(2,1)S(1)}, f32[512,256]{1,0:T(8,128)S(1)}, f32[512,256]{1,0:T(8,128)S(1)}, bf16[512,5...) custom-call(s32[3]{0:T(128)S(1)} %pad_add_fusion.where, ...), custom_call_target="tpu_custom_call" | custom-call | tf_op jit(solution)/shard_map/pre/pallas_call | solution.py:55
  37.7 3.4 %collective-permute-done.6.q_for = bf16[528,512]{1,0:T(8,128)(2,1)S(1)} collective-permute-done((bf16[528,512]{1,0:T(8,128)(2,1)S(1)}, bf16[528,512]{1,0:T(8,128)(2,1)S(1)}, u32[]{:S(2)}, u32[]{:S(2)}) %collective-permute-start.6) | collective-permute-done | bytes 540704 | tf_op jit(solution)/shard_map/ppermute | solution.py:442
  41.1 2.8 %pre.3 = (bf16[512,512]{1,0:T(8,128)(2,1)S(1)}, bf16[512,512]{1,0:T(8,128)(2,1)S(1)}, f32[512,256]{1,0:T(8,128)S(1)}, f32[512,256]{1,0:T(8,128)S(1)}, bf16[512,5...) custom-call(s32[3]{0:T(128)S(1)} %pad_add_fusion.where, ...), custom_call_target="tpu_custom_call" | custom-call | tf_op jit(solution)/shard_map/pre/pallas_call | solution.py:55
  43.9 3.3 %attend_upper.1 = (bf16[512,512]{1,0:T(8,128)(2,1)S(1)}, bf16[512,512]{1,0:T(8,128)(2,1)S(1)}, bf16[512,1024]{1,0:T(8,128)(2,1)S(1)}, bf16[512,1024]{1,0:T(8,128)(2,1)S(1)}) custom-call(s32[3]{0:T(128)S(1)} %pad_add_fusion.where, bf16[512,512]{1,0:T(8,128)(2,1)S(1)} %get-tuple-element.98.q_own.rest_8_, bf16[528,512]{1,0:T(8,128)(2,1)S(1)} %collective-permute-done.6.q_for, ...), custom_call_target="tpu_custom_call" | custom-call | tf_op jit(solution)/shard_map/attend_upper/pallas_call | solution.py:55
  47.2 0.9 collective-permute-done.7.halo_b
  48.1 0.5 collective-permute-start.9
  48.6 1.4 %collective-permute-done.8.halo2_a = bf16[256,1024]{1,0:T(8,128)(2,1)S(1)} collective-permute-done((bf16[256,1024]{1,0:T(8,128)(2,1)S(1)}, bf16[256,1024]{1,0:T(8,128)(2,1)S(1)}, u32[]{:S(2)}, u32[]{:S(2)}) %collective-permute-start.8) | collective-permute-done | bytes 524320 | tf_op jit(solution)/shard_map/ppermute | solution.py:442
  50.0 0.7 collective-permute-done.9.halo2_b
  50.8 3.2 %attend_lower.1 = (bf16[512,512]{1,0:T(8,128)(2,1)S(1)}, bf16[512,512]{1,0:T(8,128)(2,1)S(1)}, bf16[512,512]{1,0:T(8,128)(2,1)S(1)}) custom-call(s32[3]{0:T(128)S(1)} %pad_add_fusion.where, bf16[512,512]{1,0:T(8,128)(2,1)S(1)} %get-tuple-element.98.q_own.rest_8_, bf16[528,512]{1,0:T(8,128)(2,1)S(1)} %collective-permute-done.6.q_for, f32[2,512]{1,0:T(2,128)S(1)} %copy-done, ...), custom_call_target="tpu_custom_call" | custom-call | tf_op jit(solution)/shard_map/attend_lower/pallas_call | solution.py:55
  54.2 2.3 %grad_first.1.before = f32[3,256,512]{2,1,0:T(8,128)S(1)} custom-call(s32[3]{0:T(128)S(1)} %pad_add_fusion.where, bf16[512,512]{1,0:T(8,128)(2,1)S(1)} %get-tuple-element.155.e0, bf16[512,512]{1,0:T(8,128)(2,1)S(1)} %collective-permute-done.11.e1, bf16[512,512]{1,0:T(8,128)(2,1)S(1)} %get-tuple-element.156.k0, bf16[512,512]{1,0:T(8,128)(2,1)S(1)} %get-tuple-element.157.k1, ...), custom_call_target="tpu_custom_call" | custom-call | tf_op jit(solution)/shard_map/grad_first/pallas_call | solution.py:55
  56.5 2.5 %grad_second.1 = (f32[3,64,512]{2,1,0:T(8,128)S(1)}, bf16[3,64,512]{2,1,0:T(8,128)(2,1)S(1)}, bf16[3,64,512]{2,1,0:T(8,128)(2,1)S(1)}, bf16[3,64,512]{2,1,0:T(8,128)(2,1)S(1)}) custom-call(s32[3]{0:T(128)S(1)} %pad_add_fusion.where, bf16[512,512]{1,0:T(8,128)(2,1)S(1)} %get-tuple-element.145.e0, bf16[512,512]{1,0:T(8,128)(2,1)S(1)} %collective-permute-done.10.e1, ...), custom_call_target="tpu_custom_call" | custom-call | tf_op jit(solution)/shard_map/grad_second/pallas_call | solution.py:55
  59.0 1.0 collective-permute-start.15
  60.0 2.1 %collective-permute-start.12 = (bf16[3,64,512]{2,1,0:T(8,128)(2,1)S(1)}, bf16[3,64,512]{2,1,0:T(8,128)(2,1)S(1)}, u32[]{:S(2)}, u32[]{:S(2)}) collective-permute-start(bf16[3,64,512]{2,1,0:T(8,128)(2,1)S(1)} %get-tuple-element.165), channel_id=1, source_target_pairs={{0,4},{4,8},{8,12},{12,0},{1,5},{5,9},{9,13},{13,1},{2,6},{6,10},{... | collective-permute-start | bytes 589832 | tf_op jit(solution)/shard_map/ppermute | solution.py:445
  62.0 2.6 %collective-permute-start.13 = (bf16[3,64,512]{2,1,0:T(8,128)(2,1)S(1)}, bf16[3,64,512]{2,1,0:T(8,128)(2,1)S(1)}, u32[]{:S(2)}, u32[]{:S(2)}) collective-permute-start(bf16[3,64,512]{2,1,0:T(8,128)(2,1)S(1)} %get-tuple-element.166), channel_id=1, source_target_pairs={{0,8},{4,12},{8,0},{12,4},{1,9},{5,13},{9,1},{13,5},{2,10},{6,14},... | collective-permute-start | bytes 589832 | tf_op jit(solution)/shard_map/ppermute | solution.py:445
  64.7 1.3 %collective-permute-start.14 = (bf16[3,64,512]{2,1,0:T(8,128)(2,1)S(1)}, bf16[3,64,512]{2,1,0:T(8,128)(2,1)S(1)}, u32[]{:S(2)}, u32[]{:S(2)}) collective-permute-start(bf16[3,64,512]{2,1,0:T(8,128)(2,1)S(1)} %get-tuple-element.167), channel_id=1, source_target_pairs={{0,12},{4,0},{8,4},{12,8},{1,13},{5,1},{9,5},{13,9},{2,14},{6,2},{... | collective-permute-start | bytes 589832 | tf_op jit(solution)/shard_map/ppermute | solution.py:445
  66.0 3.9 %collective-permute-done.12.rest_0_ = bf16[3,64,512]{2,1,0:T(8,128)(2,1)S(1)} collective-permute-done((bf16[3,64,512]{2,1,0:T(8,128)(2,1)S(1)}, bf16[3,64,512]{2,1,0:T(8,128)(2,1)S(1)}, u32[]{:S(2)}, u32[]{:S(2)}) %collective-permute-start.12) | collective-permute-done | bytes 196640 | tf_op jit(solution)/shard_map/ppermute | solution.py:445
  69.9 7.9 %collective-permute-done.13.rest_1_ = bf16[3,64,512]{2,1,0:T(8,128)(2,1)S(1)} collective-permute-done((bf16[3,64,512]{2,1,0:T(8,128)(2,1)S(1)}, bf16[3,64,512]{2,1,0:T(8,128)(2,1)S(1)}, u32[]{:S(2)}, u32[]{:S(2)}) %collective-permute-start.13) | collective-permute-done | bytes 196640 | tf_op jit(solution)/shard_map/ppermute | solution.py:445
  77.8 0.8 update.1.rest_0_
  78.6 5.8 %collective-permute-start.18 = (bf16[3,64,512]{2,1,0:T(8,128)(2,1)S(1)}, bf16[3,64,512]{2,1,0:T(8,128)(2,1)S(1)}, u32[]{:S(2)}, u32[]{:S(2)}) collective-permute-start(bf16[3,64,512]{2,1,0:T(8,128)(2,1)S(1)} %update.1.rest_0_), channel_id=1, source_target_pairs={{0,12},{4,0},{8,4},{12,8},{1,13},{5,1},{9,5},{13,9},{2,14},{6,2},{... | collective-permute-start | bytes 589832 | tf_op jit(solution)/shard_map/ppermute | solution.py:445
  84.4 1.5 %collective-permute-start.19 = (bf16[3,64,512]{2,1,0:T(8,128)(2,1)S(1)}, bf16[3,64,512]{2,1,0:T(8,128)(2,1)S(1)}, u32[]{:S(2)}, u32[]{:S(2)}) collective-permute-start(bf16[3,64,512]{2,1,0:T(8,128)(2,1)S(1)} %update.1.rest_0_), channel_id=1, source_target_pairs={{0,2},{2,0},{1,3},{3,1},{4,6},{6,4},{5,7},{7,5},{8,10},{10,8},{9,1... | collective-permute-start | bytes 589832 | tf_op jit(solution)/shard_map/ppermute | solution.py:442
  85.9 0.8 collective-permute-start.17
  86.7 3.0 %collective-permute-done.18.rest_3_ = bf16[3,64,512]{2,1,0:T(8,128)(2,1)S(1)} collective-permute-done((bf16[3,64,512]{2,1,0:T(8,128)(2,1)S(1)}, bf16[3,64,512]{2,1,0:T(8,128)(2,1)S(1)}, u32[]{:S(2)}, u32[]{:S(2)}) %collective-permute-start.18) | collective-permute-done | bytes 196640 | tf_op jit(solution)/shard_map/ppermute | solution.py:445
  89.7 1.5 %collective-permute-start.20 = (bf16[3,64,512]{2,1,0:T(8,128)(2,1)S(1)}, bf16[3,64,512]{2,1,0:T(8,128)(2,1)S(1)}, u32[]{:S(2)}, u32[]{:S(2)}) collective-permute-start(bf16[3,64,512]{2,1,0:T(8,128)(2,1)S(1)} %collective-permute-done.18.rest_3_), channel_id=1, source_target_pairs={{0,2},{2,0},{1,3},{3,1},{4,6},{6,4},{5,7},{7,5},{8,10},{10,8},{9,1... | collective-permute-start | bytes 589832 | tf_op jit(solution)/shard_map/ppermute | solution.py:442
  91.2 2.9 %collective-permute-done.16.rest_1_ = bf16[3,64,512]{2,1,0:T(8,128)(2,1)S(1)} collective-permute-done((bf16[3,64,512]{2,1,0:T(8,128)(2,1)S(1)}, bf16[3,64,512]{2,1,0:T(8,128)(2,1)S(1)}, u32[]{:S(2)}, u32[]{:S(2)}) %collective-permute-start.16) | collective-permute-done | bytes 196640 | tf_op jit(solution)/shard_map/ppermute | solution.py:445
  94.1 1.5 %collective-permute-start.21 = (bf16[3,64,512]{2,1,0:T(8,128)(2,1)S(1)}, bf16[3,64,512]{2,1,0:T(8,128)(2,1)S(1)}, u32[]{:S(2)}, u32[]{:S(2)}) collective-permute-start(bf16[3,64,512]{2,1,0:T(8,128)(2,1)S(1)} %collective-permute-done.16.rest_1_), channel_id=1, source_target_pairs={{0,2},{2,0},{1,3},{3,1},{4,6},{6,4},{5,7},{7,5},{8,10},{10,8},{9,1... | collective-permute-start | bytes 589832 | tf_op jit(solution)/shard_map/ppermute | solution.py:442
  95.6 6.6 %collective-permute-done.17.rest_2_ = bf16[3,64,512]{2,1,0:T(8,128)(2,1)S(1)} collective-permute-done((bf16[3,64,512]{2,1,0:T(8,128)(2,1)S(1)}, bf16[3,64,512]{2,1,0:T(8,128)(2,1)S(1)}, u32[]{:S(2)}, u32[]{:S(2)}) %collective-permute-start.17) | collective-permute-done | bytes 196640 | tf_op jit(solution)/shard_map/ppermute | solution.py:445
  102.2 1.5 %collective-permute-start.26 = (bf16[3,64,512]{2,1,0:T(8,128)(2,1)S(1)}, bf16[3,64,512]{2,1,0:T(8,128)(2,1)S(1)}, u32[]{:S(2)}, u32[]{:S(2)}) collective-permute-start(bf16[3,64,512]{2,1,0:T(8,128)(2,1)S(1)} %collective-permute-done.17.rest_2_), channel_id=1, source_target_pairs={{0,2},{2,0},{1,3},{3,1},{4,6},{6,4},{5,7},{7,5},{8,10},{10,8},{9,1... | collective-permute-start | bytes 589832 | tf_op jit(solution)/shard_map/ppermute | solution.py:442
  103.8 0.5 collective-permute-start.23
  104.4 0.4 collective-permute-start.25
  104.8 3.4 %collective-permute-done.26.rest_2_ = bf16[3,64,512]{2,1,0:T(8,128)(2,1)S(1)} collective-permute-done((bf16[3,64,512]{2,1,0:T(8,128)(2,1)S(1)}, bf16[3,64,512]{2,1,0:T(8,128)(2,1)S(1)}, u32[]{:S(2)}, u32[]{:S(2)}) %collective-permute-start.26) | collective-permute-done | bytes 196640 | tf_op jit(solution)/shard_map/ppermute | solution.py:442
  108.3 0.5 collective-permute-start.28
  108.9 0.4 collective-permute-start.30
  109.3 2.6 %read_own.1 = (bf16[512,1024]{1,0:T(8,128)(2,1)}, bf16[1536,512]{1,0:T(8,128)(2,1)S(1)}, bf16[512,512]{1,0:T(8,128)(2,1)S(1)}) custom-call(s32[3]{0:T(128)S(1)} %pad_add_fusion.where, bf16[3,64,512]{2,1,0:T(8,128)(2,1)S(1)} %update.1.rest_0_, bf16[3,64,512]{2,1,0:T(8,128)(2,1)S(1)} %collective-permute-done.16.rest_1_, ...), custom_call_target="tpu_custom_call" | custom-call | tf_op jit(solution)/shard_map/read_own/pallas_call | solution.py:388
  112.0 3.3 %read_other.1 = (bf16[512,1024]{1,0:T(8,128)(2,1)}, bf16[192,512]{1,0:T(8,128)(2,1)}) custom-call(s32[3]{0:T(128)S(1)} %pad_add_fusion.where, bf16[3,64,512]{2,1,0:T(8,128)(2,1)S(1)} %collective-permute-done.19.rest_0_, bf16[3,64,512]{2,1,0:T(8,128)(2,1)S(1)} %collective-permute-done.21.rest_1_, ...), custom_call_target="tpu_custom_call", output_to_operand_aliasing={{0}: (12, {})} | custom-call | tf_op jit(solution)/shard_map/read_other/pallas_call | solution.py:419
  (41 shorter events, 1.4 us)
Async XLA Ops:
  3.1 16.0 %collective-permute-start = (bf16[256,1024]{1,0:T(8,128)(2,1)}, bf16[256,1024]{1,0:T(8,128)(2,1)S(1)}, u32[]{:S(2)}, u32[]{:S(2)}) collective-permute-start(bf16[256,1024]{1,0:T(8,128)(2,1)} %pack.3), channel_id=1, source_target_pairs={{0,2},{2,0},{1,3},{3,1},{4,6},{6,4},{5,7},{7,5},{8,10},{10,8},{9,1... | collective-permute-start | bytes 1572872 | tf_op jit(solution)/shard_map/ppermute | solution.py:442
  8.5 1.9 %copy-start = (f32[2,512]{1,0:T(2,128)S(1)}, f32[2,512]{1,0:T(2,128)}, u32[]{:S(2)}) copy-start(f32[2,512]{1,0:T(2,128)} %rates.5) | copy-start | bytes 12292
  8.5 21.8 %collective-permute-start.1 = (bf16[256,1024]{1,0:T(8,128)(2,1)}, bf16[256,1024]{1,0:T(8,128)(2,1)S(1)}, u32[]{:S(2)}, u32[]{:S(2)}) collective-permute-start(bf16[256,1024]{1,0:T(8,128)(2,1)} %pack.4), channel_id=1, source_target_pairs={{0,2},{2,0},{1,3},{3,1},{4,6},{6,4},{5,7},{7,5},{8,10},{10,8},{9,1... | collective-permute-start | bytes 1572872 | tf_op jit(solution)/shard_map/ppermute | solution.py:442
  10.4 15.0 %collective-permute-start.2 = (bf16[512,1024]{1,0:T(8,128)(2,1)S(1)}, bf16[512,1024]{1,0:T(8,128)(2,1)S(1)}, u32[]{:S(2)}, u32[]{:S(2)}) collective-permute-start(bf16[512,1024]{1,0:T(8,128)(2,1)S(1)} %pack.5.own), channel_id=1, source_target_pairs={{0,1},{1,0},{2,3},{3,2},{4,5},{5,4},{6,7},{7,6},{8,9},{9,8},{10,11... | collective-permute-start | bytes 3145736 | tf_op jit(solution)/shard_map/ppermute | solution.py:442
  10.5 1.7 %copy-start.2 = (bf16[1024,512]{1,0:T(8,128)(2,1)S(1)}, bf16[1024,512]{1,0:T(8,128)(2,1)}, u32[]{:S(2)}) copy-start(bf16[1024,512]{1,0:T(8,128)(2,1)} %param.13) | copy-start | bytes 3145732
  12.1 1.5 %copy-start.1 = (bf16[512,1024]{1,0:T(8,128)(2,1)S(1)}, bf16[512,1024]{1,0:T(8,128)(2,1)}, u32[]{:S(2)}) copy-start(bf16[512,1024]{1,0:T(8,128)(2,1)} %query) | copy-start | bytes 3145732
  12.2 1.8 %copy-start.3 = (bf16[1024,512]{1,0:T(8,128)(2,1)S(1)}, bf16[1024,512]{1,0:T(8,128)(2,1)}, u32[]{:S(2)}) copy-start(bf16[1024,512]{1,0:T(8,128)(2,1)} %param.11) | copy-start | bytes 3145732
  19.7 10.6 %collective-permute-start.3 = (bf16[256,1024]{1,0:T(8,128)(2,1)S(1)}, bf16[256,1024]{1,0:T(8,128)(2,1)S(1)}, u32[]{:S(2)}, u32[]{:S(2)}) collective-permute-start(bf16[256,1024]{1,0:T(8,128)(2,1)S(1)} %collective-permute-done.foreign.rest_0_.for_a), channel_id=1, source_target_pairs={{0,1},{1,0},{2,3},{3,2},{4,5},{5,4},{6,7},{7,6},{8,9},{9,8},{10,11... | collective-permute-start | bytes 1572872 | tf_op jit(solution)/shard_map/ppermute | solution.py:442
  19.8 21.3 %collective-permute-start.6 = (bf16[528,512]{1,0:T(8,128)(2,1)S(1)}, bf16[528,512]{1,0:T(8,128)(2,1)S(1)}, u32[]{:S(2)}, u32[]{:S(2)}) collective-permute-start(bf16[528,512]{1,0:T(8,128)(2,1)S(1)} %pack_q.1), channel_id=1, source_target_pairs={{0,2},{2,0},{1,3},{3,1},{4,6},{6,4},{5,7},{7,5},{8,10},{10,8},{9,1... | collective-permute-start | bytes 1622024 | tf_op jit(solution)/shard_map/ppermute | solution.py:442
  21.9 15.8 %collective-permute-start.5 = (bf16[256,1024]{1,0:T(8,128)(2,1)S(1)}, bf16[256,1024]{1,0:T(8,128)(2,1)S(1)}, u32[]{:S(2)}, u32[]{:S(2)}) collective-permute-start(bf16[256,1024]{1,0:T(8,128)(2,1)S(1)} %pick.2), channel_id=1, source_target_pairs={{0,4},{4,8},{8,12},{1,5},{5,9},{9,13},{2,6},{6,10},{10,14},{3,7},{... | collective-permute-start | bytes 1572872 | tf_op jit(solution)/shard_map/ppermute | solution.py:445
  30.9 6.7 %collective-permute-start.4 = (bf16[256,1024]{1,0:T(8,128)(2,1)S(1)}, bf16[256,1024]{1,0:T(8,128)(2,1)S(1)}, u32[]{:S(2)}, u32[]{:S(2)}) collective-permute-start(bf16[256,1024]{1,0:T(8,128)(2,1)S(1)} %collective-permute-done.1.foreign.rest_1_.for_b), channel_id=1, source_target_pairs={{0,1},{1,0},{2,3},{3,2},{4,5},{5,4},{6,7},{7,6},{8,9},{9,8},{10,11... | collective-permute-start | bytes 1572872 | tf_op jit(solution)/shard_map/ppermute | solution.py:442
  31.0 17.1 %collective-permute-start.7 = (bf16[256,1024]{1,0:T(8,128)(2,1)S(1)}, bf16[256,1024]{1,0:T(8,128)(2,1)S(1)}, u32[]{:S(2)}, u32[]{:S(2)}) collective-permute-start(bf16[256,1024]{1,0:T(8,128)(2,1)S(1)} %pick.3), channel_id=1, source_target_pairs={{0,4},{4,8},{8,12},{1,5},{5,9},{9,13},{2,6},{6,10},{10,14},{3,7},{... | collective-permute-start | bytes 1572872 | tf_op jit(solution)/shard_map/ppermute | solution.py:445
  48.1 1.9 %collective-permute-start.8 = (bf16[256,1024]{1,0:T(8,128)(2,1)S(1)}, bf16[256,1024]{1,0:T(8,128)(2,1)S(1)}, u32[]{:S(2)}, u32[]{:S(2)}) collective-permute-start(bf16[256,1024]{1,0:T(8,128)(2,1)S(1)} %collective-permute-done.5.halo_a), channel_id=1, source_target_pairs={{0,1},{1,0},{2,3},{3,2},{4,5},{5,4},{6,7},{7,6},{8,9},{9,8},{10,11... | collective-permute-start | bytes 1572872 | tf_op jit(solution)/shard_map/ppermute | solution.py:442
  48.1 2.7 %collective-permute-start.9 = (bf16[256,1024]{1,0:T(8,128)(2,1)S(1)}, bf16[256,1024]{1,0:T(8,128)(2,1)S(1)}, u32[]{:S(2)}, u32[]{:S(2)}) collective-permute-start(bf16[256,1024]{1,0:T(8,128)(2,1)S(1)} %collective-permute-done.7.halo_b), channel_id=1, source_target_pairs={{0,1},{1,0},{2,3},{3,2},{4,5},{5,4},{6,7},{7,6},{8,9},{9,8},{10,11... | collective-permute-start | bytes 1572872 | tf_op jit(solution)/shard_map/ppermute | solution.py:442
  48.6 5.6 %collective-permute-start.11 = (bf16[512,512]{1,0:T(8,128)(2,1)S(1)}, bf16[512,512]{1,0:T(8,128)(2,1)S(1)}, u32[]{:S(2)}, u32[]{:S(2)}) collective-permute-start(bf16[512,512]{1,0:T(8,128)(2,1)S(1)} %get-tuple-element.155.e0), channel_id=1, source_target_pairs={{0,1},{1,0},{2,3},{3,2},{4,5},{5,4},{6,7},{7,6},{8,9},{9,8},{10,11... | collective-permute-start | bytes 1572872 | tf_op jit(solution)/shard_map/ppermute | solution.py:442
  54.0 2.5 %collective-permute-start.10 = (bf16[512,512]{1,0:T(8,128)(2,1)S(1)}, bf16[512,512]{1,0:T(8,128)(2,1)S(1)}, u32[]{:S(2)}, u32[]{:S(2)}) collective-permute-start(bf16[512,512]{1,0:T(8,128)(2,1)S(1)} %get-tuple-element.145.e0), channel_id=1, source_target_pairs={{0,1},{1,0},{2,3},{3,2},{4,5},{5,4},{6,7},{7,6},{8,9},{9,8},{10,11... | collective-permute-start | bytes 1572872 | tf_op jit(solution)/shard_map/ppermute | solution.py:442
  59.0 18.8 %collective-permute-start.15 = (bf16[512,512]{1,0:T(8,128)(2,1)S(1)}, bf16[512,512]{1,0:T(8,128)(2,1)S(1)}, u32[]{:S(2)}, u32[]{:S(2)}) collective-permute-start(bf16[512,512]{1,0:T(8,128)(2,1)S(1)} %get-tuple-element.169), channel_id=1, source_target_pairs={{0,2},{2,0},{1,3},{3,1},{4,6},{6,4},{5,7},{7,5},{8,10},{10,8},{9,1... | collective-permute-start | bytes 1572872 | tf_op jit(solution)/shard_map/ppermute | solution.py:442
  60.0 10.0 %collective-permute-start.12 = (bf16[3,64,512]{2,1,0:T(8,128)(2,1)S(1)}, bf16[3,64,512]{2,1,0:T(8,128)(2,1)S(1)}, u32[]{:S(2)}, u32[]{:S(2)}) collective-permute-start(bf16[3,64,512]{2,1,0:T(8,128)(2,1)S(1)} %get-tuple-element.165), channel_id=1, source_target_pairs={{0,4},{4,8},{8,12},{12,0},{1,5},{5,9},{9,13},{13,1},{2,6},{6,10},{... | collective-permute-start | bytes 589832 | tf_op jit(solution)/shard_map/ppermute | solution.py:445
  62.0 15.8 %collective-permute-start.13 = (bf16[3,64,512]{2,1,0:T(8,128)(2,1)S(1)}, bf16[3,64,512]{2,1,0:T(8,128)(2,1)S(1)}, u32[]{:S(2)}, u32[]{:S(2)}) collective-permute-start(bf16[3,64,512]{2,1,0:T(8,128)(2,1)S(1)} %get-tuple-element.166), channel_id=1, source_target_pairs={{0,8},{4,12},{8,0},{12,4},{1,9},{5,13},{9,1},{13,5},{2,10},{6,14},... | collective-permute-start | bytes 589832 | tf_op jit(solution)/shard_map/ppermute | solution.py:445
  64.7 13.1 %collective-permute-start.14 = (bf16[3,64,512]{2,1,0:T(8,128)(2,1)S(1)}, bf16[3,64,512]{2,1,0:T(8,128)(2,1)S(1)}, u32[]{:S(2)}, u32[]{:S(2)}) collective-permute-start(bf16[3,64,512]{2,1,0:T(8,128)(2,1)S(1)} %get-tuple-element.167), channel_id=1, source_target_pairs={{0,12},{4,0},{8,4},{12,8},{1,13},{5,1},{9,5},{13,9},{2,14},{6,2},{... | collective-permute-start | bytes 589832 | tf_op jit(solution)/shard_map/ppermute | solution.py:445
  78.6 11.1 %collective-permute-start.18 = (bf16[3,64,512]{2,1,0:T(8,128)(2,1)S(1)}, bf16[3,64,512]{2,1,0:T(8,128)(2,1)S(1)}, u32[]{:S(2)}, u32[]{:S(2)}) collective-permute-start(bf16[3,64,512]{2,1,0:T(8,128)(2,1)S(1)} %update.1.rest_0_), channel_id=1, source_target_pairs={{0,12},{4,0},{8,4},{12,8},{1,13},{5,1},{9,5},{13,9},{2,14},{6,2},{... | collective-permute-start | bytes 589832 | tf_op jit(solution)/shard_map/ppermute | solution.py:445
  84.4 9.7 %collective-permute-start.16 = (bf16[3,64,512]{2,1,0:T(8,128)(2,1)S(1)}, bf16[3,64,512]{2,1,0:T(8,128)(2,1)S(1)}, u32[]{:S(2)}, u32[]{:S(2)}) collective-permute-start(bf16[3,64,512]{2,1,0:T(8,128)(2,1)S(1)} %update.1.rest_0_), channel_id=1, source_target_pairs={{0,4},{4,8},{8,12},{12,0},{1,5},{5,9},{9,13},{13,1},{2,6},{6,10},{... | collective-permute-start | bytes 589832 | tf_op jit(solution)/shard_map/ppermute | solution.py:445
  84.4 19.4 %collective-permute-start.19 = (bf16[3,64,512]{2,1,0:T(8,128)(2,1)S(1)}, bf16[3,64,512]{2,1,0:T(8,128)(2,1)S(1)}, u32[]{:S(2)}, u32[]{:S(2)}) collective-permute-start(bf16[3,64,512]{2,1,0:T(8,128)(2,1)S(1)} %update.1.rest_0_), channel_id=1, source_target_pairs={{0,2},{2,0},{1,3},{3,1},{4,6},{6,4},{5,7},{7,5},{8,10},{10,8},{9,1... | collective-permute-start | bytes 589832 | tf_op jit(solution)/shard_map/ppermute | solution.py:442
  85.9 16.4 %collective-permute-start.17 = (bf16[3,64,512]{2,1,0:T(8,128)(2,1)S(1)}, bf16[3,64,512]{2,1,0:T(8,128)(2,1)S(1)}, u32[]{:S(2)}, u32[]{:S(2)}) collective-permute-start(bf16[3,64,512]{2,1,0:T(8,128)(2,1)S(1)} %update.1.rest_0_), channel_id=1, source_target_pairs={{0,8},{4,12},{8,0},{12,4},{1,9},{5,13},{9,1},{13,5},{2,10},{6,14},... | collective-permute-start | bytes 589832 | tf_op jit(solution)/shard_map/ppermute | solution.py:445
  89.7 14.0 %collective-permute-start.20 = (bf16[3,64,512]{2,1,0:T(8,128)(2,1)S(1)}, bf16[3,64,512]{2,1,0:T(8,128)(2,1)S(1)}, u32[]{:S(2)}, u32[]{:S(2)}) collective-permute-start(bf16[3,64,512]{2,1,0:T(8,128)(2,1)S(1)} %collective-permute-done.18.rest_3_), channel_id=1, source_target_pairs={{0,2},{2,0},{1,3},{3,1},{4,6},{6,4},{5,7},{7,5},{8,10},{10,8},{9,1... | collective-permute-start | bytes 589832 | tf_op jit(solution)/shard_map/ppermute | solution.py:442
  94.1 9.6 %collective-permute-start.21 = (bf16[3,64,512]{2,1,0:T(8,128)(2,1)S(1)}, bf16[3,64,512]{2,1,0:T(8,128)(2,1)S(1)}, u32[]{:S(2)}, u32[]{:S(2)}) collective-permute-start(bf16[3,64,512]{2,1,0:T(8,128)(2,1)S(1)} %collective-permute-done.16.rest_1_), channel_id=1, source_target_pairs={{0,2},{2,0},{1,3},{3,1},{4,6},{6,4},{5,7},{7,5},{8,10},{10,8},{9,1... | collective-permute-start | bytes 589832 | tf_op jit(solution)/shard_map/ppermute | solution.py:442
  102.2 6.0 %collective-permute-start.26 = (bf16[3,64,512]{2,1,0:T(8,128)(2,1)S(1)}, bf16[3,64,512]{2,1,0:T(8,128)(2,1)S(1)}, u32[]{:S(2)}, u32[]{:S(2)}) collective-permute-start(bf16[3,64,512]{2,1,0:T(8,128)(2,1)S(1)} %collective-permute-done.17.rest_2_), channel_id=1, source_target_pairs={{0,2},{2,0},{1,3},{3,1},{4,6},{6,4},{5,7},{7,5},{8,10},{10,8},{9,1... | collective-permute-start | bytes 589832 | tf_op jit(solution)/shard_map/ppermute | solution.py:442
  103.7 4.5 %collective-permute-start.22 = (bf16[3,64,512]{2,1,0:T(8,128)(2,1)S(1)}, bf16[3,64,512]{2,1,0:T(8,128)(2,1)S(1)}, u32[]{:S(2)}, u32[]{:S(2)}) collective-permute-start(bf16[3,64,512]{2,1,0:T(8,128)(2,1)S(1)} %update.1.rest_0_), channel_id=1, source_target_pairs={{0,1},{1,0},{2,3},{3,2},{4,5},{5,4},{6,7},{7,6},{8,9},{9,8},{10,11... | collective-permute-start | bytes 589832 | tf_op jit(solution)/shard_map/ppermute | solution.py:442
  103.8 4.4 %collective-permute-start.23 = (bf16[3,64,512]{2,1,0:T(8,128)(2,1)S(1)}, bf16[3,64,512]{2,1,0:T(8,128)(2,1)S(1)}, u32[]{:S(2)}, u32[]{:S(2)}) collective-permute-start(bf16[3,64,512]{2,1,0:T(8,128)(2,1)S(1)} %collective-permute-done.16.rest_1_), channel_id=1, source_target_pairs={{0,1},{1,0},{2,3},{3,2},{4,5},{5,4},{6,7},{7,6},{8,9},{9,8},{10,11... | collective-permute-start | bytes 589832 | tf_op jit(solution)/shard_map/ppermute | solution.py:442
  104.3 3.9 %collective-permute-start.24 = (bf16[3,64,512]{2,1,0:T(8,128)(2,1)S(1)}, bf16[3,64,512]{2,1,0:T(8,128)(2,1)S(1)}, u32[]{:S(2)}, u32[]{:S(2)}) collective-permute-start(bf16[3,64,512]{2,1,0:T(8,128)(2,1)S(1)} %collective-permute-done.17.rest_2_), channel_id=1, source_target_pairs={{0,1},{1,0},{2,3},{3,2},{4,5},{5,4},{6,7},{7,6},{8,9},{9,8},{10,11... | collective-permute-start | bytes 589832 | tf_op jit(solution)/shard_map/ppermute | solution.py:442
  104.4 3.8 %collective-permute-start.25 = (bf16[3,64,512]{2,1,0:T(8,128)(2,1)S(1)}, bf16[3,64,512]{2,1,0:T(8,128)(2,1)S(1)}, u32[]{:S(2)}, u32[]{:S(2)}) collective-permute-start(bf16[3,64,512]{2,1,0:T(8,128)(2,1)S(1)} %collective-permute-done.18.rest_3_), channel_id=1, source_target_pairs={{0,1},{1,0},{2,3},{3,2},{4,5},{5,4},{6,7},{7,6},{8,9},{9,8},{10,11... | collective-permute-start | bytes 589832 | tf_op jit(solution)/shard_map/ppermute | solution.py:442
  108.2 3.7 %collective-permute-start.27 = (bf16[3,64,512]{2,1,0:T(8,128)(2,1)S(1)}, bf16[3,64,512]{2,1,0:T(8,128)(2,1)S(1)}, u32[]{:S(2)}, u32[]{:S(2)}) collective-permute-start(bf16[3,64,512]{2,1,0:T(8,128)(2,1)S(1)} %collective-permute-done.19.rest_0_), channel_id=1, source_target_pairs={{0,1},{1,0},{2,3},{3,2},{4,5},{5,4},{6,7},{7,6},{8,9},{9,8},{10,11... | collective-permute-start | bytes 589832 | tf_op jit(solution)/shard_map/ppermute | solution.py:442
  108.3 3.7 %collective-permute-start.28 = (bf16[3,64,512]{2,1,0:T(8,128)(2,1)S(1)}, bf16[3,64,512]{2,1,0:T(8,128)(2,1)S(1)}, u32[]{:S(2)}, u32[]{:S(2)}) collective-permute-start(bf16[3,64,512]{2,1,0:T(8,128)(2,1)S(1)} %collective-permute-done.21.rest_1_), channel_id=1, source_target_pairs={{0,1},{1,0},{2,3},{3,2},{4,5},{5,4},{6,7},{7,6},{8,9},{9,8},{10,11... | collective-permute-start | bytes 589832 | tf_op jit(solution)/shard_map/ppermute | solution.py:442
  108.8 3.2 %collective-permute-start.29 = (bf16[3,64,512]{2,1,0:T(8,128)(2,1)S(1)}, bf16[3,64,512]{2,1,0:T(8,128)(2,1)S(1)}, u32[]{:S(2)}, u32[]{:S(2)}) collective-permute-start(bf16[3,64,512]{2,1,0:T(8,128)(2,1)S(1)} %collective-permute-done.26.rest_2_), channel_id=1, source_target_pairs={{0,1},{1,0},{2,3},{3,2},{4,5},{5,4},{6,7},{7,6},{8,9},{9,8},{10,11... | collective-permute-start | bytes 589832 | tf_op jit(solution)/shard_map/ppermute | solution.py:442
  108.9 3.1 %collective-permute-start.30 = (bf16[3,64,512]{2,1,0:T(8,128)(2,1)S(1)}, bf16[3,64,512]{2,1,0:T(8,128)(2,1)S(1)}, u32[]{:S(2)}, u32[]{:S(2)}) collective-permute-start(bf16[3,64,512]{2,1,0:T(8,128)(2,1)S(1)} %collective-permute-done.20.rest_3_), channel_id=1, source_target_pairs={{0,1},{1,0},{2,3},{3,2},{4,5},{5,4},{6,7},{7,6},{8,9},{9,8},{10,11... | collective-permute-start | bytes 589832 | tf_op jit(solution)/shard_map/ppermute | solution.py:442

commit v9 on v8

--- a/solution.py
+++ b/solution.py
@@ -105,7 +105,7 @@
     return pl.pallas_call(
         functools.partial(pack_kernel, first, count, own),
         in_specs=[SM] + [pl.BlockSpec(memory_space=pl.ANY)] * 2,
-        out_specs=VM,
+        out_specs=VM if own else pl.BlockSpec(memory_space=pl.ANY),
         out_shape=shape((count, 2 * HD)),
         scratch_shapes=[pltpu.SemaphoreType.DMA((2,))],
         compiler_params=PARAMS,
@@ -396,11 +396,8 @@
     )(where, *pieces, q, att, q_rest)
 
 
-def read_other_kernel(zs, count, where, *rest):
-    pieces, (qn, att, mine, half_filled, out, weights, full, work, sems) = (
-        rest[: 2 * zs],
-        rest[2 * zs :],
-    )
+def collect_kernel(zs, count, where, *rest):
+    pieces, (mine, full, weights) = rest[: 2 * zs], rest[2 * zs :]
     y, core, z = where[0], where[1], where[2]
     gather(zs, where, pieces, 3, full)
     step = math.gcd(count, HD)
@@ -411,25 +408,24 @@
         at = lax.div(r, 2 * HD) * HD + lax.rem(r, HD)
         rows = pl.ds(pl.multiple_of(at, step), step)
         weights[c * step : (c + 1) * step, :] = jnp.where(head == y, mine[rows, :], full[rows, :])
-    read(lambda rows: qn[rows, :], att, full, out, 1 - y, work, sems)
-
-
-def read_other(zs, where, count, pieces, qn, att, mine, half_filled):
+
+
+def read_other_kernel(where, qn, att, full, half_filled, out, work, sems):
+    read(lambda rows: qn[rows, :], att, full, out, 1 - where[0], work, sems)
+
+
+def read_other(where, qn, att, full, half_filled):
     anyspec = pl.BlockSpec(memory_space=pl.ANY)
     return pl.pallas_call(
-        functools.partial(read_other_kernel, zs, count),
-        in_specs=[SM] + [VM] * (2 * zs + 3) + [anyspec],
-        out_specs=[anyspec, VM],
-        out_shape=[shape((BLK, H * HD)), shape((count, HD))],
-        scratch_shapes=[
-            pltpu.VMEM((3 * HD, HD), BF),
-            pltpu.VMEM((BLK, HD), BF),
-            pltpu.SemaphoreType.DMA((2,)),
-        ],
-        input_output_aliases={2 * zs + 4: 0},
+        read_other_kernel,
+        in_specs=[SM] + [VM] * 3 + [anyspec],
+        out_specs=anyspec,
+        out_shape=shape((BLK, H * HD)),
+        scratch_shapes=[pltpu.VMEM((BLK, HD), BF), pltpu.SemaphoreType.DMA((2,))],
+        input_output_aliases={4: 0},
         compiler_params=PARAMS,
         name="read_other",
-    )(where, *pieces, qn, att, mine, half_filled)
+    )(where, qn, att, full, half_filled)
 
 
 def local(queries, key_rows, value_rows, step_rates, w_gate, w_up, w_down):
@@ -522,15 +518,16 @@
     others = [others[d] for d in range(zs)]
     gate = [*pieces[1:], others[0], others[zs - 1], others[1]]
     pieces2 = [swap(after(p, gate), "core") for p in pieces]
-    pieces2, others = lax.optimization_barrier((pieces2, others))
-    others2 = [swap(p, "core") for d, p in enumerate(others)]
     half_filled, full, qn_rest = read_own(zs, where, pieces + pieces2, q_own, att_own, q_rest)
+    far = range(2, zs - 1)
+    others2 = [swap(after(p, full) if d in far else p, "core") for d, p in enumerate(others)]
     count = 3 * H * HD // (4 * zs)
-    return tuple(
-        read_other(
-            zs, where, count, others + others2, qn_rest, att_back, full, half_filled
-        )
-    )
+    full_rest, own_weights = call(
+        functools.partial(collect_kernel, zs, count),
+        "collect",
+        [shape((3 * HD, HD)), shape((count, HD))],
+    )(where, *others, *others2, full)
+    return read_other(where, qn_rest, att_back, full_rest, half_filled), own_weights
 
 
 def solution(mesh):

time: 116 us -> 143 us (1.23); the launches traced: 115 us -> 141 us
  Pallas kernels: 36.4 us -> 67.2 us
  waiting for transfers between devices: 40.3 us -> 35.7 us
    pallas_call x3, Pallas kernels: 6.52 us -> 36.8 us  [pack(): pl.pallas_call(functools.partial(pack_kernel, first, count, own), in_spec...]
    ppermute x23, waiting for transfers between devices: 15.1 us -> 6.36 us  [swap(): return lax.ppermute(value, axis, SWAP)]
    ppermute x8, waiting for transfers between devices: 25.2 us -> 29.3 us  [shift(): lax.ppermute(value, 'z', [(i, (i + d) % zs) for i in range(zs) if ring or...]
    pallas_call x10 -> x11, Pallas kernels: 22.3 us -> 23.7 us  [run(): pl.pallas_call(kernel, in_specs=[SM] + [VM] * len(args), out_specs=[VM] *...]
  transfers between devices with their start and end apart: 31 -> 31, of which waited for: 12 -> 12; matrix products, arithmetic and copies ran while one was open for 1% -> 1% of each run, Pallas kernels for 24% -> 30%
where the time goes in v9:
time: 143 us; the launch traced here: 141 us
  Pallas kernels  67.2 us (47%)
  waiting for transfers between devices  35.7 us (25%)
  starting transfers between devices  34.8 us (24%)
  other arithmetic  1.76 us (1%)
    pallas_call x3, Pallas kernels, pack(): pl.pallas_call(functools.partial(pack_kernel, first, count, own), in_spec...  36.8 us
    ppermute x8, waiting for transfers between devices, shift(): lax.ppermute(value, 'z', [(i, (i + d) % zs) for i in range(zs) if ring or...  29.3 us
    pallas_call x11, Pallas kernels, run(): pl.pallas_call(kernel, in_specs=[SM] + [VM] * len(args), out_specs=[VM] *...  23.7 us
    ppermute x8, starting transfers between devices, shift(): lax.ppermute(value, 'z', [(i, (i + d) % zs) for i in range(zs) if ring or...  20 us
    ppermute x23, starting transfers between devices, swap(): return lax.ppermute(value, axis, SWAP)  14.8 us
    ppermute x23, waiting for transfers between devices, swap(): return lax.ppermute(value, axis, SWAP)  6.36 us
  transfers between devices with their start and end apart: 31, of which 12 were waited for; matrix products, arithmetic and copies ran while one was open for 1% of the time, Pallas kernels for 30%

profile of v9, /device:TPU:0, one launch (start us, length us, event | category | flops | bytes accessed | tf_op | source)
XLA Modules:
  0.0 140.9 jit_solution(6366791058948362337)
XLA Ops:
  0.7 17.5 %pack.3 = bf16[256,1024]{1,0:T(8,128)(2,1)} custom-call(s32[3]{0:T(128)S(1)} %pad_add_fusion.where, bf16[512,1024]{1,0:T(8,128)(2,1)} %key.3, bf16[512,1024]{1,0:T(8,128)(2,1)} %value.5), custom_call_target="tpu_custom_call" | custom-call | tf_op jit(solution)/shard_map/pack/pallas_call | solution.py:105
  18.3 3.0 %collective-permute-start = (bf16[256,1024]{1,0:T(8,128)(2,1)}, bf16[256,1024]{1,0:T(8,128)(2,1)S(1)}, u32[]{:S(2)}, u32[]{:S(2)}) collective-permute-start(bf16[256,1024]{1,0:T(8,128)(2,1)} %pack.3), channel_id=1, source_target_pairs={{0,2},{2,0},{1,3},{3,1},{4,6},{6,4},{5,7},{7,5},{8,10},{10,8},{9,1... | collective-permute-start | bytes 1572872 | tf_op jit(solution)/shard_map/ppermute | solution.py:438
  21.3 17.5 %pack.4 = bf16[256,1024]{1,0:T(8,128)(2,1)} custom-call(s32[3]{0:T(128)S(1)} %pad_add_fusion.where, bf16[512,1024]{1,0:T(8,128)(2,1)} %key.3, bf16[512,1024]{1,0:T(8,128)(2,1)} %value.5), custom_call_target="tpu_custom_call" | custom-call | tf_op jit(solution)/shard_map/pack/pallas_call | solution.py:105
  38.9 1.8 %pack.5.own = bf16[512,1024]{1,0:T(8,128)(2,1)S(1)} custom-call(s32[3]{0:T(128)S(1)} %pad_add_fusion.where, bf16[512,1024]{1,0:T(8,128)(2,1)} %key.3, bf16[512,1024]{1,0:T(8,128)(2,1)} %value.5), custom_call_target="tpu_custom_call" | custom-call | tf_op jit(solution)/shard_map/pack/pallas_call | solution.py:105
  40.8 1.6 %pack_q.1 = bf16[528,512]{1,0:T(8,128)(2,1)S(1)} custom-call(s32[3]{0:T(128)S(1)} %pad_add_fusion.where, bf16[512,1024]{1,0:T(8,128)(2,1)} %query, f32[2,512]{1,0:T(2,128)S(1)} %copy-done), custom_call_target="tpu_custom_call" | custom-call | tf_op jit(solution)/shard_map/pack_q/pallas_call | solution.py:74
  42.5 1.5 %slice_select_fusion = (bf16[512,512]{1,0:T(8,128)(2,1)S(1)}, bf16[512,512]{1,0:T(8,128)(2,1)S(1)}) fusion(bf16[1024,512]{1,0:T(8,128)(2,1)S(1)} %copy-done.2, pred[]{:T(512)S(6)} %eq.2, bf16[1024,512]{1,0:T(8,128)(2,1)} %param.12), kind=kLoop, calls=%fused_computation | loop fusion | flops 524288 | bytes 3145729 | tf_op jit(solution)/shard_map/jit(_where)/select_n | solution.py:460
  44.5 0.6 pick.2
  45.1 0.5 collective-permute-start.3
  45.7 2.0 %collective-permute-start.6 = (bf16[528,512]{1,0:T(8,128)(2,1)S(1)}, bf16[528,512]{1,0:T(8,128)(2,1)S(1)}, u32[]{:S(2)}, u32[]{:S(2)}) collective-permute-start(bf16[528,512]{1,0:T(8,128)(2,1)S(1)} %pack_q.1), channel_id=1, source_target_pairs={{0,2},{2,0},{1,3},{3,1},{4,6},{6,4},{5,7},{7,5},{8,10},{10,8},{9,1... | collective-permute-start | bytes 1622024 | tf_op jit(solution)/shard_map/ppermute | solution.py:438
  47.7 3.5 %collective-permute-start.5 = (bf16[256,1024]{1,0:T(8,128)(2,1)S(1)}, bf16[256,1024]{1,0:T(8,128)(2,1)S(1)}, u32[]{:S(2)}, u32[]{:S(2)}) collective-permute-start(bf16[256,1024]{1,0:T(8,128)(2,1)S(1)} %pick.2), channel_id=1, source_target_pairs={{0,4},{4,8},{8,12},{1,5},{5,9},{9,13},{2,6},{6,10},{10,14},{3,7},{... | collective-permute-start | bytes 1572872 | tf_op jit(solution)/shard_map/ppermute | solution.py:441
  51.2 3.7 %pre_own.1 = (bf16[512,512]{1,0:T(8,128)(2,1)S(1)}, bf16[512,512]{1,0:T(8,128)(2,1)S(1)}, f32[512,256]{1,0:T(8,128)S(1)}, f32[512,256]{1,0:T(8,128)S(1)}, bf16[5...) custom-call(s32[3]{0:T(128)S(1)} %pad_add_fusion.where, ...), custom_call_target="tpu_custom_call" | custom-call | tf_op jit(solution)/shard_map/pre_own/pallas_call | solution.py:55
  54.9 0.6 pick.3
  55.6 3.5 %collective-permute-start.7 = (bf16[256,1024]{1,0:T(8,128)(2,1)S(1)}, bf16[256,1024]{1,0:T(8,128)(2,1)S(1)}, u32[]{:S(2)}, u32[]{:S(2)}) collective-permute-start(bf16[256,1024]{1,0:T(8,128)(2,1)S(1)} %pick.3), channel_id=1, source_target_pairs={{0,4},{4,8},{8,12},{1,5},{5,9},{9,13},{2,6},{6,10},{10,14},{3,7},{... | collective-permute-start | bytes 1572872 | tf_op jit(solution)/shard_map/ppermute | solution.py:441
  59.1 2.6 %pre.2 = (bf16[512,512]{1,0:T(8,128)(2,1)S(1)}, bf16[512,512]{1,0:T(8,128)(2,1)S(1)}, f32[512,256]{1,0:T(8,128)S(1)}, f32[512,256]{1,0:T(8,128)S(1)}, bf16[512,5...) custom-call(s32[3]{0:T(128)S(1)} %pad_add_fusion.where, ...), custom_call_target="tpu_custom_call" | custom-call | tf_op jit(solution)/shard_map/pre/pallas_call | solution.py:55
  61.7 1.8 %collective-permute-done.5.halo_a = bf16[256,1024]{1,0:T(8,128)(2,1)S(1)} collective-permute-done((bf16[256,1024]{1,0:T(8,128)(2,1)S(1)}, bf16[256,1024]{1,0:T(8,128)(2,1)S(1)}, u32[]{:S(2)}, u32[]{:S(2)}) %collective-permute-start.5) | collective-permute-done | bytes 524320 | tf_op jit(solution)/shard_map/ppermute | solution.py:441
  63.5 0.6 collective-permute-done.6.q_for
  64.1 2.8 %pre.3 = (bf16[512,512]{1,0:T(8,128)(2,1)S(1)}, bf16[512,512]{1,0:T(8,128)(2,1)S(1)}, f32[512,256]{1,0:T(8,128)S(1)}, f32[512,256]{1,0:T(8,128)S(1)}, bf16[512,5...) custom-call(s32[3]{0:T(128)S(1)} %pad_add_fusion.where, ...), custom_call_target="tpu_custom_call" | custom-call | tf_op jit(solution)/shard_map/pre/pallas_call | solution.py:55
  66.9 3.3 %attend_upper.1 = (bf16[512,512]{1,0:T(8,128)(2,1)S(1)}, bf16[512,512]{1,0:T(8,128)(2,1)S(1)}, bf16[512,1024]{1,0:T(8,128)(2,1)S(1)}, bf16[512,1024]{1,0:T(8,128)(2,1)S(1)}) custom-call(s32[3]{0:T(128)S(1)} %pad_add_fusion.where, bf16[512,512]{1,0:T(8,128)(2,1)S(1)} %get-tuple-element.93.q_own.rest_8_, bf16[528,512]{1,0:T(8,128)(2,1)S(1)} %collective-permute-done.6.q_for, ...), custom_call_target="tpu_custom_call" | custom-call | tf_op jit(solution)/shard_map/attend_upper/pallas_call | solution.py:55
  70.2 3.3 %collective-permute-done.7.halo_b = bf16[256,1024]{1,0:T(8,128)(2,1)S(1)} collective-permute-done((bf16[256,1024]{1,0:T(8,128)(2,1)S(1)}, bf16[256,1024]{1,0:T(8,128)(2,1)S(1)}, u32[]{:S(2)}, u32[]{:S(2)}) %collective-permute-start.7) | collective-permute-done | bytes 524320 | tf_op jit(solution)/shard_map/ppermute | solution.py:441
  73.5 0.5 collective-permute-start.9
  74.0 1.4 collective-permute-done.8.halo2_a
  75.4 0.7 collective-permute-done.9.halo2_b
  76.2 3.2 %attend_lower.1 = (bf16[512,512]{1,0:T(8,128)(2,1)S(1)}, bf16[512,512]{1,0:T(8,128)(2,1)S(1)}, bf16[512,512]{1,0:T(8,128)(2,1)S(1)}) custom-call(s32[3]{0:T(128)S(1)} %pad_add_fusion.where, bf16[512,512]{1,0:T(8,128)(2,1)S(1)} %get-tuple-element.93.q_own.rest_8_, bf16[528,512]{1,0:T(8,128)(2,1)S(1)} %collective-permute-done.6.q_for, f32[2,512]{1,0:T(2,128)S(1)} %copy-done, ...), custom_call_target="tpu_custom_call" | custom-call | tf_op jit(solution)/shard_map/attend_lower/pallas_call | solution.py:55
  79.6 2.3 %grad_first.1.before = f32[3,256,512]{2,1,0:T(8,128)S(1)} custom-call(s32[3]{0:T(128)S(1)} %pad_add_fusion.where, bf16[512,512]{1,0:T(8,128)(2,1)S(1)} %get-tuple-element.150.e0, bf16[512,512]{1,0:T(8,128)(2,1)S(1)} %collective-permute-done.11.e1, bf16[512,512]{1,0:T(8,128)(2,1)S(1)} %get-tuple-element.151.k0, bf16[512,512]{1,0:T(8,128)(2,1)S(1)} %get-tuple-element.152.k1, ...), custom_call_target="tpu_custom_call" | custom-call | tf_op jit(solution)/shard_map/grad_first/pallas_call | solution.py:55
  81.9 2.5 %grad_second.1 = (f32[3,64,512]{2,1,0:T(8,128)S(1)}, bf16[3,64,512]{2,1,0:T(8,128)(2,1)S(1)}, bf16[3,64,512]{2,1,0:T(8,128)(2,1)S(1)}, bf16[3,64,512]{2,1,0:T(8,128)(2,1)S(1)}) custom-call(s32[3]{0:T(128)S(1)} %pad_add_fusion.where, bf16[512,512]{1,0:T(8,128)(2,1)S(1)} %get-tuple-element.140.e0, bf16[512,512]{1,0:T(8,128)(2,1)S(1)} %collective-permute-done.10.e1, ...), custom_call_target="tpu_custom_call" | custom-call | tf_op jit(solution)/shard_map/grad_second/pallas_call | solution.py:55
  84.4 0.6 collective-permute-start.15
  85.0 2.5 %collective-permute-start.12 = (bf16[3,64,512]{2,1,0:T(8,128)(2,1)S(1)}, bf16[3,64,512]{2,1,0:T(8,128)(2,1)S(1)}, u32[]{:S(2)}, u32[]{:S(2)}) collective-permute-start(bf16[3,64,512]{2,1,0:T(8,128)(2,1)S(1)} %get-tuple-element.160), channel_id=1, source_target_pairs={{0,4},{4,8},{8,12},{12,0},{1,5},{5,9},{9,13},{13,1},{2,6},{6,10},{... | collective-permute-start | bytes 589832 | tf_op jit(solution)/shard_map/ppermute | solution.py:441
  87.5 2.6 %collective-permute-start.13 = (bf16[3,64,512]{2,1,0:T(8,128)(2,1)S(1)}, bf16[3,64,512]{2,1,0:T(8,128)(2,1)S(1)}, u32[]{:S(2)}, u32[]{:S(2)}) collective-permute-start(bf16[3,64,512]{2,1,0:T(8,128)(2,1)S(1)} %get-tuple-element.161), channel_id=1, source_target_pairs={{0,8},{4,12},{8,0},{12,4},{1,9},{5,13},{9,1},{13,5},{2,10},{6,14},... | collective-permute-start | bytes 589832 | tf_op jit(solution)/shard_map/ppermute | solution.py:441
  90.0 1.4 collective-permute-start.14
  91.4 3.9 %collective-permute-done.12.rest_0_ = bf16[3,64,512]{2,1,0:T(8,128)(2,1)S(1)} collective-permute-done((bf16[3,64,512]{2,1,0:T(8,128)(2,1)S(1)}, bf16[3,64,512]{2,1,0:T(8,128)(2,1)S(1)}, u32[]{:S(2)}, u32[]{:S(2)}) %collective-permute-start.12) | collective-permute-done | bytes 196640 | tf_op jit(solution)/shard_map/ppermute | solution.py:441
  95.3 7.9 %collective-permute-done.13.rest_1_ = bf16[3,64,512]{2,1,0:T(8,128)(2,1)S(1)} collective-permute-done((bf16[3,64,512]{2,1,0:T(8,128)(2,1)S(1)}, bf16[3,64,512]{2,1,0:T(8,128)(2,1)S(1)}, u32[]{:S(2)}, u32[]{:S(2)}) %collective-permute-start.13) | collective-permute-done | bytes 196640 | tf_op jit(solution)/shard_map/ppermute | solution.py:441
  103.2 0.8 update.1.rest_0_
  104.0 5.8 %collective-permute-start.18 = (bf16[3,64,512]{2,1,0:T(8,128)(2,1)S(1)}, bf16[3,64,512]{2,1,0:T(8,128)(2,1)S(1)}, u32[]{:S(2)}, u32[]{:S(2)}) collective-permute-start(bf16[3,64,512]{2,1,0:T(8,128)(2,1)S(1)} %update.1.rest_0_), channel_id=1, source_target_pairs={{0,12},{4,0},{8,4},{12,8},{1,13},{5,1},{9,5},{13,9},{2,14},{6,2},{... | collective-permute-start | bytes 589832 | tf_op jit(solution)/shard_map/ppermute | solution.py:441
  109.7 1.5 %collective-permute-start.19 = (bf16[3,64,512]{2,1,0:T(8,128)(2,1)S(1)}, bf16[3,64,512]{2,1,0:T(8,128)(2,1)S(1)}, u32[]{:S(2)}, u32[]{:S(2)}) collective-permute-start(bf16[3,64,512]{2,1,0:T(8,128)(2,1)S(1)} %update.1.rest_0_), channel_id=1, source_target_pairs={{0,2},{2,0},{1,3},{3,1},{4,6},{6,4},{5,7},{7,5},{8,10},{10,8},{9,1... | collective-permute-start | bytes 589832 | tf_op jit(solution)/shard_map/ppermute | solution.py:438
  111.3 0.8 collective-permute-start.17
  112.1 3.0 %collective-permute-done.18.rest_3_ = bf16[3,64,512]{2,1,0:T(8,128)(2,1)S(1)} collective-permute-done((bf16[3,64,512]{2,1,0:T(8,128)(2,1)S(1)}, bf16[3,64,512]{2,1,0:T(8,128)(2,1)S(1)}, u32[]{:S(2)}, u32[]{:S(2)}) %collective-permute-start.18) | collective-permute-done | bytes 196640 | tf_op jit(solution)/shard_map/ppermute | solution.py:441
  115.1 1.5 %collective-permute-start.20 = (bf16[3,64,512]{2,1,0:T(8,128)(2,1)S(1)}, bf16[3,64,512]{2,1,0:T(8,128)(2,1)S(1)}, u32[]{:S(2)}, u32[]{:S(2)}) collective-permute-start(bf16[3,64,512]{2,1,0:T(8,128)(2,1)S(1)} %collective-permute-done.18.rest_3_), channel_id=1, source_target_pairs={{0,2},{2,0},{1,3},{3,1},{4,6},{6,4},{5,7},{7,5},{8,10},{10,8},{9,1... | collective-permute-start | bytes 589832 | tf_op jit(solution)/shard_map/ppermute | solution.py:438
  116.6 2.8 %collective-permute-done.16.rest_1_ = bf16[3,64,512]{2,1,0:T(8,128)(2,1)S(1)} collective-permute-done((bf16[3,64,512]{2,1,0:T(8,128)(2,1)S(1)}, bf16[3,64,512]{2,1,0:T(8,128)(2,1)S(1)}, u32[]{:S(2)}, u32[]{:S(2)}) %collective-permute-start.16) | collective-permute-done | bytes 196640 | tf_op jit(solution)/shard_map/ppermute | solution.py:441
  119.5 1.5 %collective-permute-start.21 = (bf16[3,64,512]{2,1,0:T(8,128)(2,1)S(1)}, bf16[3,64,512]{2,1,0:T(8,128)(2,1)S(1)}, u32[]{:S(2)}, u32[]{:S(2)}) collective-permute-start(bf16[3,64,512]{2,1,0:T(8,128)(2,1)S(1)} %collective-permute-done.16.rest_1_), channel_id=1, source_target_pairs={{0,2},{2,0},{1,3},{3,1},{4,6},{6,4},{5,7},{7,5},{8,10},{10,8},{9,1... | collective-permute-start | bytes 589832 | tf_op jit(solution)/shard_map/ppermute | solution.py:438
  121.0 6.6 %collective-permute-done.17.rest_2_ = bf16[3,64,512]{2,1,0:T(8,128)(2,1)S(1)} collective-permute-done((bf16[3,64,512]{2,1,0:T(8,128)(2,1)S(1)}, bf16[3,64,512]{2,1,0:T(8,128)(2,1)S(1)}, u32[]{:S(2)}, u32[]{:S(2)}) %collective-permute-start.17) | collective-permute-done | bytes 196640 | tf_op jit(solution)/shard_map/ppermute | solution.py:441
  127.6 0.5 collective-permute-start.23
  128.6 1.5 %collective-permute-start.26 = (bf16[3,64,512]{2,1,0:T(8,128)(2,1)S(1)}, bf16[3,64,512]{2,1,0:T(8,128)(2,1)S(1)}, u32[]{:S(2)}, u32[]{:S(2)}) collective-permute-start(bf16[3,64,512]{2,1,0:T(8,128)(2,1)S(1)} %collective-permute-done.17.rest_2_), channel_id=1, source_target_pairs={{0,2},{2,0},{1,3},{3,1},{4,6},{6,4},{5,7},{7,5},{8,10},{10,8},{9,1... | collective-permute-start | bytes 589832 | tf_op jit(solution)/shard_map/ppermute | solution.py:438
  130.2 0.5 collective-permute-start.30
  130.7 2.6 %read_own.1 = (bf16[512,1024]{1,0:T(8,128)(2,1)}, bf16[1536,512]{1,0:T(8,128)(2,1)S(1)}, bf16[512,512]{1,0:T(8,128)(2,1)S(1)}) custom-call(s32[3]{0:T(128)S(1)} %pad_add_fusion.where, bf16[3,64,512]{2,1,0:T(8,128)(2,1)S(1)} %update.1.rest_0_, bf16[3,64,512]{2,1,0:T(8,128)(2,1)S(1)} %collective-permute-done.16.rest_1_, ...), custom_call_target="tpu_custom_call" | custom-call | tf_op jit(solution)/shard_map/read_own/pallas_call | solution.py:388
  133.4 2.1 %collective-permute-done.26.rest_2_ = bf16[3,64,512]{2,1,0:T(8,128)(2,1)S(1)} collective-permute-done((bf16[3,64,512]{2,1,0:T(8,128)(2,1)S(1)}, bf16[3,64,512]{2,1,0:T(8,128)(2,1)S(1)}, u32[]{:S(2)}, u32[]{:S(2)}) %collective-permute-start.26) | collective-permute-done | bytes 196640 | tf_op jit(solution)/shard_map/ppermute | solution.py:438
  135.5 1.4 %collective-permute-done.29.rest_6_ = bf16[3,64,512]{2,1,0:T(8,128)(2,1)S(1)} collective-permute-done((bf16[3,64,512]{2,1,0:T(8,128)(2,1)S(1)}, bf16[3,64,512]{2,1,0:T(8,128)(2,1)S(1)}, u32[]{:S(2)}, u32[]{:S(2)}) %collective-permute-start.29) | collective-permute-done | bytes 196640 | tf_op jit(solution)/shard_map/ppermute | solution.py:438
  136.9 1.3 collect.1
  138.3 2.5 %read_other.1 = bf16[512,1024]{1,0:T(8,128)(2,1)} custom-call(s32[3]{0:T(128)S(1)} %pad_add_fusion.where, bf16[512,512]{1,0:T(8,128)(2,1)S(1)} %get-tuple-element.173.qn, bf16[512,512]{1,0:T(8,128)(2,1)S(1)} %collective-permute-done.15.att, bf16[1536,512]{1,0:T(8,128)(2,1)S(1)} %get-tuple-element.177.full, ...), custom_call_target="tpu_custom_call", output_to_operand_aliasing={{}: (4, {})} | custom-call | tf_op jit(solution)/shard_map/read_other/pallas_call | solution.py:419
  (42 shorter events, 1.6 us)
Async XLA Ops:
  18.3 26.2 %collective-permute-start = (bf16[256,1024]{1,0:T(8,128)(2,1)}, bf16[256,1024]{1,0:T(8,128)(2,1)S(1)}, u32[]{:S(2)}, u32[]{:S(2)}) collective-permute-start(bf16[256,1024]{1,0:T(8,128)(2,1)} %pack.3), channel_id=1, source_target_pairs={{0,2},{2,0},{1,3},{3,1},{4,6},{6,4},{5,7},{7,5},{8,10},{10,8},{9,1... | collective-permute-start | bytes 1572872 | tf_op jit(solution)/shard_map/ppermute | solution.py:438
  38.8 1.9 %copy-start = (f32[2,512]{1,0:T(2,128)S(1)}, f32[2,512]{1,0:T(2,128)}, u32[]{:S(2)}) copy-start(f32[2,512]{1,0:T(2,128)} %rates.5) | copy-start | bytes 12292
  38.9 16.0 %collective-permute-start.1 = (bf16[256,1024]{1,0:T(8,128)(2,1)}, bf16[256,1024]{1,0:T(8,128)(2,1)S(1)}, u32[]{:S(2)}, u32[]{:S(2)}) collective-permute-start(bf16[256,1024]{1,0:T(8,128)(2,1)} %pack.4), channel_id=1, source_target_pairs={{0,2},{2,0},{1,3},{3,1},{4,6},{6,4},{5,7},{7,5},{8,10},{10,8},{9,1... | collective-permute-start | bytes 1572872 | tf_op jit(solution)/shard_map/ppermute | solution.py:438
  40.7 10.5 %collective-permute-start.2 = (bf16[512,1024]{1,0:T(8,128)(2,1)S(1)}, bf16[512,1024]{1,0:T(8,128)(2,1)S(1)}, u32[]{:S(2)}, u32[]{:S(2)}) collective-permute-start(bf16[512,1024]{1,0:T(8,128)(2,1)S(1)} %pack.5.own), channel_id=1, source_target_pairs={{0,1},{1,0},{2,3},{3,2},{4,5},{5,4},{6,7},{7,6},{8,9},{9,8},{10,11... | collective-permute-start | bytes 3145736 | tf_op jit(solution)/shard_map/ppermute | solution.py:438
  40.8 1.7 %copy-start.2 = (bf16[1024,512]{1,0:T(8,128)(2,1)S(1)}, bf16[1024,512]{1,0:T(8,128)(2,1)}, u32[]{:S(2)}) copy-start(bf16[1024,512]{1,0:T(8,128)(2,1)} %param.13) | copy-start | bytes 3145732
  42.5 1.5 %copy-start.1 = (bf16[512,1024]{1,0:T(8,128)(2,1)S(1)}, bf16[512,1024]{1,0:T(8,128)(2,1)}, u32[]{:S(2)}) copy-start(bf16[512,1024]{1,0:T(8,128)(2,1)} %query) | copy-start | bytes 3145732
  42.5 1.8 %copy-start.3 = (bf16[1024,512]{1,0:T(8,128)(2,1)S(1)}, bf16[1024,512]{1,0:T(8,128)(2,1)}, u32[]{:S(2)}) copy-start(bf16[1024,512]{1,0:T(8,128)(2,1)} %param.11) | copy-start | bytes 3145732
  45.1 9.8 %collective-permute-start.3 = (bf16[256,1024]{1,0:T(8,128)(2,1)S(1)}, bf16[256,1024]{1,0:T(8,128)(2,1)S(1)}, u32[]{:S(2)}, u32[]{:S(2)}) collective-permute-start(bf16[256,1024]{1,0:T(8,128)(2,1)S(1)} %collective-permute-done.foreign.rest_0_.for_a), channel_id=1, source_target_pairs={{0,1},{1,0},{2,3},{3,2},{4,5},{5,4},{6,7},{7,6},{8,9},{9,8},{10,11... | collective-permute-start | bytes 1572872 | tf_op jit(solution)/shard_map/ppermute | solution.py:438
  45.7 18.5 %collective-permute-start.6 = (bf16[528,512]{1,0:T(8,128)(2,1)S(1)}, bf16[528,512]{1,0:T(8,128)(2,1)S(1)}, u32[]{:S(2)}, u32[]{:S(2)}) collective-permute-start(bf16[528,512]{1,0:T(8,128)(2,1)S(1)} %pack_q.1), channel_id=1, source_target_pairs={{0,2},{2,0},{1,3},{3,1},{4,6},{6,4},{5,7},{7,5},{8,10},{10,8},{9,1... | collective-permute-start | bytes 1622024 | tf_op jit(solution)/shard_map/ppermute | solution.py:438
  47.7 15.8 %collective-permute-start.5 = (bf16[256,1024]{1,0:T(8,128)(2,1)S(1)}, bf16[256,1024]{1,0:T(8,128)(2,1)S(1)}, u32[]{:S(2)}, u32[]{:S(2)}) collective-permute-start(bf16[256,1024]{1,0:T(8,128)(2,1)S(1)} %pick.2), channel_id=1, source_target_pairs={{0,4},{4,8},{8,12},{1,5},{5,9},{9,13},{2,6},{6,10},{10,14},{3,7},{... | collective-permute-start | bytes 1572872 | tf_op jit(solution)/shard_map/ppermute | solution.py:441
  55.5 8.0 %collective-permute-start.4 = (bf16[256,1024]{1,0:T(8,128)(2,1)S(1)}, bf16[256,1024]{1,0:T(8,128)(2,1)S(1)}, u32[]{:S(2)}, u32[]{:S(2)}) collective-permute-start(bf16[256,1024]{1,0:T(8,128)(2,1)S(1)} %collective-permute-done.1.foreign.rest_1_.for_b), channel_id=1, source_target_pairs={{0,1},{1,0},{2,3},{3,2},{4,5},{5,4},{6,7},{7,6},{8,9},{9,8},{10,11... | collective-permute-start | bytes 1572872 | tf_op jit(solution)/shard_map/ppermute | solution.py:438
  55.6 17.9 %collective-permute-start.7 = (bf16[256,1024]{1,0:T(8,128)(2,1)S(1)}, bf16[256,1024]{1,0:T(8,128)(2,1)S(1)}, u32[]{:S(2)}, u32[]{:S(2)}) collective-permute-start(bf16[256,1024]{1,0:T(8,128)(2,1)S(1)} %pick.3), channel_id=1, source_target_pairs={{0,4},{4,8},{8,12},{1,5},{5,9},{9,13},{2,6},{6,10},{10,14},{3,7},{... | collective-permute-start | bytes 1572872 | tf_op jit(solution)/shard_map/ppermute | solution.py:441
  73.5 1.9 %collective-permute-start.8 = (bf16[256,1024]{1,0:T(8,128)(2,1)S(1)}, bf16[256,1024]{1,0:T(8,128)(2,1)S(1)}, u32[]{:S(2)}, u32[]{:S(2)}) collective-permute-start(bf16[256,1024]{1,0:T(8,128)(2,1)S(1)} %collective-permute-done.5.halo_a), channel_id=1, source_target_pairs={{0,1},{1,0},{2,3},{3,2},{4,5},{5,4},{6,7},{7,6},{8,9},{9,8},{10,11... | collective-permute-start | bytes 1572872 | tf_op jit(solution)/shard_map/ppermute | solution.py:438
  73.5 2.7 %collective-permute-start.9 = (bf16[256,1024]{1,0:T(8,128)(2,1)S(1)}, bf16[256,1024]{1,0:T(8,128)(2,1)S(1)}, u32[]{:S(2)}, u32[]{:S(2)}) collective-permute-start(bf16[256,1024]{1,0:T(8,128)(2,1)S(1)} %collective-permute-done.7.halo_b), channel_id=1, source_target_pairs={{0,1},{1,0},{2,3},{3,2},{4,5},{5,4},{6,7},{7,6},{8,9},{9,8},{10,11... | collective-permute-start | bytes 1572872 | tf_op jit(solution)/shard_map/ppermute | solution.py:438
  74.0 5.6 %collective-permute-start.11 = (bf16[512,512]{1,0:T(8,128)(2,1)S(1)}, bf16[512,512]{1,0:T(8,128)(2,1)S(1)}, u32[]{:S(2)}, u32[]{:S(2)}) collective-permute-start(bf16[512,512]{1,0:T(8,128)(2,1)S(1)} %get-tuple-element.150.e0), channel_id=1, source_target_pairs={{0,1},{1,0},{2,3},{3,2},{4,5},{5,4},{6,7},{7,6},{8,9},{9,8},{10,11... | collective-permute-start | bytes 1572872 | tf_op jit(solution)/shard_map/ppermute | solution.py:438
  79.4 2.5 %collective-permute-start.10 = (bf16[512,512]{1,0:T(8,128)(2,1)S(1)}, bf16[512,512]{1,0:T(8,128)(2,1)S(1)}, u32[]{:S(2)}, u32[]{:S(2)}) collective-permute-start(bf16[512,512]{1,0:T(8,128)(2,1)S(1)} %get-tuple-element.140.e0), channel_id=1, source_target_pairs={{0,1},{1,0},{2,3},{3,2},{4,5},{5,4},{6,7},{7,6},{8,9},{9,8},{10,11... | collective-permute-start | bytes 1572872 | tf_op jit(solution)/shard_map/ppermute | solution.py:438
  84.4 18.8 %collective-permute-start.15 = (bf16[512,512]{1,0:T(8,128)(2,1)S(1)}, bf16[512,512]{1,0:T(8,128)(2,1)S(1)}, u32[]{:S(2)}, u32[]{:S(2)}) collective-permute-start(bf16[512,512]{1,0:T(8,128)(2,1)S(1)} %get-tuple-element.164), channel_id=1, source_target_pairs={{0,2},{2,0},{1,3},{3,1},{4,6},{6,4},{5,7},{7,5},{8,10},{10,8},{9,1... | collective-permute-start | bytes 1572872 | tf_op jit(solution)/shard_map/ppermute | solution.py:438
  85.0 10.3 %collective-permute-start.12 = (bf16[3,64,512]{2,1,0:T(8,128)(2,1)S(1)}, bf16[3,64,512]{2,1,0:T(8,128)(2,1)S(1)}, u32[]{:S(2)}, u32[]{:S(2)}) collective-permute-start(bf16[3,64,512]{2,1,0:T(8,128)(2,1)S(1)} %get-tuple-element.160), channel_id=1, source_target_pairs={{0,4},{4,8},{8,12},{12,0},{1,5},{5,9},{9,13},{13,1},{2,6},{6,10},{... | collective-permute-start | bytes 589832 | tf_op jit(solution)/shard_map/ppermute | solution.py:441
  87.5 15.7 %collective-permute-start.13 = (bf16[3,64,512]{2,1,0:T(8,128)(2,1)S(1)}, bf16[3,64,512]{2,1,0:T(8,128)(2,1)S(1)}, u32[]{:S(2)}, u32[]{:S(2)}) collective-permute-start(bf16[3,64,512]{2,1,0:T(8,128)(2,1)S(1)} %get-tuple-element.161), channel_id=1, source_target_pairs={{0,8},{4,12},{8,0},{12,4},{1,9},{5,13},{9,1},{13,5},{2,10},{6,14},... | collective-permute-start | bytes 589832 | tf_op jit(solution)/shard_map/ppermute | solution.py:441
  90.0 13.1 %collective-permute-start.14 = (bf16[3,64,512]{2,1,0:T(8,128)(2,1)S(1)}, bf16[3,64,512]{2,1,0:T(8,128)(2,1)S(1)}, u32[]{:S(2)}, u32[]{:S(2)}) collective-permute-start(bf16[3,64,512]{2,1,0:T(8,128)(2,1)S(1)} %get-tuple-element.162), channel_id=1, source_target_pairs={{0,12},{4,0},{8,4},{12,8},{1,13},{5,1},{9,5},{13,9},{2,14},{6,2},{... | collective-permute-start | bytes 589832 | tf_op jit(solution)/shard_map/ppermute | solution.py:441
  104.0 11.2 %collective-permute-start.18 = (bf16[3,64,512]{2,1,0:T(8,128)(2,1)S(1)}, bf16[3,64,512]{2,1,0:T(8,128)(2,1)S(1)}, u32[]{:S(2)}, u32[]{:S(2)}) collective-permute-start(bf16[3,64,512]{2,1,0:T(8,128)(2,1)S(1)} %update.1.rest_0_), channel_id=1, source_target_pairs={{0,12},{4,0},{8,4},{12,8},{1,13},{5,1},{9,5},{13,9},{2,14},{6,2},{... | collective-permute-start | bytes 589832 | tf_op jit(solution)/shard_map/ppermute | solution.py:441
  109.7 9.7 %collective-permute-start.16 = (bf16[3,64,512]{2,1,0:T(8,128)(2,1)S(1)}, bf16[3,64,512]{2,1,0:T(8,128)(2,1)S(1)}, u32[]{:S(2)}, u32[]{:S(2)}) collective-permute-start(bf16[3,64,512]{2,1,0:T(8,128)(2,1)S(1)} %update.1.rest_0_), channel_id=1, source_target_pairs={{0,4},{4,8},{8,12},{12,0},{1,5},{5,9},{9,13},{13,1},{2,6},{6,10},{... | collective-permute-start | bytes 589832 | tf_op jit(solution)/shard_map/ppermute | solution.py:441
  109.7 11.3 %collective-permute-start.19 = (bf16[3,64,512]{2,1,0:T(8,128)(2,1)S(1)}, bf16[3,64,512]{2,1,0:T(8,128)(2,1)S(1)}, u32[]{:S(2)}, u32[]{:S(2)}) collective-permute-start(bf16[3,64,512]{2,1,0:T(8,128)(2,1)S(1)} %update.1.rest_0_), channel_id=1, source_target_pairs={{0,2},{2,0},{1,3},{3,1},{4,6},{6,4},{5,7},{7,5},{8,10},{10,8},{9,1... | collective-permute-start | bytes 589832 | tf_op jit(solution)/shard_map/ppermute | solution.py:438
  111.3 16.3 %collective-permute-start.17 = (bf16[3,64,512]{2,1,0:T(8,128)(2,1)S(1)}, bf16[3,64,512]{2,1,0:T(8,128)(2,1)S(1)}, u32[]{:S(2)}, u32[]{:S(2)}) collective-permute-start(bf16[3,64,512]{2,1,0:T(8,128)(2,1)S(1)} %update.1.rest_0_), channel_id=1, source_target_pairs={{0,8},{4,12},{8,0},{12,4},{1,9},{5,13},{9,1},{13,5},{2,10},{6,14},... | collective-permute-start | bytes 589832 | tf_op jit(solution)/shard_map/ppermute | solution.py:441
  115.1 12.5 %collective-permute-start.20 = (bf16[3,64,512]{2,1,0:T(8,128)(2,1)S(1)}, bf16[3,64,512]{2,1,0:T(8,128)(2,1)S(1)}, u32[]{:S(2)}, u32[]{:S(2)}) collective-permute-start(bf16[3,64,512]{2,1,0:T(8,128)(2,1)S(1)} %collective-permute-done.18.rest_3_), channel_id=1, source_target_pairs={{0,2},{2,0},{1,3},{3,1},{4,6},{6,4},{5,7},{7,5},{8,10},{10,8},{9,1... | collective-permute-start | bytes 589832 | tf_op jit(solution)/shard_map/ppermute | solution.py:438
  119.5 8.1 %collective-permute-start.21 = (bf16[3,64,512]{2,1,0:T(8,128)(2,1)S(1)}, bf16[3,64,512]{2,1,0:T(8,128)(2,1)S(1)}, u32[]{:S(2)}, u32[]{:S(2)}) collective-permute-start(bf16[3,64,512]{2,1,0:T(8,128)(2,1)S(1)} %collective-permute-done.16.rest_1_), channel_id=1, source_target_pairs={{0,2},{2,0},{1,3},{3,1},{4,6},{6,4},{5,7},{7,5},{8,10},{10,8},{9,1... | collective-permute-start | bytes 589832 | tf_op jit(solution)/shard_map/ppermute | solution.py:438
  127.6 2.6 %collective-permute-start.22 = (bf16[3,64,512]{2,1,0:T(8,128)(2,1)S(1)}, bf16[3,64,512]{2,1,0:T(8,128)(2,1)S(1)}, u32[]{:S(2)}, u32[]{:S(2)}) collective-permute-start(bf16[3,64,512]{2,1,0:T(8,128)(2,1)S(1)} %update.1.rest_0_), channel_id=1, source_target_pairs={{0,1},{1,0},{2,3},{3,2},{4,5},{5,4},{6,7},{7,6},{8,9},{9,8},{10,11... | collective-permute-start | bytes 589832 | tf_op jit(solution)/shard_map/ppermute | solution.py:438
  127.6 2.6 %collective-permute-start.23 = (bf16[3,64,512]{2,1,0:T(8,128)(2,1)S(1)}, bf16[3,64,512]{2,1,0:T(8,128)(2,1)S(1)}, u32[]{:S(2)}, u32[]{:S(2)}) collective-permute-start(bf16[3,64,512]{2,1,0:T(8,128)(2,1)S(1)} %collective-permute-done.16.rest_1_), channel_id=1, source_target_pairs={{0,1},{1,0},{2,3},{3,2},{4,5},{5,4},{6,7},{7,6},{8,9},{9,8},{10,11... | collective-permute-start | bytes 589832 | tf_op jit(solution)/shard_map/ppermute | solution.py:438
  128.1 2.6 %collective-permute-start.24 = (bf16[3,64,512]{2,1,0:T(8,128)(2,1)S(1)}, bf16[3,64,512]{2,1,0:T(8,128)(2,1)S(1)}, u32[]{:S(2)}, u32[]{:S(2)}) collective-permute-start(bf16[3,64,512]{2,1,0:T(8,128)(2,1)S(1)} %collective-permute-done.17.rest_2_), channel_id=1, source_target_pairs={{0,1},{1,0},{2,3},{3,2},{4,5},{5,4},{6,7},{7,6},{8,9},{9,8},{10,11... | collective-permute-start | bytes 589832 | tf_op jit(solution)/shard_map/ppermute | solution.py:438
  128.2 2.6 %collective-permute-start.25 = (bf16[3,64,512]{2,1,0:T(8,128)(2,1)S(1)}, bf16[3,64,512]{2,1,0:T(8,128)(2,1)S(1)}, u32[]{:S(2)}, u32[]{:S(2)}) collective-permute-start(bf16[3,64,512]{2,1,0:T(8,128)(2,1)S(1)} %collective-permute-done.18.rest_3_), channel_id=1, source_target_pairs={{0,1},{1,0},{2,3},{3,2},{4,5},{5,4},{6,7},{7,6},{8,9},{9,8},{10,11... | collective-permute-start | bytes 589832 | tf_op jit(solution)/shard_map/ppermute | solution.py:438
  128.6 6.9 %collective-permute-start.26 = (bf16[3,64,512]{2,1,0:T(8,128)(2,1)S(1)}, bf16[3,64,512]{2,1,0:T(8,128)(2,1)S(1)}, u32[]{:S(2)}, u32[]{:S(2)}) collective-permute-start(bf16[3,64,512]{2,1,0:T(8,128)(2,1)S(1)} %collective-permute-done.17.rest_2_), channel_id=1, source_target_pairs={{0,2},{2,0},{1,3},{3,1},{4,6},{6,4},{5,7},{7,5},{8,10},{10,8},{9,1... | collective-permute-start | bytes 589832 | tf_op jit(solution)/shard_map/ppermute | solution.py:438
  130.2 5.3 %collective-permute-start.27 = (bf16[3,64,512]{2,1,0:T(8,128)(2,1)S(1)}, bf16[3,64,512]{2,1,0:T(8,128)(2,1)S(1)}, u32[]{:S(2)}, u32[]{:S(2)}) collective-permute-start(bf16[3,64,512]{2,1,0:T(8,128)(2,1)S(1)} %collective-permute-done.19.rest_0_), channel_id=1, source_target_pairs={{0,1},{1,0},{2,3},{3,2},{4,5},{5,4},{6,7},{7,6},{8,9},{9,8},{10,11... | collective-permute-start | bytes 589832 | tf_op jit(solution)/shard_map/ppermute | solution.py:438
  130.2 5.3 %collective-permute-start.30 = (bf16[3,64,512]{2,1,0:T(8,128)(2,1)S(1)}, bf16[3,64,512]{2,1,0:T(8,128)(2,1)S(1)}, u32[]{:S(2)}, u32[]{:S(2)}) collective-permute-start(bf16[3,64,512]{2,1,0:T(8,128)(2,1)S(1)} %collective-permute-done.20.rest_3_), channel_id=1, source_target_pairs={{0,1},{1,0},{2,3},{3,2},{4,5},{5,4},{6,7},{7,6},{8,9},{9,8},{10,11... | collective-permute-start | bytes 589832 | tf_op jit(solution)/shard_map/ppermute | solution.py:438
  130.7 4.8 %collective-permute-start.28 = (bf16[3,64,512]{2,1,0:T(8,128)(2,1)S(1)}, bf16[3,64,512]{2,1,0:T(8,128)(2,1)S(1)}, u32[]{:S(2)}, u32[]{:S(2)}) collective-permute-start(bf16[3,64,512]{2,1,0:T(8,128)(2,1)S(1)} %collective-permute-done.21.rest_1_), channel_id=1, source_target_pairs={{0,1},{1,0},{2,3},{3,2},{4,5},{5,4},{6,7},{7,6},{8,9},{9,8},{10,11... | collective-permute-start | bytes 589832 | tf_op jit(solution)/shard_map/ppermute | solution.py:438
  135.5 1.4 %collective-permute-start.29 = (bf16[3,64,512]{2,1,0:T(8,128)(2,1)S(1)}, bf16[3,64,512]{2,1,0:T(8,128)(2,1)S(1)}, u32[]{:S(2)}, u32[]{:S(2)}) collective-permute-start(bf16[3,64,512]{2,1,0:T(8,128)(2,1)S(1)} %collective-permute-done.26.rest_2_), channel_id=1, source_target_pairs={{0,1},{1,0},{2,3},{3,2},{4,5},{5,4},{6,7},{7,6},{8,9},{9,8},{10,11... | collective-permute-start | bytes 589832 | tf_op jit(solution)/shard_map/ppermute | solution.py:438

commit v10 on v8

--- a/solution.py
+++ b/solution.py
@@ -452,8 +452,14 @@
         return lax.optimization_barrier((value, earlier))[0]
 
     q_other = pl.BlockSpec((BLK, HD), lambda i, s: (0, 1 - s[0]))
-    sent_a = pack(where, key_rows, value_rows, 0, HALF, False)
-    sent_b = pack(where, after(key_rows, sent_a), value_rows, HALF, HALF, False)
+    def paired(first, keys):
+        rows = slice(first, first + HALF)
+        left = jnp.concatenate([keys[rows, :HD], value_rows[rows, :HD]], 1)
+        right = jnp.concatenate([keys[rows, HD:], value_rows[rows, HD:]], 1)
+        return jnp.where(y == 0, right, left)
+
+    sent_a = paired(0, key_rows)
+    sent_b = paired(HALF, after(key_rows, sent_a))
     sent_q = call_blocks(
         pack_q_kernel, "pack_q", [q_other, None], [shape((BLK + RATE_ROWS, HD))]
     )(where, in_hbm(after(queries, sent_b)), step_rates)[0]

time: 116 us -> 115 us (level)
  Pallas kernels: 36.4 us -> 31.6 us
  local copies, waits for them, and re-layouts: 0.34 us -> 2.92 us
  waiting for transfers between devices: 40.3 us -> 41.6 us
    pallas_call x3 -> x1, Pallas kernels: 6.52 us -> 1.76 us  [pack(): pl.pallas_call(functools.partial(pack_kernel, first, count, own), in_spec...]
    slice x0 -> x2, local copies, waits for them, and re-layouts: none -> 1.49 us  [paired(): left = jnp.concatenate([keys[rows, :HD], value_rows[rows, :HD]], 1)]
    select_n x1, other arithmetic: 1.51 us -> 0.11 us  [local(): jnp.where(y == 0, w[:HD], w[HD:])]
    ppermute x23, waiting for transfers between devices: 15.1 us -> 16.3 us  [swap(): return lax.ppermute(value, axis, SWAP)]
  transfers between devices with their start and end apart: 31 -> 31, of which waited for: 12 -> 12; matrix products, arithmetic and copies ran while one was open for 1% -> 0% of each run, Pallas kernels for 24% -> 22%
where the time goes in v10:
time: 115 us; the launch traced here: 114 us
  waiting for transfers between devices  41.6 us (36%)
  starting transfers between devices  36.5 us (32%)
  Pallas kernels  31.6 us (27%)
  local copies, waits for them, and re-layouts  2.92 us (3%)
    ppermute x8, waiting for transfers between devices, shift(): lax.ppermute(value, 'z', [(i, (i + d) % zs) for i in range(zs) if ring or...  25.2 us
    pallas_call x10, Pallas kernels, run(): pl.pallas_call(kernel, in_specs=[SM] + [VM] * len(args), out_specs=[VM] *...  22.4 us
    ppermute x8, starting transfers between devices, shift(): lax.ppermute(value, 'z', [(i, (i + d) % zs) for i in range(zs) if ring or...  20.2 us
    ppermute x23, waiting for transfers between devices, swap(): return lax.ppermute(value, axis, SWAP)  16.3 us
    ppermute x23, starting transfers between devices, swap(): return lax.ppermute(value, axis, SWAP)  16.3 us
    pallas_call x1, Pallas kernels, read_other(): pl.pallas_call(functools.partial(read_other_kernel, zs, count), in_specs=...  3.28 us
    pallas_call x1, Pallas kernels, read_own(): pl.pallas_call(functools.partial(read_own_kernel, zs), in_specs=[SM] + [V...  2.6 us
  transfers between devices with their start and end apart: 31, of which 12 were waited for; matrix products, arithmetic and copies ran while one was open for 0% of the time, Pallas kernels for 22%

profile of v10, /device:TPU:0, one launch (start us, length us, event | category | flops | bytes accessed | tf_op | source)
XLA Modules:
  0.0 114.4 jit_solution(14820901244987217273)
XLA Ops:
  0.6 1.5 %fusion.1 = (bf16[256,512]{1,0:T(8,128)(2,1)S(1)}, bf16[256,512]{1,0:T(8,128)(2,1)S(1)}, bf16[256,512]{1,0:T(8,128)(2,1)S(1)}, bf16[256,512]{1,0:T(8,128)(2,1)S(...) fusion(bf16[512,1024]{1,0:T(8,128)(2,1)} %value.1, bf16[512,1024]{1,0:T(8,128)(2,1)} %key), kind=kLoop, calls=%fused_computation.9 | loop fusion | bytes 3145728 | tf_op jit(solution)/shard_map/slice | solution.py:457
  2.2 3.0 %collective-permute-start = (bf16[256,1024]{1,0:T(8,128)(2,1)S(1)}, bf16[256,1024]{1,0:T(8,128)(2,1)S(1)}, u32[]{:S(2)}, u32[]{:S(2)}) collective-permute-start(bf16[256,1024]{1,0:T(8,128)(2,1)S(1)} %maximum_select_fusion), channel_id=1, source_target_pairs={{0,2},{2,0},{1,3},{3,1},{4,6},{6,4},{5,7},{7,5},{8,10},{10,8},{9,1... | collective-permute-start | bytes 1572872 | tf_op jit(solution)/shard_map/ppermute | solution.py:442
  5.5 1.1 collective-permute-start.1
  6.6 1.8 %pack.1.own = bf16[512,1024]{1,0:T(8,128)(2,1)S(1)} custom-call(s32[3]{0:T(128)S(1)} %pad_add_fusion.where, bf16[512,1024]{1,0:T(8,128)(2,1)} %key, bf16[512,1024]{1,0:T(8,128)(2,1)} %value.1), custom_call_target="tpu_custom_call" | custom-call | tf_op jit(solution)/shard_map/pack/pallas_call | solution.py:105
  8.5 1.6 %pack_q.1 = bf16[528,512]{1,0:T(8,128)(2,1)S(1)} custom-call(s32[3]{0:T(128)S(1)} %pad_add_fusion.where, bf16[512,1024]{1,0:T(8,128)(2,1)} %query, f32[2,512]{1,0:T(2,128)S(1)} %copy-done), custom_call_target="tpu_custom_call" | custom-call | tf_op jit(solution)/shard_map/pack_q/pallas_call | solution.py:74
  10.3 1.1 copy-done.2
  11.9 6.2 %collective-permute-done.foreign.rest_0_.for_a = bf16[256,1024]{1,0:T(8,128)(2,1)S(1)} collective-permute-done((bf16[256,1024]{1,0:T(8,128)(2,1)S(1)}, bf16[256,1024]{1,0:T(8,128)(2,1)S(1)}, u32[]{:S(2)}, u32[]{:S(2)}) %collective-permute-start) | collective-permute-done | bytes 524320 | tf_op jit(solution)/shard_map/ppermute | solution.py:442
  18.0 0.6 pick.2
  18.7 2.1 %collective-permute-start.6 = (bf16[528,512]{1,0:T(8,128)(2,1)S(1)}, bf16[528,512]{1,0:T(8,128)(2,1)S(1)}, u32[]{:S(2)}, u32[]{:S(2)}) collective-permute-start(bf16[528,512]{1,0:T(8,128)(2,1)S(1)} %pack_q.1), channel_id=1, source_target_pairs={{0,2},{2,0},{1,3},{3,1},{4,6},{6,4},{5,7},{7,5},{8,10},{10,8},{9,1... | collective-permute-start | bytes 1622024 | tf_op jit(solution)/shard_map/ppermute | solution.py:442
  20.8 3.5 %collective-permute-start.5 = (bf16[256,1024]{1,0:T(8,128)(2,1)S(1)}, bf16[256,1024]{1,0:T(8,128)(2,1)S(1)}, u32[]{:S(2)}, u32[]{:S(2)}) collective-permute-start(bf16[256,1024]{1,0:T(8,128)(2,1)S(1)} %pick.2), channel_id=1, source_target_pairs={{0,4},{4,8},{8,12},{1,5},{5,9},{9,13},{2,6},{6,10},{10,14},{3,7},{... | collective-permute-start | bytes 1572872 | tf_op jit(solution)/shard_map/ppermute | solution.py:445
  24.4 3.7 %pre_own.1 = (bf16[512,512]{1,0:T(8,128)(2,1)S(1)}, bf16[512,512]{1,0:T(8,128)(2,1)S(1)}, f32[512,256]{1,0:T(8,128)S(1)}, f32[512,256]{1,0:T(8,128)S(1)}, bf16[5...) custom-call(s32[3]{0:T(128)S(1)} %pad_add_fusion.where, ...), custom_call_target="tpu_custom_call" | custom-call | tf_op jit(solution)/shard_map/pre_own/pallas_call | solution.py:55
  28.1 1.2 %collective-permute-done.1.foreign.rest_1_.for_b = bf16[256,1024]{1,0:T(8,128)(2,1)S(1)} collective-permute-done((bf16[256,1024]{1,0:T(8,128)(2,1)S(1)}, bf16[256,1024]{1,0:T(8,128)(2,1)S(1)}, u32[]{:S(2)}, u32[]{:S(2)}) %collective-permute-start.1) | collective-permute-done | bytes 524320 | tf_op jit(solution)/shard_map/ppermute | solution.py:442
  29.3 0.6 pick.3
  30.0 4.1 %collective-permute-start.7 = (bf16[256,1024]{1,0:T(8,128)(2,1)S(1)}, bf16[256,1024]{1,0:T(8,128)(2,1)S(1)}, u32[]{:S(2)}, u32[]{:S(2)}) collective-permute-start(bf16[256,1024]{1,0:T(8,128)(2,1)S(1)} %pick.3), channel_id=1, source_target_pairs={{0,4},{4,8},{8,12},{1,5},{5,9},{9,13},{2,6},{6,10},{10,14},{3,7},{... | collective-permute-start | bytes 1572872 | tf_op jit(solution)/shard_map/ppermute | solution.py:445
  34.0 2.6 %pre.2 = (bf16[512,512]{1,0:T(8,128)(2,1)S(1)}, bf16[512,512]{1,0:T(8,128)(2,1)S(1)}, f32[512,256]{1,0:T(8,128)S(1)}, f32[512,256]{1,0:T(8,128)S(1)}, bf16[512,5...) custom-call(s32[3]{0:T(128)S(1)} %pad_add_fusion.where, ...), custom_call_target="tpu_custom_call" | custom-call | tf_op jit(solution)/shard_map/pre/pallas_call | solution.py:55
  36.6 3.4 %collective-permute-done.6.q_for = bf16[528,512]{1,0:T(8,128)(2,1)S(1)} collective-permute-done((bf16[528,512]{1,0:T(8,128)(2,1)S(1)}, bf16[528,512]{1,0:T(8,128)(2,1)S(1)}, u32[]{:S(2)}, u32[]{:S(2)}) %collective-permute-start.6) | collective-permute-done | bytes 540704 | tf_op jit(solution)/shard_map/ppermute | solution.py:442
  40.0 2.8 %pre.3 = (bf16[512,512]{1,0:T(8,128)(2,1)S(1)}, bf16[512,512]{1,0:T(8,128)(2,1)S(1)}, f32[512,256]{1,0:T(8,128)S(1)}, f32[512,256]{1,0:T(8,128)S(1)}, bf16[512,5...) custom-call(s32[3]{0:T(128)S(1)} %pad_add_fusion.where, ...), custom_call_target="tpu_custom_call" | custom-call | tf_op jit(solution)/shard_map/pre/pallas_call | solution.py:55
  42.8 3.3 %attend_upper.1 = (bf16[512,512]{1,0:T(8,128)(2,1)S(1)}, bf16[512,512]{1,0:T(8,128)(2,1)S(1)}, bf16[512,1024]{1,0:T(8,128)(2,1)S(1)}, bf16[512,1024]{1,0:T(8,128)(2,1)S(1)}) custom-call(s32[3]{0:T(128)S(1)} %pad_add_fusion.where, bf16[512,512]{1,0:T(8,128)(2,1)S(1)} %get-tuple-element.98.q_own.rest_8_, bf16[528,512]{1,0:T(8,128)(2,1)S(1)} %collective-permute-done.6.q_for, ...), custom_call_target="tpu_custom_call" | custom-call | tf_op jit(solution)/shard_map/attend_upper/pallas_call | solution.py:55
  46.1 0.9 collective-permute-done.7.halo_b
  47.1 0.5 collective-permute-start.9
  47.6 1.4 %collective-permute-done.8.halo2_a = bf16[256,1024]{1,0:T(8,128)(2,1)S(1)} collective-permute-done((bf16[256,1024]{1,0:T(8,128)(2,1)S(1)}, bf16[256,1024]{1,0:T(8,128)(2,1)S(1)}, u32[]{:S(2)}, u32[]{:S(2)}) %collective-permute-start.8) | collective-permute-done | bytes 524320 | tf_op jit(solution)/shard_map/ppermute | solution.py:442
  49.0 0.7 collective-permute-done.9.halo2_b
  49.7 3.2 %attend_lower.1 = (bf16[512,512]{1,0:T(8,128)(2,1)S(1)}, bf16[512,512]{1,0:T(8,128)(2,1)S(1)}, bf16[512,512]{1,0:T(8,128)(2,1)S(1)}) custom-call(s32[3]{0:T(128)S(1)} %pad_add_fusion.where, bf16[512,512]{1,0:T(8,128)(2,1)S(1)} %get-tuple-element.98.q_own.rest_8_, bf16[528,512]{1,0:T(8,128)(2,1)S(1)} %collective-permute-done.6.q_for, f32[2,512]{1,0:T(2,128)S(1)} %copy-done, ...), custom_call_target="tpu_custom_call" | custom-call | tf_op jit(solution)/shard_map/attend_lower/pallas_call | solution.py:55
  53.2 2.3 %grad_first.1.before = f32[3,256,512]{2,1,0:T(8,128)S(1)} custom-call(s32[3]{0:T(128)S(1)} %pad_add_fusion.where, bf16[512,512]{1,0:T(8,128)(2,1)S(1)} %get-tuple-element.155.e0, bf16[512,512]{1,0:T(8,128)(2,1)S(1)} %collective-permute-done.11.e1, bf16[512,512]{1,0:T(8,128)(2,1)S(1)} %get-tuple-element.156.k0, bf16[512,512]{1,0:T(8,128)(2,1)S(1)} %get-tuple-element.157.k1, ...), custom_call_target="tpu_custom_call" | custom-call | tf_op jit(solution)/shard_map/grad_first/pallas_call | solution.py:55
  55.4 2.5 %grad_second.1 = (f32[3,64,512]{2,1,0:T(8,128)S(1)}, bf16[3,64,512]{2,1,0:T(8,128)(2,1)S(1)}, bf16[3,64,512]{2,1,0:T(8,128)(2,1)S(1)}, bf16[3,64,512]{2,1,0:T(8,128)(2,1)S(1)}) custom-call(s32[3]{0:T(128)S(1)} %pad_add_fusion.where, bf16[512,512]{1,0:T(8,128)(2,1)S(1)} %get-tuple-element.145.e0, bf16[512,512]{1,0:T(8,128)(2,1)S(1)} %collective-permute-done.10.e1, ...), custom_call_target="tpu_custom_call" | custom-call | tf_op jit(solution)/shard_map/grad_second/pallas_call | solution.py:55
  57.9 1.0 collective-permute-start.15
  58.9 2.1 %collective-permute-start.12 = (bf16[3,64,512]{2,1,0:T(8,128)(2,1)S(1)}, bf16[3,64,512]{2,1,0:T(8,128)(2,1)S(1)}, u32[]{:S(2)}, u32[]{:S(2)}) collective-permute-start(bf16[3,64,512]{2,1,0:T(8,128)(2,1)S(1)} %get-tuple-element.165), channel_id=1, source_target_pairs={{0,4},{4,8},{8,12},{12,0},{1,5},{5,9},{9,13},{13,1},{2,6},{6,10},{... | collective-permute-start | bytes 589832 | tf_op jit(solution)/shard_map/ppermute | solution.py:445
  61.0 2.6 %collective-permute-start.13 = (bf16[3,64,512]{2,1,0:T(8,128)(2,1)S(1)}, bf16[3,64,512]{2,1,0:T(8,128)(2,1)S(1)}, u32[]{:S(2)}, u32[]{:S(2)}) collective-permute-start(bf16[3,64,512]{2,1,0:T(8,128)(2,1)S(1)} %get-tuple-element.166), channel_id=1, source_target_pairs={{0,8},{4,12},{8,0},{12,4},{1,9},{5,13},{9,1},{13,5},{2,10},{6,14},... | collective-permute-start | bytes 589832 | tf_op jit(solution)/shard_map/ppermute | solution.py:445
  63.6 1.3 %collective-permute-start.14 = (bf16[3,64,512]{2,1,0:T(8,128)(2,1)S(1)}, bf16[3,64,512]{2,1,0:T(8,128)(2,1)S(1)}, u32[]{:S(2)}, u32[]{:S(2)}) collective-permute-start(bf16[3,64,512]{2,1,0:T(8,128)(2,1)S(1)} %get-tuple-element.167), channel_id=1, source_target_pairs={{0,12},{4,0},{8,4},{12,8},{1,13},{5,1},{9,5},{13,9},{2,14},{6,2},{... | collective-permute-start | bytes 589832 | tf_op jit(solution)/shard_map/ppermute | solution.py:445
  64.9 3.9 %collective-permute-done.12.rest_0_ = bf16[3,64,512]{2,1,0:T(8,128)(2,1)S(1)} collective-permute-done((bf16[3,64,512]{2,1,0:T(8,128)(2,1)S(1)}, bf16[3,64,512]{2,1,0:T(8,128)(2,1)S(1)}, u32[]{:S(2)}, u32[]{:S(2)}) %collective-permute-start.12) | collective-permute-done | bytes 196640 | tf_op jit(solution)/shard_map/ppermute | solution.py:445
  68.9 7.9 %collective-permute-done.13.rest_1_ = bf16[3,64,512]{2,1,0:T(8,128)(2,1)S(1)} collective-permute-done((bf16[3,64,512]{2,1,0:T(8,128)(2,1)S(1)}, bf16[3,64,512]{2,1,0:T(8,128)(2,1)S(1)}, u32[]{:S(2)}, u32[]{:S(2)}) %collective-permute-start.13) | collective-permute-done | bytes 196640 | tf_op jit(solution)/shard_map/ppermute | solution.py:445
  76.7 0.8 update.1.rest_0_
  77.5 5.8 %collective-permute-start.18 = (bf16[3,64,512]{2,1,0:T(8,128)(2,1)S(1)}, bf16[3,64,512]{2,1,0:T(8,128)(2,1)S(1)}, u32[]{:S(2)}, u32[]{:S(2)}) collective-permute-start(bf16[3,64,512]{2,1,0:T(8,128)(2,1)S(1)} %update.1.rest_0_), channel_id=1, source_target_pairs={{0,12},{4,0},{8,4},{12,8},{1,13},{5,1},{9,5},{13,9},{2,14},{6,2},{... | collective-permute-start | bytes 589832 | tf_op jit(solution)/shard_map/ppermute | solution.py:445
  83.3 1.5 %collective-permute-start.19 = (bf16[3,64,512]{2,1,0:T(8,128)(2,1)S(1)}, bf16[3,64,512]{2,1,0:T(8,128)(2,1)S(1)}, u32[]{:S(2)}, u32[]{:S(2)}) collective-permute-start(bf16[3,64,512]{2,1,0:T(8,128)(2,1)S(1)} %update.1.rest_0_), channel_id=1, source_target_pairs={{0,2},{2,0},{1,3},{3,1},{4,6},{6,4},{5,7},{7,5},{8,10},{10,8},{9,1... | collective-permute-start | bytes 589832 | tf_op jit(solution)/shard_map/ppermute | solution.py:442
  84.8 0.8 collective-permute-start.17
  85.6 3.0 %collective-permute-done.18.rest_3_ = bf16[3,64,512]{2,1,0:T(8,128)(2,1)S(1)} collective-permute-done((bf16[3,64,512]{2,1,0:T(8,128)(2,1)S(1)}, bf16[3,64,512]{2,1,0:T(8,128)(2,1)S(1)}, u32[]{:S(2)}, u32[]{:S(2)}) %collective-permute-start.18) | collective-permute-done | bytes 196640 | tf_op jit(solution)/shard_map/ppermute | solution.py:445
  88.7 1.5 %collective-permute-start.20 = (bf16[3,64,512]{2,1,0:T(8,128)(2,1)S(1)}, bf16[3,64,512]{2,1,0:T(8,128)(2,1)S(1)}, u32[]{:S(2)}, u32[]{:S(2)}) collective-permute-start(bf16[3,64,512]{2,1,0:T(8,128)(2,1)S(1)} %collective-permute-done.18.rest_3_), channel_id=1, source_target_pairs={{0,2},{2,0},{1,3},{3,1},{4,6},{6,4},{5,7},{7,5},{8,10},{10,8},{9,1... | collective-permute-start | bytes 589832 | tf_op jit(solution)/shard_map/ppermute | solution.py:442
  90.2 2.9 %collective-permute-done.16.rest_1_ = bf16[3,64,512]{2,1,0:T(8,128)(2,1)S(1)} collective-permute-done((bf16[3,64,512]{2,1,0:T(8,128)(2,1)S(1)}, bf16[3,64,512]{2,1,0:T(8,128)(2,1)S(1)}, u32[]{:S(2)}, u32[]{:S(2)}) %collective-permute-start.16) | collective-permute-done | bytes 196640 | tf_op jit(solution)/shard_map/ppermute | solution.py:445
  93.0 1.5 %collective-permute-start.21 = (bf16[3,64,512]{2,1,0:T(8,128)(2,1)S(1)}, bf16[3,64,512]{2,1,0:T(8,128)(2,1)S(1)}, u32[]{:S(2)}, u32[]{:S(2)}) collective-permute-start(bf16[3,64,512]{2,1,0:T(8,128)(2,1)S(1)} %collective-permute-done.16.rest_1_), channel_id=1, source_target_pairs={{0,2},{2,0},{1,3},{3,1},{4,6},{6,4},{5,7},{7,5},{8,10},{10,8},{9,1... | collective-permute-start | bytes 589832 | tf_op jit(solution)/shard_map/ppermute | solution.py:442
  94.5 6.6 %collective-permute-done.17.rest_2_ = bf16[3,64,512]{2,1,0:T(8,128)(2,1)S(1)} collective-permute-done((bf16[3,64,512]{2,1,0:T(8,128)(2,1)S(1)}, bf16[3,64,512]{2,1,0:T(8,128)(2,1)S(1)}, u32[]{:S(2)}, u32[]{:S(2)}) %collective-permute-start.17) | collective-permute-done | bytes 196640 | tf_op jit(solution)/shard_map/ppermute | solution.py:445
  101.2 1.5 %collective-permute-start.26 = (bf16[3,64,512]{2,1,0:T(8,128)(2,1)S(1)}, bf16[3,64,512]{2,1,0:T(8,128)(2,1)S(1)}, u32[]{:S(2)}, u32[]{:S(2)}) collective-permute-start(bf16[3,64,512]{2,1,0:T(8,128)(2,1)S(1)} %collective-permute-done.17.rest_2_), channel_id=1, source_target_pairs={{0,2},{2,0},{1,3},{3,1},{4,6},{6,4},{5,7},{7,5},{8,10},{10,8},{9,1... | collective-permute-start | bytes 589832 | tf_op jit(solution)/shard_map/ppermute | solution.py:442
  102.8 0.5 collective-permute-start.23
  103.3 0.4 collective-permute-start.25
  103.8 3.4 %collective-permute-done.26.rest_2_ = bf16[3,64,512]{2,1,0:T(8,128)(2,1)S(1)} collective-permute-done((bf16[3,64,512]{2,1,0:T(8,128)(2,1)S(1)}, bf16[3,64,512]{2,1,0:T(8,128)(2,1)S(1)}, u32[]{:S(2)}, u32[]{:S(2)}) %collective-permute-start.26) | collective-permute-done | bytes 196640 | tf_op jit(solution)/shard_map/ppermute | solution.py:442
  107.2 0.5 collective-permute-start.28
  107.8 0.4 collective-permute-start.30
  108.3 2.6 %read_own.1 = (bf16[512,1024]{1,0:T(8,128)(2,1)}, bf16[1536,512]{1,0:T(8,128)(2,1)S(1)}, bf16[512,512]{1,0:T(8,128)(2,1)S(1)}) custom-call(s32[3]{0:T(128)S(1)} %pad_add_fusion.where, bf16[3,64,512]{2,1,0:T(8,128)(2,1)S(1)} %update.1.rest_0_, bf16[3,64,512]{2,1,0:T(8,128)(2,1)S(1)} %collective-permute-done.16.rest_1_, ...), custom_call_target="tpu_custom_call" | custom-call | tf_op jit(solution)/shard_map/read_own/pallas_call | solution.py:388
  110.9 3.3 %read_other.1 = (bf16[512,1024]{1,0:T(8,128)(2,1)}, bf16[192,512]{1,0:T(8,128)(2,1)}) custom-call(s32[3]{0:T(128)S(1)} %pad_add_fusion.where, bf16[3,64,512]{2,1,0:T(8,128)(2,1)S(1)} %collective-permute-done.19.rest_0_, bf16[3,64,512]{2,1,0:T(8,128)(2,1)S(1)} %collective-permute-done.21.rest_1_, ...), custom_call_target="tpu_custom_call", output_to_operand_aliasing={{0}: (12, {})} | custom-call | tf_op jit(solution)/shard_map/read_other/pallas_call | solution.py:419
  (47 shorter events, 1.8 us)
Async XLA Ops:
  2.1 3.2 %copy-start.1 = (bf16[512,1024]{1,0:T(8,128)(2,1)S(1)}, bf16[512,1024]{1,0:T(8,128)(2,1)}, u32[]{:S(2)}) copy-start(bf16[512,1024]{1,0:T(8,128)(2,1)} %key) | copy-start | bytes 3145732
  2.2 15.8 %collective-permute-start = (bf16[256,1024]{1,0:T(8,128)(2,1)S(1)}, bf16[256,1024]{1,0:T(8,128)(2,1)S(1)}, u32[]{:S(2)}, u32[]{:S(2)}) collective-permute-start(bf16[256,1024]{1,0:T(8,128)(2,1)S(1)} %maximum_select_fusion), channel_id=1, source_target_pairs={{0,2},{2,0},{1,3},{3,1},{4,6},{6,4},{5,7},{7,5},{8,10},{10,8},{9,1... | collective-permute-start | bytes 1572872 | tf_op jit(solution)/shard_map/ppermute | solution.py:442
  5.5 23.8 %collective-permute-start.1 = (bf16[256,1024]{1,0:T(8,128)(2,1)S(1)}, bf16[256,1024]{1,0:T(8,128)(2,1)S(1)}, u32[]{:S(2)}, u32[]{:S(2)}) collective-permute-start(bf16[256,1024]{1,0:T(8,128)(2,1)S(1)} %maximum_select_fusion.1), channel_id=1, source_target_pairs={{0,2},{2,0},{1,3},{3,1},{4,6},{6,4},{5,7},{7,5},{8,10},{10,8},{9,1... | collective-permute-start | bytes 1572872 | tf_op jit(solution)/shard_map/ppermute | solution.py:442
  6.6 1.9 %copy-start = (f32[2,512]{1,0:T(2,128)S(1)}, f32[2,512]{1,0:T(2,128)}, u32[]{:S(2)}) copy-start(f32[2,512]{1,0:T(2,128)} %rates.5) | copy-start | bytes 12292
  6.6 3.5 %copy-start.4 = (bf16[1024,512]{1,0:T(8,128)(2,1)S(1)}, bf16[1024,512]{1,0:T(8,128)(2,1)}, u32[]{:S(2)}) copy-start(bf16[1024,512]{1,0:T(8,128)(2,1)} %param.12) | copy-start | bytes 3145732
  8.4 1.8 %copy-start.3 = (bf16[1024,512]{1,0:T(8,128)(2,1)S(1)}, bf16[1024,512]{1,0:T(8,128)(2,1)}, u32[]{:S(2)}) copy-start(bf16[1024,512]{1,0:T(8,128)(2,1)} %param.13) | copy-start | bytes 3145732
  8.4 16.0 %collective-permute-start.2 = (bf16[512,1024]{1,0:T(8,128)(2,1)S(1)}, bf16[512,1024]{1,0:T(8,128)(2,1)S(1)}, u32[]{:S(2)}, u32[]{:S(2)}) collective-permute-start(bf16[512,1024]{1,0:T(8,128)(2,1)S(1)} %pack.1.own), channel_id=1, source_target_pairs={{0,1},{1,0},{2,3},{3,2},{4,5},{5,4},{6,7},{7,6},{8,9},{9,8},{10,11... | collective-permute-start | bytes 3145736 | tf_op jit(solution)/shard_map/ppermute | solution.py:442
  10.1 1.2 %copy-start.2 = (bf16[512,1024]{1,0:T(8,128)(2,1)S(1)}, bf16[512,1024]{1,0:T(8,128)(2,1)}, u32[]{:S(2)}) copy-start(bf16[512,1024]{1,0:T(8,128)(2,1)} %query) | copy-start | bytes 3145732
  10.2 1.5 %copy-start.5 = (bf16[1024,512]{1,0:T(8,128)(2,1)S(1)}, bf16[1024,512]{1,0:T(8,128)(2,1)}, u32[]{:S(2)}) copy-start(bf16[1024,512]{1,0:T(8,128)(2,1)} %param.11) | copy-start | bytes 3145732
  18.6 10.6 %collective-permute-start.3 = (bf16[256,1024]{1,0:T(8,128)(2,1)S(1)}, bf16[256,1024]{1,0:T(8,128)(2,1)S(1)}, u32[]{:S(2)}, u32[]{:S(2)}) collective-permute-start(bf16[256,1024]{1,0:T(8,128)(2,1)S(1)} %collective-permute-done.foreign.rest_0_.for_a), channel_id=1, source_target_pairs={{0,1},{1,0},{2,3},{3,2},{4,5},{5,4},{6,7},{7,6},{8,9},{9,8},{10,11... | collective-permute-start | bytes 1572872 | tf_op jit(solution)/shard_map/ppermute | solution.py:442
  18.7 21.3 %collective-permute-start.6 = (bf16[528,512]{1,0:T(8,128)(2,1)S(1)}, bf16[528,512]{1,0:T(8,128)(2,1)S(1)}, u32[]{:S(2)}, u32[]{:S(2)}) collective-permute-start(bf16[528,512]{1,0:T(8,128)(2,1)S(1)} %pack_q.1), channel_id=1, source_target_pairs={{0,2},{2,0},{1,3},{3,1},{4,6},{6,4},{5,7},{7,5},{8,10},{10,8},{9,1... | collective-permute-start | bytes 1622024 | tf_op jit(solution)/shard_map/ppermute | solution.py:442
  20.8 15.8 %collective-permute-start.5 = (bf16[256,1024]{1,0:T(8,128)(2,1)S(1)}, bf16[256,1024]{1,0:T(8,128)(2,1)S(1)}, u32[]{:S(2)}, u32[]{:S(2)}) collective-permute-start(bf16[256,1024]{1,0:T(8,128)(2,1)S(1)} %pick.2), channel_id=1, source_target_pairs={{0,4},{4,8},{8,12},{1,5},{5,9},{9,13},{2,6},{6,10},{10,14},{3,7},{... | collective-permute-start | bytes 1572872 | tf_op jit(solution)/shard_map/ppermute | solution.py:445
  29.9 6.7 %collective-permute-start.4 = (bf16[256,1024]{1,0:T(8,128)(2,1)S(1)}, bf16[256,1024]{1,0:T(8,128)(2,1)S(1)}, u32[]{:S(2)}, u32[]{:S(2)}) collective-permute-start(bf16[256,1024]{1,0:T(8,128)(2,1)S(1)} %collective-permute-done.1.foreign.rest_1_.for_b), channel_id=1, source_target_pairs={{0,1},{1,0},{2,3},{3,2},{4,5},{5,4},{6,7},{7,6},{8,9},{9,8},{10,11... | collective-permute-start | bytes 1572872 | tf_op jit(solution)/shard_map/ppermute | solution.py:442
  30.0 17.1 %collective-permute-start.7 = (bf16[256,1024]{1,0:T(8,128)(2,1)S(1)}, bf16[256,1024]{1,0:T(8,128)(2,1)S(1)}, u32[]{:S(2)}, u32[]{:S(2)}) collective-permute-start(bf16[256,1024]{1,0:T(8,128)(2,1)S(1)} %pick.3), channel_id=1, source_target_pairs={{0,4},{4,8},{8,12},{1,5},{5,9},{9,13},{2,6},{6,10},{10,14},{3,7},{... | collective-permute-start | bytes 1572872 | tf_op jit(solution)/shard_map/ppermute | solution.py:445
  47.1 1.9 %collective-permute-start.8 = (bf16[256,1024]{1,0:T(8,128)(2,1)S(1)}, bf16[256,1024]{1,0:T(8,128)(2,1)S(1)}, u32[]{:S(2)}, u32[]{:S(2)}) collective-permute-start(bf16[256,1024]{1,0:T(8,128)(2,1)S(1)} %collective-permute-done.5.halo_a), channel_id=1, source_target_pairs={{0,1},{1,0},{2,3},{3,2},{4,5},{5,4},{6,7},{7,6},{8,9},{9,8},{10,11... | collective-permute-start | bytes 1572872 | tf_op jit(solution)/shard_map/ppermute | solution.py:442
  47.1 2.7 %collective-permute-start.9 = (bf16[256,1024]{1,0:T(8,128)(2,1)S(1)}, bf16[256,1024]{1,0:T(8,128)(2,1)S(1)}, u32[]{:S(2)}, u32[]{:S(2)}) collective-permute-start(bf16[256,1024]{1,0:T(8,128)(2,1)S(1)} %collective-permute-done.7.halo_b), channel_id=1, source_target_pairs={{0,1},{1,0},{2,3},{3,2},{4,5},{5,4},{6,7},{7,6},{8,9},{9,8},{10,11... | collective-permute-start | bytes 1572872 | tf_op jit(solution)/shard_map/ppermute | solution.py:442
  47.6 5.6 %collective-permute-start.11 = (bf16[512,512]{1,0:T(8,128)(2,1)S(1)}, bf16[512,512]{1,0:T(8,128)(2,1)S(1)}, u32[]{:S(2)}, u32[]{:S(2)}) collective-permute-start(bf16[512,512]{1,0:T(8,128)(2,1)S(1)} %get-tuple-element.155.e0), channel_id=1, source_target_pairs={{0,1},{1,0},{2,3},{3,2},{4,5},{5,4},{6,7},{7,6},{8,9},{9,8},{10,11... | collective-permute-start | bytes 1572872 | tf_op jit(solution)/shard_map/ppermute | solution.py:442
  53.0 2.5 %collective-permute-start.10 = (bf16[512,512]{1,0:T(8,128)(2,1)S(1)}, bf16[512,512]{1,0:T(8,128)(2,1)S(1)}, u32[]{:S(2)}, u32[]{:S(2)}) collective-permute-start(bf16[512,512]{1,0:T(8,128)(2,1)S(1)} %get-tuple-element.145.e0), channel_id=1, source_target_pairs={{0,1},{1,0},{2,3},{3,2},{4,5},{5,4},{6,7},{7,6},{8,9},{9,8},{10,11... | collective-permute-start | bytes 1572872 | tf_op jit(solution)/shard_map/ppermute | solution.py:442
  57.9 18.8 %collective-permute-start.15 = (bf16[512,512]{1,0:T(8,128)(2,1)S(1)}, bf16[512,512]{1,0:T(8,128)(2,1)S(1)}, u32[]{:S(2)}, u32[]{:S(2)}) collective-permute-start(bf16[512,512]{1,0:T(8,128)(2,1)S(1)} %get-tuple-element.169), channel_id=1, source_target_pairs={{0,2},{2,0},{1,3},{3,1},{4,6},{6,4},{5,7},{7,5},{8,10},{10,8},{9,1... | collective-permute-start | bytes 1572872 | tf_op jit(solution)/shard_map/ppermute | solution.py:442
  58.9 9.9 %collective-permute-start.12 = (bf16[3,64,512]{2,1,0:T(8,128)(2,1)S(1)}, bf16[3,64,512]{2,1,0:T(8,128)(2,1)S(1)}, u32[]{:S(2)}, u32[]{:S(2)}) collective-permute-start(bf16[3,64,512]{2,1,0:T(8,128)(2,1)S(1)} %get-tuple-element.165), channel_id=1, source_target_pairs={{0,4},{4,8},{8,12},{12,0},{1,5},{5,9},{9,13},{13,1},{2,6},{6,10},{... | collective-permute-start | bytes 589832 | tf_op jit(solution)/shard_map/ppermute | solution.py:445
  61.0 15.8 %collective-permute-start.13 = (bf16[3,64,512]{2,1,0:T(8,128)(2,1)S(1)}, bf16[3,64,512]{2,1,0:T(8,128)(2,1)S(1)}, u32[]{:S(2)}, u32[]{:S(2)}) collective-permute-start(bf16[3,64,512]{2,1,0:T(8,128)(2,1)S(1)} %get-tuple-element.166), channel_id=1, source_target_pairs={{0,8},{4,12},{8,0},{12,4},{1,9},{5,13},{9,1},{13,5},{2,10},{6,14},... | collective-permute-start | bytes 589832 | tf_op jit(solution)/shard_map/ppermute | solution.py:445
  63.6 13.1 %collective-permute-start.14 = (bf16[3,64,512]{2,1,0:T(8,128)(2,1)S(1)}, bf16[3,64,512]{2,1,0:T(8,128)(2,1)S(1)}, u32[]{:S(2)}, u32[]{:S(2)}) collective-permute-start(bf16[3,64,512]{2,1,0:T(8,128)(2,1)S(1)} %get-tuple-element.167), channel_id=1, source_target_pairs={{0,12},{4,0},{8,4},{12,8},{1,13},{5,1},{9,5},{13,9},{2,14},{6,2},{... | collective-permute-start | bytes 589832 | tf_op jit(solution)/shard_map/ppermute | solution.py:445
  77.5 11.1 %collective-permute-start.18 = (bf16[3,64,512]{2,1,0:T(8,128)(2,1)S(1)}, bf16[3,64,512]{2,1,0:T(8,128)(2,1)S(1)}, u32[]{:S(2)}, u32[]{:S(2)}) collective-permute-start(bf16[3,64,512]{2,1,0:T(8,128)(2,1)S(1)} %update.1.rest_0_), channel_id=1, source_target_pairs={{0,12},{4,0},{8,4},{12,8},{1,13},{5,1},{9,5},{13,9},{2,14},{6,2},{... | collective-permute-start | bytes 589832 | tf_op jit(solution)/shard_map/ppermute | solution.py:445
  83.3 9.7 %collective-permute-start.16 = (bf16[3,64,512]{2,1,0:T(8,128)(2,1)S(1)}, bf16[3,64,512]{2,1,0:T(8,128)(2,1)S(1)}, u32[]{:S(2)}, u32[]{:S(2)}) collective-permute-start(bf16[3,64,512]{2,1,0:T(8,128)(2,1)S(1)} %update.1.rest_0_), channel_id=1, source_target_pairs={{0,4},{4,8},{8,12},{12,0},{1,5},{5,9},{9,13},{13,1},{2,6},{6,10},{... | collective-permute-start | bytes 589832 | tf_op jit(solution)/shard_map/ppermute | solution.py:445
  83.3 19.4 %collective-permute-start.19 = (bf16[3,64,512]{2,1,0:T(8,128)(2,1)S(1)}, bf16[3,64,512]{2,1,0:T(8,128)(2,1)S(1)}, u32[]{:S(2)}, u32[]{:S(2)}) collective-permute-start(bf16[3,64,512]{2,1,0:T(8,128)(2,1)S(1)} %update.1.rest_0_), channel_id=1, source_target_pairs={{0,2},{2,0},{1,3},{3,1},{4,6},{6,4},{5,7},{7,5},{8,10},{10,8},{9,1... | collective-permute-start | bytes 589832 | tf_op jit(solution)/shard_map/ppermute | solution.py:442
  84.8 16.4 %collective-permute-start.17 = (bf16[3,64,512]{2,1,0:T(8,128)(2,1)S(1)}, bf16[3,64,512]{2,1,0:T(8,128)(2,1)S(1)}, u32[]{:S(2)}, u32[]{:S(2)}) collective-permute-start(bf16[3,64,512]{2,1,0:T(8,128)(2,1)S(1)} %update.1.rest_0_), channel_id=1, source_target_pairs={{0,8},{4,12},{8,0},{12,4},{1,9},{5,13},{9,1},{13,5},{2,10},{6,14},... | collective-permute-start | bytes 589832 | tf_op jit(solution)/shard_map/ppermute | solution.py:445
  88.7 14.0 %collective-permute-start.20 = (bf16[3,64,512]{2,1,0:T(8,128)(2,1)S(1)}, bf16[3,64,512]{2,1,0:T(8,128)(2,1)S(1)}, u32[]{:S(2)}, u32[]{:S(2)}) collective-permute-start(bf16[3,64,512]{2,1,0:T(8,128)(2,1)S(1)} %collective-permute-done.18.rest_3_), channel_id=1, source_target_pairs={{0,2},{2,0},{1,3},{3,1},{4,6},{6,4},{5,7},{7,5},{8,10},{10,8},{9,1... | collective-permute-start | bytes 589832 | tf_op jit(solution)/shard_map/ppermute | solution.py:442
  93.0 9.6 %collective-permute-start.21 = (bf16[3,64,512]{2,1,0:T(8,128)(2,1)S(1)}, bf16[3,64,512]{2,1,0:T(8,128)(2,1)S(1)}, u32[]{:S(2)}, u32[]{:S(2)}) collective-permute-start(bf16[3,64,512]{2,1,0:T(8,128)(2,1)S(1)} %collective-permute-done.16.rest_1_), channel_id=1, source_target_pairs={{0,2},{2,0},{1,3},{3,1},{4,6},{6,4},{5,7},{7,5},{8,10},{10,8},{9,1... | collective-permute-start | bytes 589832 | tf_op jit(solution)/shard_map/ppermute | solution.py:442
  101.2 6.0 %collective-permute-start.26 = (bf16[3,64,512]{2,1,0:T(8,128)(2,1)S(1)}, bf16[3,64,512]{2,1,0:T(8,128)(2,1)S(1)}, u32[]{:S(2)}, u32[]{:S(2)}) collective-permute-start(bf16[3,64,512]{2,1,0:T(8,128)(2,1)S(1)} %collective-permute-done.17.rest_2_), channel_id=1, source_target_pairs={{0,2},{2,0},{1,3},{3,1},{4,6},{6,4},{5,7},{7,5},{8,10},{10,8},{9,1... | collective-permute-start | bytes 589832 | tf_op jit(solution)/shard_map/ppermute | solution.py:442
  102.7 4.5 %collective-permute-start.22 = (bf16[3,64,512]{2,1,0:T(8,128)(2,1)S(1)}, bf16[3,64,512]{2,1,0:T(8,128)(2,1)S(1)}, u32[]{:S(2)}, u32[]{:S(2)}) collective-permute-start(bf16[3,64,512]{2,1,0:T(8,128)(2,1)S(1)} %update.1.rest_0_), channel_id=1, source_target_pairs={{0,1},{1,0},{2,3},{3,2},{4,5},{5,4},{6,7},{7,6},{8,9},{9,8},{10,11... | collective-permute-start | bytes 589832 | tf_op jit(solution)/shard_map/ppermute | solution.py:442
  102.8 4.4 %collective-permute-start.23 = (bf16[3,64,512]{2,1,0:T(8,128)(2,1)S(1)}, bf16[3,64,512]{2,1,0:T(8,128)(2,1)S(1)}, u32[]{:S(2)}, u32[]{:S(2)}) collective-permute-start(bf16[3,64,512]{2,1,0:T(8,128)(2,1)S(1)} %collective-permute-done.16.rest_1_), channel_id=1, source_target_pairs={{0,1},{1,0},{2,3},{3,2},{4,5},{5,4},{6,7},{7,6},{8,9},{9,8},{10,11... | collective-permute-start | bytes 589832 | tf_op jit(solution)/shard_map/ppermute | solution.py:442
  103.3 3.9 %collective-permute-start.24 = (bf16[3,64,512]{2,1,0:T(8,128)(2,1)S(1)}, bf16[3,64,512]{2,1,0:T(8,128)(2,1)S(1)}, u32[]{:S(2)}, u32[]{:S(2)}) collective-permute-start(bf16[3,64,512]{2,1,0:T(8,128)(2,1)S(1)} %collective-permute-done.17.rest_2_), channel_id=1, source_target_pairs={{0,1},{1,0},{2,3},{3,2},{4,5},{5,4},{6,7},{7,6},{8,9},{9,8},{10,11... | collective-permute-start | bytes 589832 | tf_op jit(solution)/shard_map/ppermute | solution.py:442
  103.3 3.8 %collective-permute-start.25 = (bf16[3,64,512]{2,1,0:T(8,128)(2,1)S(1)}, bf16[3,64,512]{2,1,0:T(8,128)(2,1)S(1)}, u32[]{:S(2)}, u32[]{:S(2)}) collective-permute-start(bf16[3,64,512]{2,1,0:T(8,128)(2,1)S(1)} %collective-permute-done.18.rest_3_), channel_id=1, source_target_pairs={{0,1},{1,0},{2,3},{3,2},{4,5},{5,4},{6,7},{7,6},{8,9},{9,8},{10,11... | collective-permute-start | bytes 589832 | tf_op jit(solution)/shard_map/ppermute | solution.py:442
  107.2 3.7 %collective-permute-start.27 = (bf16[3,64,512]{2,1,0:T(8,128)(2,1)S(1)}, bf16[3,64,512]{2,1,0:T(8,128)(2,1)S(1)}, u32[]{:S(2)}, u32[]{:S(2)}) collective-permute-start(bf16[3,64,512]{2,1,0:T(8,128)(2,1)S(1)} %collective-permute-done.19.rest_0_), channel_id=1, source_target_pairs={{0,1},{1,0},{2,3},{3,2},{4,5},{5,4},{6,7},{7,6},{8,9},{9,8},{10,11... | collective-permute-start | bytes 589832 | tf_op jit(solution)/shard_map/ppermute | solution.py:442
  107.2 3.6 %collective-permute-start.28 = (bf16[3,64,512]{2,1,0:T(8,128)(2,1)S(1)}, bf16[3,64,512]{2,1,0:T(8,128)(2,1)S(1)}, u32[]{:S(2)}, u32[]{:S(2)}) collective-permute-start(bf16[3,64,512]{2,1,0:T(8,128)(2,1)S(1)} %collective-permute-done.21.rest_1_), channel_id=1, source_target_pairs={{0,1},{1,0},{2,3},{3,2},{4,5},{5,4},{6,7},{7,6},{8,9},{9,8},{10,11... | collective-permute-start | bytes 589832 | tf_op jit(solution)/shard_map/ppermute | solution.py:442
  107.7 3.1 %collective-permute-start.29 = (bf16[3,64,512]{2,1,0:T(8,128)(2,1)S(1)}, bf16[3,64,512]{2,1,0:T(8,128)(2,1)S(1)}, u32[]{:S(2)}, u32[]{:S(2)}) collective-permute-start(bf16[3,64,512]{2,1,0:T(8,128)(2,1)S(1)} %collective-permute-done.26.rest_2_), channel_id=1, source_target_pairs={{0,1},{1,0},{2,3},{3,2},{4,5},{5,4},{6,7},{7,6},{8,9},{9,8},{10,11... | collective-permute-start | bytes 589832 | tf_op jit(solution)/shard_map/ppermute | solution.py:442
  107.8 3.1 %collective-permute-start.30 = (bf16[3,64,512]{2,1,0:T(8,128)(2,1)S(1)}, bf16[3,64,512]{2,1,0:T(8,128)(2,1)S(1)}, u32[]{:S(2)}, u32[]{:S(2)}) collective-permute-start(bf16[3,64,512]{2,1,0:T(8,128)(2,1)S(1)} %collective-permute-done.20.rest_3_), channel_id=1, source_target_pairs={{0,1},{1,0},{2,3},{3,2},{4,5},{5,4},{6,7},{7,6},{8,9},{9,8},{10,11... | collective-permute-start | bytes 589832 | tf_op jit(solution)/shard_map/ppermute | solution.py:442

commit v11 on v10

--- a/solution.py
+++ b/solution.py
@@ -362,8 +362,8 @@
 def read(qn, att, full, out, head, work, sems):
     column = pl.ds(pl.multiple_of(head * HD, HD), HD)
     copies = []
-    for c in range(2):
-        rows = pl.ds(c * HALF, HALF)
+    for c in range(1):
+        rows = pl.ds(0, BLK)
         x = qn(rows)
         hg = mm_t(x, full[0:HD, :])
         hu = mm_t(x, full[HD : 2 * HD, :])
@@ -516,7 +516,7 @@
         [pltpu.VMEM(total.shape, F32)],
     )(where, err_low, err_low2, *factors_of(low, low2), wd, before)
     got = [shift(s, d) for d, s in enumerate(sends, 1)]
-    att_back = swap(after(att_for, own_sum), "y")
+    att_back = swap(after(att_for, before), "y")
     got, att_back = lax.optimization_barrier((got, att_back))
     piece = call(functools.partial(update_kernel, zs), "update", [shape((3, rows, HD))])(
         where, own_sum, *got, wg, wu, wd

time: 115 us -> 115 us (level)
    ppermute x23, waiting for transfers between devices: 16.3 us -> 21.1 us  [swap(): return lax.ppermute(value, axis, SWAP)]
    ppermute x8, waiting for transfers between devices: 25.2 us -> 20.6 us  [shift(): lax.ppermute(value, 'z', [(i, (i + d) % zs) for i in range(zs) if ring or...]
  transfers between devices with their start and end apart: 31 -> 31, of which waited for: 12 -> 12; matrix products, arithmetic and copies ran while one was open for 0% -> 0% of each run, Pallas kernels for 22% -> 24%
where the time goes in v11:
time: 115 us; the launch traced here: 114 us
  waiting for transfers between devices  41.7 us (36%)
  starting transfers between devices  36.5 us (32%)
  Pallas kernels  31.5 us (27%)
  local copies, waits for them, and re-layouts  2.92 us (3%)
    pallas_call x10, Pallas kernels, run(): pl.pallas_call(kernel, in_specs=[SM] + [VM] * len(args), out_specs=[VM] *...  22.3 us
    ppermute x23, waiting for transfers between devices, swap(): return lax.ppermute(value, axis, SWAP)  21.1 us
    ppermute x8, waiting for transfers between devices, shift(): lax.ppermute(value, 'z', [(i, (i + d) % zs) for i in range(zs) if ring or...  20.6 us
    ppermute x8, starting transfers between devices, shift(): lax.ppermute(value, 'z', [(i, (i + d) % zs) for i in range(zs) if ring or...  20.2 us
    ppermute x23, starting transfers between devices, swap(): return lax.ppermute(value, axis, SWAP)  16.3 us
    pallas_call x1, Pallas kernels, read_other(): pl.pallas_call(functools.partial(read_other_kernel, zs, count), in_specs=...  3.18 us
    pallas_call x1, Pallas kernels, read_own(): pl.pallas_call(functools.partial(read_own_kernel, zs), in_specs=[SM] + [V...  2.56 us
  transfers between devices with their start and end apart: 31, of which 12 were waited for; matrix products, arithmetic and copies ran while one was open for 0% of the time, Pallas kernels for 24%

profile of v11, /device:TPU:0, one launch (start us, length us, event | category | flops | bytes accessed | tf_op | source)
XLA Modules:
  0.0 114.3 jit_solution(14192886275539374383)
XLA Ops:
  0.6 1.5 %fusion.1 = (bf16[256,512]{1,0:T(8,128)(2,1)S(1)}, bf16[256,512]{1,0:T(8,128)(2,1)S(1)}, bf16[256,512]{1,0:T(8,128)(2,1)S(1)}, bf16[256,512]{1,0:T(8,128)(2,1)S(...) fusion(bf16[512,1024]{1,0:T(8,128)(2,1)} %value.1, bf16[512,1024]{1,0:T(8,128)(2,1)} %key), kind=kLoop, calls=%fused_computation.9 | loop fusion | bytes 3145728 | tf_op jit(solution)/shard_map/slice | solution.py:457
  2.2 3.0 %collective-permute-start = (bf16[256,1024]{1,0:T(8,128)(2,1)S(1)}, bf16[256,1024]{1,0:T(8,128)(2,1)S(1)}, u32[]{:S(2)}, u32[]{:S(2)}) collective-permute-start(bf16[256,1024]{1,0:T(8,128)(2,1)S(1)} %maximum_select_fusion), channel_id=1, source_target_pairs={{0,2},{2,0},{1,3},{3,1},{4,6},{6,4},{5,7},{7,5},{8,10},{10,8},{9,1... | collective-permute-start | bytes 1572872 | tf_op jit(solution)/shard_map/ppermute | solution.py:442
  5.5 1.1 collective-permute-start.1
  6.6 1.8 %pack.1.own = bf16[512,1024]{1,0:T(8,128)(2,1)S(1)} custom-call(s32[3]{0:T(128)S(1)} %pad_add_fusion.where, bf16[512,1024]{1,0:T(8,128)(2,1)} %key, bf16[512,1024]{1,0:T(8,128)(2,1)} %value.1), custom_call_target="tpu_custom_call" | custom-call | tf_op jit(solution)/shard_map/pack/pallas_call | solution.py:105
  8.5 1.6 %pack_q.1 = bf16[528,512]{1,0:T(8,128)(2,1)S(1)} custom-call(s32[3]{0:T(128)S(1)} %pad_add_fusion.where, bf16[512,1024]{1,0:T(8,128)(2,1)} %query, f32[2,512]{1,0:T(2,128)S(1)} %copy-done), custom_call_target="tpu_custom_call" | custom-call | tf_op jit(solution)/shard_map/pack_q/pallas_call | solution.py:74
  10.3 1.1 copy-done.2
  11.9 6.2 %collective-permute-done.foreign.rest_0_.for_a = bf16[256,1024]{1,0:T(8,128)(2,1)S(1)} collective-permute-done((bf16[256,1024]{1,0:T(8,128)(2,1)S(1)}, bf16[256,1024]{1,0:T(8,128)(2,1)S(1)}, u32[]{:S(2)}, u32[]{:S(2)}) %collective-permute-start) | collective-permute-done | bytes 524320 | tf_op jit(solution)/shard_map/ppermute | solution.py:442
  18.0 0.6 pick.2
  18.7 2.1 %collective-permute-start.6 = (bf16[528,512]{1,0:T(8,128)(2,1)S(1)}, bf16[528,512]{1,0:T(8,128)(2,1)S(1)}, u32[]{:S(2)}, u32[]{:S(2)}) collective-permute-start(bf16[528,512]{1,0:T(8,128)(2,1)S(1)} %pack_q.1), channel_id=1, source_target_pairs={{0,2},{2,0},{1,3},{3,1},{4,6},{6,4},{5,7},{7,5},{8,10},{10,8},{9,1... | collective-permute-start | bytes 1622024 | tf_op jit(solution)/shard_map/ppermute | solution.py:442
  20.8 3.5 %collective-permute-start.5 = (bf16[256,1024]{1,0:T(8,128)(2,1)S(1)}, bf16[256,1024]{1,0:T(8,128)(2,1)S(1)}, u32[]{:S(2)}, u32[]{:S(2)}) collective-permute-start(bf16[256,1024]{1,0:T(8,128)(2,1)S(1)} %pick.2), channel_id=1, source_target_pairs={{0,4},{4,8},{8,12},{1,5},{5,9},{9,13},{2,6},{6,10},{10,14},{3,7},{... | collective-permute-start | bytes 1572872 | tf_op jit(solution)/shard_map/ppermute | solution.py:445
  24.4 3.7 %pre_own.1 = (bf16[512,512]{1,0:T(8,128)(2,1)S(1)}, bf16[512,512]{1,0:T(8,128)(2,1)S(1)}, f32[512,256]{1,0:T(8,128)S(1)}, f32[512,256]{1,0:T(8,128)S(1)}, bf16[5...) custom-call(s32[3]{0:T(128)S(1)} %pad_add_fusion.where, ...), custom_call_target="tpu_custom_call" | custom-call | tf_op jit(solution)/shard_map/pre_own/pallas_call | solution.py:55
  28.1 1.2 %collective-permute-done.1.foreign.rest_1_.for_b = bf16[256,1024]{1,0:T(8,128)(2,1)S(1)} collective-permute-done((bf16[256,1024]{1,0:T(8,128)(2,1)S(1)}, bf16[256,1024]{1,0:T(8,128)(2,1)S(1)}, u32[]{:S(2)}, u32[]{:S(2)}) %collective-permute-start.1) | collective-permute-done | bytes 524320 | tf_op jit(solution)/shard_map/ppermute | solution.py:442
  29.3 0.6 pick.3
  30.0 4.1 %collective-permute-start.7 = (bf16[256,1024]{1,0:T(8,128)(2,1)S(1)}, bf16[256,1024]{1,0:T(8,128)(2,1)S(1)}, u32[]{:S(2)}, u32[]{:S(2)}) collective-permute-start(bf16[256,1024]{1,0:T(8,128)(2,1)S(1)} %pick.3), channel_id=1, source_target_pairs={{0,4},{4,8},{8,12},{1,5},{5,9},{9,13},{2,6},{6,10},{10,14},{3,7},{... | collective-permute-start | bytes 1572872 | tf_op jit(solution)/shard_map/ppermute | solution.py:445
  34.0 2.6 %pre.2 = (bf16[512,512]{1,0:T(8,128)(2,1)S(1)}, bf16[512,512]{1,0:T(8,128)(2,1)S(1)}, f32[512,256]{1,0:T(8,128)S(1)}, f32[512,256]{1,0:T(8,128)S(1)}, bf16[512,5...) custom-call(s32[3]{0:T(128)S(1)} %pad_add_fusion.where, ...), custom_call_target="tpu_custom_call" | custom-call | tf_op jit(solution)/shard_map/pre/pallas_call | solution.py:55
  36.6 3.4 %collective-permute-done.6.q_for = bf16[528,512]{1,0:T(8,128)(2,1)S(1)} collective-permute-done((bf16[528,512]{1,0:T(8,128)(2,1)S(1)}, bf16[528,512]{1,0:T(8,128)(2,1)S(1)}, u32[]{:S(2)}, u32[]{:S(2)}) %collective-permute-start.6) | collective-permute-done | bytes 540704 | tf_op jit(solution)/shard_map/ppermute | solution.py:442
  40.0 2.8 %pre.3 = (bf16[512,512]{1,0:T(8,128)(2,1)S(1)}, bf16[512,512]{1,0:T(8,128)(2,1)S(1)}, f32[512,256]{1,0:T(8,128)S(1)}, f32[512,256]{1,0:T(8,128)S(1)}, bf16[512,5...) custom-call(s32[3]{0:T(128)S(1)} %pad_add_fusion.where, ...), custom_call_target="tpu_custom_call" | custom-call | tf_op jit(solution)/shard_map/pre/pallas_call | solution.py:55
  42.8 3.3 %attend_upper.1 = (bf16[512,512]{1,0:T(8,128)(2,1)S(1)}, bf16[512,512]{1,0:T(8,128)(2,1)S(1)}, bf16[512,1024]{1,0:T(8,128)(2,1)S(1)}, bf16[512,1024]{1,0:T(8,128)(2,1)S(1)}) custom-call(s32[3]{0:T(128)S(1)} %pad_add_fusion.where, bf16[512,512]{1,0:T(8,128)(2,1)S(1)} %get-tuple-element.98.q_own.rest_8_, bf16[528,512]{1,0:T(8,128)(2,1)S(1)} %collective-permute-done.6.q_for, ...), custom_call_target="tpu_custom_call" | custom-call | tf_op jit(solution)/shard_map/attend_upper/pallas_call | solution.py:55
  46.1 0.9 collective-permute-done.7.halo_b
  47.1 0.5 collective-permute-start.9
  47.6 1.4 %collective-permute-done.8.halo2_a = bf16[256,1024]{1,0:T(8,128)(2,1)S(1)} collective-permute-done((bf16[256,1024]{1,0:T(8,128)(2,1)S(1)}, bf16[256,1024]{1,0:T(8,128)(2,1)S(1)}, u32[]{:S(2)}, u32[]{:S(2)}) %collective-permute-start.8) | collective-permute-done | bytes 524320 | tf_op jit(solution)/shard_map/ppermute | solution.py:442
  49.0 0.7 collective-permute-done.9.halo2_b
  49.7 3.2 %attend_lower.1 = (bf16[512,512]{1,0:T(8,128)(2,1)S(1)}, bf16[512,512]{1,0:T(8,128)(2,1)S(1)}, bf16[512,512]{1,0:T(8,128)(2,1)S(1)}) custom-call(s32[3]{0:T(128)S(1)} %pad_add_fusion.where, bf16[512,512]{1,0:T(8,128)(2,1)S(1)} %get-tuple-element.98.q_own.rest_8_, bf16[528,512]{1,0:T(8,128)(2,1)S(1)} %collective-permute-done.6.q_for, f32[2,512]{1,0:T(2,128)S(1)} %copy-done, ...), custom_call_target="tpu_custom_call" | custom-call | tf_op jit(solution)/shard_map/attend_lower/pallas_call | solution.py:55
  53.2 2.3 %grad_first.1.before = f32[3,256,512]{2,1,0:T(8,128)S(1)} custom-call(s32[3]{0:T(128)S(1)} %pad_add_fusion.where, bf16[512,512]{1,0:T(8,128)(2,1)S(1)} %get-tuple-element.155.e0, bf16[512,512]{1,0:T(8,128)(2,1)S(1)} %collective-permute-done.11.e1, bf16[512,512]{1,0:T(8,128)(2,1)S(1)} %get-tuple-element.156.k0, bf16[512,512]{1,0:T(8,128)(2,1)S(1)} %get-tuple-element.157.k1, ...), custom_call_target="tpu_custom_call" | custom-call | tf_op jit(solution)/shard_map/grad_first/pallas_call | solution.py:55
  55.4 1.0 collective-permute-start.15
  56.4 2.5 %grad_second.1 = (f32[3,64,512]{2,1,0:T(8,128)S(1)}, bf16[3,64,512]{2,1,0:T(8,128)(2,1)S(1)}, bf16[3,64,512]{2,1,0:T(8,128)(2,1)S(1)}, bf16[3,64,512]{2,1,0:T(8,128)(2,1)S(1)}) custom-call(s32[3]{0:T(128)S(1)} %pad_add_fusion.where, bf16[512,512]{1,0:T(8,128)(2,1)S(1)} %get-tuple-element.145.e0, bf16[512,512]{1,0:T(8,128)(2,1)S(1)} %collective-permute-done.10.e1, ...), custom_call_target="tpu_custom_call" | custom-call | tf_op jit(solution)/shard_map/grad_second/pallas_call | solution.py:55
  58.9 2.1 %collective-permute-start.12 = (bf16[3,64,512]{2,1,0:T(8,128)(2,1)S(1)}, bf16[3,64,512]{2,1,0:T(8,128)(2,1)S(1)}, u32[]{:S(2)}, u32[]{:S(2)}) collective-permute-start(bf16[3,64,512]{2,1,0:T(8,128)(2,1)S(1)} %get-tuple-element.165), channel_id=1, source_target_pairs={{0,4},{4,8},{8,12},{12,0},{1,5},{5,9},{9,13},{13,1},{2,6},{6,10},{... | collective-permute-start | bytes 589832 | tf_op jit(solution)/shard_map/ppermute | solution.py:445
  61.0 2.6 %collective-permute-start.13 = (bf16[3,64,512]{2,1,0:T(8,128)(2,1)S(1)}, bf16[3,64,512]{2,1,0:T(8,128)(2,1)S(1)}, u32[]{:S(2)}, u32[]{:S(2)}) collective-permute-start(bf16[3,64,512]{2,1,0:T(8,128)(2,1)S(1)} %get-tuple-element.166), channel_id=1, source_target_pairs={{0,8},{4,12},{8,0},{12,4},{1,9},{5,13},{9,1},{13,5},{2,10},{6,14},... | collective-permute-start | bytes 589832 | tf_op jit(solution)/shard_map/ppermute | solution.py:445
  63.6 1.4 %collective-permute-start.14 = (bf16[3,64,512]{2,1,0:T(8,128)(2,1)S(1)}, bf16[3,64,512]{2,1,0:T(8,128)(2,1)S(1)}, u32[]{:S(2)}, u32[]{:S(2)}) collective-permute-start(bf16[3,64,512]{2,1,0:T(8,128)(2,1)S(1)} %get-tuple-element.167), channel_id=1, source_target_pairs={{0,12},{4,0},{8,4},{12,8},{1,13},{5,1},{9,5},{13,9},{2,14},{6,2},{... | collective-permute-start | bytes 589832 | tf_op jit(solution)/shard_map/ppermute | solution.py:445
  65.0 4.7 %collective-permute-done.15.rest_9_ = bf16[512,512]{1,0:T(8,128)(2,1)S(1)} collective-permute-done((bf16[512,512]{1,0:T(8,128)(2,1)S(1)}, bf16[512,512]{1,0:T(8,128)(2,1)S(1)}, u32[]{:S(2)}, u32[]{:S(2)}) %collective-permute-start.15) | collective-permute-done | bytes 524320 | tf_op jit(solution)/shard_map/ppermute | solution.py:442
  69.7 7.1 %collective-permute-done.13.rest_1_ = bf16[3,64,512]{2,1,0:T(8,128)(2,1)S(1)} collective-permute-done((bf16[3,64,512]{2,1,0:T(8,128)(2,1)S(1)}, bf16[3,64,512]{2,1,0:T(8,128)(2,1)S(1)}, u32[]{:S(2)}, u32[]{:S(2)}) %collective-permute-start.13) | collective-permute-done | bytes 196640 | tf_op jit(solution)/shard_map/ppermute | solution.py:445
  76.8 0.8 update.1.rest_0_
  77.6 5.7 %collective-permute-start.18 = (bf16[3,64,512]{2,1,0:T(8,128)(2,1)S(1)}, bf16[3,64,512]{2,1,0:T(8,128)(2,1)S(1)}, u32[]{:S(2)}, u32[]{:S(2)}) collective-permute-start(bf16[3,64,512]{2,1,0:T(8,128)(2,1)S(1)} %update.1.rest_0_), channel_id=1, source_target_pairs={{0,12},{4,0},{8,4},{12,8},{1,13},{5,1},{9,5},{13,9},{2,14},{6,2},{... | collective-permute-start | bytes 589832 | tf_op jit(solution)/shard_map/ppermute | solution.py:445
  83.3 1.5 %collective-permute-start.19 = (bf16[3,64,512]{2,1,0:T(8,128)(2,1)S(1)}, bf16[3,64,512]{2,1,0:T(8,128)(2,1)S(1)}, u32[]{:S(2)}, u32[]{:S(2)}) collective-permute-start(bf16[3,64,512]{2,1,0:T(8,128)(2,1)S(1)} %update.1.rest_0_), channel_id=1, source_target_pairs={{0,2},{2,0},{1,3},{3,1},{4,6},{6,4},{5,7},{7,5},{8,10},{10,8},{9,1... | collective-permute-start | bytes 589832 | tf_op jit(solution)/shard_map/ppermute | solution.py:442
  84.8 0.8 collective-permute-start.17
  85.7 3.0 %collective-permute-done.18.rest_3_ = bf16[3,64,512]{2,1,0:T(8,128)(2,1)S(1)} collective-permute-done((bf16[3,64,512]{2,1,0:T(8,128)(2,1)S(1)}, bf16[3,64,512]{2,1,0:T(8,128)(2,1)S(1)}, u32[]{:S(2)}, u32[]{:S(2)}) %collective-permute-start.18) | collective-permute-done | bytes 196640 | tf_op jit(solution)/shard_map/ppermute | solution.py:445
  88.7 1.5 %collective-permute-start.20 = (bf16[3,64,512]{2,1,0:T(8,128)(2,1)S(1)}, bf16[3,64,512]{2,1,0:T(8,128)(2,1)S(1)}, u32[]{:S(2)}, u32[]{:S(2)}) collective-permute-start(bf16[3,64,512]{2,1,0:T(8,128)(2,1)S(1)} %collective-permute-done.18.rest_3_), channel_id=1, source_target_pairs={{0,2},{2,0},{1,3},{3,1},{4,6},{6,4},{5,7},{7,5},{8,10},{10,8},{9,1... | collective-permute-start | bytes 589832 | tf_op jit(solution)/shard_map/ppermute | solution.py:442
  90.2 2.9 %collective-permute-done.16.rest_1_ = bf16[3,64,512]{2,1,0:T(8,128)(2,1)S(1)} collective-permute-done((bf16[3,64,512]{2,1,0:T(8,128)(2,1)S(1)}, bf16[3,64,512]{2,1,0:T(8,128)(2,1)S(1)}, u32[]{:S(2)}, u32[]{:S(2)}) %collective-permute-start.16) | collective-permute-done | bytes 196640 | tf_op jit(solution)/shard_map/ppermute | solution.py:445
  93.1 1.5 %collective-permute-start.21 = (bf16[3,64,512]{2,1,0:T(8,128)(2,1)S(1)}, bf16[3,64,512]{2,1,0:T(8,128)(2,1)S(1)}, u32[]{:S(2)}, u32[]{:S(2)}) collective-permute-start(bf16[3,64,512]{2,1,0:T(8,128)(2,1)S(1)} %collective-permute-done.16.rest_1_), channel_id=1, source_target_pairs={{0,2},{2,0},{1,3},{3,1},{4,6},{6,4},{5,7},{7,5},{8,10},{10,8},{9,1... | collective-permute-start | bytes 589832 | tf_op jit(solution)/shard_map/ppermute | solution.py:442
  94.6 6.7 %collective-permute-done.17.rest_2_ = bf16[3,64,512]{2,1,0:T(8,128)(2,1)S(1)} collective-permute-done((bf16[3,64,512]{2,1,0:T(8,128)(2,1)S(1)}, bf16[3,64,512]{2,1,0:T(8,128)(2,1)S(1)}, u32[]{:S(2)}, u32[]{:S(2)}) %collective-permute-start.17) | collective-permute-done | bytes 196640 | tf_op jit(solution)/shard_map/ppermute | solution.py:445
  101.2 1.5 %collective-permute-start.26 = (bf16[3,64,512]{2,1,0:T(8,128)(2,1)S(1)}, bf16[3,64,512]{2,1,0:T(8,128)(2,1)S(1)}, u32[]{:S(2)}, u32[]{:S(2)}) collective-permute-start(bf16[3,64,512]{2,1,0:T(8,128)(2,1)S(1)} %collective-permute-done.17.rest_2_), channel_id=1, source_target_pairs={{0,2},{2,0},{1,3},{3,1},{4,6},{6,4},{5,7},{7,5},{8,10},{10,8},{9,1... | collective-permute-start | bytes 589832 | tf_op jit(solution)/shard_map/ppermute | solution.py:442
  102.8 0.5 collective-permute-start.23
  103.4 0.4 collective-permute-start.25
  103.8 3.4 %collective-permute-done.26.rest_2_ = bf16[3,64,512]{2,1,0:T(8,128)(2,1)S(1)} collective-permute-done((bf16[3,64,512]{2,1,0:T(8,128)(2,1)S(1)}, bf16[3,64,512]{2,1,0:T(8,128)(2,1)S(1)}, u32[]{:S(2)}, u32[]{:S(2)}) %collective-permute-start.26) | collective-permute-done | bytes 196640 | tf_op jit(solution)/shard_map/ppermute | solution.py:442
  107.3 0.5 collective-permute-start.28
  107.9 0.4 collective-permute-start.30
  108.3 2.6 %read_own.1 = (bf16[512,1024]{1,0:T(8,128)(2,1)}, bf16[1536,512]{1,0:T(8,128)(2,1)S(1)}, bf16[512,512]{1,0:T(8,128)(2,1)S(1)}) custom-call(s32[3]{0:T(128)S(1)} %pad_add_fusion.where, bf16[3,64,512]{2,1,0:T(8,128)(2,1)S(1)} %update.1.rest_0_, bf16[3,64,512]{2,1,0:T(8,128)(2,1)S(1)} %collective-permute-done.16.rest_1_, ...), custom_call_target="tpu_custom_call" | custom-call | tf_op jit(solution)/shard_map/read_own/pallas_call | solution.py:388
  110.9 3.2 %read_other.1 = (bf16[512,1024]{1,0:T(8,128)(2,1)}, bf16[192,512]{1,0:T(8,128)(2,1)}) custom-call(s32[3]{0:T(128)S(1)} %pad_add_fusion.where, bf16[3,64,512]{2,1,0:T(8,128)(2,1)S(1)} %collective-permute-done.19.rest_0_, bf16[3,64,512]{2,1,0:T(8,128)(2,1)S(1)} %collective-permute-done.21.rest_1_, ...), custom_call_target="tpu_custom_call", output_to_operand_aliasing={{0}: (12, {})} | custom-call | tf_op jit(solution)/shard_map/read_other/pallas_call | solution.py:419
  (47 shorter events, 1.8 us)
Async XLA Ops:
  2.1 3.2 %copy-start.1 = (bf16[512,1024]{1,0:T(8,128)(2,1)S(1)}, bf16[512,1024]{1,0:T(8,128)(2,1)}, u32[]{:S(2)}) copy-start(bf16[512,1024]{1,0:T(8,128)(2,1)} %key) | copy-start | bytes 3145732
  2.2 15.8 %collective-permute-start = (bf16[256,1024]{1,0:T(8,128)(2,1)S(1)}, bf16[256,1024]{1,0:T(8,128)(2,1)S(1)}, u32[]{:S(2)}, u32[]{:S(2)}) collective-permute-start(bf16[256,1024]{1,0:T(8,128)(2,1)S(1)} %maximum_select_fusion), channel_id=1, source_target_pairs={{0,2},{2,0},{1,3},{3,1},{4,6},{6,4},{5,7},{7,5},{8,10},{10,8},{9,1... | collective-permute-start | bytes 1572872 | tf_op jit(solution)/shard_map/ppermute | solution.py:442
  5.5 23.8 %collective-permute-start.1 = (bf16[256,1024]{1,0:T(8,128)(2,1)S(1)}, bf16[256,1024]{1,0:T(8,128)(2,1)S(1)}, u32[]{:S(2)}, u32[]{:S(2)}) collective-permute-start(bf16[256,1024]{1,0:T(8,128)(2,1)S(1)} %maximum_select_fusion.1), channel_id=1, source_target_pairs={{0,2},{2,0},{1,3},{3,1},{4,6},{6,4},{5,7},{7,5},{8,10},{10,8},{9,1... | collective-permute-start | bytes 1572872 | tf_op jit(solution)/shard_map/ppermute | solution.py:442
  6.6 1.9 %copy-start = (f32[2,512]{1,0:T(2,128)S(1)}, f32[2,512]{1,0:T(2,128)}, u32[]{:S(2)}) copy-start(f32[2,512]{1,0:T(2,128)} %rates.5) | copy-start | bytes 12292
  6.6 3.5 %copy-start.4 = (bf16[1024,512]{1,0:T(8,128)(2,1)S(1)}, bf16[1024,512]{1,0:T(8,128)(2,1)}, u32[]{:S(2)}) copy-start(bf16[1024,512]{1,0:T(8,128)(2,1)} %param.12) | copy-start | bytes 3145732
  8.4 1.8 %copy-start.3 = (bf16[1024,512]{1,0:T(8,128)(2,1)S(1)}, bf16[1024,512]{1,0:T(8,128)(2,1)}, u32[]{:S(2)}) copy-start(bf16[1024,512]{1,0:T(8,128)(2,1)} %param.13) | copy-start | bytes 3145732
  8.4 16.0 %collective-permute-start.2 = (bf16[512,1024]{1,0:T(8,128)(2,1)S(1)}, bf16[512,1024]{1,0:T(8,128)(2,1)S(1)}, u32[]{:S(2)}, u32[]{:S(2)}) collective-permute-start(bf16[512,1024]{1,0:T(8,128)(2,1)S(1)} %pack.1.own), channel_id=1, source_target_pairs={{0,1},{1,0},{2,3},{3,2},{4,5},{5,4},{6,7},{7,6},{8,9},{9,8},{10,11... | collective-permute-start | bytes 3145736 | tf_op jit(solution)/shard_map/ppermute | solution.py:442
  10.1 1.2 %copy-start.2 = (bf16[512,1024]{1,0:T(8,128)(2,1)S(1)}, bf16[512,1024]{1,0:T(8,128)(2,1)}, u32[]{:S(2)}) copy-start(bf16[512,1024]{1,0:T(8,128)(2,1)} %query) | copy-start | bytes 3145732
  10.2 1.5 %copy-start.5 = (bf16[1024,512]{1,0:T(8,128)(2,1)S(1)}, bf16[1024,512]{1,0:T(8,128)(2,1)}, u32[]{:S(2)}) copy-start(bf16[1024,512]{1,0:T(8,128)(2,1)} %param.11) | copy-start | bytes 3145732
  18.6 10.6 %collective-permute-start.3 = (bf16[256,1024]{1,0:T(8,128)(2,1)S(1)}, bf16[256,1024]{1,0:T(8,128)(2,1)S(1)}, u32[]{:S(2)}, u32[]{:S(2)}) collective-permute-start(bf16[256,1024]{1,0:T(8,128)(2,1)S(1)} %collective-permute-done.foreign.rest_0_.for_a), channel_id=1, source_target_pairs={{0,1},{1,0},{2,3},{3,2},{4,5},{5,4},{6,7},{7,6},{8,9},{9,8},{10,11... | collective-permute-start | bytes 1572872 | tf_op jit(solution)/shard_map/ppermute | solution.py:442
  18.7 21.3 %collective-permute-start.6 = (bf16[528,512]{1,0:T(8,128)(2,1)S(1)}, bf16[528,512]{1,0:T(8,128)(2,1)S(1)}, u32[]{:S(2)}, u32[]{:S(2)}) collective-permute-start(bf16[528,512]{1,0:T(8,128)(2,1)S(1)} %pack_q.1), channel_id=1, source_target_pairs={{0,2},{2,0},{1,3},{3,1},{4,6},{6,4},{5,7},{7,5},{8,10},{10,8},{9,1... | collective-permute-start | bytes 1622024 | tf_op jit(solution)/shard_map/ppermute | solution.py:442
  20.8 15.8 %collective-permute-start.5 = (bf16[256,1024]{1,0:T(8,128)(2,1)S(1)}, bf16[256,1024]{1,0:T(8,128)(2,1)S(1)}, u32[]{:S(2)}, u32[]{:S(2)}) collective-permute-start(bf16[256,1024]{1,0:T(8,128)(2,1)S(1)} %pick.2), channel_id=1, source_target_pairs={{0,4},{4,8},{8,12},{1,5},{5,9},{9,13},{2,6},{6,10},{10,14},{3,7},{... | collective-permute-start | bytes 1572872 | tf_op jit(solution)/shard_map/ppermute | solution.py:445
  29.9 6.7 %collective-permute-start.4 = (bf16[256,1024]{1,0:T(8,128)(2,1)S(1)}, bf16[256,1024]{1,0:T(8,128)(2,1)S(1)}, u32[]{:S(2)}, u32[]{:S(2)}) collective-permute-start(bf16[256,1024]{1,0:T(8,128)(2,1)S(1)} %collective-permute-done.1.foreign.rest_1_.for_b), channel_id=1, source_target_pairs={{0,1},{1,0},{2,3},{3,2},{4,5},{5,4},{6,7},{7,6},{8,9},{9,8},{10,11... | collective-permute-start | bytes 1572872 | tf_op jit(solution)/shard_map/ppermute | solution.py:442
  30.0 17.1 %collective-permute-start.7 = (bf16[256,1024]{1,0:T(8,128)(2,1)S(1)}, bf16[256,1024]{1,0:T(8,128)(2,1)S(1)}, u32[]{:S(2)}, u32[]{:S(2)}) collective-permute-start(bf16[256,1024]{1,0:T(8,128)(2,1)S(1)} %pick.3), channel_id=1, source_target_pairs={{0,4},{4,8},{8,12},{1,5},{5,9},{9,13},{2,6},{6,10},{10,14},{3,7},{... | collective-permute-start | bytes 1572872 | tf_op jit(solution)/shard_map/ppermute | solution.py:445
  47.1 1.9 %collective-permute-start.8 = (bf16[256,1024]{1,0:T(8,128)(2,1)S(1)}, bf16[256,1024]{1,0:T(8,128)(2,1)S(1)}, u32[]{:S(2)}, u32[]{:S(2)}) collective-permute-start(bf16[256,1024]{1,0:T(8,128)(2,1)S(1)} %collective-permute-done.5.halo_a), channel_id=1, source_target_pairs={{0,1},{1,0},{2,3},{3,2},{4,5},{5,4},{6,7},{7,6},{8,9},{9,8},{10,11... | collective-permute-start | bytes 1572872 | tf_op jit(solution)/shard_map/ppermute | solution.py:442
  47.1 2.7 %collective-permute-start.9 = (bf16[256,1024]{1,0:T(8,128)(2,1)S(1)}, bf16[256,1024]{1,0:T(8,128)(2,1)S(1)}, u32[]{:S(2)}, u32[]{:S(2)}) collective-permute-start(bf16[256,1024]{1,0:T(8,128)(2,1)S(1)} %collective-permute-done.7.halo_b), channel_id=1, source_target_pairs={{0,1},{1,0},{2,3},{3,2},{4,5},{5,4},{6,7},{7,6},{8,9},{9,8},{10,11... | collective-permute-start | bytes 1572872 | tf_op jit(solution)/shard_map/ppermute | solution.py:442
  47.6 5.6 %collective-permute-start.11 = (bf16[512,512]{1,0:T(8,128)(2,1)S(1)}, bf16[512,512]{1,0:T(8,128)(2,1)S(1)}, u32[]{:S(2)}, u32[]{:S(2)}) collective-permute-start(bf16[512,512]{1,0:T(8,128)(2,1)S(1)} %get-tuple-element.155.e0), channel_id=1, source_target_pairs={{0,1},{1,0},{2,3},{3,2},{4,5},{5,4},{6,7},{7,6},{8,9},{9,8},{10,11... | collective-permute-start | bytes 1572872 | tf_op jit(solution)/shard_map/ppermute | solution.py:442
  53.0 3.5 %collective-permute-start.10 = (bf16[512,512]{1,0:T(8,128)(2,1)S(1)}, bf16[512,512]{1,0:T(8,128)(2,1)S(1)}, u32[]{:S(2)}, u32[]{:S(2)}) collective-permute-start(bf16[512,512]{1,0:T(8,128)(2,1)S(1)} %get-tuple-element.145.e0), channel_id=1, source_target_pairs={{0,1},{1,0},{2,3},{3,2},{4,5},{5,4},{6,7},{7,6},{8,9},{9,8},{10,11... | collective-permute-start | bytes 1572872 | tf_op jit(solution)/shard_map/ppermute | solution.py:442
  55.4 14.3 %collective-permute-start.15 = (bf16[512,512]{1,0:T(8,128)(2,1)S(1)}, bf16[512,512]{1,0:T(8,128)(2,1)S(1)}, u32[]{:S(2)}, u32[]{:S(2)}) collective-permute-start(bf16[512,512]{1,0:T(8,128)(2,1)S(1)} %get-tuple-element.169), channel_id=1, source_target_pairs={{0,2},{2,0},{1,3},{3,1},{4,6},{6,4},{5,7},{7,5},{8,10},{10,8},{9,1... | collective-permute-start | bytes 1572872 | tf_op jit(solution)/shard_map/ppermute | solution.py:442
  58.9 10.8 %collective-permute-start.12 = (bf16[3,64,512]{2,1,0:T(8,128)(2,1)S(1)}, bf16[3,64,512]{2,1,0:T(8,128)(2,1)S(1)}, u32[]{:S(2)}, u32[]{:S(2)}) collective-permute-start(bf16[3,64,512]{2,1,0:T(8,128)(2,1)S(1)} %get-tuple-element.165), channel_id=1, source_target_pairs={{0,4},{4,8},{8,12},{12,0},{1,5},{5,9},{9,13},{13,1},{2,6},{6,10},{... | collective-permute-start | bytes 589832 | tf_op jit(solution)/shard_map/ppermute | solution.py:445
  61.0 15.8 %collective-permute-start.13 = (bf16[3,64,512]{2,1,0:T(8,128)(2,1)S(1)}, bf16[3,64,512]{2,1,0:T(8,128)(2,1)S(1)}, u32[]{:S(2)}, u32[]{:S(2)}) collective-permute-start(bf16[3,64,512]{2,1,0:T(8,128)(2,1)S(1)} %get-tuple-element.166), channel_id=1, source_target_pairs={{0,8},{4,12},{8,0},{12,4},{1,9},{5,13},{9,1},{13,5},{2,10},{6,14},... | collective-permute-start | bytes 589832 | tf_op jit(solution)/shard_map/ppermute | solution.py:445
  63.6 13.2 %collective-permute-start.14 = (bf16[3,64,512]{2,1,0:T(8,128)(2,1)S(1)}, bf16[3,64,512]{2,1,0:T(8,128)(2,1)S(1)}, u32[]{:S(2)}, u32[]{:S(2)}) collective-permute-start(bf16[3,64,512]{2,1,0:T(8,128)(2,1)S(1)} %get-tuple-element.167), channel_id=1, source_target_pairs={{0,12},{4,0},{8,4},{12,8},{1,13},{5,1},{9,5},{13,9},{2,14},{6,2},{... | collective-permute-start | bytes 589832 | tf_op jit(solution)/shard_map/ppermute | solution.py:445
  77.6 11.1 %collective-permute-start.18 = (bf16[3,64,512]{2,1,0:T(8,128)(2,1)S(1)}, bf16[3,64,512]{2,1,0:T(8,128)(2,1)S(1)}, u32[]{:S(2)}, u32[]{:S(2)}) collective-permute-start(bf16[3,64,512]{2,1,0:T(8,128)(2,1)S(1)} %update.1.rest_0_), channel_id=1, source_target_pairs={{0,12},{4,0},{8,4},{12,8},{1,13},{5,1},{9,5},{13,9},{2,14},{6,2},{... | collective-permute-start | bytes 589832 | tf_op jit(solution)/shard_map/ppermute | solution.py:445
  83.3 9.7 %collective-permute-start.16 = (bf16[3,64,512]{2,1,0:T(8,128)(2,1)S(1)}, bf16[3,64,512]{2,1,0:T(8,128)(2,1)S(1)}, u32[]{:S(2)}, u32[]{:S(2)}) collective-permute-start(bf16[3,64,512]{2,1,0:T(8,128)(2,1)S(1)} %update.1.rest_0_), channel_id=1, source_target_pairs={{0,4},{4,8},{8,12},{12,0},{1,5},{5,9},{9,13},{13,1},{2,6},{6,10},{... | collective-permute-start | bytes 589832 | tf_op jit(solution)/shard_map/ppermute | solution.py:445
  83.3 19.4 %collective-permute-start.19 = (bf16[3,64,512]{2,1,0:T(8,128)(2,1)S(1)}, bf16[3,64,512]{2,1,0:T(8,128)(2,1)S(1)}, u32[]{:S(2)}, u32[]{:S(2)}) collective-permute-start(bf16[3,64,512]{2,1,0:T(8,128)(2,1)S(1)} %update.1.rest_0_), channel_id=1, source_target_pairs={{0,2},{2,0},{1,3},{3,1},{4,6},{6,4},{5,7},{7,5},{8,10},{10,8},{9,1... | collective-permute-start | bytes 589832 | tf_op jit(solution)/shard_map/ppermute | solution.py:442
  84.8 16.4 %collective-permute-start.17 = (bf16[3,64,512]{2,1,0:T(8,128)(2,1)S(1)}, bf16[3,64,512]{2,1,0:T(8,128)(2,1)S(1)}, u32[]{:S(2)}, u32[]{:S(2)}) collective-permute-start(bf16[3,64,512]{2,1,0:T(8,128)(2,1)S(1)} %update.1.rest_0_), channel_id=1, source_target_pairs={{0,8},{4,12},{8,0},{12,4},{1,9},{5,13},{9,1},{13,5},{2,10},{6,14},... | collective-permute-start | bytes 589832 | tf_op jit(solution)/shard_map/ppermute | solution.py:445
  88.7 14.0 %collective-permute-start.20 = (bf16[3,64,512]{2,1,0:T(8,128)(2,1)S(1)}, bf16[3,64,512]{2,1,0:T(8,128)(2,1)S(1)}, u32[]{:S(2)}, u32[]{:S(2)}) collective-permute-start(bf16[3,64,512]{2,1,0:T(8,128)(2,1)S(1)} %collective-permute-done.18.rest_3_), channel_id=1, source_target_pairs={{0,2},{2,0},{1,3},{3,1},{4,6},{6,4},{5,7},{7,5},{8,10},{10,8},{9,1... | collective-permute-start | bytes 589832 | tf_op jit(solution)/shard_map/ppermute | solution.py:442
  93.1 9.7 %collective-permute-start.21 = (bf16[3,64,512]{2,1,0:T(8,128)(2,1)S(1)}, bf16[3,64,512]{2,1,0:T(8,128)(2,1)S(1)}, u32[]{:S(2)}, u32[]{:S(2)}) collective-permute-start(bf16[3,64,512]{2,1,0:T(8,128)(2,1)S(1)} %collective-permute-done.16.rest_1_), channel_id=1, source_target_pairs={{0,2},{2,0},{1,3},{3,1},{4,6},{6,4},{5,7},{7,5},{8,10},{10,8},{9,1... | collective-permute-start | bytes 589832 | tf_op jit(solution)/shard_map/ppermute | solution.py:442
  101.2 6.0 %collective-permute-start.26 = (bf16[3,64,512]{2,1,0:T(8,128)(2,1)S(1)}, bf16[3,64,512]{2,1,0:T(8,128)(2,1)S(1)}, u32[]{:S(2)}, u32[]{:S(2)}) collective-permute-start(bf16[3,64,512]{2,1,0:T(8,128)(2,1)S(1)} %collective-permute-done.17.rest_2_), channel_id=1, source_target_pairs={{0,2},{2,0},{1,3},{3,1},{4,6},{6,4},{5,7},{7,5},{8,10},{10,8},{9,1... | collective-permute-start | bytes 589832 | tf_op jit(solution)/shard_map/ppermute | solution.py:442
  102.7 4.5 %collective-permute-start.22 = (bf16[3,64,512]{2,1,0:T(8,128)(2,1)S(1)}, bf16[3,64,512]{2,1,0:T(8,128)(2,1)S(1)}, u32[]{:S(2)}, u32[]{:S(2)}) collective-permute-start(bf16[3,64,512]{2,1,0:T(8,128)(2,1)S(1)} %update.1.rest_0_), channel_id=1, source_target_pairs={{0,1},{1,0},{2,3},{3,2},{4,5},{5,4},{6,7},{7,6},{8,9},{9,8},{10,11... | collective-permute-start | bytes 589832 | tf_op jit(solution)/shard_map/ppermute | solution.py:442
  102.8 4.4 %collective-permute-start.23 = (bf16[3,64,512]{2,1,0:T(8,128)(2,1)S(1)}, bf16[3,64,512]{2,1,0:T(8,128)(2,1)S(1)}, u32[]{:S(2)}, u32[]{:S(2)}) collective-permute-start(bf16[3,64,512]{2,1,0:T(8,128)(2,1)S(1)} %collective-permute-done.16.rest_1_), channel_id=1, source_target_pairs={{0,1},{1,0},{2,3},{3,2},{4,5},{5,4},{6,7},{7,6},{8,9},{9,8},{10,11... | collective-permute-start | bytes 589832 | tf_op jit(solution)/shard_map/ppermute | solution.py:442
  103.3 3.9 %collective-permute-start.24 = (bf16[3,64,512]{2,1,0:T(8,128)(2,1)S(1)}, bf16[3,64,512]{2,1,0:T(8,128)(2,1)S(1)}, u32[]{:S(2)}, u32[]{:S(2)}) collective-permute-start(bf16[3,64,512]{2,1,0:T(8,128)(2,1)S(1)} %collective-permute-done.17.rest_2_), channel_id=1, source_target_pairs={{0,1},{1,0},{2,3},{3,2},{4,5},{5,4},{6,7},{7,6},{8,9},{9,8},{10,11... | collective-permute-start | bytes 589832 | tf_op jit(solution)/shard_map/ppermute | solution.py:442
  103.4 3.9 %collective-permute-start.25 = (bf16[3,64,512]{2,1,0:T(8,128)(2,1)S(1)}, bf16[3,64,512]{2,1,0:T(8,128)(2,1)S(1)}, u32[]{:S(2)}, u32[]{:S(2)}) collective-permute-start(bf16[3,64,512]{2,1,0:T(8,128)(2,1)S(1)} %collective-permute-done.18.rest_3_), channel_id=1, source_target_pairs={{0,1},{1,0},{2,3},{3,2},{4,5},{5,4},{6,7},{7,6},{8,9},{9,8},{10,11... | collective-permute-start | bytes 589832 | tf_op jit(solution)/shard_map/ppermute | solution.py:442
  107.2 3.7 %collective-permute-start.27 = (bf16[3,64,512]{2,1,0:T(8,128)(2,1)S(1)}, bf16[3,64,512]{2,1,0:T(8,128)(2,1)S(1)}, u32[]{:S(2)}, u32[]{:S(2)}) collective-permute-start(bf16[3,64,512]{2,1,0:T(8,128)(2,1)S(1)} %collective-permute-done.19.rest_0_), channel_id=1, source_target_pairs={{0,1},{1,0},{2,3},{3,2},{4,5},{5,4},{6,7},{7,6},{8,9},{9,8},{10,11... | collective-permute-start | bytes 589832 | tf_op jit(solution)/shard_map/ppermute | solution.py:442
  107.3 3.6 %collective-permute-start.28 = (bf16[3,64,512]{2,1,0:T(8,128)(2,1)S(1)}, bf16[3,64,512]{2,1,0:T(8,128)(2,1)S(1)}, u32[]{:S(2)}, u32[]{:S(2)}) collective-permute-start(bf16[3,64,512]{2,1,0:T(8,128)(2,1)S(1)} %collective-permute-done.21.rest_1_), channel_id=1, source_target_pairs={{0,1},{1,0},{2,3},{3,2},{4,5},{5,4},{6,7},{7,6},{8,9},{9,8},{10,11... | collective-permute-start | bytes 589832 | tf_op jit(solution)/shard_map/ppermute | solution.py:442
  107.8 3.1 %collective-permute-start.29 = (bf16[3,64,512]{2,1,0:T(8,128)(2,1)S(1)}, bf16[3,64,512]{2,1,0:T(8,128)(2,1)S(1)}, u32[]{:S(2)}, u32[]{:S(2)}) collective-permute-start(bf16[3,64,512]{2,1,0:T(8,128)(2,1)S(1)} %collective-permute-done.26.rest_2_), channel_id=1, source_target_pairs={{0,1},{1,0},{2,3},{3,2},{4,5},{5,4},{6,7},{7,6},{8,9},{9,8},{10,11... | collective-permute-start | bytes 589832 | tf_op jit(solution)/shard_map/ppermute | solution.py:442
  107.9 3.0 %collective-permute-start.30 = (bf16[3,64,512]{2,1,0:T(8,128)(2,1)S(1)}, bf16[3,64,512]{2,1,0:T(8,128)(2,1)S(1)}, u32[]{:S(2)}, u32[]{:S(2)}) collective-permute-start(bf16[3,64,512]{2,1,0:T(8,128)(2,1)S(1)} %collective-permute-done.20.rest_3_), channel_id=1, source_target_pairs={{0,1},{1,0},{2,3},{3,2},{4,5},{5,4},{6,7},{7,6},{8,9},{9,8},{10,11... | collective-permute-start | bytes 589832 | tf_op jit(solution)/shard_map/ppermute | solution.py:442
